TPU v7x, 32 devices: a whole 2x2x4 slice. The times are simulated.
32 devices in a mesh: groups: 2 (over y), ctx: 4 (over z), fsdp: 2 (over x), head: 2 (over core).
Axes of the slice: x: 2, y: 2, z: 4, core: 2. Of those that a mesh axis runs over, the one named last changes fastest.
Arguments:
- tokens: bfloat16 [1024, 2304], P(('groups', 'ctx')), parts along dimension 0, may hold values from -6 to 6
- w_query: bfloat16 [2304, 4096], P('ctx', ('fsdp', 'head')), may hold values from -0.125 to 0.125
- w_key: bfloat16 [2304, 4096], P('ctx', ('fsdp', 'head')), may hold values from -0.125 to 0.125
- w_value: bfloat16 [2304, 4096], P('ctx', ('fsdp', 'head')), may hold values from -0.125 to 0.125
- beta_logit: float32 [32, 1024], P(('fsdp', 'head'), ('groups', 'ctx')), parts along dimension 1, may hold values from -6 to 6
- log_decay: float32 [1024, 4096], P(('groups', 'ctx'), ('fsdp', 'head')), parts along dimension 0, may hold values from -0.6 to 0, as said below
- grad_out: bfloat16 [1024, 4096], P(('groups', 'ctx'), ('fsdp', 'head')), parts along dimension 0, may hold values from -6 to 6
Outputs:
- attn_out: bfloat16 [1024, 4096], P(('groups', 'ctx'), ('fsdp', 'head')), parts along dimension 0
- grad_w_query: float32 [4608, 4096], P(('groups', 'ctx'), ('fsdp', 'head')), parts along dimension 0
- grad_w_key: float32 [4608, 4096], P(('groups', 'ctx'), ('fsdp', 'head')), parts along dimension 0
- grad_w_value: float32 [4608, 4096], P(('groups', 'ctx'), ('fsdp', 'head')), parts along dimension 0
- grad_beta: float32 [32, 1024], P(('fsdp', 'head'), ('groups', 'ctx')), parts along dimension 1
- grad_decay: float32 [1024, 4096], P(('groups', 'ctx'), ('fsdp', 'head')), parts along dimension 0
There are 2 independent parts, one for each index of `groups`. A program takes and returns all parts, laid end to end along the dimension named above; an argument that names none is the same for every part. Nothing has to cross between parts.
Inputs may be any that keep to these rules, and one draw needn't show every extreme that they name: `log_decay`: every entry is at most zero.
All inputs are finite; a program needn't handle non-finite values.
Results may differ from a plain program's by a relative error of at most 0.014.
Values may be sent and summed in bfloat16 or wider, within the bound.
No kernel may reach another device: no remote copies, remote signals or barrier semaphores. Data moves between devices by JAX's collectives and lax.ppermute only.
A program may use at most 128 MiB of HBM per device.

v0:
```python
import jax
import jax.numpy as jnp
from jax import lax
from jax.sharding import PartitionSpec as P

DK = 128
DV = 128
SPAN = 64


epsilon = 1e-06


def prefix_2(x, axis, join, neutral, backward):
    count = lax.axis_size(axis)
    place = lax.axis_index(axis)
    ahead = count - 1 - place if backward else place
    gathered = jax.tree.map(
        lambda a, kind: lax.all_gather(a.astype(kind), axis), x, (jnp.bfloat16, jnp.bfloat16)
    )
    state = jax.tree.map(lambda a, e: jnp.zeros_like(a) + jnp.asarray(e, a.dtype), x, neutral)

    def one(hop, state):
        source = count - 1 - hop if backward else hop
        return join(
            state,
            jax.tree.map(
                lambda a, own: lax.dynamic_index_in_dim(a, source, 0, False).astype(own.dtype),
                gathered,
                x,
            ),
        )

    return lax.fori_loop(0, ahead, one, state)


def normalize(vectors):
    return vectors * lax.rsqrt(jnp.sum(vectors * vectors, axis=-1, keepdims=True) + epsilon)


def heads_first(matrix, heads):
    return matrix.reshape(matrix.shape[0], heads, -1).transpose(1, 0, 2)


def span_step(memory, queries, key_vecs, val_vecs, strength, forgetting_exponent):
    largest_value = lax.Precision.HIGHEST
    length = queries.shape[1]
    cumulate = jnp.cumsum(forgetting_exponent, axis=1)
    growth = jnp.exp(cumulate)
    shrink = jnp.exp(-cumulate)
    key_up = key_vecs * growth
    key_down = key_vecs * shrink
    query_up = queries * growth
    row_ids = lax.broadcasted_iota(jnp.int32, (length, length), 0)
    col_ids = lax.broadcasted_iota(jnp.int32, (length, length), 1)
    strict = (row_ids > col_ids).astype(jnp.float32)
    within = (row_ids >= col_ids).astype(jnp.float32)
    affinity = jnp.einsum("bcd,bsd->bcs", key_up, key_down, precision=largest_value) * strict
    system = jnp.eye(length, dtype=jnp.float32) + strength[:, :, None] * affinity
    target = strength[:, :, None] * (
        val_vecs - jnp.einsum("bcd,bdw->bcw", key_up, memory, precision=largest_value)
    )
    update = lax.linalg.triangular_solve(system, target, left_side=True, lower=True)
    scores = jnp.einsum("bcd,bsd->bcs", query_up, key_down, precision=largest_value) * within
    emitted = jnp.einsum("bcd,bdw->bcw", query_up, memory, precision=largest_value)
    emitted = emitted + jnp.einsum("bcs,bsw->bcw", scores, update, precision=largest_value)
    at_end = growth[:, -1, :]
    renewed = at_end[:, :, None] * memory + jnp.einsum(
        "bsd,bsw->bdw", key_down * at_end[:, None, :], update, precision=largest_value
    )
    return (emitted, renewed)


def scan_spans(memory, queries, key_vecs, val_vecs, strength, forgetting_exponent):
    count = queries.shape[1] // SPAN

    def to_blocks(array):
        shaped = array.reshape((array.shape[0], count, SPAN) + array.shape[2:])
        return jnp.swapaxes(shaped, 0, 1)

    def advance(carried, blocks):
        emitted, renewed = span_step(carried, *blocks)
        return (renewed, emitted)

    blocks = (
        to_blocks(queries),
        to_blocks(key_vecs),
        to_blocks(val_vecs),
        to_blocks(strength),
        to_blocks(forgetting_exponent),
    )
    final, emitted = lax.scan(advance, memory, blocks)
    emitted = jnp.swapaxes(emitted, 0, 1)
    return (emitted.reshape(emitted.shape[0], count * SPAN, emitted.shape[-1]), final)


def compose(earlier, later):
    largest_value = lax.Precision.HIGHEST
    joined = jnp.einsum("hij,hjk->hik", later[0], earlier[0], precision=largest_value)
    shifted = jnp.einsum("hij,hjv->hiv", later[0], earlier[1], precision=largest_value) + later[1]
    return (joined, shifted)


def per_device(tokens, w_query, w_key, w_value, beta_logit, log_decay, grad_out):
    largest_value = lax.Precision.HIGHEST
    length = tokens.shape[0]
    columns = w_query.shape[1]
    heads = columns // DK
    shard_rows = (
        lax.all_gather(w_query, "ctx", axis=0, tiled=True),
        lax.all_gather(w_key, "ctx", axis=0, tiled=True),
        lax.all_gather(w_value, "ctx", axis=0, tiled=True),
    )
    window = tokens
    query_raw, key_raw, value_raw = tuple(
        (jnp.dot(window, weights, preferred_element_type=jnp.float32) for weights in shard_rows)
    )

    def shard_pass(query_in, key_in, value_in, logits, log_gates):
        queries = normalize(heads_first(query_in, heads))
        key_vecs = normalize(heads_first(key_in, heads))
        val_vecs = heads_first(value_in, heads)
        widened = jnp.concatenate([jnp.zeros((heads, length, DK), jnp.float32), val_vecs], axis=2)
        initial = jnp.concatenate(
            [
                jnp.broadcast_to(jnp.eye(DK, dtype=jnp.float32), (heads, DK, DK)),
                jnp.zeros((heads, DK, DV), jnp.float32),
            ],
            axis=2,
        )
        return scan_spans(
            initial,
            queries,
            key_vecs,
            widened,
            jax.nn.sigmoid(logits),
            heads_first(log_gates, heads),
        )

    (mixed, final), pullback = jax.vjp(
        shard_pass, query_raw, key_raw, value_raw, beta_logit, log_decay
    )
    transit = final[:, :, :DK]
    offset = final[:, :, DK:]
    query_carried_over = mixed[:, :, :DK]
    local_output = mixed[:, :, DK:]
    output_cotangent = grad_out.reshape(length, heads, DV).transpose(1, 0, 2).astype(jnp.float32)
    contribution = jnp.einsum(
        "mij,mif->mjf", query_carried_over, output_cotangent, precision=largest_value
    )
    identity = (
        jnp.broadcast_to(jnp.eye(DK, dtype=jnp.float32), (heads, DK, DK)),
        jnp.zeros((heads, DK, DV), jnp.float32),
    )
    prefix = prefix_2((transit, offset), "ctx", compose, identity, False)
    incoming_state = prefix[1]
    suffix = prefix_2((jnp.swapaxes(transit, 1, 2), contribution), "ctx", compose, identity, True)
    adjoint_state = suffix[1]
    complete_output = local_output + jnp.einsum(
        "npg,ngj->npj", query_carried_over, incoming_state, precision=largest_value
    )
    attn_out = complete_output.transpose(1, 0, 2).reshape(length, heads * DV).astype(jnp.bfloat16)
    d_mixed = jnp.concatenate(
        [
            jnp.einsum("efu,egu->efg", output_cotangent, incoming_state, precision=largest_value),
            output_cotangent,
        ],
        axis=2,
    )
    d_final = jnp.concatenate(
        [
            jnp.einsum("pgx,pcx->pgc", adjoint_state, incoming_state, precision=largest_value),
            adjoint_state,
        ],
        axis=2,
    )
    d_query, d_key, d_value, grad_beta, grad_decay = pullback((d_mixed, d_final))
    grad_projected = jnp.concatenate([d_query, d_key, d_value], axis=1).astype(jnp.bfloat16)
    window = tokens
    summed = lax.psum_scatter(
        jnp.einsum("td,tc->dc", window, grad_projected, preferred_element_type=jnp.float32).astype(
            jnp.bfloat16
        ),
        "ctx",
        scatter_dimension=0,
        tiled=True,
    ).astype(jnp.float32)
    return (
        attn_out,
        summed[:, :columns],
        summed[:, columns : 2 * columns],
        summed[:, 2 * columns :],
        grad_beta,
        grad_decay,
    )


def solution(mesh):
    return jax.shard_map(
        per_device,
        mesh=mesh,
        in_specs=(
            P(("groups", "ctx"), None),
            P("ctx", ("fsdp", "head")),
            P("ctx", ("fsdp", "head")),
            P("ctx", ("fsdp", "head")),
            P(("fsdp", "head"), ("groups", "ctx")),
            P(("groups", "ctx"), ("fsdp", "head")),
            P(("groups", "ctx"), ("fsdp", "head")),
        ),
        out_specs=(
            P(("groups", "ctx"), ("fsdp", "head")),
            P(("groups", "ctx"), ("fsdp", "head")),
            P(("groups", "ctx"), ("fsdp", "head")),
            P(("groups", "ctx"), ("fsdp", "head")),
            P(("fsdp", "head"), ("groups", "ctx")),
            P(("groups", "ctx"), ("fsdp", "head")),
        ),
        check_vma=False,
    )
```

profile of v0, /device:TPU:0, one launch (start us, length us, event | category | flops | bytes accessed | tf_op | source)
XLA Modules:
  0.0 981.4 jit_solution(2539370356951474262)
XLA Ops:
  10.7 91.0 %all-gather.14.cloned.1.call-done = bf16[2304,1024]{1,0:T(8,128)(2,1)} async-done(((bf16[576,1024]{1,0:T(8,128)(2,1)}), bf16[2304,1024]{1,0:T(8,128)(2,1)}) %all-gather.14.cloned.1.call-update) | async-done | bytes 4718608 | tf_op jit(solution)/shard_map/all_gather | solution.py:112
  101.8 3.1 convolution_bitcast_fusion.2
  104.9 86.3 %all-gather.12.cloned.1.call-done = bf16[2304,1024]{1,0:T(8,128)(2,1)} async-done(((bf16[576,1024]{1,0:T(8,128)(2,1)}), bf16[2304,1024]{1,0:T(8,128)(2,1)}) %all-gather.12.cloned.1.call-update) | async-done | bytes 4718608 | tf_op jit(solution)/shard_map/all_gather | solution.py:111
  191.2 3.1 convolution_bitcast_fusion.3
  196.1 84.6 %all-gather.16.cloned.1.call-done = bf16[2304,1024]{1,0:T(8,128)(2,1)} async-done(((bf16[576,1024]{1,0:T(8,128)(2,1)}), bf16[2304,1024]{1,0:T(8,128)(2,1)}) %all-gather.16.cloned.1.call-update) | async-done | bytes 4718608 | tf_op jit(solution)/shard_map/all_gather | solution.py:110
  280.7 3.1 convolution_bitcast_fusion.1
  291.3 118.0 %while.99 = (s32[]{:T(128)}, f32[8,128,256]{2,1,0:T(8,128)S(1)}, f32[2,8,64,256]{3,2,1,0:T(8,128)}, f32[2,8,64,128]{3,1,2,0:T(8,128)}, f32[2,8,64,128]{3,1,2,0:T...) while((s32[]{:T(128)}, f32[8,128,256]{2,1,0:T(8,128)S(1)}, ...), condition=%wide.region_4.5_spmd.clone, body=%wide.region_2.4_spmd.clone.sunk | while | flops 911929344 | bytes 61819628 | solution.py:92
  301.3 40.7 %custom-call.30 = f32[8,1,64,64]{2,3,1,0:T(8,128)} custom-call(f32[8,1,64,64]{3,2,1,0:T(8,128)} %select_bitcast_fusion.4), custom_call_target="InvertDiagBlocksLowerTriangular" | custom-call | tf_op jit(solution)/shard_map/jvp()/while/body/eval_jaxpr/triangular_solve | solution.py:63
  360.3 40.7 %custom-call.30 = f32[8,1,64,64]{2,3,1,0:T(8,128)} custom-call(f32[8,1,64,64]{3,2,1,0:T(8,128)} %select_bitcast_fusion.4), custom_call_target="InvertDiagBlocksLowerTriangular" | custom-call | tf_op jit(solution)/shard_map/jvp()/while/body/eval_jaxpr/triangular_solve | solution.py:63
  418.1 18.8 %all-gather.18.cloned.1.call-done = bf16[32,128,128]{2,1,0:T(8,128)(2,1)} async-done(((bf16[8,128,128]{2,1,0:T(8,128)(2,1)}), bf16[32,128,128]{2,1,0:T(8,128)(2,1)}) %all-gather.18.cloned.1.call-update) | async-done | bytes 1048592 | tf_op jit(solution)/shard_map/all_gather | solution.py:19
  436.9 29.4 %all-gather.20.cloned.1.call-done = bf16[32,128,128]{2,1,0:T(8,128)(2,1)} async-done(((bf16[8,128,128]{2,1,0:T(8,128)(2,1)}), bf16[32,128,128]{2,1,0:T(8,128)(2,1)}) %all-gather.20.cloned.1.call-update) | async-done | bytes 1048592 | tf_op jit(solution)/shard_map/all_gather | solution.py:19
  466.5 28.8 %all-gather.22.cloned.1.call-done = bf16[32,128,128]{2,1,0:T(8,128)(2,1)} async-done(((bf16[8,128,128]{2,1,0:T(8,128)(2,1)}), bf16[32,128,128]{2,1,0:T(8,128)(2,1)}) %all-gather.22.cloned.1.call-update) | async-done | bytes 1048592 | tf_op jit(solution)/shard_map/all_gather | solution.py:19
  495.3 29.0 %all-gather.24.cloned.1.call-done = bf16[32,128,128]{2,1,0:T(8,128)(2,1)} async-done(((bf16[8,128,128]{2,1,0:T(8,128)(2,1)}), bf16[32,128,128]{2,1,0:T(8,128)(2,1)}) %all-gather.24.cloned.1.call-update) | async-done | bytes 1048592 | tf_op jit(solution)/shard_map/all_gather | solution.py:19
  524.3 4.5 while.98
  531.9 2.1 pad_maximum_fusion.1
  539.0 146.1 %while.100 = (s32[]{:T(128)}, f32[8,128,256]{2,1,0:T(8,128)S(1)}, f32[2,8,64,128]{3,2,0,1:T(8,128)}, f32[2,8,64,128]{3,2,0,1:T(8,128)}, bf16[2,8,64,256]{3,2,0,1...) while((s32[]{:T(128)}, f32[8,128,256]{2,1,0:T(8,128)S(1)}, ...), condition=%wide.region_15.16_spmd.clone, body=%wide.region_9.15_spmd.clone.sunk | while | flops 1845250560 | bytes 78595960 | solution.py:92
  545.3 2.1 convolution_add_fusion.24
  551.6 39.3 %custom-call.31 = f32[8,1,64,64]{2,3,1,0:T(8,128)S(1)} custom-call(f32[8,1,64,64]{3,2,1,0:T(8,128)S(1)} %select_bitcast_fusion.5), custom_call_target="InvertDiagBlocksLowerTriangular" | custom-call | tf_op jit(solution)/shard_map/transpose(jvp())/while/body/eval_jaxpr/triangular_solve | solution.py:63
  590.9 2.4 bitcast_dynamic-update-slice_fusion.23
  593.4 2.6 convolution_add_fusion.26
  618.3 2.1 convolution_add_fusion.24
  624.5 39.3 %custom-call.31 = f32[8,1,64,64]{2,3,1,0:T(8,128)S(1)} custom-call(f32[8,1,64,64]{3,2,1,0:T(8,128)S(1)} %select_bitcast_fusion.5), custom_call_target="InvertDiagBlocksLowerTriangular" | custom-call | tf_op jit(solution)/shard_map/transpose(jvp())/while/body/eval_jaxpr/triangular_solve | solution.py:63
  663.9 2.5 bitcast_dynamic-update-slice_fusion.23
  666.3 2.6 convolution_add_fusion.26
  690.5 10.4 %fusion.100 = bf16[2304,3072]{0,1:T(8,128)(2,1)} fusion(bf16[128,2304]{1,0:T(8,128)(2,1)S(1)} %copy-done, bf16[128,1024]{0,1:T(8,128)(2,1)S(1)} %bitcast.565, bf16[128,1024]{0,1:T(8,128)(2,1)S(1)} %bitcast.566, bf16[128,1024]{0,1:T(8,128)(2,1)S(1)} %bitcast.567), kind=kOutput, calls=%fused_computation.179 | convolution fusion | flops 1821376512 | bytes 15532032 | tf_op jit(solution)/shard_map/td,tc->dc/dot_general | solution.py:181
  700.9 18.6 %copy.247 = bf16[2304,3072]{1,0:T(8,128)(2,1)} copy(bf16[2304,3072]{0,1:T(8,128)(2,1)} %fusion.100) | data formatting | bytes 28311552
  724.3 230.9 %reduce-scatter.4.cloned.1.call-done = bf16[576,3072]{1,0:T(8,128)(2,1)} async-done(((bf16[2304,3072]{1,0:T(8,128)(2,1)}), bf16[576,3072]{1,0:T(8,128)(2,1)}) %reduce-scatter.4.cloned.1.call-update) | async-done | bytes 3538960
  955.2 6.1 copy.248
  961.2 5.0 fusion.128
  966.2 3.1 copy.234
  969.3 3.1 copy.235
  972.4 2.0 copy.236
  (370 shorter events, 132.3 us)
Async XLA Ops:
  7.2 94.6 %copy-start = (bf16[128,2304]{1,0:T(8,128)(2,1)S(1)}, bf16[128,2304]{1,0:T(8,128)(2,1)}, u32[]{:S(2)}) copy-start(bf16[128,2304]{1,0:T(8,128)(2,1)} %param.15) | copy-start | bytes 1769476
  7.2 94.5 %all-gather.14.cloned.1.call-start = ((), (), s32[]{:S(2)}) async-start(), calls=%async_computation.2 | async-start | bytes 5898240 | tf_op jit(solution)/shard_map/all_gather | solution.py:112
  7.9 183.3 %all-gather.12.cloned.1.call-start = ((), (), s32[]{:S(2)}) async-start(), calls=%async_computation.1 | async-start | bytes 5898240 | tf_op jit(solution)/shard_map/all_gather | solution.py:111
  8.7 272.0 %all-gather.16.cloned.1.call-start = ((), (), s32[]{:S(2)}) async-start(), calls=%async_computation.3 | async-start | bytes 5898240 | tf_op jit(solution)/shard_map/all_gather | solution.py:110
  9.4 427.5 %all-gather.18.cloned.1.call-start = ((), (), s32[]{:S(2)}) async-start(), calls=%async_computation.4 | async-start | bytes 1310720 | tf_op jit(solution)/shard_map/all_gather | solution.py:19
  283.8 5.8 copy-start.21
  292.4 4.4 copy-start.23
  292.4 4.4 copy-start.25
  351.4 4.4 copy-start.23
  351.4 4.4 copy-start.25
  409.3 8.3 copy-start.2
  410.4 56.0 %all-gather.20.cloned.1.call-start = ((), (), s32[]{:S(2)}) async-start(), calls=%async_computation.5 | async-start | bytes 1310720 | tf_op jit(solution)/shard_map/all_gather | solution.py:19
  411.0 84.3 %all-gather.22.cloned.1.call-start = ((), (), s32[]{:S(2)}) async-start(), calls=%async_computation.6 | async-start | bytes 1310720 | tf_op jit(solution)/shard_map/all_gather | solution.py:19
  412.9 111.4 %all-gather.24.cloned.1.call-start = ((), (), s32[]{:S(2)}) async-start(), calls=%async_computation.7 | async-start | bytes 1310720 | tf_op jit(solution)/shard_map/all_gather | solution.py:19
  417.7 537.5 %reduce-scatter.4.cloned.1.call-start = ((), (), s32[]{:S(2)}) async-start(), calls=%async_computation.8 | async-start | bytes 17694720
  466.4 63.9 %copy-start.10 = (f32[8,128,128]{2,1,0:T(8,128)}, f32[8,128,128]{2,1,0:T(8,128)S(1)}, u32[]{:S(2)}) copy-start(f32[8,128,128]{2,1,0:T(8,128)S(1)} %get-tuple-element.949) | copy-start | bytes 1572868
  545.3 5.2 copy-start.4
  590.9 6.8 copy-start.5
  590.9 6.8 copy-start.12
  593.4 5.6 copy-start.44
  601.5 5.1 copy-start.30
  601.5 5.1 copy-start.33
  601.5 5.2 copy-start.1
  603.5 4.4 copy-start.9
  618.3 5.2 copy-start.4
  663.8 6.8 copy-start.5
  663.8 6.8 copy-start.12
  666.3 5.6 copy-start.44
  674.5 5.1 copy-start.30
  674.5 5.1 copy-start.33
  674.5 5.2 copy-start.1
  676.5 4.4 copy-start.9
  (65 other events, 146.5 us)
Sparse Core Ops, SparseCore 0:
  9.6 92.0 all-gather.13
  103.3 87.8 all-gather.11
  192.8 87.8 all-gather.15
  410.5 26.3 all-gather.17
  438.9 27.4 all-gather.19
  467.8 27.4 all-gather.21
  496.8 27.4 all-gather.23
  719.7 235.3 reduce-scatter.3
where the time goes:
time: 992 us; the launch traced here: 981 us
  waiting for transfers between devices  602 us (61%)
  other arithmetic  184 us (19%)
  matrix products  95.1 us (10%)
  local copies, waits for them, and re-layouts  83.6 us (8%)
  between operations  14.8 us (1%)
    unnamed x9, waiting for transfers between devices  234 us
    another operation x12, other arithmetic, span_step(): lax.linalg.triangular_solve(system, target, left_side=True, lower=True)  164 us
    all_gather x4, waiting for transfers between devices, prefix_2(): lax.all_gather(a.astype(kind), axis)  106 us
    all_gather x1, waiting for transfers between devices, per_device(): lax.all_gather(w_value, 'ctx', axis=0, tiled=True)  91 us
    all_gather x1, waiting for transfers between devices, per_device(): lax.all_gather(w_key, 'ctx', axis=0, tiled=True)  86.3 us
    all_gather x1, waiting for transfers between devices, per_device(): lax.all_gather(w_query, 'ctx', axis=0, tiled=True)  84.6 us
    unnamed x40, local copies, waits for them, and re-layouts  40 us
  transfers between devices with their start and end apart: 8, of which 8 were waited for; matrix products, arithmetic and copies ran while one was open for 2% of the time, Pallas kernels for 0%

commit v1 on v0

--- a/solution.py
+++ b/solution.py
@@ -1,14 +1,391 @@
+import functools
+
 import jax
 import jax.numpy as jnp
 from jax import lax
+from jax.experimental import pallas as pl
+from jax.experimental.pallas import tpu as pltpu
 from jax.sharding import PartitionSpec as P
 
 DK = 128
 DV = 128
 SPAN = 64
-
+CHUNK = 128
+TAIL = 16
+HEAD_COLUMNS = 2 * DK + DV
 
 epsilon = 1e-06
+HIGHEST = lax.Precision.HIGHEST
+NN = (((1,), (0,)), ((), ()))
+NT = (((1,), (1,)), ((), ()))
+TN = (((0,), (0,)), ((), ()))
+
+
+def narrow(x):
+    return x.astype(jnp.bfloat16)
+
+
+def dot(a, b, dims, passes):
+    if passes == 6:
+        return lax.dot_general(a, b, dims, precision=HIGHEST, preferred_element_type=jnp.float32)
+    a_high, b_high = narrow(a), narrow(b)
+    total = lax.dot_general(a_high, b_high, dims, preferred_element_type=jnp.float32)
+    if passes >= 3:
+        a_low = narrow(a - a_high.astype(jnp.float32))
+        b_low = narrow(b - b_high.astype(jnp.float32))
+        total = total + lax.dot_general(a_high, b_low, dims, preferred_element_type=jnp.float32)
+        total = total + lax.dot_general(a_low, b_high, dims, preferred_element_type=jnp.float32)
+    return total
+
+
+PASSES = dict(
+    decay=6, pairs=6, inverse=6, solve=6, read=6, carry=6, sent=6, scan=6, emit=6, update=6,
+    d_update=6, d_value=6, d_pairs=6, d_up=6, d_up_state=6, d_kd=6, d_kend=6, d_decay=6,
+)
+
+
+def run(name, a, b, dims):
+    return dot(a, b, dims, PASSES[name])
+
+
+def recurrence(raw_ref, decay_ref, logit_ref, cot_ref, out_ref, grad_ref, dlogit_ref, ddecay_ref):
+    count = raw_ref.shape[0] // CHUNK
+    spans = range(count)
+    rows = lax.broadcasted_iota(jnp.int32, (CHUNK, CHUNK), 0)
+    cols = lax.broadcasted_iota(jnp.int32, (CHUNK, CHUNK), 1)
+    within = rows >= cols
+    strict = rows > cols
+    diagonal = rows == cols
+    running = within.astype(jnp.float32)
+
+    q, k, v, rq, rk, up, down, end = [], [], [], [], [], [], [], []
+    qu, ku, kd, kend, beta_row, cot = [], [], [], [], [], []
+    for n in spans:
+        here = slice(n * CHUNK, (n + 1) * CHUNK)
+        q_raw = raw_ref[here, 0:DK]
+        k_raw = raw_ref[here, DK : 2 * DK]
+        v.append(raw_ref[here, 2 * DK : 3 * DK])
+        rq.append(lax.rsqrt(jnp.sum(q_raw * q_raw, axis=1, keepdims=True) + epsilon))
+        rk.append(lax.rsqrt(jnp.sum(k_raw * k_raw, axis=1, keepdims=True) + epsilon))
+        q.append(q_raw * rq[n])
+        k.append(k_raw * rk[n])
+        summed = run("decay", running, decay_ref[here, :], NN)
+        up.append(jnp.exp(summed))
+        down.append(jnp.exp(-summed))
+        end.append(up[n][CHUNK - 1 : CHUNK, :])
+        qu.append(q[n] * up[n])
+        ku.append(k[n] * up[n])
+        kd.append(k[n] * down[n])
+        kend.append(kd[n] * end[n])
+        beta_row.append(jax.nn.sigmoid(logit_ref[n : n + 1, :]))
+        cot.append(cot_ref[here, :])
+
+    scores, system, inverse = [], [], []
+    for n in spans:
+        pairs = run("pairs", jnp.concatenate([qu[n], ku[n]], axis=0), kd[n], NT)
+        scores.append(jnp.where(within, pairs[:CHUNK], 0.0))
+        beta_col = jnp.transpose(jnp.broadcast_to(beta_row[n], (CHUNK, CHUNK)))
+        system.append(jnp.where(strict, pairs[CHUNK:] * beta_col, 0.0))
+        pair_block = (rows // 2) == (cols // 2)
+        inverse.append(diagonal.astype(jnp.float32) - jnp.where(pair_block, system[n], 0.0))
+    size = 2
+    while size < CHUNK:
+        joined = ((rows // (2 * size)) == (cols // (2 * size))) & ((rows // size) != (cols // size))
+        halves = [run("inverse", jnp.where(joined, system[n], 0.0), inverse[n], NN) for n in spans]
+        inverse = [inverse[n] - run("inverse", inverse[n], halves[n], NN) for n in spans]
+        size *= 2
+
+    solve = [inverse[n] * beta_row[n] for n in spans]
+    wu = [run("solve", solve[n], jnp.concatenate([ku[n], v[n]], axis=1), NN) for n in spans]
+    pwu = [run("read", scores[n], wu[n], NN) for n in spans]
+    kwu = [run("carry", kend[n], wu[n], TN) for n in spans]
+    query_through = [qu[n] - pwu[n][:, :DK] for n in spans]
+    transit = [
+        jnp.where(diagonal, jnp.broadcast_to(end[n], (DK, DK)), 0.0) - kwu[n][:, :DK] for n in spans
+    ]
+    sent = [run("sent", query_through[n], cot[n], TN) for n in spans]
+
+    state = [None] * (count + 1)
+    adjoint = [None] * (count + 1)
+    for n in spans:
+        m = count - 1 - n
+        own = kwu[n][:, DK:]
+        state[n + 1] = own if n == 0 else run("scan", transit[n], state[n], NN) + own
+        adjoint[m] = sent[m] if n == 0 else run("scan", transit[m], adjoint[m + 1], TN) + sent[m]
+
+    for n in spans:
+        here = slice(n * CHUNK, (n + 1) * CHUNK)
+        w = wu[n][:, :DK]
+        update = wu[n][:, DK:]
+        emitted = pwu[n][:, DK:]
+        d_update = run("d_update", scores[n], cot[n], TN)
+        if n > 0:
+            emitted = emitted + run("emit", query_through[n], state[n], NN)
+            update = update - run("update", w, state[n], NN)
+        if n < count - 1:
+            d_update = d_update + run("d_update", kend[n], adjoint[n + 1], NN)
+        out_ref[n] = emitted.astype(out_ref.dtype)
+        d_value = run("d_value", solve[n], d_update, TN)
+        both = jnp.concatenate([cot[n], -d_value], axis=0)
+        pairs = run("d_pairs", both, update, NT)
+        d_pairs = jnp.concatenate(
+            [jnp.where(within, pairs[:CHUNK], 0.0), jnp.where(strict, pairs[CHUNK:], 0.0)], axis=0
+        )
+        d_up = run("d_up", d_pairs, kd[n], NN)
+        if n > 0:
+            d_up = d_up + run("d_up_state", both, state[n], NT)
+        d_qu, d_ku = d_up[:CHUNK], d_up[CHUNK:]
+        d_kd = run("d_kd", d_pairs, jnp.concatenate([qu[n], ku[n]], axis=0), TN)
+        d_k = d_ku * up[n] + d_kd * down[n]
+        d_sum = d_qu * qu[n] + d_ku * ku[n] - d_kd * kd[n]
+        d_decay_end = jnp.zeros((1, DK), jnp.float32)
+        if n < count - 1:
+            d_kend = run("d_kend", update, adjoint[n + 1], NT)
+            d_k = d_k + d_kend * (end[n] * down[n])
+            ended = d_kend * kend[n]
+            d_sum = d_sum - ended
+            d_decay_end = jnp.sum(ended, axis=0, keepdims=True)
+            if n > 0:
+                kept = jnp.sum(jnp.transpose(adjoint[n + 1] * state[n]), axis=0, keepdims=True)
+                d_decay_end = d_decay_end + end[n] * kept
+        ddecay_ref[n] = (run("d_decay", running, d_sum, TN) + d_decay_end).astype(ddecay_ref.dtype)
+        d_q = d_qu * up[n]
+        d_q = rq[n] * (d_q - q[n] * jnp.sum(q[n] * d_q, axis=1, keepdims=True))
+        d_k = rk[n] * (d_k - k[n] * jnp.sum(k[n] * d_k, axis=1, keepdims=True))
+        grad_ref[here, 0:DK] = d_q.astype(grad_ref.dtype)
+        grad_ref[here, DK : 2 * DK] = d_k.astype(grad_ref.dtype)
+        grad_ref[here, 2 * DK : 3 * DK] = d_value.astype(grad_ref.dtype)
+        aligned = jnp.sum(jnp.transpose(d_value * update), axis=0, keepdims=True)
+        dlogit_ref[n : n + 1, :] = aligned * jnp.exp(-logit_ref[n : n + 1, :])
+
+
+def split_two(x):
+    high = narrow(x)
+    return high, narrow(x - high.astype(jnp.float32))
+
+
+def tail_rows(x):
+    high, low = split_two(x)
+    index = lax.broadcasted_iota(jnp.int32, (TAIL, x.shape[1]), 0)
+    high = jnp.broadcast_to(high.astype(jnp.float32), index.shape)
+    low = jnp.broadcast_to(low.astype(jnp.float32), index.shape)
+    return narrow(jnp.where(index == 0, high, jnp.where(index == 1, low, 0.0)))
+
+
+def lanes(start):
+    return pl.ds(pl.multiple_of(start, DK), DK)
+
+
+def pack_small_kernel(where_ref, tokens_ref, decay_ref, cot_ref, logit_ref, tok_ref, *x_refs):
+    ctx = len(x_refs)
+    place, block = where_ref[0], where_ref[2]
+    share = tok_ref.shape[1]
+    for j in range(tokens_ref.shape[1] // share):
+
+        @pl.when(block == j)
+        def _(j=j):
+            tok_ref[...] = tokens_ref[:, j * share : (j + 1) * share]
+
+    for d in range(ctx):
+        target = lax.rem(place + d, ctx)
+        for s in range(2):
+            lane = slice(s * DK, (s + 1) * DK)
+            column = lanes((2 * target + s) * DK)
+            x_refs[d][0:CHUNK, lane] = narrow(decay_ref[:, column])
+            x_refs[d][CHUNK : 2 * CHUNK, lane] = cot_ref[:, column]
+            x_refs[d][2 * CHUNK :, lane] = tail_rows(logit_ref[pl.ds(2 * target + s, 1), :])
+
+
+def pack_weights_kernel(where_ref, wq_ref, wk_ref, wv_ref, *out_refs):
+    ctx = len(out_refs) // 2
+    place, group = where_ref[0], where_ref[1]
+    half = wq_ref.shape[0] // 2
+    upper = pl.ds(pl.multiple_of(group * half, 32), half)
+    for s in range(2):
+        for d in range(ctx):
+            target = lax.rem(place + d, ctx)
+            column = lanes((2 * target + s) * DK)
+            for part, ref in enumerate((wq_ref, wk_ref, wv_ref)):
+                rows = slice(None) if d == 0 else upper
+                out_refs[s * ctx + d][:, part * DK : (part + 1) * DK] = ref[rows, column]
+
+
+def head_kernel(ctx, slot, where_ref, *refs):
+    tok_refs, refs = refs[:4], refs[4:]
+    own_ref, refs = refs[0], refs[1:]
+    direct, refs = refs[: ctx - 1], refs[ctx - 1 :]
+    swapped, refs = refs[: ctx - 1], refs[ctx - 1 :]
+    x_refs, refs = refs[:ctx], refs[ctx:]
+    grad_ref, back_refs = refs[0], refs[1 : 1 + ctx]
+    w, raw, decay, cot, logit, out, dlogit, ddecay = refs[1 + ctx :]
+    place, group = where_ref[0], where_ref[1]
+    share = own_ref.shape[0]
+    half = share // 2
+    w[pl.ds(pl.multiple_of(place * share, 32), share), :] = own_ref[...]
+    lane = slice(slot * DK, (slot + 1) * DK)
+    for d in range(ctx):
+        source = lax.rem(place + ctx - d, ctx)
+        if d > 0:
+            for kind, ref in ((group, direct[d - 1]), (1 - group, swapped[d - 1])):
+                w[pl.ds(pl.multiple_of(source * share + kind * half, 32), half), :] = ref[...]
+        rows = pl.ds(pl.multiple_of(source * CHUNK, CHUNK), CHUNK)
+        decay[rows, :] = x_refs[d][0:CHUNK, lane].astype(jnp.float32)
+        cot[rows, :] = x_refs[d][CHUNK : 2 * CHUNK, lane].astype(jnp.float32)
+        tail = x_refs[d][2 * CHUNK :, lane].astype(jnp.float32)
+        logit[pl.ds(source, 1), :] = tail[0:1] + tail[1:2]
+    projected = 0.0
+    for j in range(4):
+        block = where_ref[2 + j]
+        projected = projected + lax.dot_general(
+            tok_refs[j][...],
+            w[pl.ds(pl.multiple_of(block * share, 32), share), :],
+            NN,
+            preferred_element_type=jnp.float32,
+        )
+    for d in range(ctx):
+        source = lax.rem(place + ctx - d, ctx)
+        raw[pl.ds(pl.multiple_of(source * CHUNK, CHUNK), CHUNK), :] = projected[d * CHUNK : (d + 1) * CHUNK]
+    recurrence(raw, decay, logit, cot, out, grad_ref, dlogit, ddecay)
+    for d in range(ctx):
+        target = lax.rem(place + d, ctx)
+        back_refs[d][0:CHUNK, :] = out[target]
+        back_refs[d][CHUNK : 2 * CHUNK, :] = ddecay[target]
+        back_refs[d][2 * CHUNK :, :] = tail_rows(dlogit[pl.ds(target, 1), :])
+
+
+def weight_gradient_kernel(ctx, slot, where_ref, own_ref, *refs):
+    grad_refs, refs = refs[:ctx], refs[ctx:]
+    out_refs = refs[-3:]
+    for d in range(ctx):
+
+        @pl.when(pl.program_id(0) == d)
+        def _(d=d):
+            product = lax.dot_general(own_ref[...], grad_refs[d][...], TN, preferred_element_type=jnp.float32)
+            for part in range(3):
+                out_refs[part][...] = product[:, part * DK : (part + 1) * DK]
+
+
+def unpack_kernel(ctx, where_ref, *refs):
+    backs, (out_ref, dlogit_ref, ddecay_ref) = refs[: 2 * ctx], refs[2 * ctx :]
+    place = where_ref[0]
+    for s in range(2):
+        for d in range(ctx):
+            source = lax.rem(place + ctx - d, ctx)
+            ref = backs[s * ctx + d]
+            column = lanes((2 * source + s) * DK)
+            out_ref[:, column] = ref[0:CHUNK, :]
+            ddecay_ref[:, column] = ref[CHUNK : 2 * CHUNK, :].astype(jnp.float32)
+            tail = ref[2 * CHUNK :, :].astype(jnp.float32)
+            dlogit_ref[pl.ds(2 * source + s, 1), :] = tail[0:1] + tail[1:2]
+
+
+def head_split(tokens, w_query, w_key, w_value, beta_logit, log_decay, grad_out):
+    ctx = lax.axis_size("ctx")
+    place = lax.axis_index("ctx")
+    group = lax.axis_index("groups")
+    across, core = lax.axis_index("fsdp"), lax.axis_index("head")
+    length, depth = tokens.shape
+    share, columns = w_query.shape
+    total = ctx * length
+    bf16, f32 = jnp.bfloat16, jnp.float32
+    whole = pl.BlockSpec(memory_space=pltpu.VMEM)
+    scalars = pl.BlockSpec(memory_space=pltpu.SMEM)
+    own_block = 2 * across + core
+    where = jnp.stack(
+        [place, group, own_block, 2 * (1 - across) + core, 2 * across + 1 - core, 2 * (1 - across) + 1 - core]
+    ).astype(jnp.int32)
+
+    def shape(dims, kind):
+        return jax.ShapeDtypeStruct(dims, kind)
+
+    def along(x, axis, hop):
+        count = lax.axis_size(axis)
+        return lax.ppermute(x, axis, [(i, (i + hop) % count) for i in range(count)])
+
+    tok, *small = pl.pallas_call(
+        pack_small_kernel,
+        out_shape=[shape((length, share), bf16)] + [shape((2 * CHUNK + TAIL, 2 * DK), bf16)] * ctx,
+        in_specs=[scalars] + [whole] * 4,
+        out_specs=[whole] * (1 + ctx),
+        name="pack_small",
+    )(where, tokens, log_decay, grad_out, beta_logit)
+    packed = pl.pallas_call(
+        pack_weights_kernel,
+        out_shape=([shape((share, HEAD_COLUMNS), bf16)] + [shape((share // 2, HEAD_COLUMNS), bf16)] * (ctx - 1)) * 2,
+        in_specs=[scalars] + [whole] * 3,
+        out_specs=[whole] * (2 * ctx),
+        name="pack_weights",
+    )(where, w_query, w_key, w_value)
+
+    tok = jnp.concatenate([tok] + [along(tok, "ctx", d) for d in range(1, ctx)], axis=0)
+    tok_x = along(tok, "fsdp", 1)
+    toks = (tok, tok_x, along(tok, "head", 1), along(tok_x, "head", 1))
+    small = [small[0]] + [along(small[d], "ctx", d) for d in range(1, ctx)]
+
+    done = []
+    for slot in range(2):
+        own, *away = packed[slot * ctx : (slot + 1) * ctx]
+        direct = [along(x, "ctx", d + 1) for d, x in enumerate(away)]
+        swapped = [along(x, "groups", 1) for x in direct]
+        grad, *backs = pl.pallas_call(
+            functools.partial(head_kernel, ctx, slot),
+            out_shape=[shape((total, HEAD_COLUMNS), bf16)] + [shape((2 * CHUNK + TAIL, DK), bf16)] * ctx,
+            in_specs=[scalars] + [whole] * (4 + 1 + 2 * (ctx - 1) + ctx),
+            out_specs=[whole] * (1 + ctx),
+            scratch_shapes=[
+                pltpu.VMEM((depth, HEAD_COLUMNS), bf16),
+                pltpu.VMEM((total, HEAD_COLUMNS), f32),
+                pltpu.VMEM((total, DK), f32),
+                pltpu.VMEM((total, DV), f32),
+                pltpu.VMEM((ctx, CHUNK), f32),
+                pltpu.VMEM((ctx, CHUNK, DV), bf16),
+                pltpu.VMEM((ctx, CHUNK), f32),
+                pltpu.VMEM((ctx, CHUNK, DK), bf16),
+            ],
+            name=f"head_{slot}",
+        )(where, *toks, own, *direct, *swapped, *small)
+        grads = [grad] + [along(grad, "ctx", d) for d in range(1, ctx)]
+        backs = [backs[0]] + [along(backs[d], "ctx", d) for d in range(1, ctx)]
+        done.append((grads, backs))
+
+    picked = [jnp.where(where[2 + j] == place, toks[j], 0) for j in range(4)]
+    own_columns = picked[0] + picked[1] + picked[2] + picked[3]
+    pieces = [own_columns[d * length : (d + 1) * length] for d in range(ctx)]
+    own_columns = jnp.zeros_like(own_columns)
+    for d in range(ctx):
+        own_columns = lax.dynamic_update_slice_in_dim(
+            own_columns, pieces[d], lax.rem(place + ctx - d, ctx) * length, 0
+        )
+
+    results = None
+    for slot in range(2):
+        grads = done[slot][0]
+        anywhere = [pl.BlockSpec(memory_space=pl.ANY)] * 3 if slot else []
+        column = pl.BlockSpec(
+            (share, DK), lambda d, where_ref, s=slot: (0, 2 * lax.rem(where_ref[0] + ctx - d, ctx) + s)
+        )
+        fixed = lambda dims: pl.BlockSpec(dims, lambda d, where_ref: (0, 0))
+        results = pl.pallas_call(
+            functools.partial(weight_gradient_kernel, ctx, slot),
+            grid_spec=pltpu.PrefetchScalarGridSpec(
+                num_scalar_prefetch=1,
+                grid=(ctx,),
+                in_specs=[fixed((total, share))] + [fixed((total, HEAD_COLUMNS))] * ctx + anywhere,
+                out_specs=[column] * 3,
+            ),
+            out_shape=[shape((share, columns), f32)] * 3,
+            input_output_aliases={2 + ctx + i: i for i in range(3)} if slot else {},
+            name=f"weight_gradient_{slot}",
+        )(where, own_columns, *grads, *(results or ()))
+
+    attn_out, grad_beta, grad_decay = pl.pallas_call(
+        functools.partial(unpack_kernel, ctx),
+        out_shape=[shape((length, columns), bf16), shape((columns // DK, length), f32), shape((length, columns), f32)],
+        in_specs=[scalars] + [whole] * (2 * ctx),
+        out_specs=[whole] * 3,
+        name="unpack",
+    )(where, *done[0][1], *done[1][1])
+    return (attn_out, *results, grad_beta, grad_decay)
 
 
 def prefix_2(x, axis, join, neutral, backward):
@@ -195,9 +572,18 @@
     )
 
 
+def device_program(tokens, w_query, *rest):
+    ctx = lax.axis_size("ctx")
+    heads = w_query.shape[1] // DK
+    split = heads == 2 * ctx and ctx == 4 and tokens.shape[0] == CHUNK and w_query.shape[0] * ctx == tokens.shape[1]
+    split = split and lax.axis_size("groups") == lax.axis_size("fsdp") == lax.axis_size("head") == 2
+    split = split and w_query.shape[0] % 64 == 0
+    return (head_split if split else per_device)(tokens, w_query, *rest)
+
+
 def solution(mesh):
     return jax.shard_map(
-        per_device,
+        device_program,
         mesh=mesh,
         in_specs=(
             P(("groups", "ctx"), None),

time: 992 us -> 207 us (0.21)
  waiting for transfers between devices: 602 us -> 71.7 us
  other arithmetic: 184 us -> 0.2 us
  matrix products: 95.1 us -> 0 us
  local copies, waits for them, and re-layouts: 83.6 us -> 9.79 us
  starting transfers between devices: 0.66 us -> 67.5 us
  Pallas kernels: 0 us -> 53.3 us
  between operations: 14.8 us -> 1.01 us
    all_gather x7 -> x0, waiting for transfers between devices: 368 us -> none  [the longest x4 106 us: prefix_2(): lax.all_gather(a.astype(kind), axis)]
    unnamed x9 -> x0, waiting for transfers between devices: 234 us -> none
    another operation x26 -> x0, other arithmetic: 168 us -> none  [the longest x12 164 us: span_step(): lax.linalg.triangular_solve(system, target, left_side=True, lower=True)]
    dot_general x49 -> x0, matrix products: 83 us -> none  [the longest x6 10.7 us: span_step(): jnp.einsum('bcd,bdw->bcw', key_up, memory, precision=largest_value)]
    ppermute x0 -> x33, waiting for transfers between devices: none -> 71.7 us  [along(): return lax.ppermute(x, axis, [(i, (i + hop) % count) for i in range(count)])]
    ppermute x0 -> x33, starting transfers between devices: none -> 67.5 us  [along(): return lax.ppermute(x, axis, [(i, (i + hop) % count) for i in range(count)])]
    pallas_call x0 -> x7, Pallas kernels: none -> 53.3 us  [the longest x2 33.5 us: head_split(): pl.pallas_call(functools.partial(head_kernel, ctx, slot), out_shape=[shap...]
    unnamed x40 -> x65, local copies, waits for them, and re-layouts: 40 us -> 5.48 us
  transfers between devices with their start and end apart: 8 -> 33, of which waited for: 8 -> 11; matrix products, arithmetic and copies ran while one was open for 2% -> 2% of each run, Pallas kernels for 0% -> 22%
where the time goes in v1:
time: 207 us; the launch traced here: 203 us
  waiting for transfers between devices  71.7 us (35%)
  starting transfers between devices  67.5 us (33%)
  Pallas kernels  53.3 us (26%)
  local copies, waits for them, and re-layouts  9.79 us (5%)
    ppermute x33, waiting for transfers between devices, along(): return lax.ppermute(x, axis, [(i, (i + hop) % count) for i in range(count)])  71.7 us
    ppermute x33, starting transfers between devices, along(): return lax.ppermute(x, axis, [(i, (i + hop) % count) for i in range(count)])  67.5 us
    pallas_call x2, Pallas kernels, head_split(): pl.pallas_call(functools.partial(head_kernel, ctx, slot), out_shape=[shap...  33.5 us
    pallas_call x2, Pallas kernels, head_split(): pl.pallas_call(functools.partial(weight_gradient_kernel, ctx, slot), grid...  11.4 us
    unnamed x65, local copies, waits for them, and re-layouts  5.48 us
  transfers between devices with their start and end apart: 33, of which 11 were waited for; matrix products, arithmetic and copies ran while one was open for 2% of the time, Pallas kernels for 22%

profile of v1, /device:TPU:0, one launch (start us, length us, event | category | flops | bytes accessed | tf_op | source)
XLA Modules:
  0.0 203.5 jit_solution(1073933356194082294)
XLA Ops:
  1.3 2.3 %pack_small.1 = (bf16[128,576]{1,0:T(8,128)(2,1)}, bf16[272,256]{1,0:T(8,128)(2,1)}, bf16[272,256]{1,0:T(8,128)(2,1)}, bf16[272,256]{1,0:T(8,128)(2,1)}, bf16[272,256]{1,0:T(8,128)(2,1)}) custom-call(s32[6]{0:T(128)} %stack.27.where_ref, bf16[128,2304]{1,0:T(8,128)(2,1)} %tokens_ref.1, f32[128,1024]{1,0:T(8,128)} %decay_ref.1, bf16[128,1024]{1,0:T(8,128)(2,1)} %cot_ref.1, ...), custom_call_target="tpu_custom_call" | custom-call | tf_op jit(solution)/shard_map/pack_small/pallas_call | solution.py:305
  3.6 3.0 %collective-permute-start = (bf16[128,576]{1,0:T(8,128)(2,1)}, bf16[128,576]{1,0:T(8,128)(2,1)S(1)}, u32[]{:S(2)}, u32[]{:S(2)}) collective-permute-start(bf16[128,576]{1,0:T(8,128)(2,1)} %get-tuple-element.38), channel_id=1, source_target_pairs={{0,4},{4,8},{8,12},{12,0},{1,5},{5,9},{9,13},{13,1},{2,6},{6,10},{... | collective-permute-start | bytes 442376 | tf_op jit(solution)/shard_map/ppermute | solution.py:303
  6.6 2.6 %collective-permute-start.1 = (bf16[128,576]{1,0:T(8,128)(2,1)}, bf16[128,576]{1,0:T(8,128)(2,1)S(1)}, u32[]{:S(2)}, u32[]{:S(2)}) collective-permute-start(bf16[128,576]{1,0:T(8,128)(2,1)} %get-tuple-element.38), channel_id=1, source_target_pairs={{0,8},{4,12},{8,0},{12,4},{1,9},{5,13},{9,1},{13,5},{2,10},{6,14},... | collective-permute-start | bytes 442376 | tf_op jit(solution)/shard_map/ppermute | solution.py:303
  11.5 2.4 %collective-permute-done = bf16[128,576]{1,0:T(8,128)(2,1)S(1)} collective-permute-done((bf16[128,576]{1,0:T(8,128)(2,1)}, bf16[128,576]{1,0:T(8,128)(2,1)S(1)}, u32[]{:S(2)}, u32[]{:S(2)}) %collective-permute-start) | collective-permute-done | bytes 147488 | tf_op jit(solution)/shard_map/ppermute | solution.py:303
  14.0 6.3 %collective-permute-done.1 = bf16[128,576]{1,0:T(8,128)(2,1)S(1)} collective-permute-done((bf16[128,576]{1,0:T(8,128)(2,1)}, bf16[128,576]{1,0:T(8,128)(2,1)S(1)}, u32[]{:S(2)}, u32[]{:S(2)}) %collective-permute-start.1) | collective-permute-done | bytes 147488 | tf_op jit(solution)/shard_map/ppermute | solution.py:303
  22.1 3.9 %collective-permute-start.12 = (bf16[272,256]{1,0:T(8,128)(2,1)S(1)}, bf16[272,256]{1,0:T(8,128)(2,1)S(1)}, u32[]{:S(2)}, u32[]{:S(2)}) collective-permute-start(bf16[272,256]{1,0:T(8,128)(2,1)S(1)} %copy-done.28), channel_id=1, source_target_pairs={{0,4},{4,8},{8,12},{12,0},{1,5},{5,9},{9,13},{13,1},{2,6},{6,10},{... | collective-permute-start | bytes 417800 | tf_op jit(solution)/shard_map/ppermute | solution.py:303
  26.1 3.9 %pack_weights.1 = (bf16[576,384]{1,0:T(8,128)(2,1)}, bf16[288,384]{1,0:T(8,128)(2,1)}, bf16[288,384]{1,0:T(8,128)(2,1)}, bf16[288,384]{1,0:T(8,128)(2,1)}, bf16[...) custom-call(s32[6]{0:T(128)} %stack.27.where_ref, ...), custom_call_target="tpu_custom_call" | custom-call | tf_op jit(solution)/shard_map/pack_weights/pallas_call | solution.py:312
  31.7 4.1 %collective-permute-done.3 = bf16[512,576]{0,1:T(8,128)(2,1)S(1)} collective-permute-done((bf16[512,576]{0,1:T(8,128)(2,1)S(1)}, bf16[512,576]{0,1:T(8,128)(2,1)S(1)}, u32[]{:S(2)}, u32[]{:S(2)}) %collective-permute-start.3) | collective-permute-done | bytes 589856 | tf_op jit(solution)/shard_map/ppermute | solution.py:303
  35.8 3.1 %collective-permute-start.13 = (bf16[272,256]{1,0:T(8,128)(2,1)S(1)}, bf16[272,256]{1,0:T(8,128)(2,1)S(1)}, u32[]{:S(2)}, u32[]{:S(2)}) collective-permute-start(bf16[272,256]{1,0:T(8,128)(2,1)S(1)} %copy-done.27), channel_id=1, source_target_pairs={{0,8},{4,12},{8,0},{12,4},{1,9},{5,13},{9,1},{13,5},{2,10},{6,14},... | collective-permute-start | bytes 417800 | tf_op jit(solution)/shard_map/ppermute | solution.py:303
  38.9 3.3 %collective-permute-start.14 = (bf16[272,256]{1,0:T(8,128)(2,1)S(1)}, bf16[272,256]{1,0:T(8,128)(2,1)S(1)}, u32[]{:S(2)}, u32[]{:S(2)}) collective-permute-start(bf16[272,256]{1,0:T(8,128)(2,1)S(1)} %copy-done.26), channel_id=1, source_target_pairs={{0,12},{4,0},{8,4},{12,8},{1,13},{5,1},{9,5},{13,9},{2,14},{6,2},{... | collective-permute-start | bytes 417800 | tf_op jit(solution)/shard_map/ppermute | solution.py:303
  42.3 6.2 %collective-permute-done.13.refs_13_ = bf16[272,256]{1,0:T(8,128)(2,1)S(1)} collective-permute-done((bf16[272,256]{1,0:T(8,128)(2,1)S(1)}, bf16[272,256]{1,0:T(8,128)(2,1)S(1)}, u32[]{:S(2)}, u32[]{:S(2)}) %collective-permute-start.13) | collective-permute-done | bytes 139296 | tf_op jit(solution)/shard_map/ppermute | solution.py:303
  48.4 4.4 %collective-permute-start.8 = (bf16[288,384]{1,0:T(8,128)(2,1)}, bf16[288,384]{1,0:T(8,128)(2,1)}, u32[]{:S(2)}, u32[]{:S(2)}) collective-permute-start(bf16[288,384]{1,0:T(8,128)(2,1)} %get-tuple-element.42), channel_id=1, source_target_pairs={{0,12},{4,0},{8,4},{12,8},{1,13},{5,1},{9,5},{13,9},{2,14},{6,2},{... | collective-permute-start | bytes 663560 | tf_op jit(solution)/shard_map/ppermute | solution.py:303
  52.9 6.1 %collective-permute-done.8.refs_7_ = bf16[288,384]{1,0:T(8,128)(2,1)} collective-permute-done((bf16[288,384]{1,0:T(8,128)(2,1)}, bf16[288,384]{1,0:T(8,128)(2,1)}, u32[]{:S(2)}, u32[]{:S(2)}) %collective-permute-start.8) | collective-permute-done | bytes 221216 | tf_op jit(solution)/shard_map/ppermute | solution.py:303
  59.9 4.3 %collective-permute-done.6.refs_5_ = bf16[288,384]{1,0:T(8,128)(2,1)} collective-permute-done((bf16[288,384]{1,0:T(8,128)(2,1)}, bf16[288,384]{1,0:T(8,128)(2,1)}, u32[]{:S(2)}, u32[]{:S(2)}) %collective-permute-start.6) | collective-permute-done | bytes 221216 | tf_op jit(solution)/shard_map/ppermute | solution.py:303
  64.2 2.0 collective-permute-start.20
  66.2 2.6 %collective-permute-done.18.refs_5_ = bf16[288,384]{1,0:T(8,128)(2,1)S(1)} collective-permute-done((bf16[288,384]{1,0:T(8,128)(2,1)}, bf16[288,384]{1,0:T(8,128)(2,1)S(1)}, u32[]{:S(2)}, u32[]{:S(2)}) %collective-permute-start.18) | collective-permute-done | bytes 221216 | tf_op jit(solution)/shard_map/ppermute | solution.py:303
  70.3 7.5 %collective-permute-done.19.refs_6_ = bf16[288,384]{1,0:T(8,128)(2,1)} collective-permute-done((bf16[288,384]{1,0:T(8,128)(2,1)}, bf16[288,384]{1,0:T(8,128)(2,1)}, u32[]{:S(2)}, u32[]{:S(2)}) %collective-permute-start.19) | collective-permute-done | bytes 221216 | tf_op jit(solution)/shard_map/ppermute | solution.py:303
  86.7 4.5 %collective-permute-done.9.refs_8_ = bf16[288,384]{1,0:T(8,128)(2,1)} collective-permute-done((bf16[288,384]{1,0:T(8,128)(2,1)}, bf16[288,384]{1,0:T(8,128)(2,1)}, u32[]{:S(2)}, u32[]{:S(2)}) %collective-permute-start.9) | collective-permute-done | bytes 221216 | tf_op jit(solution)/shard_map/ppermute | solution.py:303
  91.2 16.8 %head_0.1 = (bf16[512,384]{1,0:T(8,128)(2,1)}, bf16[272,128]{1,0:T(8,128)(2,1)}, bf16[272,128]{1,0:T(8,128)(2,1)}, bf16[272,128]{1,0:T(8,128)(2,1)}, bf16[272,128]{1,0:T(8,128)(2,1)}) custom-call(s32[6]{0:T(128)} %stack.27.where_ref, bf16[512,576]{1,0:T(8,128)(2,1)} %copy-done, bf16[512,576]{1,0:T(8,128)(2,1)} %copy.18.refs_1_, ...), custom_call_target="tpu_custom_call" | custom-call | tf_op jit(solution)/shard_map/head_0/pallas_call | solution.py:330
  108.0 3.3 %collective-permute-start.30 = (bf16[512,384]{1,0:T(8,128)(2,1)}, bf16[512,384]{1,0:T(8,128)(2,1)}, u32[]{:S(2)}, u32[]{:S(2)}) collective-permute-start(bf16[512,384]{1,0:T(8,128)(2,1)} %get-tuple-element.61.refs_0_), channel_id=1, source_target_pairs={{0,4},{4,8},{8,12},{12,0},{1,5},{5,9},{9,13},{13,1},{2,6},{6,10},{... | collective-permute-start | bytes 1179656 | tf_op jit(solution)/shard_map/ppermute | solution.py:303
  112.7 16.7 %head_1.1 = (bf16[512,384]{1,0:T(8,128)(2,1)}, bf16[272,128]{1,0:T(8,128)(2,1)}, bf16[272,128]{1,0:T(8,128)(2,1)}, bf16[272,128]{1,0:T(8,128)(2,1)}, bf16[272,128]{1,0:T(8,128)(2,1)}) custom-call(s32[6]{0:T(128)} %stack.27.where_ref, bf16[512,576]{1,0:T(8,128)(2,1)} %copy-done, bf16[512,576]{1,0:T(8,128)(2,1)} %copy.18.refs_1_, ...), custom_call_target="tpu_custom_call" | custom-call | tf_op jit(solution)/shard_map/head_1/pallas_call | solution.py:330
  129.5 3.4 %collective-permute-start.25 = (bf16[272,128]{1,0:T(8,128)(2,1)}, bf16[272,128]{1,0:T(8,128)(2,1)S(1)}, u32[]{:S(2)}, u32[]{:S(2)}) collective-permute-start(bf16[272,128]{1,0:T(8,128)(2,1)} %get-tuple-element.57), channel_id=1, source_target_pairs={{0,8},{4,12},{8,0},{12,4},{1,9},{5,13},{9,1},{13,5},{2,10},{6,14},... | collective-permute-start | bytes 208904 | tf_op jit(solution)/shard_map/ppermute | solution.py:303
  132.9 2.8 %collective-permute-start.26 = (bf16[272,128]{1,0:T(8,128)(2,1)}, bf16[272,128]{1,0:T(8,128)(2,1)S(1)}, u32[]{:S(2)}, u32[]{:S(2)}) collective-permute-start(bf16[272,128]{1,0:T(8,128)(2,1)} %get-tuple-element.58), channel_id=1, source_target_pairs={{0,12},{4,0},{8,4},{12,8},{1,13},{5,1},{9,5},{13,9},{2,14},{6,2},{... | collective-permute-start | bytes 208904 | tf_op jit(solution)/shard_map/ppermute | solution.py:303
  136.1 3.9 %collective-permute-start.16 = (bf16[272,128]{1,0:T(8,128)(2,1)S(1)}, bf16[272,128]{1,0:T(8,128)(2,1)S(1)}, u32[]{:S(2)}, u32[]{:S(2)}) collective-permute-start(bf16[272,128]{1,0:T(8,128)(2,1)S(1)} %copy-done.30), channel_id=1, source_target_pairs={{0,8},{4,12},{8,0},{12,4},{1,9},{5,13},{9,1},{13,5},{2,10},{6,14},... | collective-permute-start | bytes 208904 | tf_op jit(solution)/shard_map/ppermute | solution.py:303
  140.1 12.4 %collective-permute-start.17 = (bf16[272,128]{1,0:T(8,128)(2,1)S(1)}, bf16[272,128]{1,0:T(8,128)(2,1)}, u32[]{:S(2)}, u32[]{:S(2)}) collective-permute-start(bf16[272,128]{1,0:T(8,128)(2,1)S(1)} %copy-done.29), channel_id=1, source_target_pairs={{0,12},{4,0},{8,4},{12,8},{1,13},{5,1},{9,5},{13,9},{2,14},{6,2},{... | collective-permute-start | bytes 208904 | tf_op jit(solution)/shard_map/ppermute | solution.py:303
  153.4 2.0 collective-permute-start.27
  155.4 2.8 %collective-permute-start.28 = (bf16[512,384]{1,0:T(8,128)(2,1)S(1)}, bf16[512,384]{1,0:T(8,128)(2,1)S(1)}, u32[]{:S(2)}, u32[]{:S(2)}) collective-permute-start(bf16[512,384]{1,0:T(8,128)(2,1)S(1)} %copy-done.9), channel_id=1, source_target_pairs={{0,8},{4,12},{8,0},{12,4},{1,9},{5,13},{9,1},{13,5},{2,10},{6,14},... | collective-permute-start | bytes 1179656 | tf_op jit(solution)/shard_map/ppermute | solution.py:303
  159.7 2.3 %unpack.1 = (bf16[128,1024]{1,0:T(8,128)(2,1)}, f32[8,128]{1,0:T(8,128)}, f32[128,1024]{1,0:T(8,128)}) custom-call(s32[6]{0:T(128)} %stack.27.where_ref, bf16[272,128]{1,0:T(8,128)(2,1)} %get-tuple-element.47.refs_0_, bf16[272,128]{1,0:T(8,128)(2,1)} %copy-done.24, bf16[272,128]{1,0:T(8,128)(2,1)} %copy-done.25, ...), custom_call_target="tpu_custom_call" | custom-call | tf_op jit(solution)/shard_map/unpack/pallas_call | solution.py:381
  162.0 18.0 %collective-permute-done.31.refs_2_ = bf16[512,384]{1,0:T(8,128)(2,1)S(1)} collective-permute-done((bf16[512,384]{1,0:T(8,128)(2,1)S(1)}, bf16[512,384]{1,0:T(8,128)(2,1)S(1)}, u32[]{:S(2)}, u32[]{:S(2)}) %collective-permute-start.31) | collective-permute-done | bytes 393248 | tf_op jit(solution)/shard_map/ppermute | solution.py:303
  181.5 5.7 %weight_gradient_0.1 = (f32[576,1024]{1,0:T(8,128)}, f32[576,1024]{1,0:T(8,128)}, f32[576,1024]{1,0:T(8,128)}) custom-call(s32[6]{0:T(128)} %stack.27.where_ref, bf16[512,576]{1,0:T(8,128)(2,1)} %copy-done.5, bf16[512,384]{1,0:T(8,128)(2,1)} %get-tuple-element.61.refs_0_, bf16[512,384]{1,0:T(8,128)(2,1)} %collective-permute-done.30.refs_1_, ...), custom_call_target="tpu_custom_call" | custom-call | tf_op jit(solution)/shard_map/weight_gradient_0/pallas_call | solution.py:368
  187.2 9.7 %collective-permute-done.28.refs_2_ = bf16[512,384]{1,0:T(8,128)(2,1)S(1)} collective-permute-done((bf16[512,384]{1,0:T(8,128)(2,1)S(1)}, bf16[512,384]{1,0:T(8,128)(2,1)S(1)}, u32[]{:S(2)}, u32[]{:S(2)}) %collective-permute-start.28) | collective-permute-done | bytes 393248 | tf_op jit(solution)/shard_map/ppermute | solution.py:303
  197.8 5.7 %weight_gradient_1.1 = (f32[576,1024]{1,0:T(8,128)}, f32[576,1024]{1,0:T(8,128)}, f32[576,1024]{1,0:T(8,128)}) custom-call(s32[6]{0:T(128)} %stack.27.where_ref, bf16[512,576]{1,0:T(8,128)(2,1)} %copy-done.5, bf16[512,384]{1,0:T(8,128)(2,1)} %get-tuple-element.60.refs_0_, ...), custom_call_target="tpu_custom_call", output_to_operand_aliasing={{0}: (6, {}), {1}: (7, {}), {2}: (8, {})} | custom-call | tf_op jit(solution)/shard_map/weight_gradient_1/pallas_call | solution.py:368
  (118 shorter events, 24.3 us)
Async XLA Ops:
  3.6 10.4 %collective-permute-start = (bf16[128,576]{1,0:T(8,128)(2,1)}, bf16[128,576]{1,0:T(8,128)(2,1)S(1)}, u32[]{:S(2)}, u32[]{:S(2)}) collective-permute-start(bf16[128,576]{1,0:T(8,128)(2,1)} %get-tuple-element.38), channel_id=1, source_target_pairs={{0,4},{4,8},{8,12},{12,0},{1,5},{5,9},{9,13},{13,1},{2,6},{6,10},{... | collective-permute-start | bytes 442376 | tf_op jit(solution)/shard_map/ppermute | solution.py:303
  6.6 13.6 %collective-permute-start.1 = (bf16[128,576]{1,0:T(8,128)(2,1)}, bf16[128,576]{1,0:T(8,128)(2,1)S(1)}, u32[]{:S(2)}, u32[]{:S(2)}) collective-permute-start(bf16[128,576]{1,0:T(8,128)(2,1)} %get-tuple-element.38), channel_id=1, source_target_pairs={{0,8},{4,12},{8,0},{12,4},{1,9},{5,13},{9,1},{13,5},{2,10},{6,14},... | collective-permute-start | bytes 442376 | tf_op jit(solution)/shard_map/ppermute | solution.py:303
  9.2 11.1 %collective-permute-start.2 = (bf16[128,576]{1,0:T(8,128)(2,1)}, bf16[128,576]{1,0:T(8,128)(2,1)S(1)}, u32[]{:S(2)}, u32[]{:S(2)}) collective-permute-start(bf16[128,576]{1,0:T(8,128)(2,1)} %get-tuple-element.38), channel_id=1, source_target_pairs={{0,12},{4,0},{8,4},{12,8},{1,13},{5,1},{9,5},{13,9},{2,14},{6,2},{... | collective-permute-start | bytes 442376 | tf_op jit(solution)/shard_map/ppermute | solution.py:303
  20.6 15.2 %collective-permute-start.3 = (bf16[512,576]{0,1:T(8,128)(2,1)S(1)}, bf16[512,576]{0,1:T(8,128)(2,1)S(1)}, u32[]{:S(2)}, u32[]{:S(2)}) collective-permute-start(bf16[512,576]{0,1:T(8,128)(2,1)S(1)} %copy.16), channel_id=1, source_target_pairs={{0,2},{2,0},{1,3},{3,1},{4,6},{6,4},{5,7},{7,5},{8,10},{10,8},{9,1... | collective-permute-start | bytes 1769480 | tf_op jit(solution)/shard_map/ppermute | solution.py:303
  22.1 16.8 %collective-permute-start.12 = (bf16[272,256]{1,0:T(8,128)(2,1)S(1)}, bf16[272,256]{1,0:T(8,128)(2,1)S(1)}, u32[]{:S(2)}, u32[]{:S(2)}) collective-permute-start(bf16[272,256]{1,0:T(8,128)(2,1)S(1)} %copy-done.28), channel_id=1, source_target_pairs={{0,4},{4,8},{8,12},{12,0},{1,5},{5,9},{9,13},{13,1},{2,6},{6,10},{... | collective-permute-start | bytes 417800 | tf_op jit(solution)/shard_map/ppermute | solution.py:303
  30.0 22.8 %collective-permute-start.7 = (bf16[288,384]{1,0:T(8,128)(2,1)}, bf16[288,384]{1,0:T(8,128)(2,1)S(1)}, u32[]{:S(2)}, u32[]{:S(2)}) collective-permute-start(bf16[288,384]{1,0:T(8,128)(2,1)} %get-tuple-element.41), channel_id=1, source_target_pairs={{0,8},{4,12},{8,0},{12,4},{1,9},{5,13},{9,1},{13,5},{2,10},{6,14},... | collective-permute-start | bytes 663560 | tf_op jit(solution)/shard_map/ppermute | solution.py:303
  31.7 49.7 %collective-permute-start.4 = (bf16[512,576]{0,1:T(8,128)(2,1)S(1)}, bf16[512,576]{0,1:T(8,128)(2,1)S(1)}, u32[]{:S(2)}, u32[]{:S(2)}) collective-permute-start(bf16[512,576]{0,1:T(8,128)(2,1)S(1)} %copy.16), channel_id=1, source_target_pairs={{0,1},{1,0},{2,3},{3,2},{4,5},{5,4},{6,7},{7,6},{8,9},{9,8},{10,11... | collective-permute-start | bytes 1769480 | tf_op jit(solution)/shard_map/ppermute | solution.py:303
  35.8 46.1 %collective-permute-start.5 = (bf16[512,576]{0,1:T(8,128)(2,1)S(1)}, bf16[512,576]{0,1:T(8,128)(2,1)S(1)}, u32[]{:S(2)}, u32[]{:S(2)}) collective-permute-start(bf16[512,576]{0,1:T(8,128)(2,1)S(1)} %collective-permute-done.3), channel_id=1, source_target_pairs={{0,1},{1,0},{2,3},{3,2},{4,5},{5,4},{6,7},{7,6},{8,9},{9,8},{10,11... | collective-permute-start | bytes 1769480 | tf_op jit(solution)/shard_map/ppermute | solution.py:303
  35.8 12.6 %collective-permute-start.13 = (bf16[272,256]{1,0:T(8,128)(2,1)S(1)}, bf16[272,256]{1,0:T(8,128)(2,1)S(1)}, u32[]{:S(2)}, u32[]{:S(2)}) collective-permute-start(bf16[272,256]{1,0:T(8,128)(2,1)S(1)} %copy-done.27), channel_id=1, source_target_pairs={{0,8},{4,12},{8,0},{12,4},{1,9},{5,13},{9,1},{13,5},{2,10},{6,14},... | collective-permute-start | bytes 417800 | tf_op jit(solution)/shard_map/ppermute | solution.py:303
  38.9 13.8 %collective-permute-start.14 = (bf16[272,256]{1,0:T(8,128)(2,1)S(1)}, bf16[272,256]{1,0:T(8,128)(2,1)S(1)}, u32[]{:S(2)}, u32[]{:S(2)}) collective-permute-start(bf16[272,256]{1,0:T(8,128)(2,1)S(1)} %copy-done.26), channel_id=1, source_target_pairs={{0,12},{4,0},{8,4},{12,8},{1,13},{5,1},{9,5},{13,9},{2,14},{6,2},{... | collective-permute-start | bytes 417800 | tf_op jit(solution)/shard_map/ppermute | solution.py:303
  48.4 10.5 %collective-permute-start.8 = (bf16[288,384]{1,0:T(8,128)(2,1)}, bf16[288,384]{1,0:T(8,128)(2,1)}, u32[]{:S(2)}, u32[]{:S(2)}) collective-permute-start(bf16[288,384]{1,0:T(8,128)(2,1)} %get-tuple-element.42), channel_id=1, source_target_pairs={{0,12},{4,0},{8,4},{12,8},{1,13},{5,1},{9,5},{13,9},{2,14},{6,2},{... | collective-permute-start | bytes 663560 | tf_op jit(solution)/shard_map/ppermute | solution.py:303
  52.8 11.4 %collective-permute-start.6 = (bf16[288,384]{1,0:T(8,128)(2,1)}, bf16[288,384]{1,0:T(8,128)(2,1)}, u32[]{:S(2)}, u32[]{:S(2)}) collective-permute-start(bf16[288,384]{1,0:T(8,128)(2,1)} %get-tuple-element.40), channel_id=1, source_target_pairs={{0,4},{4,8},{8,12},{12,0},{1,5},{5,9},{9,13},{13,1},{2,6},{6,10},{... | collective-permute-start | bytes 663560 | tf_op jit(solution)/shard_map/ppermute | solution.py:303
  52.8 16.0 %collective-permute-start.18 = (bf16[288,384]{1,0:T(8,128)(2,1)}, bf16[288,384]{1,0:T(8,128)(2,1)S(1)}, u32[]{:S(2)}, u32[]{:S(2)}) collective-permute-start(bf16[288,384]{1,0:T(8,128)(2,1)} %get-tuple-element.52), channel_id=1, source_target_pairs={{0,4},{4,8},{8,12},{12,0},{1,5},{5,9},{9,13},{13,1},{2,6},{6,10},{... | collective-permute-start | bytes 663560 | tf_op jit(solution)/shard_map/ppermute | solution.py:303
  58.9 18.9 %collective-permute-start.19 = (bf16[288,384]{1,0:T(8,128)(2,1)}, bf16[288,384]{1,0:T(8,128)(2,1)}, u32[]{:S(2)}, u32[]{:S(2)}) collective-permute-start(bf16[288,384]{1,0:T(8,128)(2,1)} %get-tuple-element.53), channel_id=1, source_target_pairs={{0,8},{4,12},{8,0},{12,4},{1,9},{5,13},{9,1},{13,5},{2,10},{6,14},... | collective-permute-start | bytes 663560 | tf_op jit(solution)/shard_map/ppermute | solution.py:303
  64.2 15.2 %collective-permute-start.20 = (bf16[288,384]{1,0:T(8,128)(2,1)}, bf16[288,384]{1,0:T(8,128)(2,1)}, u32[]{:S(2)}, u32[]{:S(2)}) collective-permute-start(bf16[288,384]{1,0:T(8,128)(2,1)} %get-tuple-element.54), channel_id=1, source_target_pairs={{0,12},{4,0},{8,4},{12,8},{1,13},{5,1},{9,5},{13,9},{2,14},{6,2},{... | collective-permute-start | bytes 663560 | tf_op jit(solution)/shard_map/ppermute | solution.py:303
  68.8 11.1 %collective-permute-start.10 = (bf16[288,384]{1,0:T(8,128)(2,1)S(1)}, bf16[288,384]{1,0:T(8,128)(2,1)S(1)}, u32[]{:S(2)}, u32[]{:S(2)}) collective-permute-start(bf16[288,384]{1,0:T(8,128)(2,1)S(1)} %collective-permute-done.7.refs_6_), channel_id=1, source_target_pairs={{0,16},{16,0},{1,17},{17,1},{2,18},{18,2},{3,19},{19,3},{4,20},{20... | collective-permute-start | bytes 663560 | tf_op jit(solution)/shard_map/ppermute | solution.py:303
  77.8 8.9 %collective-permute-start.11 = (bf16[288,384]{1,0:T(8,128)(2,1)}, bf16[288,384]{1,0:T(8,128)(2,1)}, u32[]{:S(2)}, u32[]{:S(2)}) collective-permute-start(bf16[288,384]{1,0:T(8,128)(2,1)} %collective-permute-done.8.refs_7_), channel_id=1, source_target_pairs={{0,16},{16,0},{1,17},{17,1},{2,18},{18,2},{3,19},{19,3},{4,20},{20... | collective-permute-start | bytes 663560 | tf_op jit(solution)/shard_map/ppermute | solution.py:303
  79.4 11.8 %collective-permute-start.9 = (bf16[288,384]{1,0:T(8,128)(2,1)}, bf16[288,384]{1,0:T(8,128)(2,1)}, u32[]{:S(2)}, u32[]{:S(2)}) collective-permute-start(bf16[288,384]{1,0:T(8,128)(2,1)} %collective-permute-done.6.refs_5_), channel_id=1, source_target_pairs={{0,16},{16,0},{1,17},{17,1},{2,18},{18,2},{3,19},{19,3},{4,20},{20... | collective-permute-start | bytes 663560 | tf_op jit(solution)/shard_map/ppermute | solution.py:303
  79.9 31.4 %collective-permute-start.21 = (bf16[288,384]{1,0:T(8,128)(2,1)S(1)}, bf16[288,384]{1,0:T(8,128)(2,1)}, u32[]{:S(2)}, u32[]{:S(2)}) collective-permute-start(bf16[288,384]{1,0:T(8,128)(2,1)S(1)} %collective-permute-done.18.refs_5_), channel_id=1, source_target_pairs={{0,16},{16,0},{1,17},{17,1},{2,18},{18,2},{3,19},{19,3},{4,20},{20... | collective-permute-start | bytes 663560 | tf_op jit(solution)/shard_map/ppermute | solution.py:303
  81.4 29.9 %collective-permute-start.22 = (bf16[288,384]{1,0:T(8,128)(2,1)}, bf16[288,384]{1,0:T(8,128)(2,1)S(1)}, u32[]{:S(2)}, u32[]{:S(2)}) collective-permute-start(bf16[288,384]{1,0:T(8,128)(2,1)} %collective-permute-done.19.refs_6_), channel_id=1, source_target_pairs={{0,16},{16,0},{1,17},{17,1},{2,18},{18,2},{3,19},{19,3},{4,20},{20... | collective-permute-start | bytes 663560 | tf_op jit(solution)/shard_map/ppermute | solution.py:303
  81.9 29.4 %collective-permute-start.23 = (bf16[288,384]{1,0:T(8,128)(2,1)}, bf16[288,384]{1,0:T(8,128)(2,1)S(1)}, u32[]{:S(2)}, u32[]{:S(2)}) collective-permute-start(bf16[288,384]{1,0:T(8,128)(2,1)} %collective-permute-done.20.refs_7_), channel_id=1, source_target_pairs={{0,16},{16,0},{1,17},{17,1},{2,18},{18,2},{3,19},{19,3},{4,20},{20... | collective-permute-start | bytes 663560 | tf_op jit(solution)/shard_map/ppermute | solution.py:303
  108.0 50.2 %collective-permute-start.30 = (bf16[512,384]{1,0:T(8,128)(2,1)}, bf16[512,384]{1,0:T(8,128)(2,1)}, u32[]{:S(2)}, u32[]{:S(2)}) collective-permute-start(bf16[512,384]{1,0:T(8,128)(2,1)} %get-tuple-element.61.refs_0_), channel_id=1, source_target_pairs={{0,4},{4,8},{8,12},{12,0},{1,5},{5,9},{9,13},{13,1},{2,6},{6,10},{... | collective-permute-start | bytes 1179656 | tf_op jit(solution)/shard_map/ppermute | solution.py:303
  129.5 10.6 %collective-permute-start.25 = (bf16[272,128]{1,0:T(8,128)(2,1)}, bf16[272,128]{1,0:T(8,128)(2,1)S(1)}, u32[]{:S(2)}, u32[]{:S(2)}) collective-permute-start(bf16[272,128]{1,0:T(8,128)(2,1)} %get-tuple-element.57), channel_id=1, source_target_pairs={{0,8},{4,12},{8,0},{12,4},{1,9},{5,13},{9,1},{13,5},{2,10},{6,14},... | collective-permute-start | bytes 208904 | tf_op jit(solution)/shard_map/ppermute | solution.py:303
  132.9 19.6 %collective-permute-start.26 = (bf16[272,128]{1,0:T(8,128)(2,1)}, bf16[272,128]{1,0:T(8,128)(2,1)S(1)}, u32[]{:S(2)}, u32[]{:S(2)}) collective-permute-start(bf16[272,128]{1,0:T(8,128)(2,1)} %get-tuple-element.58), channel_id=1, source_target_pairs={{0,12},{4,0},{8,4},{12,8},{1,13},{5,1},{9,5},{13,9},{2,14},{6,2},{... | collective-permute-start | bytes 208904 | tf_op jit(solution)/shard_map/ppermute | solution.py:303
  135.8 16.8 %collective-permute-start.15 = (bf16[272,128]{1,0:T(8,128)(2,1)}, bf16[272,128]{1,0:T(8,128)(2,1)S(1)}, u32[]{:S(2)}, u32[]{:S(2)}) collective-permute-start(bf16[272,128]{1,0:T(8,128)(2,1)} %get-tuple-element.48), channel_id=1, source_target_pairs={{0,4},{4,8},{8,12},{12,0},{1,5},{5,9},{9,13},{13,1},{2,6},{6,10},{... | collective-permute-start | bytes 208904 | tf_op jit(solution)/shard_map/ppermute | solution.py:303
  136.1 16.6 %collective-permute-start.16 = (bf16[272,128]{1,0:T(8,128)(2,1)S(1)}, bf16[272,128]{1,0:T(8,128)(2,1)S(1)}, u32[]{:S(2)}, u32[]{:S(2)}) collective-permute-start(bf16[272,128]{1,0:T(8,128)(2,1)S(1)} %copy-done.30), channel_id=1, source_target_pairs={{0,8},{4,12},{8,0},{12,4},{1,9},{5,13},{9,1},{13,5},{2,10},{6,14},... | collective-permute-start | bytes 208904 | tf_op jit(solution)/shard_map/ppermute | solution.py:303
  140.1 15.3 %collective-permute-start.17 = (bf16[272,128]{1,0:T(8,128)(2,1)S(1)}, bf16[272,128]{1,0:T(8,128)(2,1)}, u32[]{:S(2)}, u32[]{:S(2)}) collective-permute-start(bf16[272,128]{1,0:T(8,128)(2,1)S(1)} %copy-done.29), channel_id=1, source_target_pairs={{0,12},{4,0},{8,4},{12,8},{1,13},{5,1},{9,5},{13,9},{2,14},{6,2},{... | collective-permute-start | bytes 208904 | tf_op jit(solution)/shard_map/ppermute | solution.py:303
  152.5 27.5 %collective-permute-start.31 = (bf16[512,384]{1,0:T(8,128)(2,1)S(1)}, bf16[512,384]{1,0:T(8,128)(2,1)S(1)}, u32[]{:S(2)}, u32[]{:S(2)}) collective-permute-start(bf16[512,384]{1,0:T(8,128)(2,1)S(1)} %copy-done.13), channel_id=1, source_target_pairs={{0,8},{4,12},{8,0},{12,4},{1,9},{5,13},{9,1},{13,5},{2,10},{6,14},... | collective-permute-start | bytes 1179656 | tf_op jit(solution)/shard_map/ppermute | solution.py:303
  152.6 27.4 %collective-permute-start.32 = (bf16[512,384]{1,0:T(8,128)(2,1)S(1)}, bf16[512,384]{1,0:T(8,128)(2,1)S(1)}, u32[]{:S(2)}, u32[]{:S(2)}) collective-permute-start(bf16[512,384]{1,0:T(8,128)(2,1)S(1)} %copy-done.13), channel_id=1, source_target_pairs={{0,12},{4,0},{8,4},{12,8},{1,13},{5,1},{9,5},{13,9},{2,14},{6,2},{... | collective-permute-start | bytes 1179656 | tf_op jit(solution)/shard_map/ppermute | solution.py:303
  153.4 33.9 %collective-permute-start.27 = (bf16[512,384]{1,0:T(8,128)(2,1)S(1)}, bf16[512,384]{1,0:T(8,128)(2,1)S(1)}, u32[]{:S(2)}, u32[]{:S(2)}) collective-permute-start(bf16[512,384]{1,0:T(8,128)(2,1)S(1)} %copy-done.9), channel_id=1, source_target_pairs={{0,4},{4,8},{8,12},{12,0},{1,5},{5,9},{9,13},{13,1},{2,6},{6,10},{... | collective-permute-start | bytes 1179656 | tf_op jit(solution)/shard_map/ppermute | solution.py:303
  155.4 41.5 %collective-permute-start.28 = (bf16[512,384]{1,0:T(8,128)(2,1)S(1)}, bf16[512,384]{1,0:T(8,128)(2,1)S(1)}, u32[]{:S(2)}, u32[]{:S(2)}) collective-permute-start(bf16[512,384]{1,0:T(8,128)(2,1)S(1)} %copy-done.9), channel_id=1, source_target_pairs={{0,8},{4,12},{8,0},{12,4},{1,9},{5,13},{9,1},{13,5},{2,10},{6,14},... | collective-permute-start | bytes 1179656 | tf_op jit(solution)/shard_map/ppermute | solution.py:303
  158.2 38.7 %collective-permute-start.29 = (bf16[512,384]{1,0:T(8,128)(2,1)S(1)}, bf16[512,384]{1,0:T(8,128)(2,1)S(1)}, u32[]{:S(2)}, u32[]{:S(2)}) collective-permute-start(bf16[512,384]{1,0:T(8,128)(2,1)S(1)} %copy-done.9), channel_id=1, source_target_pairs={{0,12},{4,0},{8,4},{12,8},{1,13},{5,1},{9,5},{13,9},{2,14},{6,2},{... | collective-permute-start | bytes 1179656 | tf_op jit(solution)/shard_map/ppermute | solution.py:303
  (32 other events, 531.6 us)

commit v2 on v1

--- a/solution.py
+++ b/solution.py
@@ -12,6 +12,7 @@
 SPAN = 64
 CHUNK = 128
 TAIL = 16
+EXTRA = 96
 HEAD_COLUMNS = 2 * DK + DV
 
 epsilon = 1e-06
@@ -39,8 +40,8 @@
 
 
 PASSES = dict(
-    decay=6, pairs=6, inverse=6, solve=6, read=6, carry=6, sent=6, scan=6, emit=6, update=6,
-    d_update=6, d_value=6, d_pairs=6, d_up=6, d_up_state=6, d_kd=6, d_kend=6, d_decay=6,
+    decay=1, pairs=3, inverse=3, solve=3, read=1, carry=3, sent=1, scan=1, emit=1, update=1,
+    d_update=3, d_value=3, d_pairs=1, d_up=1, d_up_state=1, d_kd=1, d_kend=1, d_decay=3,
 )
 
 
@@ -176,107 +177,138 @@
     return pl.ds(pl.multiple_of(start, DK), DK)
 
 
-def pack_small_kernel(where_ref, tokens_ref, decay_ref, cot_ref, logit_ref, tok_ref, *x_refs):
-    ctx = len(x_refs)
-    place, block = where_ref[0], where_ref[2]
-    share = tok_ref.shape[1]
+def tile_rows(start, size):
+    return pl.ds(pl.multiple_of(start, 32), size)
+
+
+def pack_tokens_kernel(where_ref, tokens_ref, tok_ref):
+    share = tok_ref.shape[0]
     for j in range(tokens_ref.shape[1] // share):
 
-        @pl.when(block == j)
+        @pl.when(where_ref[2] == j)
         def _(j=j):
-            tok_ref[...] = tokens_ref[:, j * share : (j + 1) * share]
-
-    for d in range(ctx):
-        target = lax.rem(place + d, ctx)
-        for s in range(2):
-            lane = slice(s * DK, (s + 1) * DK)
-            column = lanes((2 * target + s) * DK)
-            x_refs[d][0:CHUNK, lane] = narrow(decay_ref[:, column])
-            x_refs[d][CHUNK : 2 * CHUNK, lane] = cot_ref[:, column]
-            x_refs[d][2 * CHUNK :, lane] = tail_rows(logit_ref[pl.ds(2 * target + s, 1), :])
-
-
-def pack_weights_kernel(where_ref, wq_ref, wk_ref, wv_ref, *out_refs):
-    ctx = len(out_refs) // 2
+            block = tokens_ref[:, j * share : (j + 1) * share]
+            full = share // DK
+            for g in range(full):
+                tok_ref[g * CHUNK : (g + 1) * CHUNK, :] = block[:, g * DK : (g + 1) * DK]
+            rest = block[:, full * DK :]
+            tok_ref[full * CHUNK :, :] = jnp.concatenate([rest[: CHUNK // 2], rest[CHUNK // 2 :]], axis=1)
+
+
+def unpack_tokens_kernel(ctx, where_ref, *refs):
+    tok_refs, all_ref, own_ref = refs[:4], refs[4], refs[5]
+    place = where_ref[0]
+    share = own_ref.shape[0]
+    full = share // DK
+    for j in range(4):
+        block = where_ref[2 + j]
+        for d in range(ctx):
+            source = lax.rem(place + ctx - d, ctx)
+            start = source * CHUNK
+            base = d * share
+            for g in range(full):
+                piece = tok_refs[j][base + g * CHUNK : base + (g + 1) * CHUNK, :]
+                all_ref[block, tile_rows(start, CHUNK), g * DK : (g + 1) * DK] = piece
+            rest = tok_refs[j][base + full * CHUNK : base + share, :]
+            all_ref[block, tile_rows(start, CHUNK // 2), full * DK :] = rest[:, : DK // 2]
+            all_ref[block, tile_rows(start + CHUNK // 2, CHUNK // 2), full * DK :] = rest[:, DK // 2 :]
+    for n in range(ctx):
+        piece = all_ref[place, n * CHUNK : (n + 1) * CHUNK, :].astype(jnp.float32)
+        own_ref[:, n * CHUNK : (n + 1) * CHUNK] = narrow(jnp.transpose(piece))
+
+
+def pack_kernel(ctx, where_ref, wq_ref, wk_ref, wv_ref, decay_ref, cot_ref, logit_ref, *out_refs):
     place, group = where_ref[0], where_ref[1]
     half = wq_ref.shape[0] // 2
-    upper = pl.ds(pl.multiple_of(group * half, 32), half)
     for s in range(2):
         for d in range(ctx):
-            target = lax.rem(place + d, ctx)
-            column = lanes((2 * target + s) * DK)
+            head = 2 * lax.rem(place + d, ctx) + s
+            column = lanes(head * DK)
+            out = out_refs[s * ctx + d]
+            size = out.shape[0] - EXTRA
+            rows = slice(None) if d == 0 else tile_rows(group * half, half)
             for part, ref in enumerate((wq_ref, wk_ref, wv_ref)):
-                rows = slice(None) if d == 0 else upper
-                out_refs[s * ctx + d][:, part * DK : (part + 1) * DK] = ref[rows, column]
+                out[0:size, part * DK : (part + 1) * DK] = ref[rows, column]
+            decay = narrow(decay_ref[:, column])
+            cot = cot_ref[:, column]
+            out[size : size + 96, 0:DK] = decay[0:96]
+            out[size : size + 32, DK : 2 * DK] = decay[96:128]
+            out[size + 32 : size + 96, DK : 2 * DK] = cot[0:64]
+            out[size : size + 64, 2 * DK : 3 * DK] = cot[64:128]
+            out[size + 64 : size + 80, 2 * DK : 3 * DK] = tail_rows(logit_ref[pl.ds(head, 1), :])
+            out[size + 80 : size + 96, 2 * DK : 3 * DK] = jnp.zeros((16, DK), out.dtype)
 
 
 def head_kernel(ctx, slot, where_ref, *refs):
-    tok_refs, refs = refs[:4], refs[4:]
-    own_ref, refs = refs[0], refs[1:]
-    direct, refs = refs[: ctx - 1], refs[ctx - 1 :]
+    all_ref, refs = refs[0], refs[1:]
+    direct, refs = refs[:ctx], refs[ctx:]
     swapped, refs = refs[: ctx - 1], refs[ctx - 1 :]
-    x_refs, refs = refs[:ctx], refs[ctx:]
-    grad_ref, back_refs = refs[0], refs[1 : 1 + ctx]
-    w, raw, decay, cot, logit, out, dlogit, ddecay = refs[1 + ctx :]
+    if slot:
+        earlier_ref, refs = refs[0], refs[1:]
+    grad_ref, back_ref, w, raw, decay, cot, logit, out, dlogit, ddecay = refs
     place, group = where_ref[0], where_ref[1]
-    share = own_ref.shape[0]
+    share = direct[0].shape[0] - EXTRA
     half = share // 2
-    w[pl.ds(pl.multiple_of(place * share, 32), share), :] = own_ref[...]
-    lane = slice(slot * DK, (slot + 1) * DK)
     for d in range(ctx):
         source = lax.rem(place + ctx - d, ctx)
-        if d > 0:
-            for kind, ref in ((group, direct[d - 1]), (1 - group, swapped[d - 1])):
-                w[pl.ds(pl.multiple_of(source * share + kind * half, 32), half), :] = ref[...]
-        rows = pl.ds(pl.multiple_of(source * CHUNK, CHUNK), CHUNK)
-        decay[rows, :] = x_refs[d][0:CHUNK, lane].astype(jnp.float32)
-        cot[rows, :] = x_refs[d][CHUNK : 2 * CHUNK, lane].astype(jnp.float32)
-        tail = x_refs[d][2 * CHUNK :, lane].astype(jnp.float32)
+        ref = direct[d]
+        if d == 0:
+            w[tile_rows(source * share, share), :] = ref[0:share, :]
+            size = share
+        else:
+            w[tile_rows(source * share + group * half, half), :] = ref[0:half, :]
+            w[tile_rows(source * share + (1 - group) * half, half), :] = swapped[d - 1][0:half, :]
+            size = half
+        start = source * CHUNK
+        decay[tile_rows(start, 96), :] = ref[size : size + 96, 0:DK].astype(jnp.float32)
+        decay[tile_rows(start + 96, 32), :] = ref[size : size + 32, DK : 2 * DK].astype(jnp.float32)
+        cot[tile_rows(start, 64), :] = ref[size + 32 : size + 96, DK : 2 * DK].astype(jnp.float32)
+        cot[tile_rows(start + 64, 64), :] = ref[size : size + 64, 2 * DK : 3 * DK].astype(jnp.float32)
+        tail = ref[size + 64 : size + 80, 2 * DK : 3 * DK].astype(jnp.float32)
         logit[pl.ds(source, 1), :] = tail[0:1] + tail[1:2]
     projected = 0.0
-    for j in range(4):
-        block = where_ref[2 + j]
+    for j in range(ctx):
         projected = projected + lax.dot_general(
-            tok_refs[j][...],
-            w[pl.ds(pl.multiple_of(block * share, 32), share), :],
-            NN,
-            preferred_element_type=jnp.float32,
+            all_ref[j], w[j * share : (j + 1) * share, :], NN, preferred_element_type=jnp.float32
         )
-    for d in range(ctx):
-        source = lax.rem(place + ctx - d, ctx)
-        raw[pl.ds(pl.multiple_of(source * CHUNK, CHUNK), CHUNK), :] = projected[d * CHUNK : (d + 1) * CHUNK]
+    raw[...] = projected
     recurrence(raw, decay, logit, cot, out, grad_ref, dlogit, ddecay)
-    for d in range(ctx):
-        target = lax.rem(place + d, ctx)
-        back_refs[d][0:CHUNK, :] = out[target]
-        back_refs[d][CHUNK : 2 * CHUNK, :] = ddecay[target]
-        back_refs[d][2 * CHUNK :, :] = tail_rows(dlogit[pl.ds(target, 1), :])
-
-
-def weight_gradient_kernel(ctx, slot, where_ref, own_ref, *refs):
-    grad_refs, refs = refs[:ctx], refs[ctx:]
+    lane = slice(slot * DK, (slot + 1) * DK)
+    if slot:
+        back_ref[:, :, 0:DK] = earlier_ref[...]
+    for n in range(ctx):
+        back_ref[n, 0:CHUNK, lane] = out[n]
+        back_ref[n, CHUNK : 2 * CHUNK, lane] = ddecay[n]
+        back_ref[n, 2 * CHUNK :, lane] = tail_rows(dlogit[n : n + 1, :])
+
+
+def weight_gradient_kernel(steps, where_ref, own_ref, *refs):
     out_refs = refs[-3:]
-    for d in range(ctx):
-
-        @pl.when(pl.program_id(0) == d)
-        def _(d=d):
-            product = lax.dot_general(own_ref[...], grad_refs[d][...], TN, preferred_element_type=jnp.float32)
-            for part in range(3):
-                out_refs[part][...] = product[:, part * DK : (part + 1) * DK]
-
-
-def unpack_kernel(ctx, where_ref, *refs):
-    backs, (out_ref, dlogit_ref, ddecay_ref) = refs[: 2 * ctx], refs[2 * ctx :]
-    place = where_ref[0]
-    for s in range(2):
-        for d in range(ctx):
-            source = lax.rem(place + ctx - d, ctx)
-            ref = backs[s * ctx + d]
-            column = lanes((2 * source + s) * DK)
-            out_ref[:, column] = ref[0:CHUNK, :]
-            ddecay_ref[:, column] = ref[CHUNK : 2 * CHUNK, :].astype(jnp.float32)
-            tail = ref[2 * CHUNK :, :].astype(jnp.float32)
-            dlogit_ref[pl.ds(2 * source + s, 1), :] = tail[0:1] + tail[1:2]
+
+    def block(gradient):
+        product = lax.dot_general(own_ref[...], gradient, NN, preferred_element_type=jnp.float32)
+        for part in range(3):
+            out_refs[part][...] = product[:, part * DK : (part + 1) * DK]
+
+    for at, step in enumerate(steps):
+
+        @pl.when(pl.program_id(0) == at)
+        def _(at=at, step=step):
+            if step < 3:
+                block(refs[at][...])
+            else:
+                block(jnp.where(where_ref[10] == 1, refs[at + 1][...], refs[at][...]))
+
+
+def unpack_kernel(back_ref, out_ref, dlogit_ref, ddecay_ref):
+    for source in range(back_ref.shape[0]):
+        column = slice(2 * source * DK, 2 * (source + 1) * DK)
+        out_ref[:, column] = back_ref[source, 0:CHUNK, :]
+        ddecay_ref[:, column] = back_ref[source, CHUNK : 2 * CHUNK, :].astype(jnp.float32)
+        tail = back_ref[source, 2 * CHUNK :, :].astype(jnp.float32)
+        row = tail[0:1] + tail[1:2]
+        for s in range(2):
+            dlogit_ref[2 * source + s : 2 * source + s + 1, :] = row[:, s * DK : (s + 1) * DK]
 
 
 def head_split(tokens, w_query, w_key, w_value, beta_logit, log_decay, grad_out):
@@ -290,9 +322,12 @@
     bf16, f32 = jnp.bfloat16, jnp.float32
     whole = pl.BlockSpec(memory_space=pltpu.VMEM)
     scalars = pl.BlockSpec(memory_space=pltpu.SMEM)
-    own_block = 2 * across + core
+    sources = [place, place + 1 - 2 * (place % 2), (place + 2) % ctx, ctx - 1 - place]
     where = jnp.stack(
-        [place, group, own_block, 2 * (1 - across) + core, 2 * across + 1 - core, 2 * (1 - across) + 1 - core]
+        [place, group]
+        + [2 * a + c for c in (core, 1 - core) for a in (across, 1 - across)]
+        + sources
+        + [((place == 0) | (place == ctx - 1)).astype(jnp.int32)]
     ).astype(jnp.int32)
 
     def shape(dims, kind):
@@ -302,36 +337,51 @@
         count = lax.axis_size(axis)
         return lax.ppermute(x, axis, [(i, (i + hop) % count) for i in range(count)])
 
-    tok, *small = pl.pallas_call(
-        pack_small_kernel,
-        out_shape=[shape((length, share), bf16)] + [shape((2 * CHUNK + TAIL, 2 * DK), bf16)] * ctx,
-        in_specs=[scalars] + [whole] * 4,
-        out_specs=[whole] * (1 + ctx),
-        name="pack_small",
-    )(where, tokens, log_decay, grad_out, beta_logit)
+    tok = pl.pallas_call(
+        pack_tokens_kernel,
+        out_shape=shape((share, length), bf16),
+        in_specs=[scalars, whole],
+        out_specs=whole,
+        name="pack_tokens",
+    )(where, tokens)
+    sizes = [share + EXTRA] + [share // 2 + EXTRA] * (ctx - 1)
     packed = pl.pallas_call(
-        pack_weights_kernel,
-        out_shape=([shape((share, HEAD_COLUMNS), bf16)] + [shape((share // 2, HEAD_COLUMNS), bf16)] * (ctx - 1)) * 2,
-        in_specs=[scalars] + [whole] * 3,
+        functools.partial(pack_kernel, ctx),
+        out_shape=[shape((size, HEAD_COLUMNS), bf16) for size in sizes * 2],
+        in_specs=[scalars] + [whole] * 6,
         out_specs=[whole] * (2 * ctx),
-        name="pack_weights",
-    )(where, w_query, w_key, w_value)
-
-    tok = jnp.concatenate([tok] + [along(tok, "ctx", d) for d in range(1, ctx)], axis=0)
+        name="pack",
+    )(where, w_query, w_key, w_value, log_decay, grad_out, beta_logit)
+
+    near = [along(tok, "ctx", d) for d in range(1, ctx)]
+    first, near[0] = lax.optimization_barrier((packed[1:ctx], near[0]))
+    tok = jnp.concatenate([tok] + near, axis=0)
     tok_x = along(tok, "fsdp", 1)
     toks = (tok, tok_x, along(tok, "head", 1), along(tok_x, "head", 1))
-    small = [small[0]] + [along(small[d], "ctx", d) for d in range(1, ctx)]
-
-    done = []
-    for slot in range(2):
-        own, *away = packed[slot * ctx : (slot + 1) * ctx]
-        direct = [along(x, "ctx", d + 1) for d, x in enumerate(away)]
+    all_tokens, own = pl.pallas_call(
+        functools.partial(unpack_tokens_kernel, ctx),
+        out_shape=[shape((ctx, total, share), bf16), shape((share, total), bf16)],
+        in_specs=[scalars] + [whole] * 4,
+        out_specs=[whole] * 2,
+        name="unpack_tokens",
+    )(where, *toks)
+    first = [along(x, "ctx", d + 1) for d, x in enumerate(first)]
+    second, first[0] = lax.optimization_barrier((packed[ctx + 1 :], first[0]))
+    second = [along(x, "ctx", d + 1) for d, x in enumerate(second)]
+
+    grads = []
+    back = None
+    for slot, direct in enumerate((first, second)):
         swapped = [along(x, "groups", 1) for x in direct]
-        grad, *backs = pl.pallas_call(
+        earlier = [] if back is None else [back]
+        grad, back = pl.pallas_call(
             functools.partial(head_kernel, ctx, slot),
-            out_shape=[shape((total, HEAD_COLUMNS), bf16)] + [shape((2 * CHUNK + TAIL, DK), bf16)] * ctx,
-            in_specs=[scalars] + [whole] * (4 + 1 + 2 * (ctx - 1) + ctx),
-            out_specs=[whole] * (1 + ctx),
+            out_shape=[
+                shape((total, HEAD_COLUMNS), bf16),
+                shape((ctx, 2 * CHUNK + TAIL, (slot + 1) * DK), bf16),
+            ],
+            in_specs=[scalars] + [whole] * (1 + ctx + ctx - 1 + slot),
+            out_specs=[whole] * 2,
             scratch_shapes=[
                 pltpu.VMEM((depth, HEAD_COLUMNS), bf16),
                 pltpu.VMEM((total, HEAD_COLUMNS), f32),
@@ -342,49 +392,43 @@
                 pltpu.VMEM((ctx, CHUNK), f32),
                 pltpu.VMEM((ctx, CHUNK, DK), bf16),
             ],
+            cost_estimate=pl.CostEstimate(flops=12_000_000_000, transcendentals=0, bytes_accessed=8_000_000),
             name=f"head_{slot}",
-        )(where, *toks, own, *direct, *swapped, *small)
-        grads = [grad] + [along(grad, "ctx", d) for d in range(1, ctx)]
-        backs = [backs[0]] + [along(backs[d], "ctx", d) for d in range(1, ctx)]
-        done.append((grads, backs))
-
-    picked = [jnp.where(where[2 + j] == place, toks[j], 0) for j in range(4)]
-    own_columns = picked[0] + picked[1] + picked[2] + picked[3]
-    pieces = [own_columns[d * length : (d + 1) * length] for d in range(ctx)]
-    own_columns = jnp.zeros_like(own_columns)
-    for d in range(ctx):
-        own_columns = lax.dynamic_update_slice_in_dim(
-            own_columns, pieces[d], lax.rem(place + ctx - d, ctx) * length, 0
-        )
-
-    results = None
-    for slot in range(2):
-        grads = done[slot][0]
-        anywhere = [pl.BlockSpec(memory_space=pl.ANY)] * 3 if slot else []
-        column = pl.BlockSpec(
-            (share, DK), lambda d, where_ref, s=slot: (0, 2 * lax.rem(where_ref[0] + ctx - d, ctx) + s)
-        )
-        fixed = lambda dims: pl.BlockSpec(dims, lambda d, where_ref: (0, 0))
+        )(where, all_tokens, packed[slot * ctx], *direct, *swapped, *earlier)
+        two = lax.ppermute(grad, "ctx", [(0, 2), (1, 3), (2, 0), (3, 1)])
+        pair = lax.ppermute(grad, "ctx", [(0, 1), (1, 0), (2, 3), (3, 2)])
+        middle = lax.ppermute(grad, "ctx", [(1, 2), (2, 1)])
+        far = lax.ppermute(two, "ctx", [(2, 3), (1, 0)])
+        grads.append((grad, pair, two, middle, far))
+    back = lax.all_to_all(back, "ctx", 0, 0)
+
+    results = ()
+    for slot, steps in ((0, (0, 1, 2, 3)), (1, (0, 1, 2)), (1, (3,))):
+        parts = [grads[slot][step] for step in steps] + ([grads[slot][4]] if 3 in steps else [])
+        column = pl.BlockSpec((share, DK), lambda i, ref, s=slot, b=steps[0]: (0, 2 * ref[6 + b + i] + s))
+        fixed = lambda dims: pl.BlockSpec(dims, lambda i, ref: (0, 0))
         results = pl.pallas_call(
-            functools.partial(weight_gradient_kernel, ctx, slot),
+            functools.partial(weight_gradient_kernel, steps),
             grid_spec=pltpu.PrefetchScalarGridSpec(
                 num_scalar_prefetch=1,
-                grid=(ctx,),
-                in_specs=[fixed((total, share))] + [fixed((total, HEAD_COLUMNS))] * ctx + anywhere,
+                grid=(len(steps),),
+                in_specs=[fixed((share, total))]
+                + [fixed((total, HEAD_COLUMNS))] * len(parts)
+                + [pl.BlockSpec(memory_space=pl.ANY)] * len(results),
                 out_specs=[column] * 3,
             ),
             out_shape=[shape((share, columns), f32)] * 3,
-            input_output_aliases={2 + ctx + i: i for i in range(3)} if slot else {},
-            name=f"weight_gradient_{slot}",
-        )(where, own_columns, *grads, *(results or ()))
+            input_output_aliases={2 + len(parts) + i: i for i in range(len(results))},
+            name=f"weight_gradient_{slot}_{steps[0]}",
+        )(where, own, *parts, *results)
 
     attn_out, grad_beta, grad_decay = pl.pallas_call(
-        functools.partial(unpack_kernel, ctx),
+        unpack_kernel,
         out_shape=[shape((length, columns), bf16), shape((columns // DK, length), f32), shape((length, columns), f32)],
-        in_specs=[scalars] + [whole] * (2 * ctx),
+        in_specs=[whole],
         out_specs=[whole] * 3,
         name="unpack",
-    )(where, *done[0][1], *done[1][1])
+    )(back)
     return (attn_out, *results, grad_beta, grad_decay)
 
 

time: 207 us -> 196 us (0.947); the launches traced: 203 us -> 196 us
  waiting for transfers between devices: 71.7 us -> 87.4 us
  starting transfers between devices: 67.5 us -> 53.9 us
  local copies, waits for them, and re-layouts: 9.79 us -> 4.68 us
  Pallas kernels: 53.3 us -> 48.9 us
    ppermute x0 -> x8, waiting for transfers between devices: none -> 49.3 us  [the longest x2 38.6 us: head_split(): two = lax.ppermute(grad, 'ctx', [(0, 2), (1, 3), (2, 0), (3, 1)])]
    ppermute x33 -> x18, waiting for transfers between devices: 71.7 us -> 38 us  [along(): return lax.ppermute(x, axis, [(i, (i + hop) % count) for i in range(count)])]
    ppermute x33 -> x18, starting transfers between devices: 67.5 us -> 35.6 us  [along(): return lax.ppermute(x, axis, [(i, (i + hop) % count) for i in range(count)])]
    ppermute x0 -> x8, starting transfers between devices: none -> 11.6 us  [the longest x2 4.19 us: head_split(): pair = lax.ppermute(grad, 'ctx', [(0, 1), (1, 0), (2, 3), (3, 2)])]
    pallas_call x2, Pallas kernels: 33.5 us -> 23 us  [head_split(): pl.pallas_call(functools.partial(head_kernel, ctx, slot), out_shape=[shap...]
    all_to_all x0 -> x1, starting transfers between devices: none -> 6.73 us  [head_split(): back = lax.all_to_all(back, 'ctx', 0, 0)]
    pallas_call x5 -> x7, Pallas kernels: 19.9 us -> 25.9 us  [the longest x3 13.9 us: head_split(): pl.pallas_call(functools.partial(weight_gradient_kernel, steps), grid_spe...]
    ppermute x3 -> x0, local copies, waits for them, and re-layouts: 3.29 us -> none  [along(): return lax.ppermute(x, axis, [(i, (i + hop) % count) for i in range(count)])]
  transfers between devices with their start and end apart: 33 -> 27, of which waited for: 11 -> 11; matrix products, arithmetic and copies ran while one was open for 2% -> 0% of each run, Pallas kernels for 22% -> 17%
where the time goes in v2:
time: 196 us
  waiting for transfers between devices  87.4 us (45%)
  starting transfers between devices  53.9 us (28%)
  Pallas kernels  48.9 us (25%)
  local copies, waits for them, and re-layouts  4.68 us (2%)
    ppermute x2, waiting for transfers between devices, head_split(): two = lax.ppermute(grad, 'ctx', [(0, 2), (1, 3), (2, 0), (3, 1)])  38.6 us
    ppermute x18, waiting for transfers between devices, along(): return lax.ppermute(x, axis, [(i, (i + hop) % count) for i in range(count)])  38 us
    ppermute x18, starting transfers between devices, along(): return lax.ppermute(x, axis, [(i, (i + hop) % count) for i in range(count)])  35.6 us
    pallas_call x2, Pallas kernels, head_split(): pl.pallas_call(functools.partial(head_kernel, ctx, slot), out_shape=[shap...  23 us
    pallas_call x3, Pallas kernels, head_split(): pl.pallas_call(functools.partial(weight_gradient_kernel, steps), grid_spe...  13.9 us
    ppermute x2, waiting for transfers between devices, head_split(): far = lax.ppermute(two, 'ctx', [(2, 3), (1, 0)])  8.76 us
    all_to_all x1, starting transfers between devices, head_split(): back = lax.all_to_all(back, 'ctx', 0, 0)  6.73 us
    pallas_call x1, Pallas kernels, head_split(): pl.pallas_call(functools.partial(pack_kernel, ctx), out_shape=[shape((siz...  4.45 us
  transfers between devices with their start and end apart: 27, of which 11 were waited for; matrix products, arithmetic and copies ran while one was open for 0% of the time, Pallas kernels for 17%

profile of v2, /device:TPU:0, one launch (start us, length us, event | category | flops | bytes accessed | tf_op | source)
XLA Modules:
  0.0 195.8 jit_solution(3272129112417173959)
XLA Ops:
  1.3 1.8 pack_tokens.1
  3.1 3.0 %collective-permute-start = (bf16[576,128]{1,0:T(8,128)(2,1)}, bf16[576,128]{1,0:T(8,128)(2,1)S(1)}, u32[]{:S(2)}, u32[]{:S(2)}) collective-permute-start(bf16[576,128]{1,0:T(8,128)(2,1)} %pack_tokens.1), channel_id=1, source_target_pairs={{0,4},{4,8},{8,12},{12,0},{1,5},{5,9},{9,13},{13,1},{2,6},{6,10},{... | collective-permute-start | bytes 442376 | tf_op jit(solution)/shard_map/ppermute | solution.py:338
  6.1 2.6 %collective-permute-start.1 = (bf16[576,128]{1,0:T(8,128)(2,1)}, bf16[576,128]{1,0:T(8,128)(2,1)S(1)}, u32[]{:S(2)}, u32[]{:S(2)}) collective-permute-start(bf16[576,128]{1,0:T(8,128)(2,1)} %pack_tokens.1), channel_id=1, source_target_pairs={{0,8},{4,12},{8,0},{12,4},{1,9},{5,13},{9,1},{13,5},{2,10},{6,14},... | collective-permute-start | bytes 442376 | tf_op jit(solution)/shard_map/ppermute | solution.py:338
  10.0 4.5 %pack.1 = (bf16[672,384]{1,0:T(8,128)(2,1)}, bf16[384,384]{1,0:T(8,128)(2,1)}, bf16[384,384]{1,0:T(8,128)(2,1)}, bf16[384,384]{1,0:T(8,128)(2,1)}, bf16[672,384]...) custom-call(s32[11]{0:T(128)} %stack.48.where_ref, ...), custom_call_target="tpu_custom_call" | custom-call | tf_op jit(solution)/shard_map/pack/pallas_call | solution.py:348
  14.5 4.2 %collective-permute-done.1 = bf16[576,128]{1,0:T(8,128)(2,1)S(1)} collective-permute-done((bf16[576,128]{1,0:T(8,128)(2,1)}, bf16[576,128]{1,0:T(8,128)(2,1)S(1)}, u32[]{:S(2)}, u32[]{:S(2)}) %collective-permute-start.1) | collective-permute-done | bytes 147488 | tf_op jit(solution)/shard_map/ppermute | solution.py:338
  18.8 1.6 collective-permute-start.3
  20.4 3.6 %collective-permute-start.6 = (bf16[384,384]{1,0:T(8,128)(2,1)}, bf16[384,384]{1,0:T(8,128)(2,1)S(1)}, u32[]{:S(2)}, u32[]{:S(2)}) collective-permute-start(bf16[384,384]{1,0:T(8,128)(2,1)} %get-tuple-element.49), channel_id=1, source_target_pairs={{0,4},{4,8},{8,12},{12,0},{1,5},{5,9},{9,13},{13,1},{2,6},{6,10},{... | collective-permute-start | bytes 884744 | tf_op jit(solution)/shard_map/ppermute | solution.py:338
  24.0 10.0 %collective-permute-done.3.refs_1_ = bf16[2304,128]{1,0:T(8,128)(2,1)S(1)} collective-permute-done((bf16[2304,128]{1,0:T(8,128)(2,1)S(1)}, bf16[2304,128]{1,0:T(8,128)(2,1)S(1)}, u32[]{:S(2)}, u32[]{:S(2)}) %collective-permute-start.3) | collective-permute-done | bytes 589856 | tf_op jit(solution)/shard_map/ppermute | solution.py:338
  34.0 2.8 %collective-permute-start.13 = (bf16[384,384]{1,0:T(8,128)(2,1)}, bf16[384,384]{1,0:T(8,128)(2,1)S(1)}, u32[]{:S(2)}, u32[]{:S(2)}) collective-permute-start(bf16[384,384]{1,0:T(8,128)(2,1)} %get-tuple-element.55), channel_id=1, source_target_pairs={{0,8},{4,12},{8,0},{12,4},{1,9},{5,13},{9,1},{13,5},{2,10},{6,14},... | collective-permute-start | bytes 884744 | tf_op jit(solution)/shard_map/ppermute | solution.py:338
  36.8 3.3 %collective-permute-start.14 = (bf16[384,384]{1,0:T(8,128)(2,1)}, bf16[384,384]{1,0:T(8,128)(2,1)S(1)}, u32[]{:S(2)}, u32[]{:S(2)}) collective-permute-start(bf16[384,384]{1,0:T(8,128)(2,1)} %get-tuple-element.56), channel_id=1, source_target_pairs={{0,12},{4,0},{8,4},{12,8},{1,13},{5,1},{9,5},{13,9},{2,14},{6,2},{... | collective-permute-start | bytes 884744 | tf_op jit(solution)/shard_map/ppermute | solution.py:338
  40.1 1.5 collective-permute-start.15
  41.6 9.7 %collective-permute-done.13.refs_3_ = bf16[384,384]{1,0:T(8,128)(2,1)S(1)} collective-permute-done((bf16[384,384]{1,0:T(8,128)(2,1)}, bf16[384,384]{1,0:T(8,128)(2,1)S(1)}, u32[]{:S(2)}, u32[]{:S(2)}) %collective-permute-start.13) | collective-permute-done | bytes 294944 | tf_op jit(solution)/shard_map/ppermute | solution.py:338
  51.3 6.8 %collective-permute-start.7 = (bf16[384,384]{1,0:T(8,128)(2,1)}, bf16[384,384]{1,0:T(8,128)(2,1)S(1)}, u32[]{:S(2)}, u32[]{:S(2)}) collective-permute-start(bf16[384,384]{1,0:T(8,128)(2,1)} %get-tuple-element.50), channel_id=1, source_target_pairs={{0,4},{4,8},{8,12},{12,0},{1,5},{5,9},{9,13},{13,1},{2,6},{6,10},{... | collective-permute-start | bytes 884744 | tf_op jit(solution)/shard_map/ppermute | solution.py:338
  58.2 3.3 %collective-permute-start.8 = (bf16[384,384]{1,0:T(8,128)(2,1)}, bf16[384,384]{1,0:T(8,128)(2,1)}, u32[]{:S(2)}, u32[]{:S(2)}) collective-permute-start(bf16[384,384]{1,0:T(8,128)(2,1)} %get-tuple-element.51), channel_id=1, source_target_pairs={{0,8},{4,12},{8,0},{12,4},{1,9},{5,13},{9,1},{13,5},{2,10},{6,14},... | collective-permute-start | bytes 884744 | tf_op jit(solution)/shard_map/ppermute | solution.py:338
  61.5 1.6 collective-permute-start.16
  63.9 3.7 %unpack_tokens.1 = (bf16[4,512,576]{2,1,0:T(8,128)(2,1)}, bf16[576,512]{1,0:T(8,128)(2,1)}) custom-call(s32[11]{0:T(128)} %stack.48.where_ref, bf16[2304,128]{1,0:T(8,128)(2,1)} %copy-done, bf16[2304,128]{1,0:T(8,128)(2,1)} %copy-done.3, bf16[2304,128]{1,0:T(8,128)(2,1)} %copy-done.4, bf16[2304,128]{1,0:T(8,128)(2,1)} %copy-done.5), custom_call_target="tpu_custom_call" | custom-call | tf_op jit(solution)/shard_map/unpack_tokens/pallas_call | solution.py:361
  70.6 10.6 %collective-permute-done.8.refs_3_ = bf16[384,384]{1,0:T(8,128)(2,1)} collective-permute-done((bf16[384,384]{1,0:T(8,128)(2,1)}, bf16[384,384]{1,0:T(8,128)(2,1)}, u32[]{:S(2)}, u32[]{:S(2)}) %collective-permute-start.8) | collective-permute-done | bytes 294944 | tf_op jit(solution)/shard_map/ppermute | solution.py:338
  83.3 11.3 %head_0.1 = (bf16[512,384]{1,0:T(8,128)(2,1)}, bf16[4,272,128]{2,1,0:T(8,128)(2,1)}) custom-call(s32[11]{0:T(128)} %stack.48.where_ref, bf16[4,512,576]{2,1,0:T(8,128)(2,1)} %get-tuple-element.44.refs_0_, bf16[672,384]{1,0:T(8,128)(2,1)} %get-tuple-element.53.refs_1_, bf16[384,384]{1,0:T(8,128)(2,1)} %copy-done.15, bf16[384,384]{1,0:T(8,128)(2,1)} %copy-done.16, ...), custom_call_target="tpu_custom_call" | custom-call | flops 12000000000 | bytes 8000000 | tf_op jit(solution)/shard_map/head_0/pallas_call | solution.py:377
  94.6 2.0 %collective-permute-done.12.refs_7_ = bf16[384,384]{1,0:T(8,128)(2,1)S(1)} collective-permute-done((bf16[384,384]{1,0:T(8,128)(2,1)}, bf16[384,384]{1,0:T(8,128)(2,1)S(1)}, u32[]{:S(2)}, u32[]{:S(2)}) %collective-permute-start.12) | collective-permute-done | bytes 294944 | tf_op jit(solution)/shard_map/ppermute | solution.py:338
  97.3 11.7 %head_1.1 = (bf16[512,384]{1,0:T(8,128)(2,1)}, bf16[4,272,256]{2,1,0:T(8,128)(2,1)}) custom-call(s32[11]{0:T(128)} %stack.48.where_ref, bf16[4,512,576]{2,1,0:T(8,128)(2,1)} %get-tuple-element.44.refs_0_, bf16[672,384]{1,0:T(8,128)(2,1)} %get-tuple-element.45.refs_1_, bf16[384,384]{1,0:T(8,128)(2,1)} %copy-done.17, ...), custom_call_target="tpu_custom_call" | custom-call | flops 12000000000 | bytes 8000000 | tf_op jit(solution)/shard_map/head_1/pallas_call | solution.py:377
  109.0 6.7 %all-to-all-start = ((bf16[4,272,256]{2,1,0:T(8,128)(2,1)}), bf16[4,272,256]{2,1,0:T(8,128)(2,1)S(1)}, u32[]{:S(2)}, u32[]{:S(2)}) async-start(bf16[4,272,256]{2,1,0:T(8,128)(2,1)} %get-tuple-element.58), calls=%async_computation | async-start | bytes 1114112 | tf_op jit(solution)/shard_map/all_to_all | solution.py:403
  115.8 2.9 %collective-permute-start.23 = (bf16[512,384]{1,0:T(8,128)(2,1)S(1)}, bf16[512,384]{1,0:T(8,128)(2,1)S(1)}, u32[]{:S(2)}, u32[]{:S(2)}) collective-permute-start(bf16[512,384]{1,0:T(8,128)(2,1)S(1)} %copy-done.10), channel_id=1, source_target_pairs={{0,8},{4,12},{8,0},{12,4},{1,9},{5,13},{9,1},{13,5},{2,10},{6,14},... | collective-permute-start | bytes 1179656 | tf_op jit(solution)/shard_map/ppermute | solution.py:398
  121.4 34.8 %collective-permute-done.23.refs_2_ = bf16[512,384]{1,0:T(8,128)(2,1)S(1)} collective-permute-done((bf16[512,384]{1,0:T(8,128)(2,1)S(1)}, bf16[512,384]{1,0:T(8,128)(2,1)S(1)}, u32[]{:S(2)}, u32[]{:S(2)}) %collective-permute-start.23) | collective-permute-done | bytes 393248 | tf_op jit(solution)/shard_map/ppermute | solution.py:398
  157.5 2.7 %collective-permute-start.21 = (bf16[512,384]{1,0:T(8,128)(2,1)}, bf16[512,384]{1,0:T(8,128)(2,1)S(1)}, u32[]{:S(2)}, u32[]{:S(2)}) collective-permute-start(bf16[512,384]{1,0:T(8,128)(2,1)} %get-tuple-element.61.refs_0_), channel_id=1, source_target_pairs={{0,4},{4,0},{8,12},{12,8},{1,5},{5,1},{9,13},{13,9},{2,6},{6,2},{1... | collective-permute-start | bytes 1179656 | tf_op jit(solution)/shard_map/ppermute | solution.py:399
  160.9 3.8 %collective-permute-done.19.refs_2_ = bf16[512,384]{1,0:T(8,128)(2,1)S(1)} collective-permute-done((bf16[512,384]{1,0:T(8,128)(2,1)}, bf16[512,384]{1,0:T(8,128)(2,1)S(1)}, u32[]{:S(2)}, u32[]{:S(2)}) %collective-permute-start.19) | collective-permute-done | bytes 393248 | tf_op jit(solution)/shard_map/ppermute | solution.py:398
  166.0 6.1 %collective-permute-done.25.refs_4_ = bf16[512,384]{1,0:T(8,128)(2,1)S(1)} collective-permute-done((bf16[512,384]{1,0:T(8,128)(2,1)S(1)}, bf16[512,384]{1,0:T(8,128)(2,1)S(1)}, u32[]{:S(2)}, u32[]{:S(2)}) %collective-permute-start.25) | collective-permute-done | bytes 393248 | tf_op jit(solution)/shard_map/ppermute | solution.py:401
  172.9 5.7 %weight_gradient_0_0.1 = (f32[576,1024]{1,0:T(8,128)}, f32[576,1024]{1,0:T(8,128)}, f32[576,1024]{1,0:T(8,128)}) custom-call(s32[11]{0:T(128)} %stack.48.where_ref, bf16[576,512]{1,0:T(8,128)(2,1)} %get-tuple-element.60.own_ref, bf16[512,384]{1,0:T(8,128)(2,1)} %get-tuple-element.62.refs_0_, bf16[512,384]{1,0:T(8,128)(2,1)} %copy-done.12, ...), custom_call_target="tpu_custom_call" | custom-call | tf_op jit(solution)/shard_map/weight_gradient_0_0/pallas_call | solution.py:410
  178.6 2.0 %collective-permute-done.21.refs_1_ = bf16[512,384]{1,0:T(8,128)(2,1)S(1)} collective-permute-done((bf16[512,384]{1,0:T(8,128)(2,1)}, bf16[512,384]{1,0:T(8,128)(2,1)S(1)}, u32[]{:S(2)}, u32[]{:S(2)}) %collective-permute-start.21) | collective-permute-done | bytes 393248 | tf_op jit(solution)/shard_map/ppermute | solution.py:399
  181.3 4.9 %weight_gradient_1_0.1 = (f32[576,1024]{1,0:T(8,128)}, f32[576,1024]{1,0:T(8,128)}, f32[576,1024]{1,0:T(8,128)}) custom-call(s32[11]{0:T(128)} %stack.48.where_ref, bf16[576,512]{1,0:T(8,128)(2,1)} %get-tuple-element.60.own_ref, bf16[512,384]{1,0:T(8,128)(2,1)} %get-tuple-element.61.refs_0_, ...), custom_call_target="tpu_custom_call", output_to_operand_aliasing={{0}: (5, {}), {1}: (6, {}), {2}: (7, {})} | custom-call | tf_op jit(solution)/shard_map/weight_gradient_1_0/pallas_call | solution.py:410
  186.2 2.7 %collective-permute-done.20.refs_1_ = bf16[512,384]{1,0:T(8,128)(2,1)S(1)} collective-permute-done((bf16[512,384]{1,0:T(8,128)(2,1)S(1)}, bf16[512,384]{1,0:T(8,128)(2,1)S(1)}, u32[]{:S(2)}, u32[]{:S(2)}) %collective-permute-start.20) | collective-permute-done | bytes 393248 | tf_op jit(solution)/shard_map/ppermute | solution.py:401
  189.6 3.3 %weight_gradient_1_3.1 = (f32[576,1024]{1,0:T(8,128)}, f32[576,1024]{1,0:T(8,128)}, f32[576,1024]{1,0:T(8,128)}) custom-call(s32[11]{0:T(128)} %stack.48.where_ref, bf16[576,512]{1,0:T(8,128)(2,1)} %get-tuple-element.60.own_ref, bf16[512,384]{1,0:T(8,128)(2,1)} %copy-done.7, ...), custom_call_target="tpu_custom_call", output_to_operand_aliasing={{0}: (4, {}), {1}: (5, {}), {2}: (6, {})} | custom-call | tf_op jit(solution)/shard_map/weight_gradient_1_3/pallas_call | solution.py:410
  193.8 2.0 %unpack.1 = (bf16[128,1024]{1,0:T(8,128)(2,1)}, f32[8,128]{1,0:T(8,128)}, f32[128,1024]{1,0:T(8,128)}) custom-call(bf16[4,272,256]{2,1,0:T(8,128)(2,1)} %copy-done.1), custom_call_target="tpu_custom_call" | custom-call | tf_op jit(solution)/shard_map/unpack/pallas_call | solution.py:425
  (79 shorter events, 17.6 us)
Async XLA Ops:
  3.1 11.4 %collective-permute-start = (bf16[576,128]{1,0:T(8,128)(2,1)}, bf16[576,128]{1,0:T(8,128)(2,1)S(1)}, u32[]{:S(2)}, u32[]{:S(2)}) collective-permute-start(bf16[576,128]{1,0:T(8,128)(2,1)} %pack_tokens.1), channel_id=1, source_target_pairs={{0,4},{4,8},{8,12},{12,0},{1,5},{5,9},{9,13},{13,1},{2,6},{6,10},{... | collective-permute-start | bytes 442376 | tf_op jit(solution)/shard_map/ppermute | solution.py:338
  6.1 12.6 %collective-permute-start.1 = (bf16[576,128]{1,0:T(8,128)(2,1)}, bf16[576,128]{1,0:T(8,128)(2,1)S(1)}, u32[]{:S(2)}, u32[]{:S(2)}) collective-permute-start(bf16[576,128]{1,0:T(8,128)(2,1)} %pack_tokens.1), channel_id=1, source_target_pairs={{0,8},{4,12},{8,0},{12,4},{1,9},{5,13},{9,1},{13,5},{2,10},{6,14},... | collective-permute-start | bytes 442376 | tf_op jit(solution)/shard_map/ppermute | solution.py:338
  8.7 10.0 %collective-permute-start.2 = (bf16[576,128]{1,0:T(8,128)(2,1)}, bf16[576,128]{1,0:T(8,128)(2,1)S(1)}, u32[]{:S(2)}, u32[]{:S(2)}) collective-permute-start(bf16[576,128]{1,0:T(8,128)(2,1)} %pack_tokens.1), channel_id=1, source_target_pairs={{0,12},{4,0},{8,4},{12,8},{1,13},{5,1},{9,5},{13,9},{2,14},{6,2},{... | collective-permute-start | bytes 442376 | tf_op jit(solution)/shard_map/ppermute | solution.py:338
  18.8 44.9 %copy-start = (bf16[2304,128]{1,0:T(8,128)(2,1)}, bf16[2304,128]{1,0:T(8,128)(2,1)S(1)}, u32[]{:S(2)}) copy-start(bf16[2304,128]{1,0:T(8,128)(2,1)S(1)} %pad_maximum_fusion.refs_0_) | copy-start | bytes 1769476
  18.8 15.2 %collective-permute-start.3 = (bf16[2304,128]{1,0:T(8,128)(2,1)S(1)}, bf16[2304,128]{1,0:T(8,128)(2,1)S(1)}, u32[]{:S(2)}, u32[]{:S(2)}) collective-permute-start(bf16[2304,128]{1,0:T(8,128)(2,1)S(1)} %pad_maximum_fusion.refs_0_), channel_id=1, source_target_pairs={{0,2},{2,0},{1,3},{3,1},{4,6},{6,4},{5,7},{7,5},{8,10},{10,8},{9,1... | collective-permute-start | bytes 1769480 | tf_op jit(solution)/shard_map/ppermute | solution.py:338
  20.4 19.7 %collective-permute-start.6 = (bf16[384,384]{1,0:T(8,128)(2,1)}, bf16[384,384]{1,0:T(8,128)(2,1)S(1)}, u32[]{:S(2)}, u32[]{:S(2)}) collective-permute-start(bf16[384,384]{1,0:T(8,128)(2,1)} %get-tuple-element.49), channel_id=1, source_target_pairs={{0,4},{4,8},{8,12},{12,0},{1,5},{5,9},{9,13},{13,1},{2,6},{6,10},{... | collective-permute-start | bytes 884744 | tf_op jit(solution)/shard_map/ppermute | solution.py:338
  24.0 37.5 %collective-permute-start.4 = (bf16[2304,128]{1,0:T(8,128)(2,1)S(1)}, bf16[2304,128]{1,0:T(8,128)(2,1)S(1)}, u32[]{:S(2)}, u32[]{:S(2)}) collective-permute-start(bf16[2304,128]{1,0:T(8,128)(2,1)S(1)} %pad_maximum_fusion.refs_0_), channel_id=1, source_target_pairs={{0,1},{1,0},{2,3},{3,2},{4,5},{5,4},{6,7},{7,6},{8,9},{9,8},{10,11... | collective-permute-start | bytes 1769480 | tf_op jit(solution)/shard_map/ppermute | solution.py:338
  34.0 29.7 %copy-start.3 = (bf16[2304,128]{1,0:T(8,128)(2,1)}, bf16[2304,128]{1,0:T(8,128)(2,1)S(1)}, u32[]{:S(2)}) copy-start(bf16[2304,128]{1,0:T(8,128)(2,1)S(1)} %collective-permute-done.3.refs_1_) | copy-start | bytes 1769476
  34.0 29.1 %collective-permute-start.5 = (bf16[2304,128]{1,0:T(8,128)(2,1)S(1)}, bf16[2304,128]{1,0:T(8,128)(2,1)S(1)}, u32[]{:S(2)}, u32[]{:S(2)}) collective-permute-start(bf16[2304,128]{1,0:T(8,128)(2,1)S(1)} %collective-permute-done.3.refs_1_), channel_id=1, source_target_pairs={{0,1},{1,0},{2,3},{3,2},{4,5},{5,4},{6,7},{7,6},{8,9},{9,8},{10,11... | collective-permute-start | bytes 1769480 | tf_op jit(solution)/shard_map/ppermute | solution.py:338
  34.0 17.3 %collective-permute-start.13 = (bf16[384,384]{1,0:T(8,128)(2,1)}, bf16[384,384]{1,0:T(8,128)(2,1)S(1)}, u32[]{:S(2)}, u32[]{:S(2)}) collective-permute-start(bf16[384,384]{1,0:T(8,128)(2,1)} %get-tuple-element.55), channel_id=1, source_target_pairs={{0,8},{4,12},{8,0},{12,4},{1,9},{5,13},{9,1},{13,5},{2,10},{6,14},... | collective-permute-start | bytes 884744 | tf_op jit(solution)/shard_map/ppermute | solution.py:338
  36.8 21.4 %collective-permute-start.14 = (bf16[384,384]{1,0:T(8,128)(2,1)}, bf16[384,384]{1,0:T(8,128)(2,1)S(1)}, u32[]{:S(2)}, u32[]{:S(2)}) collective-permute-start(bf16[384,384]{1,0:T(8,128)(2,1)} %get-tuple-element.56), channel_id=1, source_target_pairs={{0,12},{4,0},{8,4},{12,8},{1,13},{5,1},{9,5},{13,9},{2,14},{6,2},{... | collective-permute-start | bytes 884744 | tf_op jit(solution)/shard_map/ppermute | solution.py:338
  40.1 43.2 %copy-start.15 = (bf16[384,384]{1,0:T(8,128)(2,1)}, bf16[384,384]{1,0:T(8,128)(2,1)S(1)}, u32[]{:S(2)}) copy-start(bf16[384,384]{1,0:T(8,128)(2,1)S(1)} %collective-permute-done.6.refs_2_) | copy-start | bytes 884740
  40.1 21.4 %collective-permute-start.15 = (bf16[384,384]{1,0:T(8,128)(2,1)S(1)}, bf16[384,384]{1,0:T(8,128)(2,1)S(1)}, u32[]{:S(2)}, u32[]{:S(2)}) collective-permute-start(bf16[384,384]{1,0:T(8,128)(2,1)S(1)} %collective-permute-done.6.refs_2_), channel_id=1, source_target_pairs={{0,16},{16,0},{1,17},{17,1},{2,18},{18,2},{3,19},{19,3},{4,20},{20... | collective-permute-start | bytes 884744 | tf_op jit(solution)/shard_map/ppermute | solution.py:338
  51.3 31.9 %copy-start.16 = (bf16[384,384]{1,0:T(8,128)(2,1)}, bf16[384,384]{1,0:T(8,128)(2,1)S(1)}, u32[]{:S(2)}) copy-start(bf16[384,384]{1,0:T(8,128)(2,1)S(1)} %collective-permute-done.13.refs_3_) | copy-start | bytes 884740
  51.3 17.7 %collective-permute-start.7 = (bf16[384,384]{1,0:T(8,128)(2,1)}, bf16[384,384]{1,0:T(8,128)(2,1)S(1)}, u32[]{:S(2)}, u32[]{:S(2)}) collective-permute-start(bf16[384,384]{1,0:T(8,128)(2,1)} %get-tuple-element.50), channel_id=1, source_target_pairs={{0,4},{4,8},{8,12},{12,0},{1,5},{5,9},{9,13},{13,1},{2,6},{6,10},{... | collective-permute-start | bytes 884744 | tf_op jit(solution)/shard_map/ppermute | solution.py:338
  58.2 23.0 %collective-permute-start.8 = (bf16[384,384]{1,0:T(8,128)(2,1)}, bf16[384,384]{1,0:T(8,128)(2,1)}, u32[]{:S(2)}, u32[]{:S(2)}) collective-permute-start(bf16[384,384]{1,0:T(8,128)(2,1)} %get-tuple-element.51), channel_id=1, source_target_pairs={{0,8},{4,12},{8,0},{12,4},{1,9},{5,13},{9,1},{13,5},{2,10},{6,14},... | collective-permute-start | bytes 884744 | tf_op jit(solution)/shard_map/ppermute | solution.py:338
  61.5 21.3 %collective-permute-start.9 = (bf16[384,384]{1,0:T(8,128)(2,1)}, bf16[384,384]{1,0:T(8,128)(2,1)}, u32[]{:S(2)}, u32[]{:S(2)}) collective-permute-start(bf16[384,384]{1,0:T(8,128)(2,1)} %get-tuple-element.52), channel_id=1, source_target_pairs={{0,12},{4,0},{8,4},{12,8},{1,13},{5,1},{9,5},{13,9},{2,14},{6,2},{... | collective-permute-start | bytes 884744 | tf_op jit(solution)/shard_map/ppermute | solution.py:338
  61.5 21.8 %collective-permute-start.16 = (bf16[384,384]{1,0:T(8,128)(2,1)S(1)}, bf16[384,384]{1,0:T(8,128)(2,1)}, u32[]{:S(2)}, u32[]{:S(2)}) collective-permute-start(bf16[384,384]{1,0:T(8,128)(2,1)S(1)} %collective-permute-done.13.refs_3_), channel_id=1, source_target_pairs={{0,16},{16,0},{1,17},{17,1},{2,18},{18,2},{3,19},{19,3},{4,20},{20... | collective-permute-start | bytes 884744 | tf_op jit(solution)/shard_map/ppermute | solution.py:338
  63.1 20.2 %collective-permute-start.17 = (bf16[384,384]{1,0:T(8,128)(2,1)S(1)}, bf16[384,384]{1,0:T(8,128)(2,1)}, u32[]{:S(2)}, u32[]{:S(2)}) collective-permute-start(bf16[384,384]{1,0:T(8,128)(2,1)S(1)} %collective-permute-done.14.refs_4_), channel_id=1, source_target_pairs={{0,16},{16,0},{1,17},{17,1},{2,18},{18,2},{3,19},{19,3},{4,20},{20... | collective-permute-start | bytes 884744 | tf_op jit(solution)/shard_map/ppermute | solution.py:338
  69.1 25.5 %copy-start.17 = (bf16[384,384]{1,0:T(8,128)(2,1)}, bf16[384,384]{1,0:T(8,128)(2,1)S(1)}, u32[]{:S(2)}) copy-start(bf16[384,384]{1,0:T(8,128)(2,1)S(1)} %collective-permute-done.7.refs_2_) | copy-start | bytes 884740
  69.1 25.5 %collective-permute-start.10 = (bf16[384,384]{1,0:T(8,128)(2,1)S(1)}, bf16[384,384]{1,0:T(8,128)(2,1)S(1)}, u32[]{:S(2)}, u32[]{:S(2)}) collective-permute-start(bf16[384,384]{1,0:T(8,128)(2,1)S(1)} %collective-permute-done.7.refs_2_), channel_id=1, source_target_pairs={{0,16},{16,0},{1,17},{17,1},{2,18},{18,2},{3,19},{19,3},{4,20},{20... | collective-permute-start | bytes 884744 | tf_op jit(solution)/shard_map/ppermute | solution.py:338
  81.2 13.4 %collective-permute-start.11 = (bf16[384,384]{1,0:T(8,128)(2,1)}, bf16[384,384]{1,0:T(8,128)(2,1)S(1)}, u32[]{:S(2)}, u32[]{:S(2)}) collective-permute-start(bf16[384,384]{1,0:T(8,128)(2,1)} %collective-permute-done.8.refs_3_), channel_id=1, source_target_pairs={{0,16},{16,0},{1,17},{17,1},{2,18},{18,2},{3,19},{19,3},{4,20},{20... | collective-permute-start | bytes 884744 | tf_op jit(solution)/shard_map/ppermute | solution.py:338
  82.8 13.9 %collective-permute-start.12 = (bf16[384,384]{1,0:T(8,128)(2,1)}, bf16[384,384]{1,0:T(8,128)(2,1)S(1)}, u32[]{:S(2)}, u32[]{:S(2)}) collective-permute-start(bf16[384,384]{1,0:T(8,128)(2,1)} %collective-permute-done.9.refs_4_), channel_id=1, source_target_pairs={{0,16},{16,0},{1,17},{17,1},{2,18},{18,2},{3,19},{19,3},{4,20},{20... | collective-permute-start | bytes 884744 | tf_op jit(solution)/shard_map/ppermute | solution.py:338
  109.0 83.9 %all-to-all-start = ((bf16[4,272,256]{2,1,0:T(8,128)(2,1)}), bf16[4,272,256]{2,1,0:T(8,128)(2,1)S(1)}, u32[]{:S(2)}, u32[]{:S(2)}) async-start(bf16[4,272,256]{2,1,0:T(8,128)(2,1)} %get-tuple-element.58), calls=%async_computation | async-start | bytes 1114112 | tf_op jit(solution)/shard_map/all_to_all | solution.py:403
  115.8 40.5 %collective-permute-start.23 = (bf16[512,384]{1,0:T(8,128)(2,1)S(1)}, bf16[512,384]{1,0:T(8,128)(2,1)S(1)}, u32[]{:S(2)}, u32[]{:S(2)}) collective-permute-start(bf16[512,384]{1,0:T(8,128)(2,1)S(1)} %copy-done.10), channel_id=1, source_target_pairs={{0,8},{4,12},{8,0},{12,4},{1,9},{5,13},{9,1},{13,5},{2,10},{6,14},... | collective-permute-start | bytes 1179656 | tf_op jit(solution)/shard_map/ppermute | solution.py:398
  118.7 41.6 %collective-permute-start.22 = (bf16[512,384]{1,0:T(8,128)(2,1)S(1)}, bf16[512,384]{1,0:T(8,128)(2,1)S(1)}, u32[]{:S(2)}, u32[]{:S(2)}) collective-permute-start(bf16[512,384]{1,0:T(8,128)(2,1)S(1)} %copy-done.10), channel_id=1, source_target_pairs={{0,4},{4,0},{8,12},{12,8},{1,5},{5,1},{9,13},{13,9},{2,6},{6,2},{1... | collective-permute-start | bytes 1179656 | tf_op jit(solution)/shard_map/ppermute | solution.py:399
  120.2 44.5 %collective-permute-start.19 = (bf16[512,384]{1,0:T(8,128)(2,1)}, bf16[512,384]{1,0:T(8,128)(2,1)S(1)}, u32[]{:S(2)}, u32[]{:S(2)}) collective-permute-start(bf16[512,384]{1,0:T(8,128)(2,1)} %get-tuple-element.61.refs_0_), channel_id=1, source_target_pairs={{0,8},{4,12},{8,0},{12,4},{1,9},{5,13},{9,1},{13,5},{2,10},{6,14},... | collective-permute-start | bytes 1179656 | tf_op jit(solution)/shard_map/ppermute | solution.py:398
  120.7 45.3 %collective-permute-start.24 = (bf16[512,384]{1,0:T(8,128)(2,1)S(1)}, bf16[512,384]{1,0:T(8,128)(2,1)S(1)}, u32[]{:S(2)}, u32[]{:S(2)}) collective-permute-start(bf16[512,384]{1,0:T(8,128)(2,1)S(1)} %copy-done.10), channel_id=1, source_target_pairs={{4,8},{8,4},{5,9},{9,5},{6,10},{10,6},{7,11},{11,7},{20,24},{24,20... | collective-permute-start | bytes 1179656 | tf_op jit(solution)/shard_map/ppermute | solution.py:400
  156.2 15.9 %collective-permute-start.25 = (bf16[512,384]{1,0:T(8,128)(2,1)S(1)}, bf16[512,384]{1,0:T(8,128)(2,1)S(1)}, u32[]{:S(2)}, u32[]{:S(2)}) collective-permute-start(bf16[512,384]{1,0:T(8,128)(2,1)S(1)} %collective-permute-done.23.refs_2_), channel_id=1, source_target_pairs={{8,12},{4,0},{9,13},{5,1},{10,14},{6,2},{11,15},{7,3},{24,28},{20,... | collective-permute-start | bytes 1179656 | tf_op jit(solution)/shard_map/ppermute | solution.py:401
  157.5 23.0 %collective-permute-start.21 = (bf16[512,384]{1,0:T(8,128)(2,1)}, bf16[512,384]{1,0:T(8,128)(2,1)S(1)}, u32[]{:S(2)}, u32[]{:S(2)}) collective-permute-start(bf16[512,384]{1,0:T(8,128)(2,1)} %get-tuple-element.61.refs_0_), channel_id=1, source_target_pairs={{0,4},{4,0},{8,12},{12,8},{1,5},{5,1},{9,13},{13,9},{2,6},{6,2},{1... | collective-permute-start | bytes 1179656 | tf_op jit(solution)/shard_map/ppermute | solution.py:399
  160.3 26.0 %collective-permute-start.18 = (bf16[512,384]{1,0:T(8,128)(2,1)}, bf16[512,384]{1,0:T(8,128)(2,1)S(1)}, u32[]{:S(2)}, u32[]{:S(2)}) collective-permute-start(bf16[512,384]{1,0:T(8,128)(2,1)} %get-tuple-element.61.refs_0_), channel_id=1, source_target_pairs={{4,8},{8,4},{5,9},{9,5},{6,10},{10,6},{7,11},{11,7},{20,24},{24,20... | collective-permute-start | bytes 1179656 | tf_op jit(solution)/shard_map/ppermute | solution.py:400
  164.7 24.2 %collective-permute-start.20 = (bf16[512,384]{1,0:T(8,128)(2,1)S(1)}, bf16[512,384]{1,0:T(8,128)(2,1)S(1)}, u32[]{:S(2)}, u32[]{:S(2)}) collective-permute-start(bf16[512,384]{1,0:T(8,128)(2,1)S(1)} %collective-permute-done.19.refs_2_), channel_id=1, source_target_pairs={{8,12},{4,0},{9,13},{5,1},{10,14},{6,2},{11,15},{7,3},{24,28},{20,... | collective-permute-start | bytes 1179656 | tf_op jit(solution)/shard_map/ppermute | solution.py:401
  (18 other events, 125.6 us)

commit v3 on v2

--- a/solution.py
+++ b/solution.py
@@ -333,6 +333,9 @@
     def shape(dims, kind):
         return jax.ShapeDtypeStruct(dims, kind)
 
+    def after(x, earlier):
+        return lax.optimization_barrier((x, earlier))
+
     def along(x, axis, hop):
         count = lax.axis_size(axis)
         return lax.ppermute(x, axis, [(i, (i + hop) % count) for i in range(count)])
@@ -354,10 +357,12 @@
     )(where, w_query, w_key, w_value, log_decay, grad_out, beta_logit)
 
     near = [along(tok, "ctx", d) for d in range(1, ctx)]
-    first, near[0] = lax.optimization_barrier((packed[1:ctx], near[0]))
+    first, near[0] = after(packed[1:ctx], near[0])
+    first = [along(x, "ctx", d + 1) for d, x in enumerate(first)]
     tok = jnp.concatenate([tok] + near, axis=0)
     tok_x = along(tok, "fsdp", 1)
-    toks = (tok, tok_x, along(tok, "head", 1), along(tok_x, "head", 1))
+    (tok_c, tok_xc), first = after((tok, tok_x), first)
+    toks = (tok, tok_x, along(tok_c, "head", 1), along(tok_xc, "head", 1))
     all_tokens, own = pl.pallas_call(
         functools.partial(unpack_tokens_kernel, ctx),
         out_shape=[shape((ctx, total, share), bf16), shape((share, total), bf16)],
@@ -365,14 +370,18 @@
         out_specs=[whole] * 2,
         name="unpack_tokens",
     )(where, *toks)
-    first = [along(x, "ctx", d + 1) for d, x in enumerate(first)]
-    second, first[0] = lax.optimization_barrier((packed[ctx + 1 :], first[0]))
+    first_swapped = [along(x, "groups", 1) for x in first]
+    second, (first[2], first_swapped[0], first_swapped[1]) = after(
+        packed[ctx + 1 :], (first[2], first_swapped[0], first_swapped[1])
+    )
     second = [along(x, "ctx", d + 1) for d, x in enumerate(second)]
 
     grads = []
     back = None
     for slot, direct in enumerate((first, second)):
-        swapped = [along(x, "groups", 1) for x in direct]
+        if slot:
+            direct, back = after(direct, back)
+        swapped = [along(x, "groups", 1) for x in direct] if slot else first_swapped
         earlier = [] if back is None else [back]
         grad, back = pl.pallas_call(
             functools.partial(head_kernel, ctx, slot),
@@ -395,25 +404,28 @@
             cost_estimate=pl.CostEstimate(flops=12_000_000_000, transcendentals=0, bytes_accessed=8_000_000),
             name=f"head_{slot}",
         )(where, all_tokens, packed[slot * ctx], *direct, *swapped, *earlier)
+        if slot:
+            grad, grads[0][1:3] = after(grad, grads[0][1:3])
         two = lax.ppermute(grad, "ctx", [(0, 2), (1, 3), (2, 0), (3, 1)])
         pair = lax.ppermute(grad, "ctx", [(0, 1), (1, 0), (2, 3), (3, 2)])
+        (grad, two), pair = after((grad, two), pair)
+        if slot:
+            (grad, two, back), grads[0][3:5] = after((grad, two, back), grads[0][3:5])
         middle = lax.ppermute(grad, "ctx", [(1, 2), (2, 1)])
         far = lax.ppermute(two, "ctx", [(2, 3), (1, 0)])
-        grads.append((grad, pair, two, middle, far))
+        grads.append([grad, pair, two, middle, far])
     back = lax.all_to_all(back, "ctx", 0, 0)
 
     results = ()
     for slot, steps in ((0, (0, 1, 2, 3)), (1, (0, 1, 2)), (1, (3,))):
         parts = [grads[slot][step] for step in steps] + ([grads[slot][4]] if 3 in steps else [])
         column = pl.BlockSpec((share, DK), lambda i, ref, s=slot, b=steps[0]: (0, 2 * ref[6 + b + i] + s))
-        fixed = lambda dims: pl.BlockSpec(dims, lambda i, ref: (0, 0))
         results = pl.pallas_call(
             functools.partial(weight_gradient_kernel, steps),
             grid_spec=pltpu.PrefetchScalarGridSpec(
                 num_scalar_prefetch=1,
                 grid=(len(steps),),
-                in_specs=[fixed((share, total))]
-                + [fixed((total, HEAD_COLUMNS))] * len(parts)
+                in_specs=[whole] * (1 + len(parts))
                 + [pl.BlockSpec(memory_space=pl.ANY)] * len(results),
                 out_specs=[column] * 3,
             ),

time: 196 us -> 187 us (0.954)
  waiting for transfers between devices: 87.4 us -> 75.2 us
    ppermute x2, waiting for transfers between devices: 38.6 us -> 15.7 us  [head_split(): two = lax.ppermute(grad, 'ctx', [(0, 2), (1, 3), (2, 0), (3, 1)])]
    ppermute x18, waiting for transfers between devices: 38 us -> 46.5 us  [along(): return lax.ppermute(x, axis, [(i, (i + hop) % count) for i in range(count)])]
    ppermute x2, starting transfers between devices: 3.48 us -> 11.7 us  [head_split(): two = lax.ppermute(grad, 'ctx', [(0, 2), (1, 3), (2, 0), (3, 1)])]
    ppermute x2, waiting for transfers between devices: 8.76 us -> 13 us  [head_split(): far = lax.ppermute(two, 'ctx', [(2, 3), (1, 0)])]
    ppermute x18, starting transfers between devices: 35.6 us -> 31.5 us  [along(): return lax.ppermute(x, axis, [(i, (i + hop) % count) for i in range(count)])]
    ppermute x2, waiting for transfers between devices: 1.97 us -> 0.01 us  [head_split(): pair = lax.ppermute(grad, 'ctx', [(0, 1), (1, 0), (2, 3), (3, 2)])]
  transfers between devices with their start and end apart: 27 -> 27, of which waited for: 11 -> 11; matrix products, arithmetic and copies ran while one was open for 0% -> 0% of each run, Pallas kernels for 17% -> 24%
where the time goes in v3:
time: 187 us; the launch traced here: 185 us
  waiting for transfers between devices  75.2 us (40%)
  starting transfers between devices  55.7 us (30%)
  Pallas kernels  49 us (26%)
  local copies, waits for them, and re-layouts  4.38 us (2%)
    ppermute x18, waiting for transfers between devices, along(): return lax.ppermute(x, axis, [(i, (i + hop) % count) for i in range(count)])  46.5 us
    ppermute x18, starting transfers between devices, along(): return lax.ppermute(x, axis, [(i, (i + hop) % count) for i in range(count)])  31.5 us
    pallas_call x2, Pallas kernels, head_split(): pl.pallas_call(functools.partial(head_kernel, ctx, slot), out_shape=[shap...  23 us
    ppermute x2, waiting for transfers between devices, head_split(): two = lax.ppermute(grad, 'ctx', [(0, 2), (1, 3), (2, 0), (3, 1)])  15.7 us
    pallas_call x3, Pallas kernels, head_split(): pl.pallas_call(functools.partial(weight_gradient_kernel, steps), grid_spe...  14 us
    ppermute x2, waiting for transfers between devices, head_split(): far = lax.ppermute(two, 'ctx', [(2, 3), (1, 0)])  13 us
    ppermute x2, starting transfers between devices, head_split(): two = lax.ppermute(grad, 'ctx', [(0, 2), (1, 3), (2, 0), (3, 1)])  11.7 us
    all_to_all x1, starting transfers between devices, head_split(): back = lax.all_to_all(back, 'ctx', 0, 0)  5.84 us
  transfers between devices with their start and end apart: 27, of which 11 were waited for; matrix products, arithmetic and copies ran while one was open for 0% of the time, Pallas kernels for 24%

profile of v3, /device:TPU:0, one launch (start us, length us, event | category | flops | bytes accessed | tf_op | source)
XLA Modules:
  0.0 185.1 jit_solution(10040742151815357833)
XLA Ops:
  1.3 1.8 pack_tokens.1
  3.1 3.0 %collective-permute-start = (bf16[576,128]{1,0:T(8,128)(2,1)}, bf16[576,128]{1,0:T(8,128)(2,1)S(1)}, u32[]{:S(2)}, u32[]{:S(2)}) collective-permute-start(bf16[576,128]{1,0:T(8,128)(2,1)} %pack_tokens.1), channel_id=1, source_target_pairs={{0,4},{4,8},{8,12},{12,0},{1,5},{5,9},{9,13},{13,1},{2,6},{6,10},{... | collective-permute-start | bytes 442376 | tf_op jit(solution)/shard_map/ppermute | solution.py:341
  6.2 2.6 %collective-permute-start.1 = (bf16[576,128]{1,0:T(8,128)(2,1)}, bf16[576,128]{1,0:T(8,128)(2,1)S(1)}, u32[]{:S(2)}, u32[]{:S(2)}) collective-permute-start(bf16[576,128]{1,0:T(8,128)(2,1)} %pack_tokens.1), channel_id=1, source_target_pairs={{0,8},{4,12},{8,0},{12,4},{1,9},{5,13},{9,1},{13,5},{2,10},{6,14},... | collective-permute-start | bytes 442376 | tf_op jit(solution)/shard_map/ppermute | solution.py:341
  10.1 4.5 %pack.1 = (bf16[672,384]{1,0:T(8,128)(2,1)}, bf16[384,384]{1,0:T(8,128)(2,1)}, bf16[384,384]{1,0:T(8,128)(2,1)}, bf16[384,384]{1,0:T(8,128)(2,1)}, bf16[672,384]...) custom-call(s32[11]{0:T(128)} %stack.48.where_ref, ...), custom_call_target="tpu_custom_call" | custom-call | tf_op jit(solution)/shard_map/pack/pallas_call | solution.py:351
  14.6 4.2 %collective-permute-done.1 = bf16[576,128]{1,0:T(8,128)(2,1)S(1)} collective-permute-done((bf16[576,128]{1,0:T(8,128)(2,1)}, bf16[576,128]{1,0:T(8,128)(2,1)S(1)}, u32[]{:S(2)}, u32[]{:S(2)}) %collective-permute-start.1) | collective-permute-done | bytes 147488 | tf_op jit(solution)/shard_map/ppermute | solution.py:341
  18.9 1.6 collective-permute-start.3
  20.4 3.6 %collective-permute-start.4 = (bf16[384,384]{1,0:T(8,128)(2,1)}, bf16[384,384]{1,0:T(8,128)(2,1)S(1)}, u32[]{:S(2)}, u32[]{:S(2)}) collective-permute-start(bf16[384,384]{1,0:T(8,128)(2,1)} %get-tuple-element.69), channel_id=1, source_target_pairs={{0,4},{4,8},{8,12},{12,0},{1,5},{5,9},{9,13},{13,1},{2,6},{6,10},{... | collective-permute-start | bytes 884744 | tf_op jit(solution)/shard_map/ppermute | solution.py:341
  24.0 1.6 collective-permute-start.5
  26.4 6.9 %collective-permute-done.4.refs_2_ = bf16[384,384]{1,0:T(8,128)(2,1)S(1)} collective-permute-done((bf16[384,384]{1,0:T(8,128)(2,1)}, bf16[384,384]{1,0:T(8,128)(2,1)S(1)}, u32[]{:S(2)}, u32[]{:S(2)}) %collective-permute-start.4) | collective-permute-done | bytes 294944 | tf_op jit(solution)/shard_map/ppermute | solution.py:341
  33.3 10.6 %collective-permute-done.5.refs_3_ = bf16[384,384]{1,0:T(8,128)(2,1)S(1)} collective-permute-done((bf16[384,384]{1,0:T(8,128)(2,1)}, bf16[384,384]{1,0:T(8,128)(2,1)S(1)}, u32[]{:S(2)}, u32[]{:S(2)}) %collective-permute-start.5) | collective-permute-done | bytes 294944 | tf_op jit(solution)/shard_map/ppermute | solution.py:341
  44.5 1.5 collective-permute-start.10
  48.1 6.3 %collective-permute-done.10.refs_6_ = bf16[384,384]{1,0:T(8,128)(2,1)S(1)} collective-permute-done((bf16[384,384]{1,0:T(8,128)(2,1)S(1)}, bf16[384,384]{1,0:T(8,128)(2,1)S(1)}, u32[]{:S(2)}, u32[]{:S(2)}) %collective-permute-start.10) | collective-permute-done | bytes 294944 | tf_op jit(solution)/shard_map/ppermute | solution.py:341
  54.4 6.3 %collective-permute-done.9.refs_5_ = bf16[384,384]{1,0:T(8,128)(2,1)S(1)} collective-permute-done((bf16[384,384]{1,0:T(8,128)(2,1)S(1)}, bf16[384,384]{1,0:T(8,128)(2,1)S(1)}, u32[]{:S(2)}, u32[]{:S(2)}) %collective-permute-start.9) | collective-permute-done | bytes 294944 | tf_op jit(solution)/shard_map/ppermute | solution.py:341
  60.7 6.8 %collective-permute-start.11 = (bf16[384,384]{1,0:T(8,128)(2,1)}, bf16[384,384]{1,0:T(8,128)(2,1)}, u32[]{:S(2)}, u32[]{:S(2)}) collective-permute-start(bf16[384,384]{1,0:T(8,128)(2,1)} %get-tuple-element.82), channel_id=1, source_target_pairs={{0,4},{4,8},{8,12},{12,0},{1,5},{5,9},{9,13},{13,1},{2,6},{6,10},{... | collective-permute-start | bytes 884744 | tf_op jit(solution)/shard_map/ppermute | solution.py:341
  67.5 2.3 %collective-permute-start.12 = (bf16[384,384]{1,0:T(8,128)(2,1)}, bf16[384,384]{1,0:T(8,128)(2,1)}, u32[]{:S(2)}, u32[]{:S(2)}) collective-permute-start(bf16[384,384]{1,0:T(8,128)(2,1)} %get-tuple-element.83), channel_id=1, source_target_pairs={{0,8},{4,12},{8,0},{12,4},{1,9},{5,13},{9,1},{13,5},{2,10},{6,14},... | collective-permute-start | bytes 884744 | tf_op jit(solution)/shard_map/ppermute | solution.py:341
  71.5 3.7 %unpack_tokens.1 = (bf16[4,512,576]{2,1,0:T(8,128)(2,1)}, bf16[576,512]{1,0:T(8,128)(2,1)}) custom-call(s32[11]{0:T(128)} %stack.48.where_ref, bf16[2304,128]{1,0:T(8,128)(2,1)} %copy-done, bf16[2304,128]{1,0:T(8,128)(2,1)} %copy-done.3, bf16[2304,128]{1,0:T(8,128)(2,1)} %copy-done.4, bf16[2304,128]{1,0:T(8,128)(2,1)} %copy-done.5), custom_call_target="tpu_custom_call" | custom-call | tf_op jit(solution)/shard_map/unpack_tokens/pallas_call | solution.py:366
  75.2 11.3 %head_0.1 = (bf16[512,384]{1,0:T(8,128)(2,1)}, bf16[4,272,128]{2,1,0:T(8,128)(2,1)}) custom-call(s32[11]{0:T(128)} %stack.48.where_ref, bf16[4,512,576]{2,1,0:T(8,128)(2,1)} %get-tuple-element.74.refs_0_, bf16[672,384]{1,0:T(8,128)(2,1)} %get-tuple-element.85.refs_1_, bf16[384,384]{1,0:T(8,128)(2,1)} %copy-done.15, bf16[384,384]{1,0:T(8,128)(2,1)} %copy-done.16, ...), custom_call_target="tpu_custom_call" | custom-call | flops 12000000000 | bytes 8000000 | tf_op jit(solution)/shard_map/head_0/pallas_call | solution.py:386
  87.9 1.5 collective-permute-start.15
  91.5 5.8 %collective-permute-start.18 = (bf16[512,384]{1,0:T(8,128)(2,1)}, bf16[512,384]{1,0:T(8,128)(2,1)S(1)}, u32[]{:S(2)}, u32[]{:S(2)}) collective-permute-start(bf16[512,384]{1,0:T(8,128)(2,1)} %get-tuple-element.102.refs_0_), channel_id=1, source_target_pairs={{0,8},{4,12},{8,0},{12,4},{1,9},{5,13},{9,1},{13,5},{2,10},{6,14},... | collective-permute-start | bytes 1179656 | tf_op jit(solution)/shard_map/ppermute | solution.py:409
  97.2 1.6 collective-permute-start.19
  98.8 5.5 %collective-permute-done.16.refs_6_ = bf16[384,384]{1,0:T(8,128)(2,1)S(1)} collective-permute-done((bf16[384,384]{1,0:T(8,128)(2,1)}, bf16[384,384]{1,0:T(8,128)(2,1)S(1)}, u32[]{:S(2)}, u32[]{:S(2)}) %collective-permute-start.16) | collective-permute-done | bytes 294944 | tf_op jit(solution)/shard_map/ppermute | solution.py:341
  104.3 5.3 %collective-permute-done.17.refs_7_ = bf16[384,384]{1,0:T(8,128)(2,1)S(1)} collective-permute-done((bf16[384,384]{1,0:T(8,128)(2,1)}, bf16[384,384]{1,0:T(8,128)(2,1)S(1)}, u32[]{:S(2)}, u32[]{:S(2)}) %collective-permute-start.17) | collective-permute-done | bytes 294944 | tf_op jit(solution)/shard_map/ppermute | solution.py:341
  110.3 11.7 %head_1.1 = (bf16[512,384]{1,0:T(8,128)(2,1)}, bf16[4,272,256]{2,1,0:T(8,128)(2,1)}) custom-call(s32[11]{0:T(128)} %stack.48.where_ref, bf16[4,512,576]{2,1,0:T(8,128)(2,1)} %get-tuple-element.74.refs_0_, bf16[672,384]{1,0:T(8,128)(2,1)} %get-tuple-element.75.refs_1_, bf16[384,384]{1,0:T(8,128)(2,1)} %collective-permute-done.11.refs_2_, ...), custom_call_target="tpu_custom_call" | custom-call | flops 12000000000 | bytes 8000000 | tf_op jit(solution)/shard_map/head_1/pallas_call | solution.py:386
  122.1 5.9 %collective-permute-start.20 = (bf16[512,384]{1,0:T(8,128)(2,1)}, bf16[512,384]{1,0:T(8,128)(2,1)S(1)}, u32[]{:S(2)}, u32[]{:S(2)}) collective-permute-start(bf16[512,384]{1,0:T(8,128)(2,1)} %get-tuple-element.106.refs_0_), channel_id=1, source_target_pairs={{0,8},{4,12},{8,0},{12,4},{1,9},{5,13},{9,1},{13,5},{2,10},{6,14},... | collective-permute-start | bytes 1179656 | tf_op jit(solution)/shard_map/ppermute | solution.py:409
  131.1 15.6 %collective-permute-done.20.refs_2_ = bf16[512,384]{1,0:T(8,128)(2,1)S(1)} collective-permute-done((bf16[512,384]{1,0:T(8,128)(2,1)}, bf16[512,384]{1,0:T(8,128)(2,1)S(1)}, u32[]{:S(2)}, u32[]{:S(2)}) %collective-permute-start.20) | collective-permute-done | bytes 393248 | tf_op jit(solution)/shard_map/ppermute | solution.py:409
  146.7 6.8 %collective-permute-done.23.refs_4_ = bf16[512,384]{1,0:T(8,128)(2,1)S(1)} collective-permute-done((bf16[512,384]{1,0:T(8,128)(2,1)S(1)}, bf16[512,384]{1,0:T(8,128)(2,1)S(1)}, u32[]{:S(2)}, u32[]{:S(2)}) %collective-permute-start.23) | collective-permute-done | bytes 393248 | tf_op jit(solution)/shard_map/ppermute | solution.py:415
  153.5 5.8 %all-to-all-start = ((bf16[4,272,256]{2,1,0:T(8,128)(2,1)}), bf16[4,272,256]{2,1,0:T(8,128)(2,1)S(1)}, u32[]{:S(2)}, u32[]{:S(2)}) async-start(bf16[4,272,256]{2,1,0:T(8,128)(2,1)} %get-tuple-element.103), calls=%async_computation | async-start | bytes 1114112 | tf_op jit(solution)/shard_map/all_to_all | solution.py:417
  161.4 5.7 %weight_gradient_0_0.1 = (f32[576,1024]{1,0:T(8,128)}, f32[576,1024]{1,0:T(8,128)}, f32[576,1024]{1,0:T(8,128)}) custom-call(s32[11]{0:T(128)} %stack.48.where_ref, bf16[576,512]{1,0:T(8,128)(2,1)} %get-tuple-element.105.own_ref, bf16[512,384]{1,0:T(8,128)(2,1)} %get-tuple-element.102.refs_0_, bf16[512,384]{1,0:T(8,128)(2,1)} %copy-done.12, ...), custom_call_target="tpu_custom_call" | custom-call | tf_op jit(solution)/shard_map/weight_gradient_0_0/pallas_call | solution.py:423
  167.1 4.9 %weight_gradient_1_0.1 = (f32[576,1024]{1,0:T(8,128)}, f32[576,1024]{1,0:T(8,128)}, f32[576,1024]{1,0:T(8,128)}) custom-call(s32[11]{0:T(128)} %stack.48.where_ref, bf16[576,512]{1,0:T(8,128)(2,1)} %get-tuple-element.105.own_ref, bf16[512,384]{1,0:T(8,128)(2,1)} %get-tuple-element.106.refs_0_, ...), custom_call_target="tpu_custom_call", output_to_operand_aliasing={{0}: (5, {}), {1}: (6, {}), {2}: (7, {})} | custom-call | tf_op jit(solution)/shard_map/weight_gradient_1_0/pallas_call | solution.py:423
  172.0 6.2 %collective-permute-done.25.refs_1_ = bf16[512,384]{1,0:T(8,128)(2,1)S(1)} collective-permute-done((bf16[512,384]{1,0:T(8,128)(2,1)S(1)}, bf16[512,384]{1,0:T(8,128)(2,1)S(1)}, u32[]{:S(2)}, u32[]{:S(2)}) %collective-permute-start.25) | collective-permute-done | bytes 393248 | tf_op jit(solution)/shard_map/ppermute | solution.py:415
  179.0 3.3 %weight_gradient_1_3.1 = (f32[576,1024]{1,0:T(8,128)}, f32[576,1024]{1,0:T(8,128)}, f32[576,1024]{1,0:T(8,128)}) custom-call(s32[11]{0:T(128)} %stack.48.where_ref, bf16[576,512]{1,0:T(8,128)(2,1)} %get-tuple-element.105.own_ref, bf16[512,384]{1,0:T(8,128)(2,1)} %copy-done.8, ...), custom_call_target="tpu_custom_call", output_to_operand_aliasing={{0}: (4, {}), {1}: (5, {}), {2}: (6, {})} | custom-call | tf_op jit(solution)/shard_map/weight_gradient_1_3/pallas_call | solution.py:423
  183.1 2.0 %unpack.1 = (bf16[128,1024]{1,0:T(8,128)(2,1)}, f32[8,128]{1,0:T(8,128)}, f32[128,1024]{1,0:T(8,128)}) custom-call(bf16[4,272,256]{2,1,0:T(8,128)(2,1)} %copy-done.1), custom_call_target="tpu_custom_call" | custom-call | tf_op jit(solution)/shard_map/unpack/pallas_call | solution.py:437
  (79 shorter events, 17.8 us)
Async XLA Ops:
  3.1 11.4 %collective-permute-start = (bf16[576,128]{1,0:T(8,128)(2,1)}, bf16[576,128]{1,0:T(8,128)(2,1)S(1)}, u32[]{:S(2)}, u32[]{:S(2)}) collective-permute-start(bf16[576,128]{1,0:T(8,128)(2,1)} %pack_tokens.1), channel_id=1, source_target_pairs={{0,4},{4,8},{8,12},{12,0},{1,5},{5,9},{9,13},{13,1},{2,6},{6,10},{... | collective-permute-start | bytes 442376 | tf_op jit(solution)/shard_map/ppermute | solution.py:341
  6.2 12.6 %collective-permute-start.1 = (bf16[576,128]{1,0:T(8,128)(2,1)}, bf16[576,128]{1,0:T(8,128)(2,1)S(1)}, u32[]{:S(2)}, u32[]{:S(2)}) collective-permute-start(bf16[576,128]{1,0:T(8,128)(2,1)} %pack_tokens.1), channel_id=1, source_target_pairs={{0,8},{4,12},{8,0},{12,4},{1,9},{5,13},{9,1},{13,5},{2,10},{6,14},... | collective-permute-start | bytes 442376 | tf_op jit(solution)/shard_map/ppermute | solution.py:341
  8.8 10.0 %collective-permute-start.2 = (bf16[576,128]{1,0:T(8,128)(2,1)}, bf16[576,128]{1,0:T(8,128)(2,1)S(1)}, u32[]{:S(2)}, u32[]{:S(2)}) collective-permute-start(bf16[576,128]{1,0:T(8,128)(2,1)} %pack_tokens.1), channel_id=1, source_target_pairs={{0,12},{4,0},{8,4},{12,8},{1,13},{5,1},{9,5},{13,9},{2,14},{6,2},{... | collective-permute-start | bytes 442376 | tf_op jit(solution)/shard_map/ppermute | solution.py:341
  18.8 51.3 %copy-start = (bf16[2304,128]{1,0:T(8,128)(2,1)}, bf16[2304,128]{1,0:T(8,128)(2,1)S(1)}, u32[]{:S(2)}) copy-start(bf16[2304,128]{1,0:T(8,128)(2,1)S(1)} %pad_maximum_fusion.refs_0_) | copy-start | bytes 1769476
  18.9 25.1 %collective-permute-start.3 = (bf16[2304,128]{1,0:T(8,128)(2,1)S(1)}, bf16[2304,128]{1,0:T(8,128)(2,1)S(1)}, u32[]{:S(2)}, u32[]{:S(2)}) collective-permute-start(bf16[2304,128]{1,0:T(8,128)(2,1)S(1)} %pad_maximum_fusion.refs_0_), channel_id=1, source_target_pairs={{0,2},{2,0},{1,3},{3,1},{4,6},{6,4},{5,7},{7,5},{8,10},{10,8},{9,1... | collective-permute-start | bytes 1769480 | tf_op jit(solution)/shard_map/ppermute | solution.py:341
  20.4 12.9 %collective-permute-start.4 = (bf16[384,384]{1,0:T(8,128)(2,1)}, bf16[384,384]{1,0:T(8,128)(2,1)S(1)}, u32[]{:S(2)}, u32[]{:S(2)}) collective-permute-start(bf16[384,384]{1,0:T(8,128)(2,1)} %get-tuple-element.69), channel_id=1, source_target_pairs={{0,4},{4,8},{8,12},{12,0},{1,5},{5,9},{9,13},{13,1},{2,6},{6,10},{... | collective-permute-start | bytes 884744 | tf_op jit(solution)/shard_map/ppermute | solution.py:341
  24.0 19.9 %collective-permute-start.5 = (bf16[384,384]{1,0:T(8,128)(2,1)}, bf16[384,384]{1,0:T(8,128)(2,1)S(1)}, u32[]{:S(2)}, u32[]{:S(2)}) collective-permute-start(bf16[384,384]{1,0:T(8,128)(2,1)} %get-tuple-element.70), channel_id=1, source_target_pairs={{0,8},{4,12},{8,0},{12,4},{1,9},{5,13},{9,1},{13,5},{2,10},{6,14},... | collective-permute-start | bytes 884744 | tf_op jit(solution)/shard_map/ppermute | solution.py:341
  25.6 18.3 %collective-permute-start.6 = (bf16[384,384]{1,0:T(8,128)(2,1)}, bf16[384,384]{1,0:T(8,128)(2,1)S(1)}, u32[]{:S(2)}, u32[]{:S(2)}) collective-permute-start(bf16[384,384]{1,0:T(8,128)(2,1)} %get-tuple-element.71), channel_id=1, source_target_pairs={{0,12},{4,0},{8,4},{12,8},{1,13},{5,1},{9,5},{13,9},{2,14},{6,2},{... | collective-permute-start | bytes 884744 | tf_op jit(solution)/shard_map/ppermute | solution.py:341
  33.3 41.9 %copy-start.15 = (bf16[384,384]{1,0:T(8,128)(2,1)}, bf16[384,384]{1,0:T(8,128)(2,1)S(1)}, u32[]{:S(2)}) copy-start(bf16[384,384]{1,0:T(8,128)(2,1)S(1)} %collective-permute-done.4.refs_2_) | copy-start | bytes 884740
  44.0 31.3 %copy-start.17 = (bf16[384,384]{1,0:T(8,128)(2,1)}, bf16[384,384]{1,0:T(8,128)(2,1)S(1)}, u32[]{:S(2)}) copy-start(bf16[384,384]{1,0:T(8,128)(2,1)S(1)} %collective-permute-done.6.refs_4_) | copy-start | bytes 884740
  44.0 25.9 %collective-permute-start.7 = (bf16[2304,128]{1,0:T(8,128)(2,1)S(1)}, bf16[2304,128]{1,0:T(8,128)(2,1)S(1)}, u32[]{:S(2)}, u32[]{:S(2)}) collective-permute-start(bf16[2304,128]{1,0:T(8,128)(2,1)S(1)} %pad_maximum_fusion.refs_0_), channel_id=1, source_target_pairs={{0,1},{1,0},{2,3},{3,2},{4,5},{5,4},{6,7},{7,6},{8,9},{9,8},{10,11... | collective-permute-start | bytes 1769480 | tf_op jit(solution)/shard_map/ppermute | solution.py:341
  44.1 26.1 %collective-permute-start.8 = (bf16[2304,128]{1,0:T(8,128)(2,1)S(1)}, bf16[2304,128]{1,0:T(8,128)(2,1)S(1)}, u32[]{:S(2)}, u32[]{:S(2)}) collective-permute-start(bf16[2304,128]{1,0:T(8,128)(2,1)S(1)} %collective-permute-done.3.refs_1_), channel_id=1, source_target_pairs={{0,1},{1,0},{2,3},{3,2},{4,5},{5,4},{6,7},{7,6},{8,9},{9,8},{10,11... | collective-permute-start | bytes 1769480 | tf_op jit(solution)/shard_map/ppermute | solution.py:341
  44.5 9.9 %collective-permute-start.10 = (bf16[384,384]{1,0:T(8,128)(2,1)S(1)}, bf16[384,384]{1,0:T(8,128)(2,1)S(1)}, u32[]{:S(2)}, u32[]{:S(2)}) collective-permute-start(bf16[384,384]{1,0:T(8,128)(2,1)S(1)} %collective-permute-done.5.refs_3_), channel_id=1, source_target_pairs={{0,16},{16,0},{1,17},{17,1},{2,18},{18,2},{3,19},{19,3},{4,20},{20... | collective-permute-start | bytes 884744 | tf_op jit(solution)/shard_map/ppermute | solution.py:341
  46.1 14.7 %collective-permute-start.9 = (bf16[384,384]{1,0:T(8,128)(2,1)S(1)}, bf16[384,384]{1,0:T(8,128)(2,1)S(1)}, u32[]{:S(2)}, u32[]{:S(2)}) collective-permute-start(bf16[384,384]{1,0:T(8,128)(2,1)S(1)} %collective-permute-done.4.refs_2_), channel_id=1, source_target_pairs={{0,16},{16,0},{1,17},{17,1},{2,18},{18,2},{3,19},{19,3},{4,20},{20... | collective-permute-start | bytes 884744 | tf_op jit(solution)/shard_map/ppermute | solution.py:341
  46.6 28.6 %collective-permute-start.14 = (bf16[384,384]{1,0:T(8,128)(2,1)S(1)}, bf16[384,384]{1,0:T(8,128)(2,1)}, u32[]{:S(2)}, u32[]{:S(2)}) collective-permute-start(bf16[384,384]{1,0:T(8,128)(2,1)S(1)} %collective-permute-done.6.refs_4_), channel_id=1, source_target_pairs={{0,16},{16,0},{1,17},{17,1},{2,18},{18,2},{3,19},{19,3},{4,20},{20... | collective-permute-start | bytes 884744 | tf_op jit(solution)/shard_map/ppermute | solution.py:341
  60.7 25.8 %collective-permute-start.11 = (bf16[384,384]{1,0:T(8,128)(2,1)}, bf16[384,384]{1,0:T(8,128)(2,1)}, u32[]{:S(2)}, u32[]{:S(2)}) collective-permute-start(bf16[384,384]{1,0:T(8,128)(2,1)} %get-tuple-element.82), channel_id=1, source_target_pairs={{0,4},{4,8},{8,12},{12,0},{1,5},{5,9},{9,13},{13,1},{2,6},{6,10},{... | collective-permute-start | bytes 884744 | tf_op jit(solution)/shard_map/ppermute | solution.py:341
  67.5 20.4 %collective-permute-start.12 = (bf16[384,384]{1,0:T(8,128)(2,1)}, bf16[384,384]{1,0:T(8,128)(2,1)}, u32[]{:S(2)}, u32[]{:S(2)}) collective-permute-start(bf16[384,384]{1,0:T(8,128)(2,1)} %get-tuple-element.83), channel_id=1, source_target_pairs={{0,8},{4,12},{8,0},{12,4},{1,9},{5,13},{9,1},{13,5},{2,10},{6,14},... | collective-permute-start | bytes 884744 | tf_op jit(solution)/shard_map/ppermute | solution.py:341
  69.8 18.1 %collective-permute-start.13 = (bf16[384,384]{1,0:T(8,128)(2,1)}, bf16[384,384]{1,0:T(8,128)(2,1)}, u32[]{:S(2)}, u32[]{:S(2)}) collective-permute-start(bf16[384,384]{1,0:T(8,128)(2,1)} %get-tuple-element.84), channel_id=1, source_target_pairs={{0,12},{4,0},{8,4},{12,8},{1,13},{5,1},{9,5},{13,9},{2,14},{6,2},{... | collective-permute-start | bytes 884744 | tf_op jit(solution)/shard_map/ppermute | solution.py:341
  87.9 10.9 %collective-permute-start.15 = (bf16[384,384]{1,0:T(8,128)(2,1)}, bf16[384,384]{1,0:T(8,128)(2,1)S(1)}, u32[]{:S(2)}, u32[]{:S(2)}) collective-permute-start(bf16[384,384]{1,0:T(8,128)(2,1)} %collective-permute-done.11.refs_2_), channel_id=1, source_target_pairs={{0,16},{16,0},{1,17},{17,1},{2,18},{18,2},{3,19},{19,3},{4,20},{20... | collective-permute-start | bytes 884744 | tf_op jit(solution)/shard_map/ppermute | solution.py:341
  89.4 14.9 %collective-permute-start.16 = (bf16[384,384]{1,0:T(8,128)(2,1)}, bf16[384,384]{1,0:T(8,128)(2,1)S(1)}, u32[]{:S(2)}, u32[]{:S(2)}) collective-permute-start(bf16[384,384]{1,0:T(8,128)(2,1)} %collective-permute-done.12.refs_3_), channel_id=1, source_target_pairs={{0,16},{16,0},{1,17},{17,1},{2,18},{18,2},{3,19},{19,3},{4,20},{20... | collective-permute-start | bytes 884744 | tf_op jit(solution)/shard_map/ppermute | solution.py:341
  89.9 19.7 %collective-permute-start.17 = (bf16[384,384]{1,0:T(8,128)(2,1)}, bf16[384,384]{1,0:T(8,128)(2,1)S(1)}, u32[]{:S(2)}, u32[]{:S(2)}) collective-permute-start(bf16[384,384]{1,0:T(8,128)(2,1)} %collective-permute-done.13.refs_4_), channel_id=1, source_target_pairs={{0,16},{16,0},{1,17},{17,1},{2,18},{18,2},{3,19},{19,3},{4,20},{20... | collective-permute-start | bytes 884744 | tf_op jit(solution)/shard_map/ppermute | solution.py:341
  91.5 30.6 %collective-permute-start.18 = (bf16[512,384]{1,0:T(8,128)(2,1)}, bf16[512,384]{1,0:T(8,128)(2,1)S(1)}, u32[]{:S(2)}, u32[]{:S(2)}) collective-permute-start(bf16[512,384]{1,0:T(8,128)(2,1)} %get-tuple-element.102.refs_0_), channel_id=1, source_target_pairs={{0,8},{4,12},{8,0},{12,4},{1,9},{5,13},{9,1},{13,5},{2,10},{6,14},... | collective-permute-start | bytes 1179656 | tf_op jit(solution)/shard_map/ppermute | solution.py:409
  97.2 24.8 %collective-permute-start.19 = (bf16[512,384]{1,0:T(8,128)(2,1)}, bf16[512,384]{1,0:T(8,128)(2,1)S(1)}, u32[]{:S(2)}, u32[]{:S(2)}) collective-permute-start(bf16[512,384]{1,0:T(8,128)(2,1)} %get-tuple-element.102.refs_0_), channel_id=1, source_target_pairs={{0,4},{4,0},{8,12},{12,8},{1,5},{5,1},{9,13},{13,9},{2,6},{6,2},{1... | collective-permute-start | bytes 1179656 | tf_op jit(solution)/shard_map/ppermute | solution.py:410
  122.0 39.3 %copy-start.11 = (bf16[512,384]{1,0:T(8,128)(2,1)}, bf16[512,384]{1,0:T(8,128)(2,1)S(1)}, u32[]{:S(2)}) copy-start(bf16[512,384]{1,0:T(8,128)(2,1)S(1)} %collective-permute-done.18.refs_2_) | copy-start | bytes 1179652
  122.0 39.3 %copy-start.12 = (bf16[512,384]{1,0:T(8,128)(2,1)}, bf16[512,384]{1,0:T(8,128)(2,1)S(1)}, u32[]{:S(2)}) copy-start(bf16[512,384]{1,0:T(8,128)(2,1)S(1)} %collective-permute-done.19.refs_1_) | copy-start | bytes 1179652
  122.1 24.7 %collective-permute-start.20 = (bf16[512,384]{1,0:T(8,128)(2,1)}, bf16[512,384]{1,0:T(8,128)(2,1)S(1)}, u32[]{:S(2)}, u32[]{:S(2)}) collective-permute-start(bf16[512,384]{1,0:T(8,128)(2,1)} %get-tuple-element.106.refs_0_), channel_id=1, source_target_pairs={{0,8},{4,12},{8,0},{12,4},{1,9},{5,13},{9,1},{13,5},{2,10},{6,14},... | collective-permute-start | bytes 1179656 | tf_op jit(solution)/shard_map/ppermute | solution.py:409
  128.0 18.7 %collective-permute-start.21 = (bf16[512,384]{1,0:T(8,128)(2,1)}, bf16[512,384]{1,0:T(8,128)(2,1)S(1)}, u32[]{:S(2)}, u32[]{:S(2)}) collective-permute-start(bf16[512,384]{1,0:T(8,128)(2,1)} %get-tuple-element.106.refs_0_), channel_id=1, source_target_pairs={{0,4},{4,0},{8,12},{12,8},{1,5},{5,1},{9,13},{13,9},{2,6},{6,2},{1... | collective-permute-start | bytes 1179656 | tf_op jit(solution)/shard_map/ppermute | solution.py:410
  129.1 17.6 %collective-permute-start.22 = (bf16[512,384]{1,0:T(8,128)(2,1)S(1)}, bf16[512,384]{1,0:T(8,128)(2,1)S(1)}, u32[]{:S(2)}, u32[]{:S(2)}) collective-permute-start(bf16[512,384]{1,0:T(8,128)(2,1)S(1)} %copy-done.10), channel_id=1, source_target_pairs={{4,8},{8,4},{5,9},{9,5},{6,10},{10,6},{7,11},{11,7},{20,24},{24,20... | collective-permute-start | bytes 1179656 | tf_op jit(solution)/shard_map/ppermute | solution.py:414
  129.8 23.7 %collective-permute-start.23 = (bf16[512,384]{1,0:T(8,128)(2,1)S(1)}, bf16[512,384]{1,0:T(8,128)(2,1)S(1)}, u32[]{:S(2)}, u32[]{:S(2)}) collective-permute-start(bf16[512,384]{1,0:T(8,128)(2,1)S(1)} %collective-permute-done.18.refs_2_), channel_id=1, source_target_pairs={{8,12},{4,0},{9,13},{5,1},{10,14},{6,2},{11,15},{7,3},{24,28},{20,... | collective-permute-start | bytes 1179656 | tf_op jit(solution)/shard_map/ppermute | solution.py:415
  153.5 28.8 %all-to-all-start = ((bf16[4,272,256]{2,1,0:T(8,128)(2,1)}), bf16[4,272,256]{2,1,0:T(8,128)(2,1)S(1)}, u32[]{:S(2)}, u32[]{:S(2)}) async-start(bf16[4,272,256]{2,1,0:T(8,128)(2,1)} %get-tuple-element.103), calls=%async_computation | async-start | bytes 1114112 | tf_op jit(solution)/shard_map/all_to_all | solution.py:417
  159.4 12.6 %collective-permute-start.24 = (bf16[512,384]{1,0:T(8,128)(2,1)}, bf16[512,384]{1,0:T(8,128)(2,1)S(1)}, u32[]{:S(2)}, u32[]{:S(2)}) collective-permute-start(bf16[512,384]{1,0:T(8,128)(2,1)} %get-tuple-element.106.refs_0_), channel_id=1, source_target_pairs={{4,8},{8,4},{5,9},{9,5},{6,10},{10,6},{7,11},{11,7},{20,24},{24,20... | collective-permute-start | bytes 1179656 | tf_op jit(solution)/shard_map/ppermute | solution.py:414
  160.0 18.2 %collective-permute-start.25 = (bf16[512,384]{1,0:T(8,128)(2,1)S(1)}, bf16[512,384]{1,0:T(8,128)(2,1)S(1)}, u32[]{:S(2)}, u32[]{:S(2)}) collective-permute-start(bf16[512,384]{1,0:T(8,128)(2,1)S(1)} %collective-permute-done.20.refs_2_), channel_id=1, source_target_pairs={{8,12},{4,0},{9,13},{5,1},{10,14},{6,2},{11,15},{7,3},{24,28},{20,... | collective-permute-start | bytes 1179656 | tf_op jit(solution)/shard_map/ppermute | solution.py:415
  (18 other events, 201.4 us)

commit v4 on v3

--- a/solution.py
+++ b/solution.py
@@ -282,7 +282,7 @@
         back_ref[n, 2 * CHUNK :, lane] = tail_rows(dlogit[n : n + 1, :])
 
 
-def weight_gradient_kernel(steps, where_ref, own_ref, *refs):
+def weight_gradient_kernel(steps, forwarded, where_ref, own_ref, *refs):
     out_refs = refs[-3:]
 
     def block(gradient):
@@ -294,10 +294,10 @@
 
         @pl.when(pl.program_id(0) == at)
         def _(at=at, step=step):
-            if step < 3:
+            if step < 3 or not forwarded:
                 block(refs[at][...])
             else:
-                block(jnp.where(where_ref[10] == 1, refs[at + 1][...], refs[at][...]))
+                block(jnp.where(where_ref[14] == 1, refs[at + 1][...], refs[at][...]))
 
 
 def unpack_kernel(back_ref, out_ref, dlogit_ref, ddecay_ref):
@@ -326,6 +326,7 @@
     where = jnp.stack(
         [place, group]
         + [2 * a + c for c in (core, 1 - core) for a in (across, 1 - across)]
+        + [(place + ctx - d) % ctx for d in range(ctx)]
         + sources
         + [((place == 0) | (place == ctx - 1)).astype(jnp.int32)]
     ).astype(jnp.int32)
@@ -361,8 +362,11 @@
     first = [along(x, "ctx", d + 1) for d, x in enumerate(first)]
     tok = jnp.concatenate([tok] + near, axis=0)
     tok_x = along(tok, "fsdp", 1)
-    (tok_c, tok_xc), first = after((tok, tok_x), first)
+    half = share // 2
+    swapped = [along(first[0][:half], "groups", 1)]
+    (tok_c, tok_xc, first[1], first[2]), swapped[0] = after((tok, tok_x, first[1], first[2]), swapped[0])
     toks = (tok, tok_x, along(tok_c, "head", 1), along(tok_xc, "head", 1))
+    swapped += [along(x[:half], "groups", 1) for x in first[1:]]
     all_tokens, own = pl.pallas_call(
         functools.partial(unpack_tokens_kernel, ctx),
         out_shape=[shape((ctx, total, share), bf16), shape((share, total), bf16)],
@@ -370,10 +374,7 @@
         out_specs=[whole] * 2,
         name="unpack_tokens",
     )(where, *toks)
-    first_swapped = [along(x, "groups", 1) for x in first]
-    second, (first[2], first_swapped[0], first_swapped[1]) = after(
-        packed[ctx + 1 :], (first[2], first_swapped[0], first_swapped[1])
-    )
+    second, (first[1], first[2], own) = after(packed[ctx + 1 :], (first[1], first[2], own))
     second = [along(x, "ctx", d + 1) for d, x in enumerate(second)]
 
     grads = []
@@ -381,7 +382,7 @@
     for slot, direct in enumerate((first, second)):
         if slot:
             direct, back = after(direct, back)
-        swapped = [along(x, "groups", 1) for x in direct] if slot else first_swapped
+            swapped = [along(x[:half], "groups", 1) for x in direct]
         earlier = [] if back is None else [back]
         grad, back = pl.pallas_call(
             functools.partial(head_kernel, ctx, slot),
@@ -404,13 +405,14 @@
             cost_estimate=pl.CostEstimate(flops=12_000_000_000, transcendentals=0, bytes_accessed=8_000_000),
             name=f"head_{slot}",
         )(where, all_tokens, packed[slot * ctx], *direct, *swapped, *earlier)
-        if slot:
-            grad, grads[0][1:3] = after(grad, grads[0][1:3])
+        if slot == 0:
+            hops = [along(grad, "ctx", d) for d in range(1, ctx)]
+            grads.append([grad] + hops)
+            continue
+        (grad, back), grads[0] = after((grad, back), grads[0])
         two = lax.ppermute(grad, "ctx", [(0, 2), (1, 3), (2, 0), (3, 1)])
         pair = lax.ppermute(grad, "ctx", [(0, 1), (1, 0), (2, 3), (3, 2)])
         (grad, two), pair = after((grad, two), pair)
-        if slot:
-            (grad, two, back), grads[0][3:5] = after((grad, two, back), grads[0][3:5])
         middle = lax.ppermute(grad, "ctx", [(1, 2), (2, 1)])
         far = lax.ppermute(two, "ctx", [(2, 3), (1, 0)])
         grads.append([grad, pair, two, middle, far])
@@ -418,10 +420,10 @@
 
     results = ()
     for slot, steps in ((0, (0, 1, 2, 3)), (1, (0, 1, 2)), (1, (3,))):
-        parts = [grads[slot][step] for step in steps] + ([grads[slot][4]] if 3 in steps else [])
-        column = pl.BlockSpec((share, DK), lambda i, ref, s=slot, b=steps[0]: (0, 2 * ref[6 + b + i] + s))
+        parts = [grads[slot][step] for step in steps] + ([grads[slot][4]] if slot and 3 in steps else [])
+        column = pl.BlockSpec((share, DK), lambda i, ref, s=slot, b=steps[0]: (0, 2 * ref[6 + 4 * s + b + i] + s))
         results = pl.pallas_call(
-            functools.partial(weight_gradient_kernel, steps),
+            functools.partial(weight_gradient_kernel, steps, slot == 1),
             grid_spec=pltpu.PrefetchScalarGridSpec(
                 num_scalar_prefetch=1,
                 grid=(len(steps),),

time: 187 us -> 180 us (0.963)
  waiting for transfers between devices: 75.2 us -> 63.1 us
  starting transfers between devices: 55.7 us -> 61.5 us
    ppermute x2 -> x1, waiting for transfers between devices: 13 us -> 0.01 us  [head_split(): far = lax.ppermute(two, 'ctx', [(2, 3), (1, 0)])]
    ppermute x18 -> x21, starting transfers between devices: 31.5 us -> 42.6 us  [along(): return lax.ppermute(x, axis, [(i, (i + hop) % count) for i in range(count)])]
    ppermute x2 -> x1, waiting for transfers between devices: 15.7 us -> 26.4 us  [head_split(): two = lax.ppermute(grad, 'ctx', [(0, 2), (1, 3), (2, 0), (3, 1)])]
    ppermute x18 -> x21, waiting for transfers between devices: 46.5 us -> 36.7 us  [along(): return lax.ppermute(x, axis, [(i, (i + hop) % count) for i in range(count)])]
    ppermute x2 -> x1, starting transfers between devices: 11.7 us -> 2.92 us  [head_split(): two = lax.ppermute(grad, 'ctx', [(0, 2), (1, 3), (2, 0), (3, 1)])]
    all_to_all x1, starting transfers between devices: 5.84 us -> 12.5 us  [head_split(): back = lax.all_to_all(back, 'ctx', 0, 0)]
  transfers between devices with their start and end apart: 27 -> 26, of which waited for: 11 -> 7; matrix products, arithmetic and copies ran while one was open for 0% -> 0% of each run, Pallas kernels for 24% -> 25%
where the time goes in v4:
time: 180 us; the launch traced here: 179 us
  waiting for transfers between devices  63.1 us (35%)
  starting transfers between devices  61.5 us (34%)
  Pallas kernels  48.4 us (27%)
  local copies, waits for them, and re-layouts  5.39 us (3%)
    ppermute x21, starting transfers between devices, along(): return lax.ppermute(x, axis, [(i, (i + hop) % count) for i in range(count)])  42.6 us
    ppermute x21, waiting for transfers between devices, along(): return lax.ppermute(x, axis, [(i, (i + hop) % count) for i in range(count)])  36.7 us
    ppermute x1, waiting for transfers between devices, head_split(): two = lax.ppermute(grad, 'ctx', [(0, 2), (1, 3), (2, 0), (3, 1)])  26.4 us
    pallas_call x2, Pallas kernels, head_split(): pl.pallas_call(functools.partial(head_kernel, ctx, slot), out_shape=[shap...  22.6 us
    pallas_call x3, Pallas kernels, head_split(): pl.pallas_call(functools.partial(weight_gradient_kernel, steps, slot == 1...  13.8 us
    all_to_all x1, starting transfers between devices, head_split(): back = lax.all_to_all(back, 'ctx', 0, 0)  12.5 us
    unnamed x46, local copies, waits for them, and re-layouts  4.64 us
    pallas_call x1, Pallas kernels, head_split(): pl.pallas_call(functools.partial(pack_kernel, ctx), out_shape=[shape((siz...  4.45 us
  transfers between devices with their start and end apart: 26, of which 7 were waited for; matrix products, arithmetic and copies ran while one was open for 0% of the time, Pallas kernels for 25%

profile of v4, /device:TPU:0, one launch (start us, length us, event | category | flops | bytes accessed | tf_op | source)
XLA Modules:
  0.0 179.4 jit_solution(17865024507522463911)
XLA Ops:
  1.3 1.8 %pack_tokens.1 = bf16[576,128]{1,0:T(8,128)(2,1)} custom-call(s32[15]{0:T(128)} %stack.61.where_ref, bf16[128,2304]{1,0:T(8,128)(2,1)} %tokens_ref.1), custom_call_target="tpu_custom_call" | custom-call | tf_op jit(solution)/shard_map/pack_tokens/pallas_call | solution.py:344
  3.1 3.0 %collective-permute-start = (bf16[576,128]{1,0:T(8,128)(2,1)}, bf16[576,128]{1,0:T(8,128)(2,1)S(1)}, u32[]{:S(2)}, u32[]{:S(2)}) collective-permute-start(bf16[576,128]{1,0:T(8,128)(2,1)} %pack_tokens.1), channel_id=1, source_target_pairs={{0,4},{4,8},{8,12},{12,0},{1,5},{5,9},{9,13},{13,1},{2,6},{6,10},{... | collective-permute-start | bytes 442376 | tf_op jit(solution)/shard_map/ppermute | solution.py:342
  6.1 2.6 %collective-permute-start.1 = (bf16[576,128]{1,0:T(8,128)(2,1)}, bf16[576,128]{1,0:T(8,128)(2,1)S(1)}, u32[]{:S(2)}, u32[]{:S(2)}) collective-permute-start(bf16[576,128]{1,0:T(8,128)(2,1)} %pack_tokens.1), channel_id=1, source_target_pairs={{0,8},{4,12},{8,0},{12,4},{1,9},{5,13},{9,1},{13,5},{2,10},{6,14},... | collective-permute-start | bytes 442376 | tf_op jit(solution)/shard_map/ppermute | solution.py:342
  10.1 4.4 %pack.1 = (bf16[672,384]{1,0:T(8,128)(2,1)}, bf16[384,384]{1,0:T(8,128)(2,1)}, bf16[384,384]{1,0:T(8,128)(2,1)}, bf16[384,384]{1,0:T(8,128)(2,1)}, bf16[672,384]...) custom-call(s32[15]{0:T(128)} %stack.61.where_ref, ...), custom_call_target="tpu_custom_call" | custom-call | tf_op jit(solution)/shard_map/pack/pallas_call | solution.py:352
  14.5 4.2 %collective-permute-done.1 = bf16[576,128]{1,0:T(8,128)(2,1)S(1)} collective-permute-done((bf16[576,128]{1,0:T(8,128)(2,1)}, bf16[576,128]{1,0:T(8,128)(2,1)S(1)}, u32[]{:S(2)}, u32[]{:S(2)}) %collective-permute-start.1) | collective-permute-done | bytes 147488 | tf_op jit(solution)/shard_map/ppermute | solution.py:342
  18.8 1.6 collective-permute-start.3
  20.4 3.6 %collective-permute-start.6 = (bf16[384,384]{1,0:T(8,128)(2,1)}, bf16[384,384]{1,0:T(8,128)(2,1)S(1)}, u32[]{:S(2)}, u32[]{:S(2)}) collective-permute-start(bf16[384,384]{1,0:T(8,128)(2,1)} %get-tuple-element.66), channel_id=1, source_target_pairs={{0,4},{4,8},{8,12},{12,0},{1,5},{5,9},{9,13},{13,1},{2,6},{6,10},{... | collective-permute-start | bytes 884744 | tf_op jit(solution)/shard_map/ppermute | solution.py:342
  24.0 1.6 collective-permute-start.4
  26.4 6.9 %collective-permute-done.6.refs_2_ = bf16[384,384]{1,0:T(8,128)(2,1)S(1)} collective-permute-done((bf16[384,384]{1,0:T(8,128)(2,1)}, bf16[384,384]{1,0:T(8,128)(2,1)S(1)}, u32[]{:S(2)}, u32[]{:S(2)}) %collective-permute-start.6) | collective-permute-done | bytes 294944 | tf_op jit(solution)/shard_map/ppermute | solution.py:342
  33.3 1.6 collective-permute-start.7
  34.9 9.0 %collective-permute-done.4.refs_3_ = bf16[384,384]{1,0:T(8,128)(2,1)S(1)} collective-permute-done((bf16[384,384]{1,0:T(8,128)(2,1)}, bf16[384,384]{1,0:T(8,128)(2,1)S(1)}, u32[]{:S(2)}, u32[]{:S(2)}) %collective-permute-start.4) | collective-permute-done | bytes 294944 | tf_op jit(solution)/shard_map/ppermute | solution.py:342
  44.7 1.6 collective-permute-start.13
  48.5 3.7 %unpack_tokens.1 = (bf16[4,512,576]{2,1,0:T(8,128)(2,1)}, bf16[576,512]{1,0:T(8,128)(2,1)}) custom-call(s32[15]{0:T(128)} %stack.61.where_ref, bf16[2304,128]{1,0:T(8,128)(2,1)} %copy-done, bf16[2304,128]{1,0:T(8,128)(2,1)} %copy-done.3, bf16[2304,128]{1,0:T(8,128)(2,1)} %copy-done.4, bf16[2304,128]{1,0:T(8,128)(2,1)} %copy-done.5), custom_call_target="tpu_custom_call" | custom-call | tf_op jit(solution)/shard_map/unpack_tokens/pallas_call | solution.py:370
  52.3 6.8 %collective-permute-start.10 = (bf16[384,384]{1,0:T(8,128)(2,1)}, bf16[384,384]{1,0:T(8,128)(2,1)S(1)}, u32[]{:S(2)}, u32[]{:S(2)}) collective-permute-start(bf16[384,384]{1,0:T(8,128)(2,1)} %get-tuple-element.77), channel_id=1, source_target_pairs={{0,4},{4,8},{8,12},{12,0},{1,5},{5,9},{9,13},{13,1},{2,6},{6,10},{... | collective-permute-start | bytes 884744 | tf_op jit(solution)/shard_map/ppermute | solution.py:342
  59.1 2.3 %collective-permute-start.11 = (bf16[384,384]{1,0:T(8,128)(2,1)}, bf16[384,384]{1,0:T(8,128)(2,1)S(1)}, u32[]{:S(2)}, u32[]{:S(2)}) collective-permute-start(bf16[384,384]{1,0:T(8,128)(2,1)} %get-tuple-element.78), channel_id=1, source_target_pairs={{0,8},{4,12},{8,0},{12,4},{1,9},{5,13},{9,1},{13,5},{2,10},{6,14},... | collective-permute-start | bytes 884744 | tf_op jit(solution)/shard_map/ppermute | solution.py:342
  61.4 11.2 %head_0.1 = (bf16[512,384]{1,0:T(8,128)(2,1)}, bf16[4,272,128]{2,1,0:T(8,128)(2,1)}) custom-call(s32[15]{0:T(128)} %stack.61.where_ref, bf16[4,512,576]{2,1,0:T(8,128)(2,1)} %get-tuple-element.69.refs_0_, bf16[672,384]{1,0:T(8,128)(2,1)} %get-tuple-element.80.refs_1_, bf16[384,384]{1,0:T(8,128)(2,1)} %copy-done.13, bf16[384,384]{1,0:T(8,128)(2,1)} %copy-done.14, ...), custom_call_target="tpu_custom_call" | custom-call | flops 12000000000 | bytes 8000000 | tf_op jit(solution)/shard_map/head_0/pallas_call | solution.py:387
  72.7 8.2 %collective-permute-done.11.refs_3_ = bf16[384,384]{1,0:T(8,128)(2,1)S(1)} collective-permute-done((bf16[384,384]{1,0:T(8,128)(2,1)}, bf16[384,384]{1,0:T(8,128)(2,1)S(1)}, u32[]{:S(2)}, u32[]{:S(2)}) %collective-permute-start.11) | collective-permute-done | bytes 294944 | tf_op jit(solution)/shard_map/ppermute | solution.py:342
  80.9 1.6 collective-permute-start.15
  83.1 1.6 collective-permute-start.17
  84.7 6.8 %collective-permute-start.18 = (bf16[512,384]{1,0:T(8,128)(2,1)}, bf16[512,384]{1,0:T(8,128)(2,1)S(1)}, u32[]{:S(2)}, u32[]{:S(2)}) collective-permute-start(bf16[512,384]{1,0:T(8,128)(2,1)} %get-tuple-element.99.refs_0_), channel_id=1, source_target_pairs={{0,4},{4,8},{8,12},{12,0},{1,5},{5,9},{9,13},{13,1},{2,6},{6,10},{... | collective-permute-start | bytes 1179656 | tf_op jit(solution)/shard_map/ppermute | solution.py:342
  92.1 4.1 %collective-permute-start.20 = (bf16[512,384]{1,0:T(8,128)(2,1)}, bf16[512,384]{1,0:T(8,128)(2,1)S(1)}, u32[]{:S(2)}, u32[]{:S(2)}) collective-permute-start(bf16[512,384]{1,0:T(8,128)(2,1)} %get-tuple-element.99.refs_0_), channel_id=1, source_target_pairs={{0,12},{4,0},{8,4},{12,8},{1,13},{5,1},{9,5},{13,9},{2,14},{6,2},{... | collective-permute-start | bytes 1179656 | tf_op jit(solution)/shard_map/ppermute | solution.py:342
  96.2 1.6 collective-permute-done.17.refs_7_
  98.4 11.4 %head_1.1 = (bf16[512,384]{1,0:T(8,128)(2,1)}, bf16[4,272,256]{2,1,0:T(8,128)(2,1)}) custom-call(s32[15]{0:T(128)} %stack.61.where_ref, bf16[4,512,576]{2,1,0:T(8,128)(2,1)} %get-tuple-element.69.refs_0_, bf16[672,384]{1,0:T(8,128)(2,1)} %get-tuple-element.70.refs_1_, bf16[384,384]{1,0:T(8,128)(2,1)} %copy-done.15, bf16[384,384]{1,0:T(8,128)(2,1)} %copy-done.17, ...), custom_call_target="tpu_custom_call" | custom-call | flops 12000000000 | bytes 8000000 | tf_op jit(solution)/shard_map/head_1/pallas_call | solution.py:387
  109.8 6.7 %collective-permute-done.19.refs_2_ = bf16[512,384]{1,0:T(8,128)(2,1)S(1)} collective-permute-done((bf16[512,384]{1,0:T(8,128)(2,1)}, bf16[512,384]{1,0:T(8,128)(2,1)S(1)}, u32[]{:S(2)}, u32[]{:S(2)}) %collective-permute-start.19) | collective-permute-done | bytes 393248 | tf_op jit(solution)/shard_map/ppermute | solution.py:342
  116.6 12.5 %all-to-all-start = ((bf16[4,272,256]{2,1,0:T(8,128)(2,1)}), bf16[4,272,256]{2,1,0:T(8,128)(2,1)S(1)}, u32[]{:S(2)}, u32[]{:S(2)}) async-start(bf16[4,272,256]{2,1,0:T(8,128)(2,1)} %get-tuple-element.92), calls=%async_computation | async-start | bytes 1114112 | tf_op jit(solution)/shard_map/all_to_all | solution.py:419
  129.1 2.9 %collective-permute-start.21 = (bf16[512,384]{1,0:T(8,128)(2,1)}, bf16[512,384]{1,0:T(8,128)(2,1)S(1)}, u32[]{:S(2)}, u32[]{:S(2)}) collective-permute-start(bf16[512,384]{1,0:T(8,128)(2,1)} %get-tuple-element.96.refs_0_), channel_id=1, source_target_pairs={{0,8},{4,12},{8,0},{12,4},{1,9},{5,13},{9,1},{13,5},{2,10},{6,14},... | collective-permute-start | bytes 1179656 | tf_op jit(solution)/shard_map/ppermute | solution.py:413
  132.0 1.5 collective-permute-start.22
  133.5 26.4 %collective-permute-done.21.refs_2_ = bf16[512,384]{1,0:T(8,128)(2,1)S(1)} collective-permute-done((bf16[512,384]{1,0:T(8,128)(2,1)}, bf16[512,384]{1,0:T(8,128)(2,1)S(1)}, u32[]{:S(2)}, u32[]{:S(2)}) %collective-permute-start.21) | collective-permute-done | bytes 393248 | tf_op jit(solution)/shard_map/ppermute | solution.py:413
  161.9 5.6 %weight_gradient_0_0.1 = (f32[576,1024]{1,0:T(8,128)}, f32[576,1024]{1,0:T(8,128)}, f32[576,1024]{1,0:T(8,128)}) custom-call(s32[15]{0:T(128)} %stack.61.where_ref, bf16[576,512]{1,0:T(8,128)(2,1)} %get-tuple-element.94.own_ref, bf16[512,384]{1,0:T(8,128)(2,1)} %get-tuple-element.99.refs_0_, bf16[512,384]{1,0:T(8,128)(2,1)} %copy-done.10, ...), custom_call_target="tpu_custom_call" | custom-call | tf_op jit(solution)/shard_map/weight_gradient_0_0/pallas_call | solution.py:425
  167.5 4.9 %weight_gradient_1_0.1 = (f32[576,1024]{1,0:T(8,128)}, f32[576,1024]{1,0:T(8,128)}, f32[576,1024]{1,0:T(8,128)}) custom-call(s32[15]{0:T(128)} %stack.61.where_ref, bf16[576,512]{1,0:T(8,128)(2,1)} %get-tuple-element.94.own_ref, bf16[512,384]{1,0:T(8,128)(2,1)} %get-tuple-element.96.refs_0_, ...), custom_call_target="tpu_custom_call", output_to_operand_aliasing={{0}: (5, {}), {1}: (6, {}), {2}: (7, {})} | custom-call | tf_op jit(solution)/shard_map/weight_gradient_1_0/pallas_call | solution.py:425
  173.3 3.3 %weight_gradient_1_3.1 = (f32[576,1024]{1,0:T(8,128)}, f32[576,1024]{1,0:T(8,128)}, f32[576,1024]{1,0:T(8,128)}) custom-call(s32[15]{0:T(128)} %stack.61.where_ref, bf16[576,512]{1,0:T(8,128)(2,1)} %get-tuple-element.94.own_ref, bf16[512,384]{1,0:T(8,128)(2,1)} %copy-done.7, ...), custom_call_target="tpu_custom_call", output_to_operand_aliasing={{0}: (4, {}), {1}: (5, {}), {2}: (6, {})} | custom-call | tf_op jit(solution)/shard_map/weight_gradient_1_3/pallas_call | solution.py:425
  177.4 2.0 %unpack.1 = (bf16[128,1024]{1,0:T(8,128)(2,1)}, f32[8,128]{1,0:T(8,128)}, f32[128,1024]{1,0:T(8,128)}) custom-call(bf16[4,272,256]{2,1,0:T(8,128)(2,1)} %copy-done.1), custom_call_target="tpu_custom_call" | custom-call | tf_op jit(solution)/shard_map/unpack/pallas_call | solution.py:439
  (83 shorter events, 11.4 us)
Async XLA Ops:
  3.1 11.4 %collective-permute-start = (bf16[576,128]{1,0:T(8,128)(2,1)}, bf16[576,128]{1,0:T(8,128)(2,1)S(1)}, u32[]{:S(2)}, u32[]{:S(2)}) collective-permute-start(bf16[576,128]{1,0:T(8,128)(2,1)} %pack_tokens.1), channel_id=1, source_target_pairs={{0,4},{4,8},{8,12},{12,0},{1,5},{5,9},{9,13},{13,1},{2,6},{6,10},{... | collective-permute-start | bytes 442376 | tf_op jit(solution)/shard_map/ppermute | solution.py:342
  6.1 12.6 %collective-permute-start.1 = (bf16[576,128]{1,0:T(8,128)(2,1)}, bf16[576,128]{1,0:T(8,128)(2,1)S(1)}, u32[]{:S(2)}, u32[]{:S(2)}) collective-permute-start(bf16[576,128]{1,0:T(8,128)(2,1)} %pack_tokens.1), channel_id=1, source_target_pairs={{0,8},{4,12},{8,0},{12,4},{1,9},{5,13},{9,1},{13,5},{2,10},{6,14},... | collective-permute-start | bytes 442376 | tf_op jit(solution)/shard_map/ppermute | solution.py:342
  8.7 10.0 %collective-permute-start.2 = (bf16[576,128]{1,0:T(8,128)(2,1)}, bf16[576,128]{1,0:T(8,128)(2,1)S(1)}, u32[]{:S(2)}, u32[]{:S(2)}) collective-permute-start(bf16[576,128]{1,0:T(8,128)(2,1)} %pack_tokens.1), channel_id=1, source_target_pairs={{0,12},{4,0},{8,4},{12,8},{1,13},{5,1},{9,5},{13,9},{2,14},{6,2},{... | collective-permute-start | bytes 442376 | tf_op jit(solution)/shard_map/ppermute | solution.py:342
  18.8 28.1 %copy-start = (bf16[2304,128]{1,0:T(8,128)(2,1)}, bf16[2304,128]{1,0:T(8,128)(2,1)S(1)}, u32[]{:S(2)}) copy-start(bf16[2304,128]{1,0:T(8,128)(2,1)S(1)} %pad_maximum_fusion.refs_0_) | copy-start | bytes 1769476
  18.8 25.1 %collective-permute-start.3 = (bf16[2304,128]{1,0:T(8,128)(2,1)S(1)}, bf16[2304,128]{1,0:T(8,128)(2,1)S(1)}, u32[]{:S(2)}, u32[]{:S(2)}) collective-permute-start(bf16[2304,128]{1,0:T(8,128)(2,1)S(1)} %pad_maximum_fusion.refs_0_), channel_id=1, source_target_pairs={{0,2},{2,0},{1,3},{3,1},{4,6},{6,4},{5,7},{7,5},{8,10},{10,8},{9,1... | collective-permute-start | bytes 1769480 | tf_op jit(solution)/shard_map/ppermute | solution.py:342
  20.4 12.9 %collective-permute-start.6 = (bf16[384,384]{1,0:T(8,128)(2,1)}, bf16[384,384]{1,0:T(8,128)(2,1)S(1)}, u32[]{:S(2)}, u32[]{:S(2)}) collective-permute-start(bf16[384,384]{1,0:T(8,128)(2,1)} %get-tuple-element.66), channel_id=1, source_target_pairs={{0,4},{4,8},{8,12},{12,0},{1,5},{5,9},{9,13},{13,1},{2,6},{6,10},{... | collective-permute-start | bytes 884744 | tf_op jit(solution)/shard_map/ppermute | solution.py:342
  24.0 19.9 %collective-permute-start.4 = (bf16[384,384]{1,0:T(8,128)(2,1)}, bf16[384,384]{1,0:T(8,128)(2,1)S(1)}, u32[]{:S(2)}, u32[]{:S(2)}) collective-permute-start(bf16[384,384]{1,0:T(8,128)(2,1)} %get-tuple-element.64), channel_id=1, source_target_pairs={{0,8},{4,12},{8,0},{12,4},{1,9},{5,13},{9,1},{13,5},{2,10},{6,14},... | collective-permute-start | bytes 884744 | tf_op jit(solution)/shard_map/ppermute | solution.py:342
  25.6 18.3 %collective-permute-start.5 = (bf16[384,384]{1,0:T(8,128)(2,1)}, bf16[384,384]{1,0:T(8,128)(2,1)S(1)}, u32[]{:S(2)}, u32[]{:S(2)}) collective-permute-start(bf16[384,384]{1,0:T(8,128)(2,1)} %get-tuple-element.65), channel_id=1, source_target_pairs={{0,12},{4,0},{8,4},{12,8},{1,13},{5,1},{9,5},{13,9},{2,14},{6,2},{... | collective-permute-start | bytes 884744 | tf_op jit(solution)/shard_map/ppermute | solution.py:342
  33.3 28.1 %copy-start.13 = (bf16[384,384]{1,0:T(8,128)(2,1)}, bf16[384,384]{1,0:T(8,128)(2,1)S(1)}, u32[]{:S(2)}) copy-start(bf16[384,384]{1,0:T(8,128)(2,1)S(1)} %collective-permute-done.6.refs_2_) | copy-start | bytes 884740
  33.3 10.6 %collective-permute-start.7 = (bf16[288,384]{1,0:T(8,128)(2,1)S(1)}, bf16[288,384]{1,0:T(8,128)(2,1)S(1)}, u32[]{:S(2)}, u32[]{:S(2)}) collective-permute-start(bf16[288,384]{1,0:T(8,128)(2,1)S(1)} %slice.24), channel_id=1, source_target_pairs={{0,16},{16,0},{1,17},{17,1},{2,18},{18,2},{3,19},{19,3},{4,20},{20... | collective-permute-start | bytes 663560 | tf_op jit(solution)/shard_map/ppermute | solution.py:342
  44.0 2.9 %collective-permute-start.8 = (bf16[2304,128]{1,0:T(8,128)(2,1)S(1)}, bf16[2304,128]{1,0:T(8,128)(2,1)S(1)}, u32[]{:S(2)}, u32[]{:S(2)}) collective-permute-start(bf16[2304,128]{1,0:T(8,128)(2,1)S(1)} %pad_maximum_fusion.refs_0_), channel_id=1, source_target_pairs={{0,1},{1,0},{2,3},{3,2},{4,5},{5,4},{6,7},{7,6},{8,9},{9,8},{10,11... | collective-permute-start | bytes 1769480 | tf_op jit(solution)/shard_map/ppermute | solution.py:342
  44.7 2.2 %collective-permute-start.9 = (bf16[2304,128]{1,0:T(8,128)(2,1)S(1)}, bf16[2304,128]{1,0:T(8,128)(2,1)S(1)}, u32[]{:S(2)}, u32[]{:S(2)}) collective-permute-start(bf16[2304,128]{1,0:T(8,128)(2,1)S(1)} %collective-permute-done.3.refs_1_), channel_id=1, source_target_pairs={{0,1},{1,0},{2,3},{3,2},{4,5},{5,4},{6,7},{7,6},{8,9},{9,8},{10,11... | collective-permute-start | bytes 1769480 | tf_op jit(solution)/shard_map/ppermute | solution.py:342
  44.7 16.7 %collective-permute-start.13 = (bf16[288,384]{1,0:T(8,128)(2,1)S(1)}, bf16[288,384]{1,0:T(8,128)(2,1)}, u32[]{:S(2)}, u32[]{:S(2)}) collective-permute-start(bf16[288,384]{1,0:T(8,128)(2,1)S(1)} %slice.19), channel_id=1, source_target_pairs={{0,16},{16,0},{1,17},{17,1},{2,18},{18,2},{3,19},{19,3},{4,20},{20... | collective-permute-start | bytes 663560 | tf_op jit(solution)/shard_map/ppermute | solution.py:342
  46.3 15.1 %collective-permute-start.14 = (bf16[288,384]{1,0:T(8,128)(2,1)S(1)}, bf16[288,384]{1,0:T(8,128)(2,1)}, u32[]{:S(2)}, u32[]{:S(2)}) collective-permute-start(bf16[288,384]{1,0:T(8,128)(2,1)S(1)} %slice.20), channel_id=1, source_target_pairs={{0,16},{16,0},{1,17},{17,1},{2,18},{18,2},{3,19},{19,3},{4,20},{20... | collective-permute-start | bytes 663560 | tf_op jit(solution)/shard_map/ppermute | solution.py:342
  52.3 20.4 %collective-permute-start.10 = (bf16[384,384]{1,0:T(8,128)(2,1)}, bf16[384,384]{1,0:T(8,128)(2,1)S(1)}, u32[]{:S(2)}, u32[]{:S(2)}) collective-permute-start(bf16[384,384]{1,0:T(8,128)(2,1)} %get-tuple-element.77), channel_id=1, source_target_pairs={{0,4},{4,8},{8,12},{12,0},{1,5},{5,9},{9,13},{13,1},{2,6},{6,10},{... | collective-permute-start | bytes 884744 | tf_op jit(solution)/shard_map/ppermute | solution.py:342
  59.1 21.8 %collective-permute-start.11 = (bf16[384,384]{1,0:T(8,128)(2,1)}, bf16[384,384]{1,0:T(8,128)(2,1)S(1)}, u32[]{:S(2)}, u32[]{:S(2)}) collective-permute-start(bf16[384,384]{1,0:T(8,128)(2,1)} %get-tuple-element.78), channel_id=1, source_target_pairs={{0,8},{4,12},{8,0},{12,4},{1,9},{5,13},{9,1},{13,5},{2,10},{6,14},... | collective-permute-start | bytes 884744 | tf_op jit(solution)/shard_map/ppermute | solution.py:342
  61.4 19.5 %collective-permute-start.12 = (bf16[384,384]{1,0:T(8,128)(2,1)}, bf16[384,384]{1,0:T(8,128)(2,1)S(1)}, u32[]{:S(2)}, u32[]{:S(2)}) collective-permute-start(bf16[384,384]{1,0:T(8,128)(2,1)} %get-tuple-element.79), channel_id=1, source_target_pairs={{0,12},{4,0},{8,4},{12,8},{1,13},{5,1},{9,5},{13,9},{2,14},{6,2},{... | collective-permute-start | bytes 884744 | tf_op jit(solution)/shard_map/ppermute | solution.py:342
  72.7 25.1 %copy-start.15 = (bf16[384,384]{1,0:T(8,128)(2,1)}, bf16[384,384]{1,0:T(8,128)(2,1)S(1)}, u32[]{:S(2)}) copy-start(bf16[384,384]{1,0:T(8,128)(2,1)S(1)} %collective-permute-done.10.refs_2_) | copy-start | bytes 884740
  80.9 11.1 %collective-permute-start.15 = (bf16[288,384]{1,0:T(8,128)(2,1)S(1)}, bf16[288,384]{1,0:T(8,128)(2,1)S(1)}, u32[]{:S(2)}, u32[]{:S(2)}) collective-permute-start(bf16[288,384]{1,0:T(8,128)(2,1)S(1)} %slice.21), channel_id=1, source_target_pairs={{0,16},{16,0},{1,17},{17,1},{2,18},{18,2},{3,19},{19,3},{4,20},{20... | collective-permute-start | bytes 663560 | tf_op jit(solution)/shard_map/ppermute | solution.py:342
  82.5 13.6 %collective-permute-start.16 = (bf16[288,384]{1,0:T(8,128)(2,1)S(1)}, bf16[288,384]{1,0:T(8,128)(2,1)S(1)}, u32[]{:S(2)}, u32[]{:S(2)}) collective-permute-start(bf16[288,384]{1,0:T(8,128)(2,1)S(1)} %slice.22), channel_id=1, source_target_pairs={{0,16},{16,0},{1,17},{17,1},{2,18},{18,2},{3,19},{19,3},{4,20},{20... | collective-permute-start | bytes 663560 | tf_op jit(solution)/shard_map/ppermute | solution.py:342
  83.1 14.6 %collective-permute-start.17 = (bf16[288,384]{1,0:T(8,128)(2,1)S(1)}, bf16[288,384]{1,0:T(8,128)(2,1)S(1)}, u32[]{:S(2)}, u32[]{:S(2)}) collective-permute-start(bf16[288,384]{1,0:T(8,128)(2,1)S(1)} %slice.23), channel_id=1, source_target_pairs={{0,16},{16,0},{1,17},{17,1},{2,18},{18,2},{3,19},{19,3},{4,20},{20... | collective-permute-start | bytes 663560 | tf_op jit(solution)/shard_map/ppermute | solution.py:342
  84.7 25.1 %collective-permute-start.18 = (bf16[512,384]{1,0:T(8,128)(2,1)}, bf16[512,384]{1,0:T(8,128)(2,1)S(1)}, u32[]{:S(2)}, u32[]{:S(2)}) collective-permute-start(bf16[512,384]{1,0:T(8,128)(2,1)} %get-tuple-element.99.refs_0_), channel_id=1, source_target_pairs={{0,4},{4,8},{8,12},{12,0},{1,5},{5,9},{9,13},{13,1},{2,6},{6,10},{... | collective-permute-start | bytes 1179656 | tf_op jit(solution)/shard_map/ppermute | solution.py:342
  91.5 25.0 %collective-permute-start.19 = (bf16[512,384]{1,0:T(8,128)(2,1)}, bf16[512,384]{1,0:T(8,128)(2,1)S(1)}, u32[]{:S(2)}, u32[]{:S(2)}) collective-permute-start(bf16[512,384]{1,0:T(8,128)(2,1)} %get-tuple-element.99.refs_0_), channel_id=1, source_target_pairs={{0,8},{4,12},{8,0},{12,4},{1,9},{5,13},{9,1},{13,5},{2,10},{6,14},... | collective-permute-start | bytes 1179656 | tf_op jit(solution)/shard_map/ppermute | solution.py:342
  92.1 24.5 %collective-permute-start.20 = (bf16[512,384]{1,0:T(8,128)(2,1)}, bf16[512,384]{1,0:T(8,128)(2,1)S(1)}, u32[]{:S(2)}, u32[]{:S(2)}) collective-permute-start(bf16[512,384]{1,0:T(8,128)(2,1)} %get-tuple-element.99.refs_0_), channel_id=1, source_target_pairs={{0,12},{4,0},{8,4},{12,8},{1,13},{5,1},{9,5},{13,9},{2,14},{6,2},{... | collective-permute-start | bytes 1179656 | tf_op jit(solution)/shard_map/ppermute | solution.py:342
  109.8 52.0 %copy-start.10 = (bf16[512,384]{1,0:T(8,128)(2,1)}, bf16[512,384]{1,0:T(8,128)(2,1)S(1)}, u32[]{:S(2)}) copy-start(bf16[512,384]{1,0:T(8,128)(2,1)S(1)} %collective-permute-done.18.refs_1_) | copy-start | bytes 1179652
  116.6 45.3 %copy-start.11 = (bf16[512,384]{1,0:T(8,128)(2,1)}, bf16[512,384]{1,0:T(8,128)(2,1)S(1)}, u32[]{:S(2)}) copy-start(bf16[512,384]{1,0:T(8,128)(2,1)S(1)} %collective-permute-done.19.refs_2_) | copy-start | bytes 1179652
  116.6 45.3 %copy-start.12 = (bf16[512,384]{1,0:T(8,128)(2,1)}, bf16[512,384]{1,0:T(8,128)(2,1)S(1)}, u32[]{:S(2)}) copy-start(bf16[512,384]{1,0:T(8,128)(2,1)S(1)} %collective-permute-done.20.refs_3_) | copy-start | bytes 1179652
  116.6 60.1 %all-to-all-start = ((bf16[4,272,256]{2,1,0:T(8,128)(2,1)}), bf16[4,272,256]{2,1,0:T(8,128)(2,1)S(1)}, u32[]{:S(2)}, u32[]{:S(2)}) async-start(bf16[4,272,256]{2,1,0:T(8,128)(2,1)} %get-tuple-element.92), calls=%async_computation | async-start | bytes 1114112 | tf_op jit(solution)/shard_map/all_to_all | solution.py:419
  129.1 30.7 %collective-permute-start.21 = (bf16[512,384]{1,0:T(8,128)(2,1)}, bf16[512,384]{1,0:T(8,128)(2,1)S(1)}, u32[]{:S(2)}, u32[]{:S(2)}) collective-permute-start(bf16[512,384]{1,0:T(8,128)(2,1)} %get-tuple-element.96.refs_0_), channel_id=1, source_target_pairs={{0,8},{4,12},{8,0},{12,4},{1,9},{5,13},{9,1},{13,5},{2,10},{6,14},... | collective-permute-start | bytes 1179656 | tf_op jit(solution)/shard_map/ppermute | solution.py:413
  132.0 27.8 %collective-permute-start.22 = (bf16[512,384]{1,0:T(8,128)(2,1)}, bf16[512,384]{1,0:T(8,128)(2,1)S(1)}, u32[]{:S(2)}, u32[]{:S(2)}) collective-permute-start(bf16[512,384]{1,0:T(8,128)(2,1)} %get-tuple-element.96.refs_0_), channel_id=1, source_target_pairs={{0,4},{4,0},{8,12},{12,8},{1,5},{5,1},{9,13},{13,9},{2,6},{6,2},{1... | collective-permute-start | bytes 1179656 | tf_op jit(solution)/shard_map/ppermute | solution.py:414
  159.9 12.5 %collective-permute-start.23 = (bf16[512,384]{1,0:T(8,128)(2,1)}, bf16[512,384]{1,0:T(8,128)(2,1)S(1)}, u32[]{:S(2)}, u32[]{:S(2)}) collective-permute-start(bf16[512,384]{1,0:T(8,128)(2,1)} %get-tuple-element.96.refs_0_), channel_id=1, source_target_pairs={{4,8},{8,4},{5,9},{9,5},{6,10},{10,6},{7,11},{11,7},{20,24},{24,20... | collective-permute-start | bytes 1179656 | tf_op jit(solution)/shard_map/ppermute | solution.py:416
  160.5 11.8 %collective-permute-start.24 = (bf16[512,384]{1,0:T(8,128)(2,1)S(1)}, bf16[512,384]{1,0:T(8,128)(2,1)S(1)}, u32[]{:S(2)}, u32[]{:S(2)}) collective-permute-start(bf16[512,384]{1,0:T(8,128)(2,1)S(1)} %collective-permute-done.21.refs_2_), channel_id=1, source_target_pairs={{8,12},{4,0},{9,13},{5,1},{10,14},{6,2},{11,15},{7,3},{24,28},{20,... | collective-permute-start | bytes 1179656 | tf_op jit(solution)/shard_map/ppermute | solution.py:417
  (17 other events, 100.7 us)

commit v5 on v4

--- a/solution.py
+++ b/solution.py
@@ -366,7 +366,6 @@
     swapped = [along(first[0][:half], "groups", 1)]
     (tok_c, tok_xc, first[1], first[2]), swapped[0] = after((tok, tok_x, first[1], first[2]), swapped[0])
     toks = (tok, tok_x, along(tok_c, "head", 1), along(tok_xc, "head", 1))
-    swapped += [along(x[:half], "groups", 1) for x in first[1:]]
     all_tokens, own = pl.pallas_call(
         functools.partial(unpack_tokens_kernel, ctx),
         out_shape=[shape((ctx, total, share), bf16), shape((share, total), bf16)],
@@ -374,8 +373,24 @@
         out_specs=[whole] * 2,
         name="unpack_tokens",
     )(where, *toks)
-    second, (first[1], first[2], own) = after(packed[ctx + 1 :], (first[1], first[2], own))
+    swapped += [along(x[:half], "groups", 1) for x in first[1:]]
+    second, first[1:] = after(packed[ctx + 1 :], first[1:])
     second = [along(x, "ctx", d + 1) for d, x in enumerate(second)]
+
+    def products(slot, steps, parts, results):
+        column = pl.BlockSpec((share, DK), lambda i, ref: (0, 2 * ref[6 + 4 * slot + steps[0] + i] + slot))
+        return pl.pallas_call(
+            functools.partial(weight_gradient_kernel, steps, slot == 1),
+            grid_spec=pltpu.PrefetchScalarGridSpec(
+                num_scalar_prefetch=1,
+                grid=(len(steps),),
+                in_specs=[whole] * (1 + len(parts)) + [pl.BlockSpec(memory_space=pl.ANY)] * len(results),
+                out_specs=[column] * 3,
+            ),
+            out_shape=[shape((share, columns), f32)] * 3,
+            input_output_aliases={2 + len(parts) + i: i for i in range(len(results))},
+            name=f"weight_gradient_{slot}_{steps[0]}",
+        )(where, own, *parts, *results)
 
     grads = []
     back = None
@@ -409,32 +424,16 @@
             hops = [along(grad, "ctx", d) for d in range(1, ctx)]
             grads.append([grad] + hops)
             continue
-        (grad, back), grads[0] = after((grad, back), grads[0])
+        grad, grads[0] = after(grad, grads[0])
         two = lax.ppermute(grad, "ctx", [(0, 2), (1, 3), (2, 0), (3, 1)])
         pair = lax.ppermute(grad, "ctx", [(0, 1), (1, 0), (2, 3), (3, 2)])
-        (grad, two), pair = after((grad, two), pair)
+        results = products(0, (0, 1, 2, 3), grads[0], ())
+        (grad, two), (pair, results) = after((grad, two), (pair, results))
         middle = lax.ppermute(grad, "ctx", [(1, 2), (2, 1)])
         far = lax.ppermute(two, "ctx", [(2, 3), (1, 0)])
-        grads.append([grad, pair, two, middle, far])
+        results = products(1, (0, 1, 2), [grad, pair, two], results)
+        results = products(1, (3,), [middle, far], results)
     back = lax.all_to_all(back, "ctx", 0, 0)
-
-    results = ()
-    for slot, steps in ((0, (0, 1, 2, 3)), (1, (0, 1, 2)), (1, (3,))):
-        parts = [grads[slot][step] for step in steps] + ([grads[slot][4]] if slot and 3 in steps else [])
-        column = pl.BlockSpec((share, DK), lambda i, ref, s=slot, b=steps[0]: (0, 2 * ref[6 + 4 * s + b + i] + s))
-        results = pl.pallas_call(
-            functools.partial(weight_gradient_kernel, steps, slot == 1),
-            grid_spec=pltpu.PrefetchScalarGridSpec(
-                num_scalar_prefetch=1,
-                grid=(len(steps),),
-                in_specs=[whole] * (1 + len(parts))
-                + [pl.BlockSpec(memory_space=pl.ANY)] * len(results),
-                out_specs=[column] * 3,
-            ),
-            out_shape=[shape((share, columns), f32)] * 3,
-            input_output_aliases={2 + len(parts) + i: i for i in range(len(results))},
-            name=f"weight_gradient_{slot}_{steps[0]}",
-        )(where, own, *parts, *results)
 
     attn_out, grad_beta, grad_decay = pl.pallas_call(
         unpack_kernel,

time: 180 us -> 169 us (0.939)
  waiting for transfers between devices: 63.1 us -> 35.3 us
  starting transfers between devices: 61.5 us -> 78.8 us
    ppermute x1, waiting for transfers between devices: 26.4 us -> 4.27 us  [head_split(): two = lax.ppermute(grad, 'ctx', [(0, 2), (1, 3), (2, 0), (3, 1)])]
    ppermute x1, starting transfers between devices: 1.46 us -> 13.3 us  [head_split(): pair = lax.ppermute(grad, 'ctx', [(0, 1), (1, 0), (2, 3), (3, 2)])]
    ppermute x21, waiting for transfers between devices: 36.7 us -> 25.5 us  [along(): return lax.ppermute(x, axis, [(i, (i + hop) % count) for i in range(count)])]
    ppermute x1, starting transfers between devices: 2.92 us -> 13.3 us  [head_split(): two = lax.ppermute(grad, 'ctx', [(0, 2), (1, 3), (2, 0), (3, 1)])]
    ppermute x1, waiting for transfers between devices: 0.01 us -> 5.14 us  [head_split(): far = lax.ppermute(two, 'ctx', [(2, 3), (1, 0)])]
    all_to_all x1, starting transfers between devices: 12.5 us -> 8.38 us  [head_split(): back = lax.all_to_all(back, 'ctx', 0, 0)]
  transfers between devices with their start and end apart: 26 -> 26, of which waited for: 7 -> 8; matrix products, arithmetic and copies ran while one was open for 0% -> 1% of each run, Pallas kernels for 25% -> 26%
where the time goes in v5:
time: 169 us
  starting transfers between devices  78.8 us (47%)
  Pallas kernels  48.4 us (29%)
  waiting for transfers between devices  35.3 us (21%)
  local copies, waits for them, and re-layouts  5.29 us (3%)
    ppermute x21, starting transfers between devices, along(): return lax.ppermute(x, axis, [(i, (i + hop) % count) for i in range(count)])  41.8 us
    ppermute x21, waiting for transfers between devices, along(): return lax.ppermute(x, axis, [(i, (i + hop) % count) for i in range(count)])  25.5 us
    pallas_call x2, Pallas kernels, head_split(): pl.pallas_call(functools.partial(head_kernel, ctx, slot), out_shape=[shap...  22.6 us
    pallas_call x3, Pallas kernels, products(): pl.pallas_call(functools.partial(weight_gradient_kernel, steps, slot == 1...  13.8 us
    ppermute x1, starting transfers between devices, head_split(): pair = lax.ppermute(grad, 'ctx', [(0, 1), (1, 0), (2, 3), (3, 2)])  13.3 us
    ppermute x1, starting transfers between devices, head_split(): two = lax.ppermute(grad, 'ctx', [(0, 2), (1, 3), (2, 0), (3, 1)])  13.3 us
    all_to_all x1, starting transfers between devices, head_split(): back = lax.all_to_all(back, 'ctx', 0, 0)  8.38 us
    ppermute x1, waiting for transfers between devices, head_split(): far = lax.ppermute(two, 'ctx', [(2, 3), (1, 0)])  5.14 us
  transfers between devices with their start and end apart: 26, of which 8 were waited for; matrix products, arithmetic and copies ran while one was open for 1% of the time, Pallas kernels for 26%

profile of v5, /device:TPU:0, one launch (start us, length us, event | category | flops | bytes accessed | tf_op | source)
XLA Modules:
  0.0 168.7 jit_solution(5523018561139073630)
XLA Ops:
  1.3 1.8 %pack_tokens.1 = bf16[576,128]{1,0:T(8,128)(2,1)} custom-call(s32[15]{0:T(128)} %stack.61.where_ref, bf16[128,2304]{1,0:T(8,128)(2,1)} %tokens_ref.1), custom_call_target="tpu_custom_call" | custom-call | tf_op jit(solution)/shard_map/pack_tokens/pallas_call | solution.py:344
  3.1 3.0 %collective-permute-start = (bf16[576,128]{1,0:T(8,128)(2,1)}, bf16[576,128]{1,0:T(8,128)(2,1)S(1)}, u32[]{:S(2)}, u32[]{:S(2)}) collective-permute-start(bf16[576,128]{1,0:T(8,128)(2,1)} %pack_tokens.1), channel_id=1, source_target_pairs={{0,4},{4,8},{8,12},{12,0},{1,5},{5,9},{9,13},{13,1},{2,6},{6,10},{... | collective-permute-start | bytes 442376 | tf_op jit(solution)/shard_map/ppermute | solution.py:342
  6.2 2.6 %collective-permute-start.1 = (bf16[576,128]{1,0:T(8,128)(2,1)}, bf16[576,128]{1,0:T(8,128)(2,1)S(1)}, u32[]{:S(2)}, u32[]{:S(2)}) collective-permute-start(bf16[576,128]{1,0:T(8,128)(2,1)} %pack_tokens.1), channel_id=1, source_target_pairs={{0,8},{4,12},{8,0},{12,4},{1,9},{5,13},{9,1},{13,5},{2,10},{6,14},... | collective-permute-start | bytes 442376 | tf_op jit(solution)/shard_map/ppermute | solution.py:342
  10.1 4.4 %pack.1 = (bf16[672,384]{1,0:T(8,128)(2,1)}, bf16[384,384]{1,0:T(8,128)(2,1)}, bf16[384,384]{1,0:T(8,128)(2,1)}, bf16[384,384]{1,0:T(8,128)(2,1)}, bf16[672,384]...) custom-call(s32[15]{0:T(128)} %stack.61.where_ref, ...), custom_call_target="tpu_custom_call" | custom-call | tf_op jit(solution)/shard_map/pack/pallas_call | solution.py:352
  14.5 4.2 %collective-permute-done.1 = bf16[576,128]{1,0:T(8,128)(2,1)S(1)} collective-permute-done((bf16[576,128]{1,0:T(8,128)(2,1)}, bf16[576,128]{1,0:T(8,128)(2,1)S(1)}, u32[]{:S(2)}, u32[]{:S(2)}) %collective-permute-start.1) | collective-permute-done | bytes 147488 | tf_op jit(solution)/shard_map/ppermute | solution.py:342
  18.8 1.6 collective-permute-start.3
  20.4 3.6 %collective-permute-start.6 = (bf16[384,384]{1,0:T(8,128)(2,1)}, bf16[384,384]{1,0:T(8,128)(2,1)S(1)}, u32[]{:S(2)}, u32[]{:S(2)}) collective-permute-start(bf16[384,384]{1,0:T(8,128)(2,1)} %get-tuple-element.67), channel_id=1, source_target_pairs={{0,4},{4,8},{8,12},{12,0},{1,5},{5,9},{9,13},{13,1},{2,6},{6,10},{... | collective-permute-start | bytes 884744 | tf_op jit(solution)/shard_map/ppermute | solution.py:342
  24.0 1.6 collective-permute-start.4
  26.4 6.9 %collective-permute-done.6.refs_2_ = bf16[384,384]{1,0:T(8,128)(2,1)S(1)} collective-permute-done((bf16[384,384]{1,0:T(8,128)(2,1)}, bf16[384,384]{1,0:T(8,128)(2,1)S(1)}, u32[]{:S(2)}, u32[]{:S(2)}) %collective-permute-start.6) | collective-permute-done | bytes 294944 | tf_op jit(solution)/shard_map/ppermute | solution.py:342
  33.3 1.6 collective-permute-start.7
  34.9 9.0 %collective-permute-done.4.refs_3_ = bf16[384,384]{1,0:T(8,128)(2,1)S(1)} collective-permute-done((bf16[384,384]{1,0:T(8,128)(2,1)}, bf16[384,384]{1,0:T(8,128)(2,1)S(1)}, u32[]{:S(2)}, u32[]{:S(2)}) %collective-permute-start.4) | collective-permute-done | bytes 294944 | tf_op jit(solution)/shard_map/ppermute | solution.py:342
  44.7 1.6 collective-permute-start.13
  46.9 6.8 %collective-permute-start.10 = (bf16[384,384]{1,0:T(8,128)(2,1)}, bf16[384,384]{1,0:T(8,128)(2,1)S(1)}, u32[]{:S(2)}, u32[]{:S(2)}) collective-permute-start(bf16[384,384]{1,0:T(8,128)(2,1)} %get-tuple-element.77), channel_id=1, source_target_pairs={{0,4},{4,8},{8,12},{12,0},{1,5},{5,9},{9,13},{13,1},{2,6},{6,10},{... | collective-permute-start | bytes 884744 | tf_op jit(solution)/shard_map/ppermute | solution.py:342
  53.7 2.3 %collective-permute-start.11 = (bf16[384,384]{1,0:T(8,128)(2,1)}, bf16[384,384]{1,0:T(8,128)(2,1)S(1)}, u32[]{:S(2)}, u32[]{:S(2)}) collective-permute-start(bf16[384,384]{1,0:T(8,128)(2,1)} %get-tuple-element.78), channel_id=1, source_target_pairs={{0,8},{4,12},{8,0},{12,4},{1,9},{5,13},{9,1},{13,5},{2,10},{6,14},... | collective-permute-start | bytes 884744 | tf_op jit(solution)/shard_map/ppermute | solution.py:342
  56.9 3.7 %unpack_tokens.1 = (bf16[4,512,576]{2,1,0:T(8,128)(2,1)}, bf16[576,512]{1,0:T(8,128)(2,1)}) custom-call(s32[15]{0:T(128)} %stack.61.where_ref, bf16[2304,128]{1,0:T(8,128)(2,1)} %copy-done, bf16[2304,128]{1,0:T(8,128)(2,1)} %copy-done.3, bf16[2304,128]{1,0:T(8,128)(2,1)} %copy-done.4, bf16[2304,128]{1,0:T(8,128)(2,1)} %copy-done.5), custom_call_target="tpu_custom_call" | custom-call | tf_op jit(solution)/shard_map/unpack_tokens/pallas_call | solution.py:369
  60.6 11.2 %head_0.1 = (bf16[512,384]{1,0:T(8,128)(2,1)}, bf16[4,272,128]{2,1,0:T(8,128)(2,1)}) custom-call(s32[15]{0:T(128)} %stack.61.where_ref, bf16[4,512,576]{2,1,0:T(8,128)(2,1)} %get-tuple-element.70.refs_0_, bf16[672,384]{1,0:T(8,128)(2,1)} %get-tuple-element.80.refs_1_, bf16[384,384]{1,0:T(8,128)(2,1)} %copy-done.16, bf16[384,384]{1,0:T(8,128)(2,1)} %copy-done.17, ...), custom_call_target="tpu_custom_call" | custom-call | flops 12000000000 | bytes 8000000 | tf_op jit(solution)/shard_map/head_0/pallas_call | solution.py:402
  71.8 3.7 %collective-permute-done.11.refs_3_ = bf16[384,384]{1,0:T(8,128)(2,1)S(1)} collective-permute-done((bf16[384,384]{1,0:T(8,128)(2,1)}, bf16[384,384]{1,0:T(8,128)(2,1)S(1)}, u32[]{:S(2)}, u32[]{:S(2)}) %collective-permute-start.11) | collective-permute-done | bytes 294944 | tf_op jit(solution)/shard_map/ppermute | solution.py:342
  75.6 1.6 collective-permute-start.15
  78.7 1.6 collective-permute-start.17
  80.3 6.9 %collective-permute-start.18 = (bf16[512,384]{1,0:T(8,128)(2,1)}, bf16[512,384]{1,0:T(8,128)(2,1)S(1)}, u32[]{:S(2)}, u32[]{:S(2)}) collective-permute-start(bf16[512,384]{1,0:T(8,128)(2,1)} %get-tuple-element.95.refs_0_), channel_id=1, source_target_pairs={{0,4},{4,8},{8,12},{12,0},{1,5},{5,9},{9,13},{13,1},{2,6},{6,10},{... | collective-permute-start | bytes 1179656 | tf_op jit(solution)/shard_map/ppermute | solution.py:342
  87.7 3.1 %collective-permute-start.20 = (bf16[512,384]{1,0:T(8,128)(2,1)}, bf16[512,384]{1,0:T(8,128)(2,1)S(1)}, u32[]{:S(2)}, u32[]{:S(2)}) collective-permute-start(bf16[512,384]{1,0:T(8,128)(2,1)} %get-tuple-element.95.refs_0_), channel_id=1, source_target_pairs={{0,12},{4,0},{8,4},{12,8},{1,13},{5,1},{9,5},{13,9},{2,14},{6,2},{... | collective-permute-start | bytes 1179656 | tf_op jit(solution)/shard_map/ppermute | solution.py:342
  90.8 1.6 collective-permute-done.17.refs_7_
  93.1 11.4 %head_1.1 = (bf16[512,384]{1,0:T(8,128)(2,1)}, bf16[4,272,256]{2,1,0:T(8,128)(2,1)}) custom-call(s32[15]{0:T(128)} %stack.61.where_ref, bf16[4,512,576]{2,1,0:T(8,128)(2,1)} %get-tuple-element.70.refs_0_, bf16[672,384]{1,0:T(8,128)(2,1)} %get-tuple-element.71.refs_1_, bf16[384,384]{1,0:T(8,128)(2,1)} %copy-done.14, bf16[384,384]{1,0:T(8,128)(2,1)} %copy-done.15, ...), custom_call_target="tpu_custom_call" | custom-call | flops 12000000000 | bytes 8000000 | tf_op jit(solution)/shard_map/head_1/pallas_call | solution.py:402
  104.5 8.4 %all-to-all-start = ((bf16[4,272,256]{2,1,0:T(8,128)(2,1)}), bf16[4,272,256]{2,1,0:T(8,128)(2,1)S(1)}, u32[]{:S(2)}, u32[]{:S(2)}) async-start(bf16[4,272,256]{2,1,0:T(8,128)(2,1)} %get-tuple-element.89), calls=%async_computation | async-start | bytes 1114112 | tf_op jit(solution)/shard_map/all_to_all | solution.py:436
  112.9 13.3 %collective-permute-start.21 = (bf16[512,384]{1,0:T(8,128)(2,1)}, bf16[512,384]{1,0:T(8,128)(2,1)S(1)}, u32[]{:S(2)}, u32[]{:S(2)}) collective-permute-start(bf16[512,384]{1,0:T(8,128)(2,1)} %get-tuple-element.102.refs_0_), channel_id=1, source_target_pairs={{0,8},{4,12},{8,0},{12,4},{1,9},{5,13},{9,1},{13,5},{2,10},{6,14},... | collective-permute-start | bytes 1179656 | tf_op jit(solution)/shard_map/ppermute | solution.py:428
  126.2 13.3 %collective-permute-start.22 = (bf16[512,384]{1,0:T(8,128)(2,1)}, bf16[512,384]{1,0:T(8,128)(2,1)S(1)}, u32[]{:S(2)}, u32[]{:S(2)}) collective-permute-start(bf16[512,384]{1,0:T(8,128)(2,1)} %get-tuple-element.102.refs_0_), channel_id=1, source_target_pairs={{0,4},{4,0},{8,12},{12,8},{1,5},{5,1},{9,13},{13,9},{2,6},{6,2},{1... | collective-permute-start | bytes 1179656 | tf_op jit(solution)/shard_map/ppermute | solution.py:429
  139.5 5.6 %weight_gradient_0_0.1 = (f32[576,1024]{1,0:T(8,128)}, f32[576,1024]{1,0:T(8,128)}, f32[576,1024]{1,0:T(8,128)}) custom-call(s32[15]{0:T(128)} %stack.61.where_ref, bf16[576,512]{1,0:T(8,128)(2,1)} %get-tuple-element.91.own_ref, bf16[512,384]{1,0:T(8,128)(2,1)} %get-tuple-element.95.refs_0_, bf16[512,384]{1,0:T(8,128)(2,1)} %copy-done.11, ...), custom_call_target="tpu_custom_call" | custom-call | tf_op jit(solution)/shard_map/weight_gradient_0_0/pallas_call | solution.py:382
  145.1 4.3 %collective-permute-done.21.refs_2_ = bf16[512,384]{1,0:T(8,128)(2,1)S(1)} collective-permute-done((bf16[512,384]{1,0:T(8,128)(2,1)}, bf16[512,384]{1,0:T(8,128)(2,1)S(1)}, u32[]{:S(2)}, u32[]{:S(2)}) %collective-permute-start.21) | collective-permute-done | bytes 393248 | tf_op jit(solution)/shard_map/ppermute | solution.py:428
  151.7 4.9 %weight_gradient_1_0.1 = (f32[576,1024]{1,0:T(8,128)}, f32[576,1024]{1,0:T(8,128)}, f32[576,1024]{1,0:T(8,128)}) custom-call(s32[15]{0:T(128)} %stack.61.where_ref, bf16[576,512]{1,0:T(8,128)(2,1)} %get-tuple-element.91.own_ref, bf16[512,384]{1,0:T(8,128)(2,1)} %get-tuple-element.102.refs_0_, ...), custom_call_target="tpu_custom_call", output_to_operand_aliasing={{0}: (5, {}), {1}: (6, {}), {2}: (7, {})} | custom-call | tf_op jit(solution)/shard_map/weight_gradient_1_0/pallas_call | solution.py:382
  157.5 2.0 %unpack.1 = (bf16[128,1024]{1,0:T(8,128)(2,1)}, f32[8,128]{1,0:T(8,128)}, f32[128,1024]{1,0:T(8,128)}) custom-call(bf16[4,272,256]{2,1,0:T(8,128)(2,1)} %copy-done.1), custom_call_target="tpu_custom_call" | custom-call | tf_op jit(solution)/shard_map/unpack/pallas_call | solution.py:438
  159.5 5.1 %collective-permute-done.24.refs_1_ = bf16[512,384]{1,0:T(8,128)(2,1)S(1)} collective-permute-done((bf16[512,384]{1,0:T(8,128)(2,1)S(1)}, bf16[512,384]{1,0:T(8,128)(2,1)S(1)}, u32[]{:S(2)}, u32[]{:S(2)}) %collective-permute-start.24) | collective-permute-done | bytes 393248 | tf_op jit(solution)/shard_map/ppermute | solution.py:433
  165.4 3.3 %weight_gradient_1_3.1 = (f32[576,1024]{1,0:T(8,128)}, f32[576,1024]{1,0:T(8,128)}, f32[576,1024]{1,0:T(8,128)}) custom-call(s32[15]{0:T(128)} %stack.61.where_ref, bf16[576,512]{1,0:T(8,128)(2,1)} %get-tuple-element.91.own_ref, bf16[512,384]{1,0:T(8,128)(2,1)} %copy-done.8, ...), custom_call_target="tpu_custom_call", output_to_operand_aliasing={{0}: (4, {}), {1}: (5, {}), {2}: (6, {})} | custom-call | tf_op jit(solution)/shard_map/weight_gradient_1_3/pallas_call | solution.py:382
  (83 shorter events, 11.7 us)
Async XLA Ops:
  3.1 11.4 %collective-permute-start = (bf16[576,128]{1,0:T(8,128)(2,1)}, bf16[576,128]{1,0:T(8,128)(2,1)S(1)}, u32[]{:S(2)}, u32[]{:S(2)}) collective-permute-start(bf16[576,128]{1,0:T(8,128)(2,1)} %pack_tokens.1), channel_id=1, source_target_pairs={{0,4},{4,8},{8,12},{12,0},{1,5},{5,9},{9,13},{13,1},{2,6},{6,10},{... | collective-permute-start | bytes 442376 | tf_op jit(solution)/shard_map/ppermute | solution.py:342
  6.2 12.6 %collective-permute-start.1 = (bf16[576,128]{1,0:T(8,128)(2,1)}, bf16[576,128]{1,0:T(8,128)(2,1)S(1)}, u32[]{:S(2)}, u32[]{:S(2)}) collective-permute-start(bf16[576,128]{1,0:T(8,128)(2,1)} %pack_tokens.1), channel_id=1, source_target_pairs={{0,8},{4,12},{8,0},{12,4},{1,9},{5,13},{9,1},{13,5},{2,10},{6,14},... | collective-permute-start | bytes 442376 | tf_op jit(solution)/shard_map/ppermute | solution.py:342
  8.7 10.0 %collective-permute-start.2 = (bf16[576,128]{1,0:T(8,128)(2,1)}, bf16[576,128]{1,0:T(8,128)(2,1)S(1)}, u32[]{:S(2)}, u32[]{:S(2)}) collective-permute-start(bf16[576,128]{1,0:T(8,128)(2,1)} %pack_tokens.1), channel_id=1, source_target_pairs={{0,12},{4,0},{8,4},{12,8},{1,13},{5,1},{9,5},{13,9},{2,14},{6,2},{... | collective-permute-start | bytes 442376 | tf_op jit(solution)/shard_map/ppermute | solution.py:342
  18.8 37.4 %copy-start = (bf16[2304,128]{1,0:T(8,128)(2,1)}, bf16[2304,128]{1,0:T(8,128)(2,1)S(1)}, u32[]{:S(2)}) copy-start(bf16[2304,128]{1,0:T(8,128)(2,1)S(1)} %pad_maximum_fusion.refs_0_) | copy-start | bytes 1769476
  18.8 25.1 %collective-permute-start.3 = (bf16[2304,128]{1,0:T(8,128)(2,1)S(1)}, bf16[2304,128]{1,0:T(8,128)(2,1)S(1)}, u32[]{:S(2)}, u32[]{:S(2)}) collective-permute-start(bf16[2304,128]{1,0:T(8,128)(2,1)S(1)} %pad_maximum_fusion.refs_0_), channel_id=1, source_target_pairs={{0,2},{2,0},{1,3},{3,1},{4,6},{6,4},{5,7},{7,5},{8,10},{10,8},{9,1... | collective-permute-start | bytes 1769480 | tf_op jit(solution)/shard_map/ppermute | solution.py:342
  20.4 12.9 %collective-permute-start.6 = (bf16[384,384]{1,0:T(8,128)(2,1)}, bf16[384,384]{1,0:T(8,128)(2,1)S(1)}, u32[]{:S(2)}, u32[]{:S(2)}) collective-permute-start(bf16[384,384]{1,0:T(8,128)(2,1)} %get-tuple-element.67), channel_id=1, source_target_pairs={{0,4},{4,8},{8,12},{12,0},{1,5},{5,9},{9,13},{13,1},{2,6},{6,10},{... | collective-permute-start | bytes 884744 | tf_op jit(solution)/shard_map/ppermute | solution.py:342
  24.0 19.9 %collective-permute-start.4 = (bf16[384,384]{1,0:T(8,128)(2,1)}, bf16[384,384]{1,0:T(8,128)(2,1)S(1)}, u32[]{:S(2)}, u32[]{:S(2)}) collective-permute-start(bf16[384,384]{1,0:T(8,128)(2,1)} %get-tuple-element.65), channel_id=1, source_target_pairs={{0,8},{4,12},{8,0},{12,4},{1,9},{5,13},{9,1},{13,5},{2,10},{6,14},... | collective-permute-start | bytes 884744 | tf_op jit(solution)/shard_map/ppermute | solution.py:342
  25.6 18.3 %collective-permute-start.5 = (bf16[384,384]{1,0:T(8,128)(2,1)}, bf16[384,384]{1,0:T(8,128)(2,1)S(1)}, u32[]{:S(2)}, u32[]{:S(2)}) collective-permute-start(bf16[384,384]{1,0:T(8,128)(2,1)} %get-tuple-element.66), channel_id=1, source_target_pairs={{0,12},{4,0},{8,4},{12,8},{1,13},{5,1},{9,5},{13,9},{2,14},{6,2},{... | collective-permute-start | bytes 884744 | tf_op jit(solution)/shard_map/ppermute | solution.py:342
  33.3 22.7 %copy-start.16 = (bf16[384,384]{1,0:T(8,128)(2,1)}, bf16[384,384]{1,0:T(8,128)(2,1)S(1)}, u32[]{:S(2)}) copy-start(bf16[384,384]{1,0:T(8,128)(2,1)S(1)} %collective-permute-done.6.refs_2_) | copy-start | bytes 884740
  33.3 10.6 %collective-permute-start.7 = (bf16[288,384]{1,0:T(8,128)(2,1)S(1)}, bf16[288,384]{1,0:T(8,128)(2,1)S(1)}, u32[]{:S(2)}, u32[]{:S(2)}) collective-permute-start(bf16[288,384]{1,0:T(8,128)(2,1)S(1)} %slice.24), channel_id=1, source_target_pairs={{0,16},{16,0},{1,17},{17,1},{2,18},{18,2},{3,19},{19,3},{4,20},{20... | collective-permute-start | bytes 663560 | tf_op jit(solution)/shard_map/ppermute | solution.py:342
  44.0 9.7 %collective-permute-start.8 = (bf16[2304,128]{1,0:T(8,128)(2,1)S(1)}, bf16[2304,128]{1,0:T(8,128)(2,1)S(1)}, u32[]{:S(2)}, u32[]{:S(2)}) collective-permute-start(bf16[2304,128]{1,0:T(8,128)(2,1)S(1)} %pad_maximum_fusion.refs_0_), channel_id=1, source_target_pairs={{0,1},{1,0},{2,3},{3,2},{4,5},{5,4},{6,7},{7,6},{8,9},{9,8},{10,11... | collective-permute-start | bytes 1769480 | tf_op jit(solution)/shard_map/ppermute | solution.py:342
  44.7 11.3 %collective-permute-start.9 = (bf16[2304,128]{1,0:T(8,128)(2,1)S(1)}, bf16[2304,128]{1,0:T(8,128)(2,1)S(1)}, u32[]{:S(2)}, u32[]{:S(2)}) collective-permute-start(bf16[2304,128]{1,0:T(8,128)(2,1)S(1)} %collective-permute-done.3.refs_1_), channel_id=1, source_target_pairs={{0,1},{1,0},{2,3},{3,2},{4,5},{5,4},{6,7},{7,6},{8,9},{9,8},{10,11... | collective-permute-start | bytes 1769480 | tf_op jit(solution)/shard_map/ppermute | solution.py:342
  44.7 15.9 %collective-permute-start.13 = (bf16[288,384]{1,0:T(8,128)(2,1)S(1)}, bf16[288,384]{1,0:T(8,128)(2,1)}, u32[]{:S(2)}, u32[]{:S(2)}) collective-permute-start(bf16[288,384]{1,0:T(8,128)(2,1)S(1)} %slice.19), channel_id=1, source_target_pairs={{0,16},{16,0},{1,17},{17,1},{2,18},{18,2},{3,19},{19,3},{4,20},{20... | collective-permute-start | bytes 663560 | tf_op jit(solution)/shard_map/ppermute | solution.py:342
  46.3 14.3 %collective-permute-start.14 = (bf16[288,384]{1,0:T(8,128)(2,1)S(1)}, bf16[288,384]{1,0:T(8,128)(2,1)}, u32[]{:S(2)}, u32[]{:S(2)}) collective-permute-start(bf16[288,384]{1,0:T(8,128)(2,1)S(1)} %slice.20), channel_id=1, source_target_pairs={{0,16},{16,0},{1,17},{17,1},{2,18},{18,2},{3,19},{19,3},{4,20},{20... | collective-permute-start | bytes 663560 | tf_op jit(solution)/shard_map/ppermute | solution.py:342
  46.9 24.9 %collective-permute-start.10 = (bf16[384,384]{1,0:T(8,128)(2,1)}, bf16[384,384]{1,0:T(8,128)(2,1)S(1)}, u32[]{:S(2)}, u32[]{:S(2)}) collective-permute-start(bf16[384,384]{1,0:T(8,128)(2,1)} %get-tuple-element.77), channel_id=1, source_target_pairs={{0,4},{4,8},{8,12},{12,0},{1,5},{5,9},{9,13},{13,1},{2,6},{6,10},{... | collective-permute-start | bytes 884744 | tf_op jit(solution)/shard_map/ppermute | solution.py:342
  53.7 21.9 %collective-permute-start.11 = (bf16[384,384]{1,0:T(8,128)(2,1)}, bf16[384,384]{1,0:T(8,128)(2,1)S(1)}, u32[]{:S(2)}, u32[]{:S(2)}) collective-permute-start(bf16[384,384]{1,0:T(8,128)(2,1)} %get-tuple-element.78), channel_id=1, source_target_pairs={{0,8},{4,12},{8,0},{12,4},{1,9},{5,13},{9,1},{13,5},{2,10},{6,14},... | collective-permute-start | bytes 884744 | tf_op jit(solution)/shard_map/ppermute | solution.py:342
  56.0 19.5 %collective-permute-start.12 = (bf16[384,384]{1,0:T(8,128)(2,1)}, bf16[384,384]{1,0:T(8,128)(2,1)}, u32[]{:S(2)}, u32[]{:S(2)}) collective-permute-start(bf16[384,384]{1,0:T(8,128)(2,1)} %get-tuple-element.79), channel_id=1, source_target_pairs={{0,12},{4,0},{8,4},{12,8},{1,13},{5,1},{9,5},{13,9},{2,14},{6,2},{... | collective-permute-start | bytes 884744 | tf_op jit(solution)/shard_map/ppermute | solution.py:342
  75.6 12.1 %collective-permute-start.15 = (bf16[288,384]{1,0:T(8,128)(2,1)S(1)}, bf16[288,384]{1,0:T(8,128)(2,1)S(1)}, u32[]{:S(2)}, u32[]{:S(2)}) collective-permute-start(bf16[288,384]{1,0:T(8,128)(2,1)S(1)} %slice.21), channel_id=1, source_target_pairs={{0,16},{16,0},{1,17},{17,1},{2,18},{18,2},{3,19},{19,3},{4,20},{20... | collective-permute-start | bytes 663560 | tf_op jit(solution)/shard_map/ppermute | solution.py:342
  77.2 13.6 %collective-permute-start.16 = (bf16[288,384]{1,0:T(8,128)(2,1)S(1)}, bf16[288,384]{1,0:T(8,128)(2,1)S(1)}, u32[]{:S(2)}, u32[]{:S(2)}) collective-permute-start(bf16[288,384]{1,0:T(8,128)(2,1)S(1)} %slice.22), channel_id=1, source_target_pairs={{0,16},{16,0},{1,17},{17,1},{2,18},{18,2},{3,19},{19,3},{4,20},{20... | collective-permute-start | bytes 663560 | tf_op jit(solution)/shard_map/ppermute | solution.py:342
  78.7 13.7 %collective-permute-start.17 = (bf16[288,384]{1,0:T(8,128)(2,1)S(1)}, bf16[288,384]{1,0:T(8,128)(2,1)S(1)}, u32[]{:S(2)}, u32[]{:S(2)}) collective-permute-start(bf16[288,384]{1,0:T(8,128)(2,1)S(1)} %slice.23), channel_id=1, source_target_pairs={{0,16},{16,0},{1,17},{17,1},{2,18},{18,2},{3,19},{19,3},{4,20},{20... | collective-permute-start | bytes 663560 | tf_op jit(solution)/shard_map/ppermute | solution.py:342
  80.3 32.5 %collective-permute-start.18 = (bf16[512,384]{1,0:T(8,128)(2,1)}, bf16[512,384]{1,0:T(8,128)(2,1)S(1)}, u32[]{:S(2)}, u32[]{:S(2)}) collective-permute-start(bf16[512,384]{1,0:T(8,128)(2,1)} %get-tuple-element.95.refs_0_), channel_id=1, source_target_pairs={{0,4},{4,8},{8,12},{12,0},{1,5},{5,9},{9,13},{13,1},{2,6},{6,10},{... | collective-permute-start | bytes 1179656 | tf_op jit(solution)/shard_map/ppermute | solution.py:342
  87.2 25.7 %collective-permute-start.19 = (bf16[512,384]{1,0:T(8,128)(2,1)}, bf16[512,384]{1,0:T(8,128)(2,1)S(1)}, u32[]{:S(2)}, u32[]{:S(2)}) collective-permute-start(bf16[512,384]{1,0:T(8,128)(2,1)} %get-tuple-element.95.refs_0_), channel_id=1, source_target_pairs={{0,8},{4,12},{8,0},{12,4},{1,9},{5,13},{9,1},{13,5},{2,10},{6,14},... | collective-permute-start | bytes 1179656 | tf_op jit(solution)/shard_map/ppermute | solution.py:342
  87.7 25.2 %collective-permute-start.20 = (bf16[512,384]{1,0:T(8,128)(2,1)}, bf16[512,384]{1,0:T(8,128)(2,1)S(1)}, u32[]{:S(2)}, u32[]{:S(2)}) collective-permute-start(bf16[512,384]{1,0:T(8,128)(2,1)} %get-tuple-element.95.refs_0_), channel_id=1, source_target_pairs={{0,12},{4,0},{8,4},{12,8},{1,13},{5,1},{9,5},{13,9},{2,14},{6,2},{... | collective-permute-start | bytes 1179656 | tf_op jit(solution)/shard_map/ppermute | solution.py:342
  104.5 45.3 %copy-start.6 = (bf16[512,384]{1,0:T(8,128)(2,1)S(1)}, bf16[512,384]{1,0:T(8,128)(2,1)}, u32[]{:S(2)}) copy-start(bf16[512,384]{1,0:T(8,128)(2,1)} %get-tuple-element.102.refs_0_) | copy-start | bytes 1179652
  104.5 52.2 %all-to-all-start = ((bf16[4,272,256]{2,1,0:T(8,128)(2,1)}), bf16[4,272,256]{2,1,0:T(8,128)(2,1)S(1)}, u32[]{:S(2)}, u32[]{:S(2)}) async-start(bf16[4,272,256]{2,1,0:T(8,128)(2,1)} %get-tuple-element.89), calls=%async_computation | async-start | bytes 1114112 | tf_op jit(solution)/shard_map/all_to_all | solution.py:436
  112.9 26.6 %copy-start.11 = (bf16[512,384]{1,0:T(8,128)(2,1)}, bf16[512,384]{1,0:T(8,128)(2,1)S(1)}, u32[]{:S(2)}) copy-start(bf16[512,384]{1,0:T(8,128)(2,1)S(1)} %collective-permute-done.18.refs_1_) | copy-start | bytes 1179652
  112.9 26.6 %copy-start.12 = (bf16[512,384]{1,0:T(8,128)(2,1)}, bf16[512,384]{1,0:T(8,128)(2,1)S(1)}, u32[]{:S(2)}) copy-start(bf16[512,384]{1,0:T(8,128)(2,1)S(1)} %collective-permute-done.19.refs_2_) | copy-start | bytes 1179652
  112.9 26.6 %copy-start.13 = (bf16[512,384]{1,0:T(8,128)(2,1)}, bf16[512,384]{1,0:T(8,128)(2,1)S(1)}, u32[]{:S(2)}) copy-start(bf16[512,384]{1,0:T(8,128)(2,1)S(1)} %collective-permute-done.20.refs_3_) | copy-start | bytes 1179652
  112.9 36.5 %collective-permute-start.21 = (bf16[512,384]{1,0:T(8,128)(2,1)}, bf16[512,384]{1,0:T(8,128)(2,1)S(1)}, u32[]{:S(2)}, u32[]{:S(2)}) collective-permute-start(bf16[512,384]{1,0:T(8,128)(2,1)} %get-tuple-element.102.refs_0_), channel_id=1, source_target_pairs={{0,8},{4,12},{8,0},{12,4},{1,9},{5,13},{9,1},{13,5},{2,10},{6,14},... | collective-permute-start | bytes 1179656 | tf_op jit(solution)/shard_map/ppermute | solution.py:428
  126.2 23.6 %collective-permute-start.22 = (bf16[512,384]{1,0:T(8,128)(2,1)}, bf16[512,384]{1,0:T(8,128)(2,1)S(1)}, u32[]{:S(2)}, u32[]{:S(2)}) collective-permute-start(bf16[512,384]{1,0:T(8,128)(2,1)} %get-tuple-element.102.refs_0_), channel_id=1, source_target_pairs={{0,4},{4,0},{8,12},{12,8},{1,5},{5,1},{9,13},{13,9},{2,6},{6,2},{1... | collective-permute-start | bytes 1179656 | tf_op jit(solution)/shard_map/ppermute | solution.py:429
  149.7 9.7 %collective-permute-start.23 = (bf16[512,384]{1,0:T(8,128)(2,1)S(1)}, bf16[512,384]{1,0:T(8,128)(2,1)S(1)}, u32[]{:S(2)}, u32[]{:S(2)}) collective-permute-start(bf16[512,384]{1,0:T(8,128)(2,1)S(1)} %copy-done.6), channel_id=1, source_target_pairs={{4,8},{8,4},{5,9},{9,5},{6,10},{10,6},{7,11},{11,7},{20,24},{24,20... | collective-permute-start | bytes 1179656 | tf_op jit(solution)/shard_map/ppermute | solution.py:432
  150.4 14.2 %collective-permute-start.24 = (bf16[512,384]{1,0:T(8,128)(2,1)S(1)}, bf16[512,384]{1,0:T(8,128)(2,1)S(1)}, u32[]{:S(2)}, u32[]{:S(2)}) collective-permute-start(bf16[512,384]{1,0:T(8,128)(2,1)S(1)} %collective-permute-done.21.refs_2_), channel_id=1, source_target_pairs={{8,12},{4,0},{9,13},{5,1},{10,14},{6,2},{11,15},{7,3},{24,28},{20,... | collective-permute-start | bytes 1179656 | tf_op jit(solution)/shard_map/ppermute | solution.py:433
  (17 other events, 111.7 us)

commit v6 on v5

--- a/solution.py
+++ b/solution.py
@@ -13,6 +13,7 @@
 CHUNK = 128
 TAIL = 16
 EXTRA = 96
+FLOPS = (12_000_000_000, 1_000)
 HEAD_COLUMNS = 2 * DK + DV
 
 epsilon = 1e-06
@@ -396,7 +397,8 @@
     back = None
     for slot, direct in enumerate((first, second)):
         if slot:
-            direct, back = after(direct, back)
+            for d in range(ctx - 1):
+                direct[d], back = after(direct[d], back)
             swapped = [along(x[:half], "groups", 1) for x in direct]
         earlier = [] if back is None else [back]
         grad, back = pl.pallas_call(
@@ -417,7 +419,7 @@
                 pltpu.VMEM((ctx, CHUNK), f32),
                 pltpu.VMEM((ctx, CHUNK, DK), bf16),
             ],
-            cost_estimate=pl.CostEstimate(flops=12_000_000_000, transcendentals=0, bytes_accessed=8_000_000),
+            cost_estimate=pl.CostEstimate(flops=FLOPS[slot], transcendentals=0, bytes_accessed=FLOPS[slot] // 1000),
             name=f"head_{slot}",
         )(where, all_tokens, packed[slot * ctx], *direct, *swapped, *earlier)
         if slot == 0:

time: 169 us -> 172 us (1.018)
  waiting for transfers between devices: 35.3 us -> 48 us
  starting transfers between devices: 78.8 us -> 69.4 us
    ppermute x1, starting transfers between devices: 13.3 us -> 5.78 us  [head_split(): two = lax.ppermute(grad, 'ctx', [(0, 2), (1, 3), (2, 0), (3, 1)])]
    ppermute x21, waiting for transfers between devices: 25.5 us -> 33 us  [along(): return lax.ppermute(x, axis, [(i, (i + hop) % count) for i in range(count)])]
    ppermute x1, waiting for transfers between devices: 5.14 us -> 10.6 us  [head_split(): far = lax.ppermute(two, 'ctx', [(2, 3), (1, 0)])]
    all_to_all x1, starting transfers between devices: 8.38 us -> 3.6 us  [head_split(): back = lax.all_to_all(back, 'ctx', 0, 0)]
    ppermute x1, starting transfers between devices: 13.3 us -> 17.6 us  [head_split(): pair = lax.ppermute(grad, 'ctx', [(0, 1), (1, 0), (2, 3), (3, 2)])]
    unnamed x46 -> x48, local copies, waits for them, and re-layouts: 3.59 us -> 3.7 us
  transfers between devices with their start and end apart: 26 -> 26, of which waited for: 8 -> 9; matrix products, arithmetic and copies ran while one was open for 1% -> 0% of each run, Pallas kernels for 26% -> 25%
where the time goes in v6:
time: 172 us
  starting transfers between devices  69.4 us (40%)
  Pallas kernels  48.4 us (28%)
  waiting for transfers between devices  48 us (28%)
  local copies, waits for them, and re-layouts  5.16 us (3%)
    ppermute x21, starting transfers between devices, along(): return lax.ppermute(x, axis, [(i, (i + hop) % count) for i in range(count)])  40.4 us
    ppermute x21, waiting for transfers between devices, along(): return lax.ppermute(x, axis, [(i, (i + hop) % count) for i in range(count)])  33 us
    pallas_call x2, Pallas kernels, head_split(): pl.pallas_call(functools.partial(head_kernel, ctx, slot), out_shape=[shap...  22.6 us
    ppermute x1, starting transfers between devices, head_split(): pair = lax.ppermute(grad, 'ctx', [(0, 1), (1, 0), (2, 3), (3, 2)])  17.6 us
    pallas_call x3, Pallas kernels, products(): pl.pallas_call(functools.partial(weight_gradient_kernel, steps, slot == 1...  13.8 us
    ppermute x1, waiting for transfers between devices, head_split(): far = lax.ppermute(two, 'ctx', [(2, 3), (1, 0)])  10.6 us
    ppermute x1, starting transfers between devices, head_split(): two = lax.ppermute(grad, 'ctx', [(0, 2), (1, 3), (2, 0), (3, 1)])  5.78 us
    pallas_call x1, Pallas kernels, head_split(): pl.pallas_call(functools.partial(pack_kernel, ctx), out_shape=[shape((siz...  4.46 us
  transfers between devices with their start and end apart: 26, of which 9 were waited for; matrix products, arithmetic and copies ran while one was open for 0% of the time, Pallas kernels for 25%

profile of v6, /device:TPU:0, one launch (start us, length us, event | category | flops | bytes accessed | tf_op | source)
XLA Modules:
  0.0 172.0 jit_solution(10834951639632422205)
XLA Ops:
  1.3 1.8 %pack_tokens.1 = bf16[576,128]{1,0:T(8,128)(2,1)} custom-call(s32[15]{0:T(128)} %stack.61.where_ref, bf16[128,2304]{1,0:T(8,128)(2,1)} %tokens_ref.1), custom_call_target="tpu_custom_call" | custom-call | tf_op jit(solution)/shard_map/pack_tokens/pallas_call | solution.py:345
  3.1 3.0 %collective-permute-start = (bf16[576,128]{1,0:T(8,128)(2,1)}, bf16[576,128]{1,0:T(8,128)(2,1)S(1)}, u32[]{:S(2)}, u32[]{:S(2)}) collective-permute-start(bf16[576,128]{1,0:T(8,128)(2,1)} %pack_tokens.1), channel_id=1, source_target_pairs={{0,4},{4,8},{8,12},{12,0},{1,5},{5,9},{9,13},{13,1},{2,6},{6,10},{... | collective-permute-start | bytes 442376 | tf_op jit(solution)/shard_map/ppermute | solution.py:343
  6.2 2.6 %collective-permute-start.1 = (bf16[576,128]{1,0:T(8,128)(2,1)}, bf16[576,128]{1,0:T(8,128)(2,1)S(1)}, u32[]{:S(2)}, u32[]{:S(2)}) collective-permute-start(bf16[576,128]{1,0:T(8,128)(2,1)} %pack_tokens.1), channel_id=1, source_target_pairs={{0,8},{4,12},{8,0},{12,4},{1,9},{5,13},{9,1},{13,5},{2,10},{6,14},... | collective-permute-start | bytes 442376 | tf_op jit(solution)/shard_map/ppermute | solution.py:343
  10.1 4.5 %pack.1 = (bf16[672,384]{1,0:T(8,128)(2,1)}, bf16[384,384]{1,0:T(8,128)(2,1)}, bf16[384,384]{1,0:T(8,128)(2,1)}, bf16[384,384]{1,0:T(8,128)(2,1)}, bf16[672,384]...) custom-call(s32[15]{0:T(128)} %stack.61.where_ref, ...), custom_call_target="tpu_custom_call" | custom-call | tf_op jit(solution)/shard_map/pack/pallas_call | solution.py:353
  14.6 4.2 %collective-permute-done.1 = bf16[576,128]{1,0:T(8,128)(2,1)S(1)} collective-permute-done((bf16[576,128]{1,0:T(8,128)(2,1)}, bf16[576,128]{1,0:T(8,128)(2,1)S(1)}, u32[]{:S(2)}, u32[]{:S(2)}) %collective-permute-start.1) | collective-permute-done | bytes 147488 | tf_op jit(solution)/shard_map/ppermute | solution.py:343
  18.8 1.6 collective-permute-start.3
  20.4 3.6 %collective-permute-start.6 = (bf16[384,384]{1,0:T(8,128)(2,1)}, bf16[384,384]{1,0:T(8,128)(2,1)S(1)}, u32[]{:S(2)}, u32[]{:S(2)}) collective-permute-start(bf16[384,384]{1,0:T(8,128)(2,1)} %get-tuple-element.69), channel_id=1, source_target_pairs={{0,4},{4,8},{8,12},{12,0},{1,5},{5,9},{9,13},{13,1},{2,6},{6,10},{... | collective-permute-start | bytes 884744 | tf_op jit(solution)/shard_map/ppermute | solution.py:343
  26.4 6.9 %collective-permute-done.6.refs_2_ = bf16[384,384]{1,0:T(8,128)(2,1)S(1)} collective-permute-done((bf16[384,384]{1,0:T(8,128)(2,1)}, bf16[384,384]{1,0:T(8,128)(2,1)S(1)}, u32[]{:S(2)}, u32[]{:S(2)}) %collective-permute-start.6) | collective-permute-done | bytes 294944 | tf_op jit(solution)/shard_map/ppermute | solution.py:343
  33.3 1.6 collective-permute-start.7
  34.9 9.0 %collective-permute-done.4.refs_3_ = bf16[384,384]{1,0:T(8,128)(2,1)S(1)} collective-permute-done((bf16[384,384]{1,0:T(8,128)(2,1)}, bf16[384,384]{1,0:T(8,128)(2,1)S(1)}, u32[]{:S(2)}, u32[]{:S(2)}) %collective-permute-start.4) | collective-permute-done | bytes 294944 | tf_op jit(solution)/shard_map/ppermute | solution.py:343
  44.8 1.6 collective-permute-start.11
  47.6 6.7 %collective-permute-start.10 = (bf16[384,384]{1,0:T(8,128)(2,1)}, bf16[384,384]{1,0:T(8,128)(2,1)S(1)}, u32[]{:S(2)}, u32[]{:S(2)}) collective-permute-start(bf16[384,384]{1,0:T(8,128)(2,1)} %get-tuple-element.79), channel_id=1, source_target_pairs={{0,4},{4,8},{8,12},{12,0},{1,5},{5,9},{9,13},{13,1},{2,6},{6,10},{... | collective-permute-start | bytes 884744 | tf_op jit(solution)/shard_map/ppermute | solution.py:343
  54.3 2.4 %collective-permute-start.13 = (bf16[384,384]{1,0:T(8,128)(2,1)}, bf16[384,384]{1,0:T(8,128)(2,1)S(1)}, u32[]{:S(2)}, u32[]{:S(2)}) collective-permute-start(bf16[384,384]{1,0:T(8,128)(2,1)} %get-tuple-element.86), channel_id=1, source_target_pairs={{0,8},{4,12},{8,0},{12,4},{1,9},{5,13},{9,1},{13,5},{2,10},{6,14},... | collective-permute-start | bytes 884744 | tf_op jit(solution)/shard_map/ppermute | solution.py:343
  57.5 3.7 %unpack_tokens.1 = (bf16[4,512,576]{2,1,0:T(8,128)(2,1)}, bf16[576,512]{1,0:T(8,128)(2,1)}) custom-call(s32[15]{0:T(128)} %stack.61.where_ref, bf16[2304,128]{1,0:T(8,128)(2,1)} %copy-done, bf16[2304,128]{1,0:T(8,128)(2,1)} %copy-done.6, bf16[2304,128]{1,0:T(8,128)(2,1)} %copy-done.7, bf16[2304,128]{1,0:T(8,128)(2,1)} %copy-done.8), custom_call_target="tpu_custom_call" | custom-call | tf_op jit(solution)/shard_map/unpack_tokens/pallas_call | solution.py:370
  61.3 11.2 %head_0.1 = (bf16[512,384]{1,0:T(8,128)(2,1)}, bf16[4,272,128]{2,1,0:T(8,128)(2,1)}) custom-call(s32[15]{0:T(128)} %stack.61.where_ref, bf16[4,512,576]{2,1,0:T(8,128)(2,1)} %get-tuple-element.72.refs_0_, bf16[672,384]{1,0:T(8,128)(2,1)} %get-tuple-element.80.refs_1_, bf16[384,384]{1,0:T(8,128)(2,1)} %copy-done.20, bf16[384,384]{1,0:T(8,128)(2,1)} %copy-done.21, ...), custom_call_target="tpu_custom_call" | custom-call | flops 12000000000 | bytes 12000000 | tf_op jit(solution)/shard_map/head_0/pallas_call | solution.py:404
  72.5 3.7 %collective-permute-done.13.refs_3_ = bf16[384,384]{1,0:T(8,128)(2,1)S(1)} collective-permute-done((bf16[384,384]{1,0:T(8,128)(2,1)}, bf16[384,384]{1,0:T(8,128)(2,1)S(1)}, u32[]{:S(2)}, u32[]{:S(2)}) %collective-permute-start.13) | collective-permute-done | bytes 294944 | tf_op jit(solution)/shard_map/ppermute | solution.py:343
  76.3 1.6 collective-permute-start.17
  77.8 6.8 %collective-permute-start.18 = (bf16[512,384]{1,0:T(8,128)(2,1)}, bf16[512,384]{1,0:T(8,128)(2,1)S(1)}, u32[]{:S(2)}, u32[]{:S(2)}) collective-permute-start(bf16[512,384]{1,0:T(8,128)(2,1)} %get-tuple-element.99.refs_0_), channel_id=1, source_target_pairs={{0,4},{4,8},{8,12},{12,0},{1,5},{5,9},{9,13},{13,1},{2,6},{6,10},{... | collective-permute-start | bytes 1179656 | tf_op jit(solution)/shard_map/ppermute | solution.py:343
  85.1 1.9 %collective-permute-start.20 = (bf16[512,384]{1,0:T(8,128)(2,1)}, bf16[512,384]{1,0:T(8,128)(2,1)S(1)}, u32[]{:S(2)}, u32[]{:S(2)}) collective-permute-start(bf16[512,384]{1,0:T(8,128)(2,1)} %get-tuple-element.99.refs_0_), channel_id=1, source_target_pairs={{0,12},{4,0},{8,4},{12,8},{1,13},{5,1},{9,5},{13,9},{2,14},{6,2},{... | collective-permute-start | bytes 1179656 | tf_op jit(solution)/shard_map/ppermute | solution.py:343
  87.6 1.6 collective-permute-start.15
  89.2 6.2 %collective-permute-done.16.refs_6_ = bf16[288,384]{1,0:T(8,128)(2,1)S(1)} collective-permute-done((bf16[288,384]{1,0:T(8,128)(2,1)S(1)}, bf16[288,384]{1,0:T(8,128)(2,1)S(1)}, u32[]{:S(2)}, u32[]{:S(2)}) %collective-permute-start.16) | collective-permute-done | bytes 221216 | tf_op jit(solution)/shard_map/ppermute | solution.py:343
  95.5 2.9 %collective-permute-done.15.refs_5_ = bf16[288,384]{1,0:T(8,128)(2,1)S(1)} collective-permute-done((bf16[288,384]{1,0:T(8,128)(2,1)S(1)}, bf16[288,384]{1,0:T(8,128)(2,1)S(1)}, u32[]{:S(2)}, u32[]{:S(2)}) %collective-permute-start.15) | collective-permute-done | bytes 221216 | tf_op jit(solution)/shard_map/ppermute | solution.py:343
  99.0 11.4 %head_1.1 = (bf16[512,384]{1,0:T(8,128)(2,1)}, bf16[4,272,256]{2,1,0:T(8,128)(2,1)}) custom-call(s32[15]{0:T(128)} %stack.61.where_ref, bf16[4,512,576]{2,1,0:T(8,128)(2,1)} %get-tuple-element.72.refs_0_, bf16[672,384]{1,0:T(8,128)(2,1)} %get-tuple-element.73.refs_1_, bf16[384,384]{1,0:T(8,128)(2,1)} %copy-done.2, bf16[384,384]{1,0:T(8,128)(2,1)} %copy-done.3, ...), custom_call_target="tpu_custom_call" | custom-call | flops 1000 | bytes 1 | tf_op jit(solution)/shard_map/head_1/pallas_call | solution.py:404
  110.4 3.6 %all-to-all-start = ((bf16[4,272,256]{2,1,0:T(8,128)(2,1)}), bf16[4,272,256]{2,1,0:T(8,128)(2,1)S(1)}, u32[]{:S(2)}, u32[]{:S(2)}) async-start(bf16[4,272,256]{2,1,0:T(8,128)(2,1)} %get-tuple-element.93), calls=%async_computation | async-start | bytes 1114112 | tf_op jit(solution)/shard_map/all_to_all | solution.py:438
  114.1 5.8 %collective-permute-start.21 = (bf16[512,384]{1,0:T(8,128)(2,1)}, bf16[512,384]{1,0:T(8,128)(2,1)S(1)}, u32[]{:S(2)}, u32[]{:S(2)}) collective-permute-start(bf16[512,384]{1,0:T(8,128)(2,1)} %get-tuple-element.106.refs_0_), channel_id=1, source_target_pairs={{0,8},{4,12},{8,0},{12,4},{1,9},{5,13},{9,1},{13,5},{2,10},{6,14},... | collective-permute-start | bytes 1179656 | tf_op jit(solution)/shard_map/ppermute | solution.py:430
  119.9 17.6 %collective-permute-start.22 = (bf16[512,384]{1,0:T(8,128)(2,1)}, bf16[512,384]{1,0:T(8,128)(2,1)S(1)}, u32[]{:S(2)}, u32[]{:S(2)}) collective-permute-start(bf16[512,384]{1,0:T(8,128)(2,1)} %get-tuple-element.106.refs_0_), channel_id=1, source_target_pairs={{0,4},{4,0},{8,12},{12,8},{1,5},{5,1},{9,13},{13,9},{2,6},{6,2},{1... | collective-permute-start | bytes 1179656 | tf_op jit(solution)/shard_map/ppermute | solution.py:431
  137.5 5.6 %weight_gradient_0_0.1 = (f32[576,1024]{1,0:T(8,128)}, f32[576,1024]{1,0:T(8,128)}, f32[576,1024]{1,0:T(8,128)}) custom-call(s32[15]{0:T(128)} %stack.61.where_ref, bf16[576,512]{1,0:T(8,128)(2,1)} %get-tuple-element.95.own_ref, bf16[512,384]{1,0:T(8,128)(2,1)} %get-tuple-element.99.refs_0_, bf16[512,384]{1,0:T(8,128)(2,1)} %copy-done.14, ...), custom_call_target="tpu_custom_call" | custom-call | tf_op jit(solution)/shard_map/weight_gradient_0_0/pallas_call | solution.py:383
  143.1 4.3 %collective-permute-done.21.refs_2_ = bf16[512,384]{1,0:T(8,128)(2,1)S(1)} collective-permute-done((bf16[512,384]{1,0:T(8,128)(2,1)}, bf16[512,384]{1,0:T(8,128)(2,1)S(1)}, u32[]{:S(2)}, u32[]{:S(2)}) %collective-permute-start.21) | collective-permute-done | bytes 393248 | tf_op jit(solution)/shard_map/ppermute | solution.py:430
  149.5 4.9 %weight_gradient_1_0.1 = (f32[576,1024]{1,0:T(8,128)}, f32[576,1024]{1,0:T(8,128)}, f32[576,1024]{1,0:T(8,128)}) custom-call(s32[15]{0:T(128)} %stack.61.where_ref, bf16[576,512]{1,0:T(8,128)(2,1)} %get-tuple-element.95.own_ref, bf16[512,384]{1,0:T(8,128)(2,1)} %get-tuple-element.106.refs_0_, ...), custom_call_target="tpu_custom_call", output_to_operand_aliasing={{0}: (5, {}), {1}: (6, {}), {2}: (7, {})} | custom-call | tf_op jit(solution)/shard_map/weight_gradient_1_0/pallas_call | solution.py:383
  155.3 2.0 %unpack.1 = (bf16[128,1024]{1,0:T(8,128)(2,1)}, f32[8,128]{1,0:T(8,128)}, f32[128,1024]{1,0:T(8,128)}) custom-call(bf16[4,272,256]{2,1,0:T(8,128)(2,1)} %copy-done.1), custom_call_target="tpu_custom_call" | custom-call | tf_op jit(solution)/shard_map/unpack/pallas_call | solution.py:440
  157.3 10.6 %collective-permute-done.24.refs_1_ = bf16[512,384]{1,0:T(8,128)(2,1)S(1)} collective-permute-done((bf16[512,384]{1,0:T(8,128)(2,1)S(1)}, bf16[512,384]{1,0:T(8,128)(2,1)S(1)}, u32[]{:S(2)}, u32[]{:S(2)}) %collective-permute-start.24) | collective-permute-done | bytes 393248 | tf_op jit(solution)/shard_map/ppermute | solution.py:435
  168.6 3.3 %weight_gradient_1_3.1 = (f32[576,1024]{1,0:T(8,128)}, f32[576,1024]{1,0:T(8,128)}, f32[576,1024]{1,0:T(8,128)}) custom-call(s32[15]{0:T(128)} %stack.61.where_ref, bf16[576,512]{1,0:T(8,128)(2,1)} %get-tuple-element.95.own_ref, bf16[512,384]{1,0:T(8,128)(2,1)} %copy-done.11, ...), custom_call_target="tpu_custom_call", output_to_operand_aliasing={{0}: (4, {}), {1}: (5, {}), {2}: (6, {})} | custom-call | tf_op jit(solution)/shard_map/weight_gradient_1_3/pallas_call | solution.py:383
  (85 shorter events, 12.8 us)
Async XLA Ops:
  3.1 11.4 %collective-permute-start = (bf16[576,128]{1,0:T(8,128)(2,1)}, bf16[576,128]{1,0:T(8,128)(2,1)S(1)}, u32[]{:S(2)}, u32[]{:S(2)}) collective-permute-start(bf16[576,128]{1,0:T(8,128)(2,1)} %pack_tokens.1), channel_id=1, source_target_pairs={{0,4},{4,8},{8,12},{12,0},{1,5},{5,9},{9,13},{13,1},{2,6},{6,10},{... | collective-permute-start | bytes 442376 | tf_op jit(solution)/shard_map/ppermute | solution.py:343
  6.2 12.6 %collective-permute-start.1 = (bf16[576,128]{1,0:T(8,128)(2,1)}, bf16[576,128]{1,0:T(8,128)(2,1)S(1)}, u32[]{:S(2)}, u32[]{:S(2)}) collective-permute-start(bf16[576,128]{1,0:T(8,128)(2,1)} %pack_tokens.1), channel_id=1, source_target_pairs={{0,8},{4,12},{8,0},{12,4},{1,9},{5,13},{9,1},{13,5},{2,10},{6,14},... | collective-permute-start | bytes 442376 | tf_op jit(solution)/shard_map/ppermute | solution.py:343
  8.7 10.0 %collective-permute-start.2 = (bf16[576,128]{1,0:T(8,128)(2,1)}, bf16[576,128]{1,0:T(8,128)(2,1)S(1)}, u32[]{:S(2)}, u32[]{:S(2)}) collective-permute-start(bf16[576,128]{1,0:T(8,128)(2,1)} %pack_tokens.1), channel_id=1, source_target_pairs={{0,12},{4,0},{8,4},{12,8},{1,13},{5,1},{9,5},{13,9},{2,14},{6,2},{... | collective-permute-start | bytes 442376 | tf_op jit(solution)/shard_map/ppermute | solution.py:343
  18.8 38.0 %copy-start = (bf16[2304,128]{1,0:T(8,128)(2,1)}, bf16[2304,128]{1,0:T(8,128)(2,1)S(1)}, u32[]{:S(2)}) copy-start(bf16[2304,128]{1,0:T(8,128)(2,1)S(1)} %pad_maximum_fusion.refs_0_) | copy-start | bytes 1769476
  18.8 25.1 %collective-permute-start.3 = (bf16[2304,128]{1,0:T(8,128)(2,1)S(1)}, bf16[2304,128]{1,0:T(8,128)(2,1)S(1)}, u32[]{:S(2)}, u32[]{:S(2)}) collective-permute-start(bf16[2304,128]{1,0:T(8,128)(2,1)S(1)} %pad_maximum_fusion.refs_0_), channel_id=1, source_target_pairs={{0,2},{2,0},{1,3},{3,1},{4,6},{6,4},{5,7},{7,5},{8,10},{10,8},{9,1... | collective-permute-start | bytes 1769480 | tf_op jit(solution)/shard_map/ppermute | solution.py:343
  20.4 12.9 %collective-permute-start.6 = (bf16[384,384]{1,0:T(8,128)(2,1)}, bf16[384,384]{1,0:T(8,128)(2,1)S(1)}, u32[]{:S(2)}, u32[]{:S(2)}) collective-permute-start(bf16[384,384]{1,0:T(8,128)(2,1)} %get-tuple-element.69), channel_id=1, source_target_pairs={{0,4},{4,8},{8,12},{12,0},{1,5},{5,9},{9,13},{13,1},{2,6},{6,10},{... | collective-permute-start | bytes 884744 | tf_op jit(solution)/shard_map/ppermute | solution.py:343
  24.0 19.9 %collective-permute-start.4 = (bf16[384,384]{1,0:T(8,128)(2,1)}, bf16[384,384]{1,0:T(8,128)(2,1)S(1)}, u32[]{:S(2)}, u32[]{:S(2)}) collective-permute-start(bf16[384,384]{1,0:T(8,128)(2,1)} %get-tuple-element.67), channel_id=1, source_target_pairs={{0,8},{4,12},{8,0},{12,4},{1,9},{5,13},{9,1},{13,5},{2,10},{6,14},... | collective-permute-start | bytes 884744 | tf_op jit(solution)/shard_map/ppermute | solution.py:343
  25.6 18.3 %collective-permute-start.5 = (bf16[384,384]{1,0:T(8,128)(2,1)}, bf16[384,384]{1,0:T(8,128)(2,1)S(1)}, u32[]{:S(2)}, u32[]{:S(2)}) collective-permute-start(bf16[384,384]{1,0:T(8,128)(2,1)} %get-tuple-element.68), channel_id=1, source_target_pairs={{0,12},{4,0},{8,4},{12,8},{1,13},{5,1},{9,5},{13,9},{2,14},{6,2},{... | collective-permute-start | bytes 884744 | tf_op jit(solution)/shard_map/ppermute | solution.py:343
  33.3 10.6 %collective-permute-start.7 = (bf16[288,384]{1,0:T(8,128)(2,1)S(1)}, bf16[288,384]{1,0:T(8,128)(2,1)S(1)}, u32[]{:S(2)}, u32[]{:S(2)}) collective-permute-start(bf16[288,384]{1,0:T(8,128)(2,1)S(1)} %slice.24), channel_id=1, source_target_pairs={{0,16},{16,0},{1,17},{17,1},{2,18},{18,2},{3,19},{19,3},{4,20},{20... | collective-permute-start | bytes 663560 | tf_op jit(solution)/shard_map/ppermute | solution.py:343
  44.0 10.3 %collective-permute-start.8 = (bf16[2304,128]{1,0:T(8,128)(2,1)S(1)}, bf16[2304,128]{1,0:T(8,128)(2,1)S(1)}, u32[]{:S(2)}, u32[]{:S(2)}) collective-permute-start(bf16[2304,128]{1,0:T(8,128)(2,1)S(1)} %pad_maximum_fusion.refs_0_), channel_id=1, source_target_pairs={{0,1},{1,0},{2,3},{3,2},{4,5},{5,4},{6,7},{7,6},{8,9},{9,8},{10,11... | collective-permute-start | bytes 1769480 | tf_op jit(solution)/shard_map/ppermute | solution.py:343
  44.7 12.0 %collective-permute-start.9 = (bf16[2304,128]{1,0:T(8,128)(2,1)S(1)}, bf16[2304,128]{1,0:T(8,128)(2,1)S(1)}, u32[]{:S(2)}, u32[]{:S(2)}) collective-permute-start(bf16[2304,128]{1,0:T(8,128)(2,1)S(1)} %collective-permute-done.3.refs_1_), channel_id=1, source_target_pairs={{0,1},{1,0},{2,3},{3,2},{4,5},{5,4},{6,7},{7,6},{8,9},{9,8},{10,11... | collective-permute-start | bytes 1769480 | tf_op jit(solution)/shard_map/ppermute | solution.py:343
  44.8 16.5 %collective-permute-start.11 = (bf16[288,384]{1,0:T(8,128)(2,1)S(1)}, bf16[288,384]{1,0:T(8,128)(2,1)}, u32[]{:S(2)}, u32[]{:S(2)}) collective-permute-start(bf16[288,384]{1,0:T(8,128)(2,1)S(1)} %slice.19), channel_id=1, source_target_pairs={{0,16},{16,0},{1,17},{17,1},{2,18},{18,2},{3,19},{19,3},{4,20},{20... | collective-permute-start | bytes 663560 | tf_op jit(solution)/shard_map/ppermute | solution.py:343
  47.1 14.2 %collective-permute-start.12 = (bf16[288,384]{1,0:T(8,128)(2,1)}, bf16[288,384]{1,0:T(8,128)(2,1)}, u32[]{:S(2)}, u32[]{:S(2)}) collective-permute-start(bf16[288,384]{1,0:T(8,128)(2,1)} %slice.20), channel_id=1, source_target_pairs={{0,16},{16,0},{1,17},{17,1},{2,18},{18,2},{3,19},{19,3},{4,20},{20... | collective-permute-start | bytes 663560 | tf_op jit(solution)/shard_map/ppermute | solution.py:343
  47.6 24.9 %collective-permute-start.10 = (bf16[384,384]{1,0:T(8,128)(2,1)}, bf16[384,384]{1,0:T(8,128)(2,1)S(1)}, u32[]{:S(2)}, u32[]{:S(2)}) collective-permute-start(bf16[384,384]{1,0:T(8,128)(2,1)} %get-tuple-element.79), channel_id=1, source_target_pairs={{0,4},{4,8},{8,12},{12,0},{1,5},{5,9},{9,13},{13,1},{2,6},{6,10},{... | collective-permute-start | bytes 884744 | tf_op jit(solution)/shard_map/ppermute | solution.py:343
  54.3 21.9 %collective-permute-start.13 = (bf16[384,384]{1,0:T(8,128)(2,1)}, bf16[384,384]{1,0:T(8,128)(2,1)S(1)}, u32[]{:S(2)}, u32[]{:S(2)}) collective-permute-start(bf16[384,384]{1,0:T(8,128)(2,1)} %get-tuple-element.86), channel_id=1, source_target_pairs={{0,8},{4,12},{8,0},{12,4},{1,9},{5,13},{9,1},{13,5},{2,10},{6,14},... | collective-permute-start | bytes 884744 | tf_op jit(solution)/shard_map/ppermute | solution.py:343
  56.7 19.5 %collective-permute-start.14 = (bf16[384,384]{1,0:T(8,128)(2,1)}, bf16[384,384]{1,0:T(8,128)(2,1)S(1)}, u32[]{:S(2)}, u32[]{:S(2)}) collective-permute-start(bf16[384,384]{1,0:T(8,128)(2,1)} %get-tuple-element.89), channel_id=1, source_target_pairs={{0,12},{4,0},{8,4},{12,8},{1,13},{5,1},{9,5},{13,9},{2,14},{6,2},{... | collective-permute-start | bytes 884744 | tf_op jit(solution)/shard_map/ppermute | solution.py:343
  72.5 25.9 %copy-start.2 = (bf16[384,384]{1,0:T(8,128)(2,1)}, bf16[384,384]{1,0:T(8,128)(2,1)S(1)}, u32[]{:S(2)}) copy-start(bf16[384,384]{1,0:T(8,128)(2,1)S(1)} %collective-permute-done.10.refs_2_) | copy-start | bytes 884740
  76.3 11.4 %collective-permute-start.17 = (bf16[288,384]{1,0:T(8,128)(2,1)S(1)}, bf16[288,384]{1,0:T(8,128)(2,1)S(1)}, u32[]{:S(2)}, u32[]{:S(2)}) collective-permute-start(bf16[288,384]{1,0:T(8,128)(2,1)S(1)} %slice.23), channel_id=1, source_target_pairs={{0,16},{16,0},{1,17},{17,1},{2,18},{18,2},{3,19},{19,3},{4,20},{20... | collective-permute-start | bytes 663560 | tf_op jit(solution)/shard_map/ppermute | solution.py:343
  77.8 36.2 %collective-permute-start.18 = (bf16[512,384]{1,0:T(8,128)(2,1)}, bf16[512,384]{1,0:T(8,128)(2,1)S(1)}, u32[]{:S(2)}, u32[]{:S(2)}) collective-permute-start(bf16[512,384]{1,0:T(8,128)(2,1)} %get-tuple-element.99.refs_0_), channel_id=1, source_target_pairs={{0,4},{4,8},{8,12},{12,0},{1,5},{5,9},{9,13},{13,1},{2,6},{6,10},{... | collective-permute-start | bytes 1179656 | tf_op jit(solution)/shard_map/ppermute | solution.py:343
  84.6 29.4 %collective-permute-start.19 = (bf16[512,384]{1,0:T(8,128)(2,1)}, bf16[512,384]{1,0:T(8,128)(2,1)S(1)}, u32[]{:S(2)}, u32[]{:S(2)}) collective-permute-start(bf16[512,384]{1,0:T(8,128)(2,1)} %get-tuple-element.99.refs_0_), channel_id=1, source_target_pairs={{0,8},{4,12},{8,0},{12,4},{1,9},{5,13},{9,1},{13,5},{2,10},{6,14},... | collective-permute-start | bytes 1179656 | tf_op jit(solution)/shard_map/ppermute | solution.py:343
  85.1 28.9 %collective-permute-start.20 = (bf16[512,384]{1,0:T(8,128)(2,1)}, bf16[512,384]{1,0:T(8,128)(2,1)S(1)}, u32[]{:S(2)}, u32[]{:S(2)}) collective-permute-start(bf16[512,384]{1,0:T(8,128)(2,1)} %get-tuple-element.99.refs_0_), channel_id=1, source_target_pairs={{0,12},{4,0},{8,4},{12,8},{1,13},{5,1},{9,5},{13,9},{2,14},{6,2},{... | collective-permute-start | bytes 1179656 | tf_op jit(solution)/shard_map/ppermute | solution.py:343
  87.0 8.4 %collective-permute-start.16 = (bf16[288,384]{1,0:T(8,128)(2,1)S(1)}, bf16[288,384]{1,0:T(8,128)(2,1)S(1)}, u32[]{:S(2)}, u32[]{:S(2)}) collective-permute-start(bf16[288,384]{1,0:T(8,128)(2,1)S(1)} %slice.22), channel_id=1, source_target_pairs={{0,16},{16,0},{1,17},{17,1},{2,18},{18,2},{3,19},{19,3},{4,20},{20... | collective-permute-start | bytes 663560 | tf_op jit(solution)/shard_map/ppermute | solution.py:343
  87.6 10.7 %collective-permute-start.15 = (bf16[288,384]{1,0:T(8,128)(2,1)S(1)}, bf16[288,384]{1,0:T(8,128)(2,1)S(1)}, u32[]{:S(2)}, u32[]{:S(2)}) collective-permute-start(bf16[288,384]{1,0:T(8,128)(2,1)S(1)} %slice.21), channel_id=1, source_target_pairs={{0,16},{16,0},{1,17},{17,1},{2,18},{18,2},{3,19},{19,3},{4,20},{20... | collective-permute-start | bytes 663560 | tf_op jit(solution)/shard_map/ppermute | solution.py:343
  110.4 37.1 %copy-start.9 = (bf16[512,384]{1,0:T(8,128)(2,1)S(1)}, bf16[512,384]{1,0:T(8,128)(2,1)}, u32[]{:S(2)}) copy-start(bf16[512,384]{1,0:T(8,128)(2,1)} %get-tuple-element.106.refs_0_) | copy-start | bytes 1179652
  110.4 44.0 %all-to-all-start = ((bf16[4,272,256]{2,1,0:T(8,128)(2,1)}), bf16[4,272,256]{2,1,0:T(8,128)(2,1)S(1)}, u32[]{:S(2)}, u32[]{:S(2)}) async-start(bf16[4,272,256]{2,1,0:T(8,128)(2,1)} %get-tuple-element.93), calls=%async_computation | async-start | bytes 1114112 | tf_op jit(solution)/shard_map/all_to_all | solution.py:438
  114.0 23.5 %copy-start.14 = (bf16[512,384]{1,0:T(8,128)(2,1)}, bf16[512,384]{1,0:T(8,128)(2,1)S(1)}, u32[]{:S(2)}) copy-start(bf16[512,384]{1,0:T(8,128)(2,1)S(1)} %collective-permute-done.18.refs_1_) | copy-start | bytes 1179652
  114.1 23.5 %copy-start.15 = (bf16[512,384]{1,0:T(8,128)(2,1)}, bf16[512,384]{1,0:T(8,128)(2,1)S(1)}, u32[]{:S(2)}) copy-start(bf16[512,384]{1,0:T(8,128)(2,1)S(1)} %collective-permute-done.19.refs_2_) | copy-start | bytes 1179652
  114.1 23.4 %copy-start.16 = (bf16[512,384]{1,0:T(8,128)(2,1)}, bf16[512,384]{1,0:T(8,128)(2,1)S(1)}, u32[]{:S(2)}) copy-start(bf16[512,384]{1,0:T(8,128)(2,1)S(1)} %collective-permute-done.20.refs_3_) | copy-start | bytes 1179652
  114.1 33.3 %collective-permute-start.21 = (bf16[512,384]{1,0:T(8,128)(2,1)}, bf16[512,384]{1,0:T(8,128)(2,1)S(1)}, u32[]{:S(2)}, u32[]{:S(2)}) collective-permute-start(bf16[512,384]{1,0:T(8,128)(2,1)} %get-tuple-element.106.refs_0_), channel_id=1, source_target_pairs={{0,8},{4,12},{8,0},{12,4},{1,9},{5,13},{9,1},{13,5},{2,10},{6,14},... | collective-permute-start | bytes 1179656 | tf_op jit(solution)/shard_map/ppermute | solution.py:430
  119.9 27.6 %collective-permute-start.22 = (bf16[512,384]{1,0:T(8,128)(2,1)}, bf16[512,384]{1,0:T(8,128)(2,1)S(1)}, u32[]{:S(2)}, u32[]{:S(2)}) collective-permute-start(bf16[512,384]{1,0:T(8,128)(2,1)} %get-tuple-element.106.refs_0_), channel_id=1, source_target_pairs={{0,4},{4,0},{8,12},{12,8},{1,5},{5,1},{9,13},{13,9},{2,6},{6,2},{1... | collective-permute-start | bytes 1179656 | tf_op jit(solution)/shard_map/ppermute | solution.py:431
  147.5 9.8 %collective-permute-start.23 = (bf16[512,384]{1,0:T(8,128)(2,1)S(1)}, bf16[512,384]{1,0:T(8,128)(2,1)S(1)}, u32[]{:S(2)}, u32[]{:S(2)}) collective-permute-start(bf16[512,384]{1,0:T(8,128)(2,1)S(1)} %copy-done.9), channel_id=1, source_target_pairs={{4,8},{8,4},{5,9},{9,5},{6,10},{10,6},{7,11},{11,7},{20,24},{24,20... | collective-permute-start | bytes 1179656 | tf_op jit(solution)/shard_map/ppermute | solution.py:434
  148.2 19.6 %collective-permute-start.24 = (bf16[512,384]{1,0:T(8,128)(2,1)S(1)}, bf16[512,384]{1,0:T(8,128)(2,1)S(1)}, u32[]{:S(2)}, u32[]{:S(2)}) collective-permute-start(bf16[512,384]{1,0:T(8,128)(2,1)S(1)} %collective-permute-done.21.refs_2_), channel_id=1, source_target_pairs={{8,12},{4,0},{9,13},{5,1},{10,14},{6,2},{11,15},{7,3},{24,28},{20,... | collective-permute-start | bytes 1179656 | tf_op jit(solution)/shard_map/ppermute | solution.py:435
  (18 other events, 156.4 us)

commit v7 on v6

--- a/solution.py
+++ b/solution.py
@@ -13,6 +13,7 @@
 CHUNK = 128
 TAIL = 16
 EXTRA = 96
+VMEM_LIMIT = 20 * 2**20
 FLOPS = (12_000_000_000, 1_000)
 HEAD_COLUMNS = 2 * DK + DV
 
@@ -347,6 +348,7 @@
         out_shape=shape((share, length), bf16),
         in_specs=[scalars, whole],
         out_specs=whole,
+        compiler_params=pltpu.CompilerParams(vmem_limit_bytes=VMEM_LIMIT),
         name="pack_tokens",
     )(where, tokens)
     sizes = [share + EXTRA] + [share // 2 + EXTRA] * (ctx - 1)
@@ -355,6 +357,7 @@
         out_shape=[shape((size, HEAD_COLUMNS), bf16) for size in sizes * 2],
         in_specs=[scalars] + [whole] * 6,
         out_specs=[whole] * (2 * ctx),
+        compiler_params=pltpu.CompilerParams(vmem_limit_bytes=VMEM_LIMIT),
         name="pack",
     )(where, w_query, w_key, w_value, log_decay, grad_out, beta_logit)
 
@@ -372,6 +375,7 @@
         out_shape=[shape((ctx, total, share), bf16), shape((share, total), bf16)],
         in_specs=[scalars] + [whole] * 4,
         out_specs=[whole] * 2,
+        compiler_params=pltpu.CompilerParams(vmem_limit_bytes=VMEM_LIMIT),
         name="unpack_tokens",
     )(where, *toks)
     swapped += [along(x[:half], "groups", 1) for x in first[1:]]
@@ -390,6 +394,7 @@
             ),
             out_shape=[shape((share, columns), f32)] * 3,
             input_output_aliases={2 + len(parts) + i: i for i in range(len(results))},
+            compiler_params=pltpu.CompilerParams(vmem_limit_bytes=VMEM_LIMIT),
             name=f"weight_gradient_{slot}_{steps[0]}",
         )(where, own, *parts, *results)
 
@@ -420,13 +425,14 @@
                 pltpu.VMEM((ctx, CHUNK, DK), bf16),
             ],
             cost_estimate=pl.CostEstimate(flops=FLOPS[slot], transcendentals=0, bytes_accessed=FLOPS[slot] // 1000),
+            compiler_params=pltpu.CompilerParams(vmem_limit_bytes=VMEM_LIMIT),
             name=f"head_{slot}",
         )(where, all_tokens, packed[slot * ctx], *direct, *swapped, *earlier)
         if slot == 0:
             hops = [along(grad, "ctx", d) for d in range(1, ctx)]
             grads.append([grad] + hops)
             continue
-        grad, grads[0] = after(grad, grads[0])
+        grad, grads[0][1:3] = after(grad, grads[0][1:3])
         two = lax.ppermute(grad, "ctx", [(0, 2), (1, 3), (2, 0), (3, 1)])
         pair = lax.ppermute(grad, "ctx", [(0, 1), (1, 0), (2, 3), (3, 2)])
         results = products(0, (0, 1, 2, 3), grads[0], ())
@@ -442,6 +448,7 @@
         out_shape=[shape((length, columns), bf16), shape((columns // DK, length), f32), shape((length, columns), f32)],
         in_specs=[whole],
         out_specs=[whole] * 3,
+        compiler_params=pltpu.CompilerParams(vmem_limit_bytes=VMEM_LIMIT),
         name="unpack",
     )(back)
     return (attn_out, *results, grad_beta, grad_decay)

time: 172 us -> 180 us (1.047)
  waiting for transfers between devices: 48 us -> 67 us
  Pallas kernels: 48.4 us -> 31.4 us
  starting transfers between devices: 69.4 us -> 72.2 us
  local copies, waits for them, and re-layouts: 5.16 us -> 7.78 us
    all_to_all x1, starting transfers between devices: 3.6 us -> 24.8 us  [head_split(): back = lax.all_to_all(back, 'ctx', 0, 0)]
    ppermute x1, starting transfers between devices: 17.6 us -> 1.12 us  [head_split(): pair = lax.ppermute(grad, 'ctx', [(0, 1), (1, 0), (2, 3), (3, 2)])]
    ppermute x21, waiting for transfers between devices: 33 us -> 45.8 us  [along(): return lax.ppermute(x, axis, [(i, (i + hop) % count) for i in range(count)])]
    ppermute x1, waiting for transfers between devices: 4.31 us -> 14.8 us  [head_split(): two = lax.ppermute(grad, 'ctx', [(0, 2), (1, 3), (2, 0), (3, 1)])]
    ppermute x1, starting transfers between devices: 5.78 us -> 0.01 us  [head_split(): two = lax.ppermute(grad, 'ctx', [(0, 2), (1, 3), (2, 0), (3, 1)])]
    pallas_call x3, Pallas kernels: 13.8 us -> 9.23 us  [products(): pl.pallas_call(functools.partial(weight_gradient_kernel, steps, slot == 1...]
    pallas_call x2, Pallas kernels: 22.6 us -> 18.1 us  [head_split(): pl.pallas_call(functools.partial(head_kernel, ctx, slot), out_shape=[shap...]
    ppermute x1, waiting for transfers between devices: 10.6 us -> 6.33 us  [head_split(): far = lax.ppermute(two, 'ctx', [(2, 3), (1, 0)])]
  transfers between devices with their start and end apart: 26 -> 26, of which waited for: 9 -> 10; matrix products, arithmetic and copies ran while one was open for 0% -> 0% of each run, Pallas kernels for 25% -> 16%
where the time goes in v7:
time: 180 us; the launch traced here: 179 us
  starting transfers between devices  72.2 us (40%)
  waiting for transfers between devices  67 us (37%)
  Pallas kernels  31.4 us (17%)
  local copies, waits for them, and re-layouts  7.78 us (4%)
    ppermute x21, waiting for transfers between devices, along(): return lax.ppermute(x, axis, [(i, (i + hop) % count) for i in range(count)])  45.8 us
    ppermute x21, starting transfers between devices, along(): return lax.ppermute(x, axis, [(i, (i + hop) % count) for i in range(count)])  44.3 us
    all_to_all x1, starting transfers between devices, head_split(): back = lax.all_to_all(back, 'ctx', 0, 0)  24.8 us
    pallas_call x2, Pallas kernels, head_split(): pl.pallas_call(functools.partial(head_kernel, ctx, slot), out_shape=[shap...  18.1 us
    ppermute x1, waiting for transfers between devices, head_split(): two = lax.ppermute(grad, 'ctx', [(0, 2), (1, 3), (2, 0), (3, 1)])  14.8 us
    pallas_call x3, Pallas kernels, products(): pl.pallas_call(functools.partial(weight_gradient_kernel, steps, slot == 1...  9.23 us
    unnamed x14, local copies, waits for them, and re-layouts  7.55 us
    ppermute x1, waiting for transfers between devices, head_split(): far = lax.ppermute(two, 'ctx', [(2, 3), (1, 0)])  6.33 us
  transfers between devices with their start and end apart: 26, of which 10 were waited for; matrix products, arithmetic and copies ran while one was open for 0% of the time, Pallas kernels for 16%

profile of v7, /device:TPU:0, one launch (start us, length us, event | category | flops | bytes accessed | tf_op | source)
XLA Modules:
  0.0 179.2 jit_solution(16322067551337766163)
XLA Ops:
  2.5 3.1 %collective-permute-start = (bf16[576,128]{1,0:T(8,128)(2,1)S(1)}, bf16[576,128]{1,0:T(8,128)(2,1)S(1)}, u32[]{:S(2)}, u32[]{:S(2)}) collective-permute-start(bf16[576,128]{1,0:T(8,128)(2,1)S(1)} %pack_tokens.1), channel_id=1, source_target_pairs={{0,4},{4,8},{8,12},{12,0},{1,5},{5,9},{9,13},{13,1},{2,6},{6,10},{... | collective-permute-start | bytes 442376 | tf_op jit(solution)/shard_map/ppermute | solution.py:344
  5.5 2.6 %collective-permute-start.1 = (bf16[576,128]{1,0:T(8,128)(2,1)S(1)}, bf16[576,128]{1,0:T(8,128)(2,1)S(1)}, u32[]{:S(2)}, u32[]{:S(2)}) collective-permute-start(bf16[576,128]{1,0:T(8,128)(2,1)S(1)} %pack_tokens.1), channel_id=1, source_target_pairs={{0,8},{4,12},{8,0},{12,4},{1,9},{5,13},{9,1},{13,5},{2,10},{6,14},... | collective-permute-start | bytes 442376 | tf_op jit(solution)/shard_map/ppermute | solution.py:344
  8.1 1.3 collective-permute-start.2
  9.5 1.3 copy-done
  18.0 1.6 collective-permute-start.3
  19.5 3.6 %collective-permute-start.6 = (bf16[384,384]{1,0:T(8,128)(2,1)S(1)}, bf16[384,384]{1,0:T(8,128)(2,1)S(1)}, u32[]{:S(2)}, u32[]{:S(2)}) collective-permute-start(bf16[384,384]{1,0:T(8,128)(2,1)S(1)} %get-tuple-element.67), channel_id=1, source_target_pairs={{0,4},{4,8},{8,12},{12,0},{1,5},{5,9},{9,13},{13,1},{2,6},{6,10},{... | collective-permute-start | bytes 884744 | tf_op jit(solution)/shard_map/ppermute | solution.py:344
  23.1 1.6 collective-permute-start.4
  25.5 6.8 %collective-permute-done.6.refs_2_ = bf16[384,384]{1,0:T(8,128)(2,1)S(1)} collective-permute-done((bf16[384,384]{1,0:T(8,128)(2,1)S(1)}, bf16[384,384]{1,0:T(8,128)(2,1)S(1)}, u32[]{:S(2)}, u32[]{:S(2)}) %collective-permute-start.6) | collective-permute-done | bytes 294944 | tf_op jit(solution)/shard_map/ppermute | solution.py:344
  32.3 1.6 collective-permute-start.7
  33.9 9.1 %collective-permute-done.4.refs_3_ = bf16[384,384]{1,0:T(8,128)(2,1)S(1)} collective-permute-done((bf16[384,384]{1,0:T(8,128)(2,1)S(1)}, bf16[384,384]{1,0:T(8,128)(2,1)S(1)}, u32[]{:S(2)}, u32[]{:S(2)}) %collective-permute-start.4) | collective-permute-done | bytes 294944 | tf_op jit(solution)/shard_map/ppermute | solution.py:344
  43.6 1.6 collective-permute-start.11
  45.7 6.7 %collective-permute-start.10 = (bf16[384,384]{1,0:T(8,128)(2,1)S(1)}, bf16[384,384]{1,0:T(8,128)(2,1)S(1)}, u32[]{:S(2)}, u32[]{:S(2)}) collective-permute-start(bf16[384,384]{1,0:T(8,128)(2,1)S(1)} %get-tuple-element.77), channel_id=1, source_target_pairs={{0,4},{4,8},{8,12},{12,0},{1,5},{5,9},{9,13},{13,1},{2,6},{6,10},{... | collective-permute-start | bytes 884744 | tf_op jit(solution)/shard_map/ppermute | solution.py:344
  52.5 2.3 %collective-permute-start.13 = (bf16[384,384]{1,0:T(8,128)(2,1)S(1)}, bf16[384,384]{1,0:T(8,128)(2,1)S(1)}, u32[]{:S(2)}, u32[]{:S(2)}) collective-permute-start(bf16[384,384]{1,0:T(8,128)(2,1)S(1)} %get-tuple-element.84), channel_id=1, source_target_pairs={{0,8},{4,12},{8,0},{12,4},{1,9},{5,13},{9,1},{13,5},{2,10},{6,14},... | collective-permute-start | bytes 884744 | tf_op jit(solution)/shard_map/ppermute | solution.py:344
  54.8 1.3 unpack_tokens.1
  56.1 8.6 %head_0.1 = (bf16[512,384]{1,0:T(8,128)(2,1)S(1)}, bf16[4,272,128]{2,1,0:T(8,128)(2,1)S(1)}) custom-call(s32[15]{0:T(128)S(1)} %stack.61.where_ref, bf16[4,512,576]{2,1,0:T(8,128)(2,1)S(1)} %get-tuple-element.70.refs_0_, bf16[672,384]{1,0:T(8,128)(2,1)S(1)} %get-tuple-element.78.refs_1_, bf16[384,384]{1,0:T(8,128)(2,1)S(1)} %collective-permute-done.6.refs_2_, ...), custom_call_target="tpu_custom_call" | custom-call | flops 12000000000 | bytes 12000000 | tf_op jit(solution)/shard_map/head_0/pallas_call | solution.py:409
  64.8 6.6 %collective-permute-start.18 = (bf16[512,384]{1,0:T(8,128)(2,1)S(1)}, bf16[512,384]{1,0:T(8,128)(2,1)S(1)}, u32[]{:S(2)}, u32[]{:S(2)}) collective-permute-start(bf16[512,384]{1,0:T(8,128)(2,1)S(1)} %get-tuple-element.95.refs_0_), channel_id=1, source_target_pairs={{0,4},{4,8},{8,12},{12,0},{1,5},{5,9},{9,13},{13,1},{2,6},{6,10},{... | collective-permute-start | bytes 1179656 | tf_op jit(solution)/shard_map/ppermute | solution.py:344
  71.4 2.3 %collective-permute-start.19 = (bf16[512,384]{1,0:T(8,128)(2,1)S(1)}, bf16[512,384]{1,0:T(8,128)(2,1)S(1)}, u32[]{:S(2)}, u32[]{:S(2)}) collective-permute-start(bf16[512,384]{1,0:T(8,128)(2,1)S(1)} %get-tuple-element.95.refs_0_), channel_id=1, source_target_pairs={{0,8},{4,12},{8,0},{12,4},{1,9},{5,13},{9,1},{13,5},{2,10},{6,14},... | collective-permute-start | bytes 1179656 | tf_op jit(solution)/shard_map/ppermute | solution.py:344
  74.1 1.5 collective-permute-start.17
  76.3 1.5 collective-permute-start.15
  77.8 4.7 %collective-permute-done.17.refs_7_ = bf16[288,384]{1,0:T(8,128)(2,1)S(1)} collective-permute-done((bf16[288,384]{1,0:T(8,128)(2,1)S(1)}, bf16[288,384]{1,0:T(8,128)(2,1)S(1)}, u32[]{:S(2)}, u32[]{:S(2)}) %collective-permute-start.17) | collective-permute-done | bytes 221216 | tf_op jit(solution)/shard_map/ppermute | solution.py:344
  82.5 4.7 %collective-permute-done.16.refs_6_ = bf16[288,384]{1,0:T(8,128)(2,1)S(1)} collective-permute-done((bf16[288,384]{1,0:T(8,128)(2,1)S(1)}, bf16[288,384]{1,0:T(8,128)(2,1)S(1)}, u32[]{:S(2)}, u32[]{:S(2)}) %collective-permute-start.16) | collective-permute-done | bytes 221216 | tf_op jit(solution)/shard_map/ppermute | solution.py:344
  87.2 3.5 %collective-permute-done.15.refs_5_ = bf16[288,384]{1,0:T(8,128)(2,1)S(1)} collective-permute-done((bf16[288,384]{1,0:T(8,128)(2,1)S(1)}, bf16[288,384]{1,0:T(8,128)(2,1)S(1)}, u32[]{:S(2)}, u32[]{:S(2)}) %collective-permute-start.15) | collective-permute-done | bytes 221216 | tf_op jit(solution)/shard_map/ppermute | solution.py:344
  90.7 9.4 %head_1.1 = (bf16[512,384]{1,0:T(8,128)(2,1)S(1)}, bf16[4,272,256]{2,1,0:T(8,128)(2,1)}) custom-call(s32[15]{0:T(128)S(1)} %stack.61.where_ref, bf16[4,512,576]{2,1,0:T(8,128)(2,1)S(1)} %get-tuple-element.70.refs_0_, bf16[672,384]{1,0:T(8,128)(2,1)S(1)} %get-tuple-element.71.refs_1_, bf16[384,384]{1,0:T(8,128)(2,1)S(1)} %collective-permute-done.10.refs_2_, ...), custom_call_target="tpu_custom_call" | custom-call | flops 1000 | bytes 1 | tf_op jit(solution)/shard_map/head_1/pallas_call | solution.py:409
  100.2 24.8 %all-to-all-start = ((bf16[4,272,256]{2,1,0:T(8,128)(2,1)}), bf16[4,272,256]{2,1,0:T(8,128)(2,1)S(1)}, u32[]{:S(2)}, u32[]{:S(2)}) async-start(bf16[4,272,256]{2,1,0:T(8,128)(2,1)} %get-tuple-element.91), calls=%async_computation | async-start | bytes 1114112 | tf_op jit(solution)/shard_map/all_to_all | solution.py:444
  125.0 3.8 %collective-permute-start.22 = (bf16[512,384]{1,0:T(8,128)(2,1)S(1)}, bf16[512,384]{1,0:T(8,128)(2,1)S(1)}, u32[]{:S(2)}, u32[]{:S(2)}) collective-permute-start(bf16[512,384]{1,0:T(8,128)(2,1)S(1)} %get-tuple-element.95.refs_0_), channel_id=1, source_target_pairs={{0,12},{4,0},{8,4},{12,8},{1,13},{5,1},{9,5},{13,9},{2,14},{6,2},{... | collective-permute-start | bytes 1179656 | tf_op jit(solution)/shard_map/ppermute | solution.py:344
  129.9 16.0 %collective-permute-done.22.refs_3_ = bf16[512,384]{1,0:T(8,128)(2,1)S(1)} collective-permute-done((bf16[512,384]{1,0:T(8,128)(2,1)S(1)}, bf16[512,384]{1,0:T(8,128)(2,1)S(1)}, u32[]{:S(2)}, u32[]{:S(2)}) %collective-permute-start.22) | collective-permute-done | bytes 393248 | tf_op jit(solution)/shard_map/ppermute | solution.py:344
  145.9 3.9 %weight_gradient_0_0.1 = (f32[576,1024]{1,0:T(8,128)}, f32[576,1024]{1,0:T(8,128)}, f32[576,1024]{1,0:T(8,128)}) custom-call(s32[15]{0:T(128)S(1)} %stack.61.where_ref, bf16[576,512]{1,0:T(8,128)(2,1)S(1)} %get-tuple-element.93.own_ref, bf16[512,384]{1,0:T(8,128)(2,1)S(1)} %get-tuple-element.95.refs_0_, ...), custom_call_target="tpu_custom_call" | custom-call | tf_op jit(solution)/shard_map/weight_gradient_0_0/pallas_call | solution.py:387
  149.8 14.8 %collective-permute-done.20.refs_2_ = bf16[512,384]{1,0:T(8,128)(2,1)S(1)} collective-permute-done((bf16[512,384]{1,0:T(8,128)(2,1)S(1)}, bf16[512,384]{1,0:T(8,128)(2,1)S(1)}, u32[]{:S(2)}, u32[]{:S(2)}) %collective-permute-start.20) | collective-permute-done | bytes 393248 | tf_op jit(solution)/shard_map/ppermute | solution.py:436
  165.3 1.3 collective-permute-start.24
  166.6 3.4 %weight_gradient_1_0.1 = (f32[576,1024]{1,0:T(8,128)}, f32[576,1024]{1,0:T(8,128)}, f32[576,1024]{1,0:T(8,128)}) custom-call(s32[15]{0:T(128)S(1)} %stack.61.where_ref, bf16[576,512]{1,0:T(8,128)(2,1)S(1)} %get-tuple-element.93.own_ref, bf16[512,384]{1,0:T(8,128)(2,1)S(1)} %get-tuple-element.102.refs_0_, ...), custom_call_target="tpu_custom_call", output_to_operand_aliasing={{0}: (5, {}), {1}: (6, {}), {2}: (7, {})} | custom-call | tf_op jit(solution)/shard_map/weight_gradient_1_0/pallas_call | solution.py:387
  171.0 6.3 %collective-permute-done.24.refs_1_ = bf16[512,384]{1,0:T(8,128)(2,1)S(1)} collective-permute-done((bf16[512,384]{1,0:T(8,128)(2,1)S(1)}, bf16[512,384]{1,0:T(8,128)(2,1)S(1)}, u32[]{:S(2)}, u32[]{:S(2)}) %collective-permute-start.24) | collective-permute-done | bytes 393248 | tf_op jit(solution)/shard_map/ppermute | solution.py:441
  177.3 1.9 %weight_gradient_1_3.1 = (f32[576,1024]{1,0:T(8,128)}, f32[576,1024]{1,0:T(8,128)}, f32[576,1024]{1,0:T(8,128)}) custom-call(s32[15]{0:T(128)S(1)} %stack.61.where_ref, bf16[576,512]{1,0:T(8,128)(2,1)S(1)} %get-tuple-element.93.own_ref, ...), custom_call_target="tpu_custom_call", output_to_operand_aliasing={{0}: (4, {}), {1}: (5, {}), {2}: (6, {})} | custom-call | tf_op jit(solution)/shard_map/weight_gradient_1_3/pallas_call | solution.py:387
  (51 shorter events, 14.9 us)
Async XLA Ops:
  0.8 1.1 copy-start.3
  2.5 14.8 %collective-permute-start = (bf16[576,128]{1,0:T(8,128)(2,1)S(1)}, bf16[576,128]{1,0:T(8,128)(2,1)S(1)}, u32[]{:S(2)}, u32[]{:S(2)}) collective-permute-start(bf16[576,128]{1,0:T(8,128)(2,1)S(1)} %pack_tokens.1), channel_id=1, source_target_pairs={{0,4},{4,8},{8,12},{12,0},{1,5},{5,9},{9,13},{13,1},{2,6},{6,10},{... | collective-permute-start | bytes 442376 | tf_op jit(solution)/shard_map/ppermute | solution.py:344
  5.5 12.4 %collective-permute-start.1 = (bf16[576,128]{1,0:T(8,128)(2,1)S(1)}, bf16[576,128]{1,0:T(8,128)(2,1)S(1)}, u32[]{:S(2)}, u32[]{:S(2)}) collective-permute-start(bf16[576,128]{1,0:T(8,128)(2,1)S(1)} %pack_tokens.1), channel_id=1, source_target_pairs={{0,8},{4,12},{8,0},{12,4},{1,9},{5,13},{9,1},{13,5},{2,10},{6,14},... | collective-permute-start | bytes 442376 | tf_op jit(solution)/shard_map/ppermute | solution.py:344
  8.1 9.8 %collective-permute-start.2 = (bf16[576,128]{1,0:T(8,128)(2,1)S(1)}, bf16[576,128]{1,0:T(8,128)(2,1)S(1)}, u32[]{:S(2)}, u32[]{:S(2)}) collective-permute-start(bf16[576,128]{1,0:T(8,128)(2,1)S(1)} %pack_tokens.1), channel_id=1, source_target_pairs={{0,12},{4,0},{8,4},{12,8},{1,13},{5,1},{9,5},{13,9},{2,14},{6,2},{... | collective-permute-start | bytes 442376 | tf_op jit(solution)/shard_map/ppermute | solution.py:344
  9.5 1.3 copy-start
  10.7 1.3 copy-start.1
  12.0 1.3 copy-start.2
  13.3 1.0 copy-start.4
  14.3 0.9 copy-start.5
  18.0 25.0 %collective-permute-start.3 = (bf16[2304,128]{1,0:T(8,128)(2,1)S(1)}, bf16[2304,128]{1,0:T(8,128)(2,1)S(1)}, u32[]{:S(2)}, u32[]{:S(2)}) collective-permute-start(bf16[2304,128]{1,0:T(8,128)(2,1)S(1)} %pad_maximum_fusion.refs_0_), channel_id=1, source_target_pairs={{0,2},{2,0},{1,3},{3,1},{4,6},{6,4},{5,7},{7,5},{8,10},{10,8},{9,1... | collective-permute-start | bytes 1769480 | tf_op jit(solution)/shard_map/ppermute | solution.py:344
  19.5 12.8 %collective-permute-start.6 = (bf16[384,384]{1,0:T(8,128)(2,1)S(1)}, bf16[384,384]{1,0:T(8,128)(2,1)S(1)}, u32[]{:S(2)}, u32[]{:S(2)}) collective-permute-start(bf16[384,384]{1,0:T(8,128)(2,1)S(1)} %get-tuple-element.67), channel_id=1, source_target_pairs={{0,4},{4,8},{8,12},{12,0},{1,5},{5,9},{9,13},{13,1},{2,6},{6,10},{... | collective-permute-start | bytes 884744 | tf_op jit(solution)/shard_map/ppermute | solution.py:344
  23.1 19.8 %collective-permute-start.4 = (bf16[384,384]{1,0:T(8,128)(2,1)S(1)}, bf16[384,384]{1,0:T(8,128)(2,1)S(1)}, u32[]{:S(2)}, u32[]{:S(2)}) collective-permute-start(bf16[384,384]{1,0:T(8,128)(2,1)S(1)} %get-tuple-element.65), channel_id=1, source_target_pairs={{0,8},{4,12},{8,0},{12,4},{1,9},{5,13},{9,1},{13,5},{2,10},{6,14},... | collective-permute-start | bytes 884744 | tf_op jit(solution)/shard_map/ppermute | solution.py:344
  24.8 18.2 %collective-permute-start.5 = (bf16[384,384]{1,0:T(8,128)(2,1)S(1)}, bf16[384,384]{1,0:T(8,128)(2,1)S(1)}, u32[]{:S(2)}, u32[]{:S(2)}) collective-permute-start(bf16[384,384]{1,0:T(8,128)(2,1)S(1)} %get-tuple-element.66), channel_id=1, source_target_pairs={{0,12},{4,0},{8,4},{12,8},{1,13},{5,1},{9,5},{13,9},{2,14},{6,2},{... | collective-permute-start | bytes 884744 | tf_op jit(solution)/shard_map/ppermute | solution.py:344
  32.3 10.6 %collective-permute-start.7 = (bf16[288,384]{1,0:T(8,128)(2,1)S(1)}, bf16[288,384]{1,0:T(8,128)(2,1)S(1)}, u32[]{:S(2)}, u32[]{:S(2)}) collective-permute-start(bf16[288,384]{1,0:T(8,128)(2,1)S(1)} %slice.24), channel_id=1, source_target_pairs={{0,16},{16,0},{1,17},{17,1},{2,18},{18,2},{3,19},{19,3},{4,20},{20... | collective-permute-start | bytes 663560 | tf_op jit(solution)/shard_map/ppermute | solution.py:344
  42.9 9.5 %collective-permute-start.8 = (bf16[2304,128]{1,0:T(8,128)(2,1)S(1)}, bf16[2304,128]{1,0:T(8,128)(2,1)S(1)}, u32[]{:S(2)}, u32[]{:S(2)}) collective-permute-start(bf16[2304,128]{1,0:T(8,128)(2,1)S(1)} %pad_maximum_fusion.refs_0_), channel_id=1, source_target_pairs={{0,1},{1,0},{2,3},{3,2},{4,5},{5,4},{6,7},{7,6},{8,9},{9,8},{10,11... | collective-permute-start | bytes 1769480 | tf_op jit(solution)/shard_map/ppermute | solution.py:344
  43.0 11.7 %collective-permute-start.9 = (bf16[2304,128]{1,0:T(8,128)(2,1)S(1)}, bf16[2304,128]{1,0:T(8,128)(2,1)S(1)}, u32[]{:S(2)}, u32[]{:S(2)}) collective-permute-start(bf16[2304,128]{1,0:T(8,128)(2,1)S(1)} %collective-permute-done.3.refs_1_), channel_id=1, source_target_pairs={{0,1},{1,0},{2,3},{3,2},{4,5},{5,4},{6,7},{7,6},{8,9},{9,8},{10,11... | collective-permute-start | bytes 1769480 | tf_op jit(solution)/shard_map/ppermute | solution.py:344
  43.6 12.6 %collective-permute-start.11 = (bf16[288,384]{1,0:T(8,128)(2,1)S(1)}, bf16[288,384]{1,0:T(8,128)(2,1)S(1)}, u32[]{:S(2)}, u32[]{:S(2)}) collective-permute-start(bf16[288,384]{1,0:T(8,128)(2,1)S(1)} %slice.19), channel_id=1, source_target_pairs={{0,16},{16,0},{1,17},{17,1},{2,18},{18,2},{3,19},{19,3},{4,20},{20... | collective-permute-start | bytes 663560 | tf_op jit(solution)/shard_map/ppermute | solution.py:344
  45.2 11.0 %collective-permute-start.12 = (bf16[288,384]{1,0:T(8,128)(2,1)S(1)}, bf16[288,384]{1,0:T(8,128)(2,1)S(1)}, u32[]{:S(2)}, u32[]{:S(2)}) collective-permute-start(bf16[288,384]{1,0:T(8,128)(2,1)S(1)} %slice.20), channel_id=1, source_target_pairs={{0,16},{16,0},{1,17},{17,1},{2,18},{18,2},{3,19},{19,3},{4,20},{20... | collective-permute-start | bytes 663560 | tf_op jit(solution)/shard_map/ppermute | solution.py:344
  45.7 27.9 %collective-permute-start.10 = (bf16[384,384]{1,0:T(8,128)(2,1)S(1)}, bf16[384,384]{1,0:T(8,128)(2,1)S(1)}, u32[]{:S(2)}, u32[]{:S(2)}) collective-permute-start(bf16[384,384]{1,0:T(8,128)(2,1)S(1)} %get-tuple-element.77), channel_id=1, source_target_pairs={{0,4},{4,8},{8,12},{12,0},{1,5},{5,9},{9,13},{13,1},{2,6},{6,10},{... | collective-permute-start | bytes 884744 | tf_op jit(solution)/shard_map/ppermute | solution.py:344
  52.5 21.6 %collective-permute-start.13 = (bf16[384,384]{1,0:T(8,128)(2,1)S(1)}, bf16[384,384]{1,0:T(8,128)(2,1)S(1)}, u32[]{:S(2)}, u32[]{:S(2)}) collective-permute-start(bf16[384,384]{1,0:T(8,128)(2,1)S(1)} %get-tuple-element.84), channel_id=1, source_target_pairs={{0,8},{4,12},{8,0},{12,4},{1,9},{5,13},{9,1},{13,5},{2,10},{6,14},... | collective-permute-start | bytes 884744 | tf_op jit(solution)/shard_map/ppermute | solution.py:344
  54.7 19.3 %collective-permute-start.14 = (bf16[384,384]{1,0:T(8,128)(2,1)S(1)}, bf16[384,384]{1,0:T(8,128)(2,1)S(1)}, u32[]{:S(2)}, u32[]{:S(2)}) collective-permute-start(bf16[384,384]{1,0:T(8,128)(2,1)S(1)} %get-tuple-element.87), channel_id=1, source_target_pairs={{0,12},{4,0},{8,4},{12,8},{1,13},{5,1},{9,5},{13,9},{2,14},{6,2},{... | collective-permute-start | bytes 884744 | tf_op jit(solution)/shard_map/ppermute | solution.py:344
  64.8 64.0 %collective-permute-start.18 = (bf16[512,384]{1,0:T(8,128)(2,1)S(1)}, bf16[512,384]{1,0:T(8,128)(2,1)S(1)}, u32[]{:S(2)}, u32[]{:S(2)}) collective-permute-start(bf16[512,384]{1,0:T(8,128)(2,1)S(1)} %get-tuple-element.95.refs_0_), channel_id=1, source_target_pairs={{0,4},{4,8},{8,12},{12,0},{1,5},{5,9},{9,13},{13,1},{2,6},{6,10},{... | collective-permute-start | bytes 1179656 | tf_op jit(solution)/shard_map/ppermute | solution.py:344
  71.4 57.4 %collective-permute-start.19 = (bf16[512,384]{1,0:T(8,128)(2,1)S(1)}, bf16[512,384]{1,0:T(8,128)(2,1)S(1)}, u32[]{:S(2)}, u32[]{:S(2)}) collective-permute-start(bf16[512,384]{1,0:T(8,128)(2,1)S(1)} %get-tuple-element.95.refs_0_), channel_id=1, source_target_pairs={{0,8},{4,12},{8,0},{12,4},{1,9},{5,13},{9,1},{13,5},{2,10},{6,14},... | collective-permute-start | bytes 1179656 | tf_op jit(solution)/shard_map/ppermute | solution.py:344
  74.1 8.4 %collective-permute-start.17 = (bf16[288,384]{1,0:T(8,128)(2,1)S(1)}, bf16[288,384]{1,0:T(8,128)(2,1)S(1)}, u32[]{:S(2)}, u32[]{:S(2)}) collective-permute-start(bf16[288,384]{1,0:T(8,128)(2,1)S(1)} %slice.23), channel_id=1, source_target_pairs={{0,16},{16,0},{1,17},{17,1},{2,18},{18,2},{3,19},{19,3},{4,20},{20... | collective-permute-start | bytes 663560 | tf_op jit(solution)/shard_map/ppermute | solution.py:344
  75.6 11.6 %collective-permute-start.16 = (bf16[288,384]{1,0:T(8,128)(2,1)S(1)}, bf16[288,384]{1,0:T(8,128)(2,1)S(1)}, u32[]{:S(2)}, u32[]{:S(2)}) collective-permute-start(bf16[288,384]{1,0:T(8,128)(2,1)S(1)} %slice.22), channel_id=1, source_target_pairs={{0,16},{16,0},{1,17},{17,1},{2,18},{18,2},{3,19},{19,3},{4,20},{20... | collective-permute-start | bytes 663560 | tf_op jit(solution)/shard_map/ppermute | solution.py:344
  76.3 14.4 %collective-permute-start.15 = (bf16[288,384]{1,0:T(8,128)(2,1)S(1)}, bf16[288,384]{1,0:T(8,128)(2,1)S(1)}, u32[]{:S(2)}, u32[]{:S(2)}) collective-permute-start(bf16[288,384]{1,0:T(8,128)(2,1)S(1)} %slice.21), channel_id=1, source_target_pairs={{0,16},{16,0},{1,17},{17,1},{2,18},{18,2},{3,19},{19,3},{4,20},{20... | collective-permute-start | bytes 663560 | tf_op jit(solution)/shard_map/ppermute | solution.py:344
  100.2 69.9 %all-to-all-start = ((bf16[4,272,256]{2,1,0:T(8,128)(2,1)}), bf16[4,272,256]{2,1,0:T(8,128)(2,1)S(1)}, u32[]{:S(2)}, u32[]{:S(2)}) async-start(bf16[4,272,256]{2,1,0:T(8,128)(2,1)} %get-tuple-element.91), calls=%async_computation | async-start | bytes 1114112 | tf_op jit(solution)/shard_map/all_to_all | solution.py:444
  125.0 21.0 %collective-permute-start.22 = (bf16[512,384]{1,0:T(8,128)(2,1)S(1)}, bf16[512,384]{1,0:T(8,128)(2,1)S(1)}, u32[]{:S(2)}, u32[]{:S(2)}) collective-permute-start(bf16[512,384]{1,0:T(8,128)(2,1)S(1)} %get-tuple-element.95.refs_0_), channel_id=1, source_target_pairs={{0,12},{4,0},{8,4},{12,8},{1,13},{5,1},{9,5},{13,9},{2,14},{6,2},{... | collective-permute-start | bytes 1179656 | tf_op jit(solution)/shard_map/ppermute | solution.py:344
  128.8 35.9 %collective-permute-start.20 = (bf16[512,384]{1,0:T(8,128)(2,1)S(1)}, bf16[512,384]{1,0:T(8,128)(2,1)S(1)}, u32[]{:S(2)}, u32[]{:S(2)}) collective-permute-start(bf16[512,384]{1,0:T(8,128)(2,1)S(1)} %get-tuple-element.102.refs_0_), channel_id=1, source_target_pairs={{0,8},{4,12},{8,0},{12,4},{1,9},{5,13},{9,1},{13,5},{2,10},{6,14},... | collective-permute-start | bytes 1179656 | tf_op jit(solution)/shard_map/ppermute | solution.py:436
  128.8 35.9 %collective-permute-start.21 = (bf16[512,384]{1,0:T(8,128)(2,1)S(1)}, bf16[512,384]{1,0:T(8,128)(2,1)S(1)}, u32[]{:S(2)}, u32[]{:S(2)}) collective-permute-start(bf16[512,384]{1,0:T(8,128)(2,1)S(1)} %get-tuple-element.102.refs_0_), channel_id=1, source_target_pairs={{0,4},{4,0},{8,12},{12,8},{1,5},{5,1},{9,13},{13,9},{2,6},{6,2},{1... | collective-permute-start | bytes 1179656 | tf_op jit(solution)/shard_map/ppermute | solution.py:437
  164.7 6.3 %collective-permute-start.23 = (bf16[512,384]{1,0:T(8,128)(2,1)S(1)}, bf16[512,384]{1,0:T(8,128)(2,1)S(1)}, u32[]{:S(2)}, u32[]{:S(2)}) collective-permute-start(bf16[512,384]{1,0:T(8,128)(2,1)S(1)} %get-tuple-element.102.refs_0_), channel_id=1, source_target_pairs={{4,8},{8,4},{5,9},{9,5},{6,10},{10,6},{7,11},{11,7},{20,24},{24,20... | collective-permute-start | bytes 1179656 | tf_op jit(solution)/shard_map/ppermute | solution.py:440
  165.3 12.0 %collective-permute-start.24 = (bf16[512,384]{1,0:T(8,128)(2,1)S(1)}, bf16[512,384]{1,0:T(8,128)(2,1)S(1)}, u32[]{:S(2)}, u32[]{:S(2)}) collective-permute-start(bf16[512,384]{1,0:T(8,128)(2,1)S(1)} %collective-permute-done.20.refs_2_), channel_id=1, source_target_pairs={{8,12},{4,0},{9,13},{5,1},{10,14},{6,2},{11,15},{7,3},{24,28},{20,... | collective-permute-start | bytes 1179656 | tf_op jit(solution)/shard_map/ppermute | solution.py:441
  (1 other events, 0.7 us)

commit v8 on v7

--- a/solution.py
+++ b/solution.py
@@ -14,7 +14,7 @@
 TAIL = 16
 EXTRA = 96
 VMEM_LIMIT = 20 * 2**20
-FLOPS = (12_000_000_000, 1_000)
+FLOPS = (12_000_000_000, 12_000_000_000)
 HEAD_COLUMNS = 2 * DK + DV
 
 epsilon = 1e-06
@@ -432,7 +432,7 @@
             hops = [along(grad, "ctx", d) for d in range(1, ctx)]
             grads.append([grad] + hops)
             continue
-        grad, grads[0][1:3] = after(grad, grads[0][1:3])
+        grad, grads[0] = after(grad, grads[0])
         two = lax.ppermute(grad, "ctx", [(0, 2), (1, 3), (2, 0), (3, 1)])
         pair = lax.ppermute(grad, "ctx", [(0, 1), (1, 0), (2, 3), (3, 2)])
         results = products(0, (0, 1, 2, 3), grads[0], ())

time: 180 us -> 164 us (0.911)
  waiting for transfers between devices: 67 us -> 43.1 us
  starting transfers between devices: 72.2 us -> 80 us
    ppermute x21, waiting for transfers between devices: 45.8 us -> 28.9 us  [along(): return lax.ppermute(x, axis, [(i, (i + hop) % count) for i in range(count)])]
    all_to_all x1, starting transfers between devices: 24.8 us -> 8.14 us  [head_split(): back = lax.all_to_all(back, 'ctx', 0, 0)]
    ppermute x1, starting transfers between devices: 1.12 us -> 14.4 us  [head_split(): pair = lax.ppermute(grad, 'ctx', [(0, 1), (1, 0), (2, 3), (3, 2)])]
    ppermute x1, starting transfers between devices: 0.01 us -> 12.4 us  [head_split(): two = lax.ppermute(grad, 'ctx', [(0, 2), (1, 3), (2, 0), (3, 1)])]
    ppermute x1, waiting for transfers between devices: 14.8 us -> 4.97 us  [head_split(): two = lax.ppermute(grad, 'ctx', [(0, 2), (1, 3), (2, 0), (3, 1)])]
    ppermute x1, waiting for transfers between devices: 6.33 us -> 8.88 us  [head_split(): far = lax.ppermute(two, 'ctx', [(2, 3), (1, 0)])]
  transfers between devices with their start and end apart: 26 -> 26, of which waited for: 10 -> 10; matrix products, arithmetic and copies ran while one was open for 0% -> 0% of each run, Pallas kernels for 16% -> 18%
where the time goes in v8:
time: 164 us; the launch traced here: 163 us
  starting transfers between devices  80 us (49%)
  waiting for transfers between devices  43.1 us (26%)
  Pallas kernels  31.4 us (19%)
  local copies, waits for them, and re-layouts  7.78 us (5%)
    ppermute x21, starting transfers between devices, along(): return lax.ppermute(x, axis, [(i, (i + hop) % count) for i in range(count)])  43.1 us
    ppermute x21, waiting for transfers between devices, along(): return lax.ppermute(x, axis, [(i, (i + hop) % count) for i in range(count)])  28.9 us
    pallas_call x2, Pallas kernels, head_split(): pl.pallas_call(functools.partial(head_kernel, ctx, slot), out_shape=[shap...  18.1 us
    ppermute x1, starting transfers between devices, head_split(): pair = lax.ppermute(grad, 'ctx', [(0, 1), (1, 0), (2, 3), (3, 2)])  14.4 us
    ppermute x1, starting transfers between devices, head_split(): two = lax.ppermute(grad, 'ctx', [(0, 2), (1, 3), (2, 0), (3, 1)])  12.4 us
    pallas_call x3, Pallas kernels, products(): pl.pallas_call(functools.partial(weight_gradient_kernel, steps, slot == 1...  9.22 us
    ppermute x1, waiting for transfers between devices, head_split(): far = lax.ppermute(two, 'ctx', [(2, 3), (1, 0)])  8.88 us
    all_to_all x1, starting transfers between devices, head_split(): back = lax.all_to_all(back, 'ctx', 0, 0)  8.14 us
  transfers between devices with their start and end apart: 26, of which 10 were waited for; matrix products, arithmetic and copies ran while one was open for 0% of the time, Pallas kernels for 18%

profile of v8, /device:TPU:0, one launch (start us, length us, event | category | flops | bytes accessed | tf_op | source)
XLA Modules:
  0.0 163.3 jit_solution(16351057352726704707)
XLA Ops:
  2.5 3.1 %collective-permute-start = (bf16[576,128]{1,0:T(8,128)(2,1)S(1)}, bf16[576,128]{1,0:T(8,128)(2,1)S(1)}, u32[]{:S(2)}, u32[]{:S(2)}) collective-permute-start(bf16[576,128]{1,0:T(8,128)(2,1)S(1)} %pack_tokens.1), channel_id=1, source_target_pairs={{0,4},{4,8},{8,12},{12,0},{1,5},{5,9},{9,13},{13,1},{2,6},{6,10},{... | collective-permute-start | bytes 442376 | tf_op jit(solution)/shard_map/ppermute | solution.py:344
  5.5 2.6 %collective-permute-start.1 = (bf16[576,128]{1,0:T(8,128)(2,1)S(1)}, bf16[576,128]{1,0:T(8,128)(2,1)S(1)}, u32[]{:S(2)}, u32[]{:S(2)}) collective-permute-start(bf16[576,128]{1,0:T(8,128)(2,1)S(1)} %pack_tokens.1), channel_id=1, source_target_pairs={{0,8},{4,12},{8,0},{12,4},{1,9},{5,13},{9,1},{13,5},{2,10},{6,14},... | collective-permute-start | bytes 442376 | tf_op jit(solution)/shard_map/ppermute | solution.py:344
  8.1 1.3 collective-permute-start.2
  9.5 1.3 copy-done
  18.0 1.6 collective-permute-start.3
  19.5 3.6 %collective-permute-start.6 = (bf16[384,384]{1,0:T(8,128)(2,1)S(1)}, bf16[384,384]{1,0:T(8,128)(2,1)S(1)}, u32[]{:S(2)}, u32[]{:S(2)}) collective-permute-start(bf16[384,384]{1,0:T(8,128)(2,1)S(1)} %get-tuple-element.69), channel_id=1, source_target_pairs={{0,4},{4,8},{8,12},{12,0},{1,5},{5,9},{9,13},{13,1},{2,6},{6,10},{... | collective-permute-start | bytes 884744 | tf_op jit(solution)/shard_map/ppermute | solution.py:344
  23.1 1.6 collective-permute-start.4
  25.5 6.8 %collective-permute-done.6.refs_2_ = bf16[384,384]{1,0:T(8,128)(2,1)S(1)} collective-permute-done((bf16[384,384]{1,0:T(8,128)(2,1)S(1)}, bf16[384,384]{1,0:T(8,128)(2,1)S(1)}, u32[]{:S(2)}, u32[]{:S(2)}) %collective-permute-start.6) | collective-permute-done | bytes 294944 | tf_op jit(solution)/shard_map/ppermute | solution.py:344
  32.3 1.6 collective-permute-start.7
  33.9 9.1 %collective-permute-done.4.refs_3_ = bf16[384,384]{1,0:T(8,128)(2,1)S(1)} collective-permute-done((bf16[384,384]{1,0:T(8,128)(2,1)S(1)}, bf16[384,384]{1,0:T(8,128)(2,1)S(1)}, u32[]{:S(2)}, u32[]{:S(2)}) %collective-permute-start.4) | collective-permute-done | bytes 294944 | tf_op jit(solution)/shard_map/ppermute | solution.py:344
  43.6 1.6 collective-permute-start.11
  45.7 6.7 %collective-permute-start.10 = (bf16[384,384]{1,0:T(8,128)(2,1)S(1)}, bf16[384,384]{1,0:T(8,128)(2,1)S(1)}, u32[]{:S(2)}, u32[]{:S(2)}) collective-permute-start(bf16[384,384]{1,0:T(8,128)(2,1)S(1)} %get-tuple-element.79), channel_id=1, source_target_pairs={{0,4},{4,8},{8,12},{12,0},{1,5},{5,9},{9,13},{13,1},{2,6},{6,10},{... | collective-permute-start | bytes 884744 | tf_op jit(solution)/shard_map/ppermute | solution.py:344
  52.5 2.3 %collective-permute-start.13 = (bf16[384,384]{1,0:T(8,128)(2,1)S(1)}, bf16[384,384]{1,0:T(8,128)(2,1)S(1)}, u32[]{:S(2)}, u32[]{:S(2)}) collective-permute-start(bf16[384,384]{1,0:T(8,128)(2,1)S(1)} %get-tuple-element.86), channel_id=1, source_target_pairs={{0,8},{4,12},{8,0},{12,4},{1,9},{5,13},{9,1},{13,5},{2,10},{6,14},... | collective-permute-start | bytes 884744 | tf_op jit(solution)/shard_map/ppermute | solution.py:344
  54.8 1.3 unpack_tokens.1
  56.1 8.6 %head_0.1 = (bf16[512,384]{1,0:T(8,128)(2,1)S(1)}, bf16[4,272,128]{2,1,0:T(8,128)(2,1)S(1)}) custom-call(s32[15]{0:T(128)S(1)} %stack.61.where_ref, bf16[4,512,576]{2,1,0:T(8,128)(2,1)S(1)} %get-tuple-element.72.refs_0_, bf16[672,384]{1,0:T(8,128)(2,1)S(1)} %get-tuple-element.80.refs_1_, bf16[384,384]{1,0:T(8,128)(2,1)S(1)} %collective-permute-done.6.refs_2_, ...), custom_call_target="tpu_custom_call" | custom-call | flops 12000000000 | bytes 12000000 | tf_op jit(solution)/shard_map/head_0/pallas_call | solution.py:409
  64.8 8.9 %collective-permute-done.13.refs_3_ = bf16[384,384]{1,0:T(8,128)(2,1)S(1)} collective-permute-done((bf16[384,384]{1,0:T(8,128)(2,1)S(1)}, bf16[384,384]{1,0:T(8,128)(2,1)S(1)}, u32[]{:S(2)}, u32[]{:S(2)}) %collective-permute-start.13) | collective-permute-done | bytes 294944 | tf_op jit(solution)/shard_map/ppermute | solution.py:344
  73.7 1.6 collective-permute-start.17
  75.9 1.6 collective-permute-start.15
  77.5 6.8 %collective-permute-start.18 = (bf16[512,384]{1,0:T(8,128)(2,1)S(1)}, bf16[512,384]{1,0:T(8,128)(2,1)S(1)}, u32[]{:S(2)}, u32[]{:S(2)}) collective-permute-start(bf16[512,384]{1,0:T(8,128)(2,1)S(1)} %get-tuple-element.99.refs_0_), channel_id=1, source_target_pairs={{0,4},{4,8},{8,12},{12,0},{1,5},{5,9},{9,13},{13,1},{2,6},{6,10},{... | collective-permute-start | bytes 1179656 | tf_op jit(solution)/shard_map/ppermute | solution.py:344
  84.9 4.1 %collective-permute-start.20 = (bf16[512,384]{1,0:T(8,128)(2,1)S(1)}, bf16[512,384]{1,0:T(8,128)(2,1)S(1)}, u32[]{:S(2)}, u32[]{:S(2)}) collective-permute-start(bf16[512,384]{1,0:T(8,128)(2,1)S(1)} %get-tuple-element.99.refs_0_), channel_id=1, source_target_pairs={{0,12},{4,0},{8,4},{12,8},{1,13},{5,1},{9,5},{13,9},{2,14},{6,2},{... | collective-permute-start | bytes 1179656 | tf_op jit(solution)/shard_map/ppermute | solution.py:344
  88.9 1.6 collective-permute-done.15.refs_5_
  90.5 9.5 %head_1.1 = (bf16[512,384]{1,0:T(8,128)(2,1)S(1)}, bf16[4,272,256]{2,1,0:T(8,128)(2,1)}) custom-call(s32[15]{0:T(128)S(1)} %stack.61.where_ref, bf16[4,512,576]{2,1,0:T(8,128)(2,1)S(1)} %get-tuple-element.72.refs_0_, bf16[672,384]{1,0:T(8,128)(2,1)S(1)} %get-tuple-element.73.refs_1_, bf16[384,384]{1,0:T(8,128)(2,1)S(1)} %collective-permute-done.10.refs_2_, ...), custom_call_target="tpu_custom_call" | custom-call | flops 12000000000 | bytes 12000000 | tf_op jit(solution)/shard_map/head_1/pallas_call | solution.py:409
  100.0 8.1 %all-to-all-start = ((bf16[4,272,256]{2,1,0:T(8,128)(2,1)}), bf16[4,272,256]{2,1,0:T(8,128)(2,1)S(1)}, u32[]{:S(2)}, u32[]{:S(2)}) async-start(bf16[4,272,256]{2,1,0:T(8,128)(2,1)} %get-tuple-element.93), calls=%async_computation | async-start | bytes 1114112 | tf_op jit(solution)/shard_map/all_to_all | solution.py:444
  108.5 1.5 collective-permute-done.20.refs_3_
  110.1 12.4 %collective-permute-start.21 = (bf16[512,384]{1,0:T(8,128)(2,1)S(1)}, bf16[512,384]{1,0:T(8,128)(2,1)S(1)}, u32[]{:S(2)}, u32[]{:S(2)}) collective-permute-start(bf16[512,384]{1,0:T(8,128)(2,1)S(1)} %get-tuple-element.106.refs_0_), channel_id=1, source_target_pairs={{0,8},{4,12},{8,0},{12,4},{1,9},{5,13},{9,1},{13,5},{2,10},{6,14},... | collective-permute-start | bytes 1179656 | tf_op jit(solution)/shard_map/ppermute | solution.py:436
  122.5 14.4 %collective-permute-start.22 = (bf16[512,384]{1,0:T(8,128)(2,1)S(1)}, bf16[512,384]{1,0:T(8,128)(2,1)S(1)}, u32[]{:S(2)}, u32[]{:S(2)}) collective-permute-start(bf16[512,384]{1,0:T(8,128)(2,1)S(1)} %get-tuple-element.106.refs_0_), channel_id=1, source_target_pairs={{0,4},{4,0},{8,12},{12,8},{1,5},{5,1},{9,13},{13,9},{2,6},{6,2},{1... | collective-permute-start | bytes 1179656 | tf_op jit(solution)/shard_map/ppermute | solution.py:437
  136.9 3.9 %weight_gradient_0_0.1 = (f32[576,1024]{1,0:T(8,128)}, f32[576,1024]{1,0:T(8,128)}, f32[576,1024]{1,0:T(8,128)}) custom-call(s32[15]{0:T(128)S(1)} %stack.61.where_ref, bf16[576,512]{1,0:T(8,128)(2,1)S(1)} %get-tuple-element.95.own_ref, bf16[512,384]{1,0:T(8,128)(2,1)S(1)} %get-tuple-element.99.refs_0_, ...), custom_call_target="tpu_custom_call" | custom-call | tf_op jit(solution)/shard_map/weight_gradient_0_0/pallas_call | solution.py:387
  140.8 5.0 %collective-permute-done.21.refs_2_ = bf16[512,384]{1,0:T(8,128)(2,1)S(1)} collective-permute-done((bf16[512,384]{1,0:T(8,128)(2,1)S(1)}, bf16[512,384]{1,0:T(8,128)(2,1)S(1)}, u32[]{:S(2)}, u32[]{:S(2)}) %collective-permute-start.21) | collective-permute-done | bytes 393248 | tf_op jit(solution)/shard_map/ppermute | solution.py:436
  146.8 1.3 collective-permute-start.24
  148.1 3.4 %weight_gradient_1_0.1 = (f32[576,1024]{1,0:T(8,128)}, f32[576,1024]{1,0:T(8,128)}, f32[576,1024]{1,0:T(8,128)}) custom-call(s32[15]{0:T(128)S(1)} %stack.61.where_ref, bf16[576,512]{1,0:T(8,128)(2,1)S(1)} %get-tuple-element.95.own_ref, bf16[512,384]{1,0:T(8,128)(2,1)S(1)} %get-tuple-element.106.refs_0_, ...), custom_call_target="tpu_custom_call", output_to_operand_aliasing={{0}: (5, {}), {1}: (6, {}), {2}: (7, {})} | custom-call | tf_op jit(solution)/shard_map/weight_gradient_1_0/pallas_call | solution.py:387
  152.5 8.9 %collective-permute-done.24.refs_1_ = bf16[512,384]{1,0:T(8,128)(2,1)S(1)} collective-permute-done((bf16[512,384]{1,0:T(8,128)(2,1)S(1)}, bf16[512,384]{1,0:T(8,128)(2,1)S(1)}, u32[]{:S(2)}, u32[]{:S(2)}) %collective-permute-start.24) | collective-permute-done | bytes 393248 | tf_op jit(solution)/shard_map/ppermute | solution.py:441
  161.3 1.9 %weight_gradient_1_3.1 = (f32[576,1024]{1,0:T(8,128)}, f32[576,1024]{1,0:T(8,128)}, f32[576,1024]{1,0:T(8,128)}) custom-call(s32[15]{0:T(128)S(1)} %stack.61.where_ref, bf16[576,512]{1,0:T(8,128)(2,1)S(1)} %get-tuple-element.95.own_ref, ...), custom_call_target="tpu_custom_call", output_to_operand_aliasing={{0}: (4, {}), {1}: (5, {}), {2}: (6, {})} | custom-call | tf_op jit(solution)/shard_map/weight_gradient_1_3/pallas_call | solution.py:387
  (51 shorter events, 14.7 us)
Async XLA Ops:
  0.8 1.1 copy-start.3
  2.5 14.8 %collective-permute-start = (bf16[576,128]{1,0:T(8,128)(2,1)S(1)}, bf16[576,128]{1,0:T(8,128)(2,1)S(1)}, u32[]{:S(2)}, u32[]{:S(2)}) collective-permute-start(bf16[576,128]{1,0:T(8,128)(2,1)S(1)} %pack_tokens.1), channel_id=1, source_target_pairs={{0,4},{4,8},{8,12},{12,0},{1,5},{5,9},{9,13},{13,1},{2,6},{6,10},{... | collective-permute-start | bytes 442376 | tf_op jit(solution)/shard_map/ppermute | solution.py:344
  5.5 12.4 %collective-permute-start.1 = (bf16[576,128]{1,0:T(8,128)(2,1)S(1)}, bf16[576,128]{1,0:T(8,128)(2,1)S(1)}, u32[]{:S(2)}, u32[]{:S(2)}) collective-permute-start(bf16[576,128]{1,0:T(8,128)(2,1)S(1)} %pack_tokens.1), channel_id=1, source_target_pairs={{0,8},{4,12},{8,0},{12,4},{1,9},{5,13},{9,1},{13,5},{2,10},{6,14},... | collective-permute-start | bytes 442376 | tf_op jit(solution)/shard_map/ppermute | solution.py:344
  8.1 9.8 %collective-permute-start.2 = (bf16[576,128]{1,0:T(8,128)(2,1)S(1)}, bf16[576,128]{1,0:T(8,128)(2,1)S(1)}, u32[]{:S(2)}, u32[]{:S(2)}) collective-permute-start(bf16[576,128]{1,0:T(8,128)(2,1)S(1)} %pack_tokens.1), channel_id=1, source_target_pairs={{0,12},{4,0},{8,4},{12,8},{1,13},{5,1},{9,5},{13,9},{2,14},{6,2},{... | collective-permute-start | bytes 442376 | tf_op jit(solution)/shard_map/ppermute | solution.py:344
  9.5 1.3 copy-start
  10.7 1.3 copy-start.1
  12.0 1.3 copy-start.2
  13.3 1.0 copy-start.4
  14.3 0.9 copy-start.5
  18.0 25.0 %collective-permute-start.3 = (bf16[2304,128]{1,0:T(8,128)(2,1)S(1)}, bf16[2304,128]{1,0:T(8,128)(2,1)S(1)}, u32[]{:S(2)}, u32[]{:S(2)}) collective-permute-start(bf16[2304,128]{1,0:T(8,128)(2,1)S(1)} %pad_maximum_fusion.refs_0_), channel_id=1, source_target_pairs={{0,2},{2,0},{1,3},{3,1},{4,6},{6,4},{5,7},{7,5},{8,10},{10,8},{9,1... | collective-permute-start | bytes 1769480 | tf_op jit(solution)/shard_map/ppermute | solution.py:344
  19.5 12.8 %collective-permute-start.6 = (bf16[384,384]{1,0:T(8,128)(2,1)S(1)}, bf16[384,384]{1,0:T(8,128)(2,1)S(1)}, u32[]{:S(2)}, u32[]{:S(2)}) collective-permute-start(bf16[384,384]{1,0:T(8,128)(2,1)S(1)} %get-tuple-element.69), channel_id=1, source_target_pairs={{0,4},{4,8},{8,12},{12,0},{1,5},{5,9},{9,13},{13,1},{2,6},{6,10},{... | collective-permute-start | bytes 884744 | tf_op jit(solution)/shard_map/ppermute | solution.py:344
  23.1 19.8 %collective-permute-start.4 = (bf16[384,384]{1,0:T(8,128)(2,1)S(1)}, bf16[384,384]{1,0:T(8,128)(2,1)S(1)}, u32[]{:S(2)}, u32[]{:S(2)}) collective-permute-start(bf16[384,384]{1,0:T(8,128)(2,1)S(1)} %get-tuple-element.67), channel_id=1, source_target_pairs={{0,8},{4,12},{8,0},{12,4},{1,9},{5,13},{9,1},{13,5},{2,10},{6,14},... | collective-permute-start | bytes 884744 | tf_op jit(solution)/shard_map/ppermute | solution.py:344
  24.8 18.2 %collective-permute-start.5 = (bf16[384,384]{1,0:T(8,128)(2,1)S(1)}, bf16[384,384]{1,0:T(8,128)(2,1)S(1)}, u32[]{:S(2)}, u32[]{:S(2)}) collective-permute-start(bf16[384,384]{1,0:T(8,128)(2,1)S(1)} %get-tuple-element.68), channel_id=1, source_target_pairs={{0,12},{4,0},{8,4},{12,8},{1,13},{5,1},{9,5},{13,9},{2,14},{6,2},{... | collective-permute-start | bytes 884744 | tf_op jit(solution)/shard_map/ppermute | solution.py:344
  32.3 10.6 %collective-permute-start.7 = (bf16[288,384]{1,0:T(8,128)(2,1)S(1)}, bf16[288,384]{1,0:T(8,128)(2,1)S(1)}, u32[]{:S(2)}, u32[]{:S(2)}) collective-permute-start(bf16[288,384]{1,0:T(8,128)(2,1)S(1)} %slice.24), channel_id=1, source_target_pairs={{0,16},{16,0},{1,17},{17,1},{2,18},{18,2},{3,19},{19,3},{4,20},{20... | collective-permute-start | bytes 663560 | tf_op jit(solution)/shard_map/ppermute | solution.py:344
  42.9 9.5 %collective-permute-start.8 = (bf16[2304,128]{1,0:T(8,128)(2,1)S(1)}, bf16[2304,128]{1,0:T(8,128)(2,1)S(1)}, u32[]{:S(2)}, u32[]{:S(2)}) collective-permute-start(bf16[2304,128]{1,0:T(8,128)(2,1)S(1)} %pad_maximum_fusion.refs_0_), channel_id=1, source_target_pairs={{0,1},{1,0},{2,3},{3,2},{4,5},{5,4},{6,7},{7,6},{8,9},{9,8},{10,11... | collective-permute-start | bytes 1769480 | tf_op jit(solution)/shard_map/ppermute | solution.py:344
  43.0 11.7 %collective-permute-start.9 = (bf16[2304,128]{1,0:T(8,128)(2,1)S(1)}, bf16[2304,128]{1,0:T(8,128)(2,1)S(1)}, u32[]{:S(2)}, u32[]{:S(2)}) collective-permute-start(bf16[2304,128]{1,0:T(8,128)(2,1)S(1)} %collective-permute-done.3.refs_1_), channel_id=1, source_target_pairs={{0,1},{1,0},{2,3},{3,2},{4,5},{5,4},{6,7},{7,6},{8,9},{9,8},{10,11... | collective-permute-start | bytes 1769480 | tf_op jit(solution)/shard_map/ppermute | solution.py:344
  43.6 12.6 %collective-permute-start.11 = (bf16[288,384]{1,0:T(8,128)(2,1)S(1)}, bf16[288,384]{1,0:T(8,128)(2,1)S(1)}, u32[]{:S(2)}, u32[]{:S(2)}) collective-permute-start(bf16[288,384]{1,0:T(8,128)(2,1)S(1)} %slice.19), channel_id=1, source_target_pairs={{0,16},{16,0},{1,17},{17,1},{2,18},{18,2},{3,19},{19,3},{4,20},{20... | collective-permute-start | bytes 663560 | tf_op jit(solution)/shard_map/ppermute | solution.py:344
  45.2 11.0 %collective-permute-start.12 = (bf16[288,384]{1,0:T(8,128)(2,1)S(1)}, bf16[288,384]{1,0:T(8,128)(2,1)S(1)}, u32[]{:S(2)}, u32[]{:S(2)}) collective-permute-start(bf16[288,384]{1,0:T(8,128)(2,1)S(1)} %slice.20), channel_id=1, source_target_pairs={{0,16},{16,0},{1,17},{17,1},{2,18},{18,2},{3,19},{19,3},{4,20},{20... | collective-permute-start | bytes 663560 | tf_op jit(solution)/shard_map/ppermute | solution.py:344
  45.7 19.1 %collective-permute-start.10 = (bf16[384,384]{1,0:T(8,128)(2,1)S(1)}, bf16[384,384]{1,0:T(8,128)(2,1)S(1)}, u32[]{:S(2)}, u32[]{:S(2)}) collective-permute-start(bf16[384,384]{1,0:T(8,128)(2,1)S(1)} %get-tuple-element.79), channel_id=1, source_target_pairs={{0,4},{4,8},{8,12},{12,0},{1,5},{5,9},{9,13},{13,1},{2,6},{6,10},{... | collective-permute-start | bytes 884744 | tf_op jit(solution)/shard_map/ppermute | solution.py:344
  52.5 21.2 %collective-permute-start.13 = (bf16[384,384]{1,0:T(8,128)(2,1)S(1)}, bf16[384,384]{1,0:T(8,128)(2,1)S(1)}, u32[]{:S(2)}, u32[]{:S(2)}) collective-permute-start(bf16[384,384]{1,0:T(8,128)(2,1)S(1)} %get-tuple-element.86), channel_id=1, source_target_pairs={{0,8},{4,12},{8,0},{12,4},{1,9},{5,13},{9,1},{13,5},{2,10},{6,14},... | collective-permute-start | bytes 884744 | tf_op jit(solution)/shard_map/ppermute | solution.py:344
  54.7 18.9 %collective-permute-start.14 = (bf16[384,384]{1,0:T(8,128)(2,1)S(1)}, bf16[384,384]{1,0:T(8,128)(2,1)S(1)}, u32[]{:S(2)}, u32[]{:S(2)}) collective-permute-start(bf16[384,384]{1,0:T(8,128)(2,1)S(1)} %get-tuple-element.89), channel_id=1, source_target_pairs={{0,12},{4,0},{8,4},{12,8},{1,13},{5,1},{9,5},{13,9},{2,14},{6,2},{... | collective-permute-start | bytes 884744 | tf_op jit(solution)/shard_map/ppermute | solution.py:344
  73.7 11.2 %collective-permute-start.17 = (bf16[288,384]{1,0:T(8,128)(2,1)S(1)}, bf16[288,384]{1,0:T(8,128)(2,1)S(1)}, u32[]{:S(2)}, u32[]{:S(2)}) collective-permute-start(bf16[288,384]{1,0:T(8,128)(2,1)S(1)} %slice.23), channel_id=1, source_target_pairs={{0,16},{16,0},{1,17},{17,1},{2,18},{18,2},{3,19},{19,3},{4,20},{20... | collective-permute-start | bytes 663560 | tf_op jit(solution)/shard_map/ppermute | solution.py:344
  75.3 13.6 %collective-permute-start.16 = (bf16[288,384]{1,0:T(8,128)(2,1)S(1)}, bf16[288,384]{1,0:T(8,128)(2,1)S(1)}, u32[]{:S(2)}, u32[]{:S(2)}) collective-permute-start(bf16[288,384]{1,0:T(8,128)(2,1)S(1)} %slice.22), channel_id=1, source_target_pairs={{0,16},{16,0},{1,17},{17,1},{2,18},{18,2},{3,19},{19,3},{4,20},{20... | collective-permute-start | bytes 663560 | tf_op jit(solution)/shard_map/ppermute | solution.py:344
  75.9 14.6 %collective-permute-start.15 = (bf16[288,384]{1,0:T(8,128)(2,1)S(1)}, bf16[288,384]{1,0:T(8,128)(2,1)S(1)}, u32[]{:S(2)}, u32[]{:S(2)}) collective-permute-start(bf16[288,384]{1,0:T(8,128)(2,1)S(1)} %slice.21), channel_id=1, source_target_pairs={{0,16},{16,0},{1,17},{17,1},{2,18},{18,2},{3,19},{19,3},{4,20},{20... | collective-permute-start | bytes 663560 | tf_op jit(solution)/shard_map/ppermute | solution.py:344
  77.5 30.6 %collective-permute-start.18 = (bf16[512,384]{1,0:T(8,128)(2,1)S(1)}, bf16[512,384]{1,0:T(8,128)(2,1)S(1)}, u32[]{:S(2)}, u32[]{:S(2)}) collective-permute-start(bf16[512,384]{1,0:T(8,128)(2,1)S(1)} %get-tuple-element.99.refs_0_), channel_id=1, source_target_pairs={{0,4},{4,8},{8,12},{12,0},{1,5},{5,9},{9,13},{13,1},{2,6},{6,10},{... | collective-permute-start | bytes 1179656 | tf_op jit(solution)/shard_map/ppermute | solution.py:344
  84.3 24.3 %collective-permute-start.19 = (bf16[512,384]{1,0:T(8,128)(2,1)S(1)}, bf16[512,384]{1,0:T(8,128)(2,1)S(1)}, u32[]{:S(2)}, u32[]{:S(2)}) collective-permute-start(bf16[512,384]{1,0:T(8,128)(2,1)S(1)} %get-tuple-element.99.refs_0_), channel_id=1, source_target_pairs={{0,8},{4,12},{8,0},{12,4},{1,9},{5,13},{9,1},{13,5},{2,10},{6,14},... | collective-permute-start | bytes 1179656 | tf_op jit(solution)/shard_map/ppermute | solution.py:344
  84.9 25.2 %collective-permute-start.20 = (bf16[512,384]{1,0:T(8,128)(2,1)S(1)}, bf16[512,384]{1,0:T(8,128)(2,1)S(1)}, u32[]{:S(2)}, u32[]{:S(2)}) collective-permute-start(bf16[512,384]{1,0:T(8,128)(2,1)S(1)} %get-tuple-element.99.refs_0_), channel_id=1, source_target_pairs={{0,12},{4,0},{8,4},{12,8},{1,13},{5,1},{9,5},{13,9},{2,14},{6,2},{... | collective-permute-start | bytes 1179656 | tf_op jit(solution)/shard_map/ppermute | solution.py:344
  100.0 51.6 %all-to-all-start = ((bf16[4,272,256]{2,1,0:T(8,128)(2,1)}), bf16[4,272,256]{2,1,0:T(8,128)(2,1)S(1)}, u32[]{:S(2)}, u32[]{:S(2)}) async-start(bf16[4,272,256]{2,1,0:T(8,128)(2,1)} %get-tuple-element.93), calls=%async_computation | async-start | bytes 1114112 | tf_op jit(solution)/shard_map/all_to_all | solution.py:444
  110.1 35.7 %collective-permute-start.21 = (bf16[512,384]{1,0:T(8,128)(2,1)S(1)}, bf16[512,384]{1,0:T(8,128)(2,1)S(1)}, u32[]{:S(2)}, u32[]{:S(2)}) collective-permute-start(bf16[512,384]{1,0:T(8,128)(2,1)S(1)} %get-tuple-element.106.refs_0_), channel_id=1, source_target_pairs={{0,8},{4,12},{8,0},{12,4},{1,9},{5,13},{9,1},{13,5},{2,10},{6,14},... | collective-permute-start | bytes 1179656 | tf_op jit(solution)/shard_map/ppermute | solution.py:436
  122.5 23.6 %collective-permute-start.22 = (bf16[512,384]{1,0:T(8,128)(2,1)S(1)}, bf16[512,384]{1,0:T(8,128)(2,1)S(1)}, u32[]{:S(2)}, u32[]{:S(2)}) collective-permute-start(bf16[512,384]{1,0:T(8,128)(2,1)S(1)} %get-tuple-element.106.refs_0_), channel_id=1, source_target_pairs={{0,4},{4,0},{8,12},{12,8},{1,5},{5,1},{9,13},{13,9},{2,6},{6,2},{1... | collective-permute-start | bytes 1179656 | tf_op jit(solution)/shard_map/ppermute | solution.py:437
  146.1 6.3 %collective-permute-start.23 = (bf16[512,384]{1,0:T(8,128)(2,1)S(1)}, bf16[512,384]{1,0:T(8,128)(2,1)S(1)}, u32[]{:S(2)}, u32[]{:S(2)}) collective-permute-start(bf16[512,384]{1,0:T(8,128)(2,1)S(1)} %get-tuple-element.106.refs_0_), channel_id=1, source_target_pairs={{4,8},{8,4},{5,9},{9,5},{6,10},{10,6},{7,11},{11,7},{20,24},{24,20... | collective-permute-start | bytes 1179656 | tf_op jit(solution)/shard_map/ppermute | solution.py:440
  146.8 14.5 %collective-permute-start.24 = (bf16[512,384]{1,0:T(8,128)(2,1)S(1)}, bf16[512,384]{1,0:T(8,128)(2,1)S(1)}, u32[]{:S(2)}, u32[]{:S(2)}) collective-permute-start(bf16[512,384]{1,0:T(8,128)(2,1)S(1)} %collective-permute-done.21.refs_2_), channel_id=1, source_target_pairs={{8,12},{4,0},{9,13},{5,1},{10,14},{6,2},{11,15},{7,3},{24,28},{20,... | collective-permute-start | bytes 1179656 | tf_op jit(solution)/shard_map/ppermute | solution.py:441
  (1 other events, 0.7 us)

commit v9 on v8

--- a/solution.py
+++ b/solution.py
@@ -284,7 +284,7 @@
         back_ref[n, 2 * CHUNK :, lane] = tail_rows(dlogit[n : n + 1, :])
 
 
-def weight_gradient_kernel(steps, forwarded, where_ref, own_ref, *refs):
+def weight_gradient_kernel(steps, where_ref, own_ref, *refs):
     out_refs = refs[-3:]
 
     def block(gradient):
@@ -296,10 +296,10 @@
 
         @pl.when(pl.program_id(0) == at)
         def _(at=at, step=step):
-            if step < 3 or not forwarded:
+            if step < 3:
                 block(refs[at][...])
             else:
-                block(jnp.where(where_ref[14] == 1, refs[at + 1][...], refs[at][...]))
+                block(jnp.where(where_ref[10] == 1, refs[at + 1][...], refs[at][...]))
 
 
 def unpack_kernel(back_ref, out_ref, dlogit_ref, ddecay_ref):
@@ -328,7 +328,6 @@
     where = jnp.stack(
         [place, group]
         + [2 * a + c for c in (core, 1 - core) for a in (across, 1 - across)]
-        + [(place + ctx - d) % ctx for d in range(ctx)]
         + sources
         + [((place == 0) | (place == ctx - 1)).astype(jnp.int32)]
     ).astype(jnp.int32)
@@ -383,9 +382,9 @@
     second = [along(x, "ctx", d + 1) for d, x in enumerate(second)]
 
     def products(slot, steps, parts, results):
-        column = pl.BlockSpec((share, DK), lambda i, ref: (0, 2 * ref[6 + 4 * slot + steps[0] + i] + slot))
+        column = pl.BlockSpec((share, DK), lambda i, ref: (0, 2 * ref[6 + steps[0] + i] + slot))
         return pl.pallas_call(
-            functools.partial(weight_gradient_kernel, steps, slot == 1),
+            functools.partial(weight_gradient_kernel, steps),
             grid_spec=pltpu.PrefetchScalarGridSpec(
                 num_scalar_prefetch=1,
                 grid=(len(steps),),
@@ -428,19 +427,19 @@
             compiler_params=pltpu.CompilerParams(vmem_limit_bytes=VMEM_LIMIT),
             name=f"head_{slot}",
         )(where, all_tokens, packed[slot * ctx], *direct, *swapped, *earlier)
-        if slot == 0:
-            hops = [along(grad, "ctx", d) for d in range(1, ctx)]
-            grads.append([grad] + hops)
-            continue
-        grad, grads[0] = after(grad, grads[0])
+        if slot:
+            grad, grads[0][1:3] = after(grad, grads[0][1:3])
         two = lax.ppermute(grad, "ctx", [(0, 2), (1, 3), (2, 0), (3, 1)])
         pair = lax.ppermute(grad, "ctx", [(0, 1), (1, 0), (2, 3), (3, 2)])
-        results = products(0, (0, 1, 2, 3), grads[0], ())
+        results = ()
+        if slot:
+            results = products(0, (0, 1, 2, 3), grads[0], ())
         (grad, two), (pair, results) = after((grad, two), (pair, results))
         middle = lax.ppermute(grad, "ctx", [(1, 2), (2, 1)])
         far = lax.ppermute(two, "ctx", [(2, 3), (1, 0)])
-        results = products(1, (0, 1, 2), [grad, pair, two], results)
-        results = products(1, (3,), [middle, far], results)
+        grads.append([grad, pair, two, middle, far])
+    results = products(1, (0, 1, 2), grads[1][:3], results)
+    results = products(1, (3,), grads[1][3:], results)
     back = lax.all_to_all(back, "ctx", 0, 0)
 
     attn_out, grad_beta, grad_decay = pl.pallas_call(

time: 164 us -> 163 us (level)
  starting transfers between devices: 80 us -> 56.2 us
  waiting for transfers between devices: 43.1 us -> 66.2 us
    ppermute x1 -> x2, starting transfers between devices: 14.4 us -> 1.61 us  [head_split(): pair = lax.ppermute(grad, 'ctx', [(0, 1), (1, 0), (2, 3), (3, 2)])]
    ppermute x1 -> x2, waiting for transfers between devices: 4.97 us -> 17 us  [head_split(): two = lax.ppermute(grad, 'ctx', [(0, 2), (1, 3), (2, 0), (3, 1)])]
    ppermute x21 -> x18, starting transfers between devices: 43.1 us -> 31.6 us  [along(): return lax.ppermute(x, axis, [(i, (i + hop) % count) for i in range(count)])]
    ppermute x1 -> x2, waiting for transfers between devices: 8.88 us -> 18.2 us  [head_split(): far = lax.ppermute(two, 'ctx', [(2, 3), (1, 0)])]
    ppermute x21 -> x18, waiting for transfers between devices: 28.9 us -> 31 us  [along(): return lax.ppermute(x, axis, [(i, (i + hop) % count) for i in range(count)])]
    ppermute x1 -> x2, starting transfers between devices: 12.4 us -> 10.9 us  [head_split(): two = lax.ppermute(grad, 'ctx', [(0, 2), (1, 3), (2, 0), (3, 1)])]
  transfers between devices with their start and end apart: 26 -> 27, of which waited for: 10 -> 9; matrix products, arithmetic and copies ran while one was open for 0% -> 0% of each run, Pallas kernels for 18% -> 18%
where the time goes in v9:
time: 163 us
  waiting for transfers between devices  66.2 us (41%)
  starting transfers between devices  56.2 us (34%)
  Pallas kernels  31.7 us (19%)
  local copies, waits for them, and re-layouts  7.78 us (5%)
    ppermute x18, starting transfers between devices, along(): return lax.ppermute(x, axis, [(i, (i + hop) % count) for i in range(count)])  31.6 us
    ppermute x18, waiting for transfers between devices, along(): return lax.ppermute(x, axis, [(i, (i + hop) % count) for i in range(count)])  31 us
    pallas_call x2, Pallas kernels, head_split(): pl.pallas_call(functools.partial(head_kernel, ctx, slot), out_shape=[shap...  18.3 us
    ppermute x2, waiting for transfers between devices, head_split(): far = lax.ppermute(two, 'ctx', [(2, 3), (1, 0)])  18.2 us
    ppermute x2, waiting for transfers between devices, head_split(): two = lax.ppermute(grad, 'ctx', [(0, 2), (1, 3), (2, 0), (3, 1)])  17 us
    ppermute x2, starting transfers between devices, head_split(): two = lax.ppermute(grad, 'ctx', [(0, 2), (1, 3), (2, 0), (3, 1)])  10.9 us
    pallas_call x3, Pallas kernels, products(): pl.pallas_call(functools.partial(weight_gradient_kernel, steps), grid_spe...  9.24 us
    all_to_all x1, starting transfers between devices, head_split(): back = lax.all_to_all(back, 'ctx', 0, 0)  8.15 us
  transfers between devices with their start and end apart: 27, of which 9 were waited for; matrix products, arithmetic and copies ran while one was open for 0% of the time, Pallas kernels for 18%

profile of v9, /device:TPU:0, one launch (start us, length us, event | category | flops | bytes accessed | tf_op | source)
XLA Modules:
  0.0 162.7 jit_solution(4515150083305091045)
XLA Ops:
  2.4 3.1 %collective-permute-start = (bf16[576,128]{1,0:T(8,128)(2,1)S(1)}, bf16[576,128]{1,0:T(8,128)(2,1)S(1)}, u32[]{:S(2)}, u32[]{:S(2)}) collective-permute-start(bf16[576,128]{1,0:T(8,128)(2,1)S(1)} %pack_tokens.1), channel_id=1, source_target_pairs={{0,4},{4,8},{8,12},{12,0},{1,5},{5,9},{9,13},{13,1},{2,6},{6,10},{... | collective-permute-start | bytes 442376 | tf_op jit(solution)/shard_map/ppermute | solution.py:343
  5.5 2.6 %collective-permute-start.1 = (bf16[576,128]{1,0:T(8,128)(2,1)S(1)}, bf16[576,128]{1,0:T(8,128)(2,1)S(1)}, u32[]{:S(2)}, u32[]{:S(2)}) collective-permute-start(bf16[576,128]{1,0:T(8,128)(2,1)S(1)} %pack_tokens.1), channel_id=1, source_target_pairs={{0,8},{4,12},{8,0},{12,4},{1,9},{5,13},{9,1},{13,5},{2,10},{6,14},... | collective-permute-start | bytes 442376 | tf_op jit(solution)/shard_map/ppermute | solution.py:343
  8.1 1.3 collective-permute-start.2
  17.9 1.6 collective-permute-start.3
  19.5 3.6 %collective-permute-start.6 = (bf16[384,384]{1,0:T(8,128)(2,1)S(1)}, bf16[384,384]{1,0:T(8,128)(2,1)S(1)}, u32[]{:S(2)}, u32[]{:S(2)}) collective-permute-start(bf16[384,384]{1,0:T(8,128)(2,1)S(1)} %get-tuple-element.70), channel_id=1, source_target_pairs={{0,4},{4,8},{8,12},{12,0},{1,5},{5,9},{9,13},{13,1},{2,6},{6,10},{... | collective-permute-start | bytes 884744 | tf_op jit(solution)/shard_map/ppermute | solution.py:343
  23.1 1.6 %collective-permute-start.4 = (bf16[384,384]{1,0:T(8,128)(2,1)S(1)}, bf16[384,384]{1,0:T(8,128)(2,1)S(1)}, u32[]{:S(2)}, u32[]{:S(2)}) collective-permute-start(bf16[384,384]{1,0:T(8,128)(2,1)S(1)} %get-tuple-element.68), channel_id=1, source_target_pairs={{0,8},{4,12},{8,0},{12,4},{1,9},{5,13},{9,1},{13,5},{2,10},{6,14},... | collective-permute-start | bytes 884744 | tf_op jit(solution)/shard_map/ppermute | solution.py:343
  25.5 6.8 %collective-permute-done.6.refs_2_ = bf16[384,384]{1,0:T(8,128)(2,1)S(1)} collective-permute-done((bf16[384,384]{1,0:T(8,128)(2,1)S(1)}, bf16[384,384]{1,0:T(8,128)(2,1)S(1)}, u32[]{:S(2)}, u32[]{:S(2)}) %collective-permute-start.6) | collective-permute-done | bytes 294944 | tf_op jit(solution)/shard_map/ppermute | solution.py:343
  32.3 1.6 collective-permute-start.7
  33.9 9.1 %collective-permute-done.4.refs_3_ = bf16[384,384]{1,0:T(8,128)(2,1)S(1)} collective-permute-done((bf16[384,384]{1,0:T(8,128)(2,1)S(1)}, bf16[384,384]{1,0:T(8,128)(2,1)S(1)}, u32[]{:S(2)}, u32[]{:S(2)}) %collective-permute-start.4) | collective-permute-done | bytes 294944 | tf_op jit(solution)/shard_map/ppermute | solution.py:343
  43.5 1.6 collective-permute-start.11
  45.7 6.7 %collective-permute-start.10 = (bf16[384,384]{1,0:T(8,128)(2,1)S(1)}, bf16[384,384]{1,0:T(8,128)(2,1)S(1)}, u32[]{:S(2)}, u32[]{:S(2)}) collective-permute-start(bf16[384,384]{1,0:T(8,128)(2,1)S(1)} %get-tuple-element.80), channel_id=1, source_target_pairs={{0,4},{4,8},{8,12},{12,0},{1,5},{5,9},{9,13},{13,1},{2,6},{6,10},{... | collective-permute-start | bytes 884744 | tf_op jit(solution)/shard_map/ppermute | solution.py:343
  52.4 2.3 %collective-permute-start.13 = (bf16[384,384]{1,0:T(8,128)(2,1)S(1)}, bf16[384,384]{1,0:T(8,128)(2,1)S(1)}, u32[]{:S(2)}, u32[]{:S(2)}) collective-permute-start(bf16[384,384]{1,0:T(8,128)(2,1)S(1)} %get-tuple-element.87), channel_id=1, source_target_pairs={{0,8},{4,12},{8,0},{12,4},{1,9},{5,13},{9,1},{13,5},{2,10},{6,14},... | collective-permute-start | bytes 884744 | tf_op jit(solution)/shard_map/ppermute | solution.py:343
  54.8 1.3 unpack_tokens.1
  56.1 8.6 %head_0.1 = (bf16[512,384]{1,0:T(8,128)(2,1)S(1)}, bf16[4,272,128]{2,1,0:T(8,128)(2,1)S(1)}) custom-call(s32[11]{0:T(128)S(1)} %stack.48.where_ref, bf16[4,512,576]{2,1,0:T(8,128)(2,1)S(1)} %get-tuple-element.73.refs_0_, bf16[672,384]{1,0:T(8,128)(2,1)S(1)} %get-tuple-element.81.refs_1_, bf16[384,384]{1,0:T(8,128)(2,1)S(1)} %collective-permute-done.6.refs_2_, ...), custom_call_target="tpu_custom_call" | custom-call | flops 12000000000 | bytes 12000000 | tf_op jit(solution)/shard_map/head_0/pallas_call | solution.py:408
  64.8 8.9 %collective-permute-done.13.refs_3_ = bf16[384,384]{1,0:T(8,128)(2,1)S(1)} collective-permute-done((bf16[384,384]{1,0:T(8,128)(2,1)S(1)}, bf16[384,384]{1,0:T(8,128)(2,1)S(1)}, u32[]{:S(2)}, u32[]{:S(2)}) %collective-permute-start.13) | collective-permute-done | bytes 294944 | tf_op jit(solution)/shard_map/ppermute | solution.py:343
  73.7 1.6 collective-permute-start.17
  75.9 1.6 collective-permute-start.15
  77.4 5.8 %collective-permute-start.18 = (bf16[512,384]{1,0:T(8,128)(2,1)S(1)}, bf16[512,384]{1,0:T(8,128)(2,1)S(1)}, u32[]{:S(2)}, u32[]{:S(2)}) collective-permute-start(bf16[512,384]{1,0:T(8,128)(2,1)S(1)} %get-tuple-element.102.refs_0_), channel_id=1, source_target_pairs={{0,8},{4,12},{8,0},{12,4},{1,9},{5,13},{9,1},{13,5},{2,10},{6,14},... | collective-permute-start | bytes 1179656 | tf_op jit(solution)/shard_map/ppermute | solution.py:432
  83.2 1.6 collective-permute-start.19
  84.8 2.0 %collective-permute-done.16.refs_6_ = bf16[288,384]{1,0:T(8,128)(2,1)S(1)} collective-permute-done((bf16[288,384]{1,0:T(8,128)(2,1)S(1)}, bf16[288,384]{1,0:T(8,128)(2,1)S(1)}, u32[]{:S(2)}, u32[]{:S(2)}) %collective-permute-start.16) | collective-permute-done | bytes 221216 | tf_op jit(solution)/shard_map/ppermute | solution.py:343
  86.8 3.7 %collective-permute-done.15.refs_5_ = bf16[288,384]{1,0:T(8,128)(2,1)S(1)} collective-permute-done((bf16[288,384]{1,0:T(8,128)(2,1)S(1)}, bf16[288,384]{1,0:T(8,128)(2,1)S(1)}, u32[]{:S(2)}, u32[]{:S(2)}) %collective-permute-start.15) | collective-permute-done | bytes 221216 | tf_op jit(solution)/shard_map/ppermute | solution.py:343
  90.5 9.7 %head_1.1 = (bf16[512,384]{1,0:T(8,128)(2,1)S(1)}, bf16[4,272,256]{2,1,0:T(8,128)(2,1)}) custom-call(s32[11]{0:T(128)S(1)} %stack.48.where_ref, bf16[4,512,576]{2,1,0:T(8,128)(2,1)S(1)} %get-tuple-element.73.refs_0_, bf16[672,384]{1,0:T(8,128)(2,1)S(1)} %get-tuple-element.74.refs_1_, bf16[384,384]{1,0:T(8,128)(2,1)S(1)} %collective-permute-done.10.refs_2_, ...), custom_call_target="tpu_custom_call" | custom-call | flops 12000000000 | bytes 12000000 | tf_op jit(solution)/shard_map/head_1/pallas_call | solution.py:408
  100.2 8.1 %all-to-all-start = ((bf16[4,272,256]{2,1,0:T(8,128)(2,1)}), bf16[4,272,256]{2,1,0:T(8,128)(2,1)S(1)}, u32[]{:S(2)}, u32[]{:S(2)}) async-start(bf16[4,272,256]{2,1,0:T(8,128)(2,1)} %get-tuple-element.94), calls=%async_computation | async-start | bytes 1114112 | tf_op jit(solution)/shard_map/all_to_all | solution.py:443
  109.0 1.3 collective-permute-start.23
  110.3 5.1 %collective-permute-start.20 = (bf16[512,384]{1,0:T(8,128)(2,1)S(1)}, bf16[512,384]{1,0:T(8,128)(2,1)S(1)}, u32[]{:S(2)}, u32[]{:S(2)}) collective-permute-start(bf16[512,384]{1,0:T(8,128)(2,1)S(1)} %get-tuple-element.108.refs_0_), channel_id=1, source_target_pairs={{0,8},{4,12},{8,0},{12,4},{1,9},{5,13},{9,1},{13,5},{2,10},{6,14},... | collective-permute-start | bytes 1179656 | tf_op jit(solution)/shard_map/ppermute | solution.py:432
  115.4 11.8 %collective-permute-done.23.refs_4_ = bf16[512,384]{1,0:T(8,128)(2,1)S(1)} collective-permute-done((bf16[512,384]{1,0:T(8,128)(2,1)S(1)}, bf16[512,384]{1,0:T(8,128)(2,1)S(1)}, u32[]{:S(2)}, u32[]{:S(2)}) %collective-permute-start.23) | collective-permute-done | bytes 393248 | tf_op jit(solution)/shard_map/ppermute | solution.py:439
  127.2 3.9 %weight_gradient_0_0.1 = (f32[576,1024]{1,0:T(8,128)}, f32[576,1024]{1,0:T(8,128)}, f32[576,1024]{1,0:T(8,128)}) custom-call(s32[11]{0:T(128)S(1)} %stack.48.where_ref, bf16[576,512]{1,0:T(8,128)(2,1)S(1)} %get-tuple-element.96.own_ref, bf16[512,384]{1,0:T(8,128)(2,1)S(1)} %get-tuple-element.102.refs_0_, ...), custom_call_target="tpu_custom_call" | custom-call | tf_op jit(solution)/shard_map/weight_gradient_0_0/pallas_call | solution.py:386
  131.2 17.0 %collective-permute-done.20.refs_2_ = bf16[512,384]{1,0:T(8,128)(2,1)S(1)} collective-permute-done((bf16[512,384]{1,0:T(8,128)(2,1)S(1)}, bf16[512,384]{1,0:T(8,128)(2,1)S(1)}, u32[]{:S(2)}, u32[]{:S(2)}) %collective-permute-start.20) | collective-permute-done | bytes 393248 | tf_op jit(solution)/shard_map/ppermute | solution.py:432
  148.8 1.3 collective-permute-start.25
  150.1 3.4 %weight_gradient_1_0.1 = (f32[576,1024]{1,0:T(8,128)}, f32[576,1024]{1,0:T(8,128)}, f32[576,1024]{1,0:T(8,128)}) custom-call(s32[11]{0:T(128)S(1)} %stack.48.where_ref, bf16[576,512]{1,0:T(8,128)(2,1)S(1)} %get-tuple-element.96.own_ref, bf16[512,384]{1,0:T(8,128)(2,1)S(1)} %get-tuple-element.108.refs_0_, ...), custom_call_target="tpu_custom_call", output_to_operand_aliasing={{0}: (5, {}), {1}: (6, {}), {2}: (7, {})} | custom-call | tf_op jit(solution)/shard_map/weight_gradient_1_0/pallas_call | solution.py:386
  154.4 6.3 %collective-permute-done.25.refs_1_ = bf16[512,384]{1,0:T(8,128)(2,1)S(1)} collective-permute-done((bf16[512,384]{1,0:T(8,128)(2,1)S(1)}, bf16[512,384]{1,0:T(8,128)(2,1)S(1)}, u32[]{:S(2)}, u32[]{:S(2)}) %collective-permute-start.25) | collective-permute-done | bytes 393248 | tf_op jit(solution)/shard_map/ppermute | solution.py:439
  160.8 1.9 %weight_gradient_1_3.1 = (f32[576,1024]{1,0:T(8,128)}, f32[576,1024]{1,0:T(8,128)}, f32[576,1024]{1,0:T(8,128)}) custom-call(s32[11]{0:T(128)S(1)} %stack.48.where_ref, bf16[576,512]{1,0:T(8,128)(2,1)S(1)} %get-tuple-element.96.own_ref, ...), custom_call_target="tpu_custom_call", output_to_operand_aliasing={{0}: (4, {}), {1}: (5, {}), {2}: (6, {})} | custom-call | tf_op jit(solution)/shard_map/weight_gradient_1_3/pallas_call | solution.py:386
  (53 shorter events, 15.3 us)
Async XLA Ops:
  0.8 1.1 copy-start.3
  2.4 14.8 %collective-permute-start = (bf16[576,128]{1,0:T(8,128)(2,1)S(1)}, bf16[576,128]{1,0:T(8,128)(2,1)S(1)}, u32[]{:S(2)}, u32[]{:S(2)}) collective-permute-start(bf16[576,128]{1,0:T(8,128)(2,1)S(1)} %pack_tokens.1), channel_id=1, source_target_pairs={{0,4},{4,8},{8,12},{12,0},{1,5},{5,9},{9,13},{13,1},{2,6},{6,10},{... | collective-permute-start | bytes 442376 | tf_op jit(solution)/shard_map/ppermute | solution.py:343
  5.5 12.4 %collective-permute-start.1 = (bf16[576,128]{1,0:T(8,128)(2,1)S(1)}, bf16[576,128]{1,0:T(8,128)(2,1)S(1)}, u32[]{:S(2)}, u32[]{:S(2)}) collective-permute-start(bf16[576,128]{1,0:T(8,128)(2,1)S(1)} %pack_tokens.1), channel_id=1, source_target_pairs={{0,8},{4,12},{8,0},{12,4},{1,9},{5,13},{9,1},{13,5},{2,10},{6,14},... | collective-permute-start | bytes 442376 | tf_op jit(solution)/shard_map/ppermute | solution.py:343
  8.1 9.8 %collective-permute-start.2 = (bf16[576,128]{1,0:T(8,128)(2,1)S(1)}, bf16[576,128]{1,0:T(8,128)(2,1)S(1)}, u32[]{:S(2)}, u32[]{:S(2)}) collective-permute-start(bf16[576,128]{1,0:T(8,128)(2,1)S(1)} %pack_tokens.1), channel_id=1, source_target_pairs={{0,12},{4,0},{8,4},{12,8},{1,13},{5,1},{9,5},{13,9},{2,14},{6,2},{... | collective-permute-start | bytes 442376 | tf_op jit(solution)/shard_map/ppermute | solution.py:343
  9.4 1.3 copy-start
  10.7 1.3 copy-start.1
  12.0 1.3 copy-start.2
  13.3 1.0 copy-start.4
  17.9 25.0 %collective-permute-start.3 = (bf16[2304,128]{1,0:T(8,128)(2,1)S(1)}, bf16[2304,128]{1,0:T(8,128)(2,1)S(1)}, u32[]{:S(2)}, u32[]{:S(2)}) collective-permute-start(bf16[2304,128]{1,0:T(8,128)(2,1)S(1)} %pad_maximum_fusion.refs_0_), channel_id=1, source_target_pairs={{0,2},{2,0},{1,3},{3,1},{4,6},{6,4},{5,7},{7,5},{8,10},{10,8},{9,1... | collective-permute-start | bytes 1769480 | tf_op jit(solution)/shard_map/ppermute | solution.py:343
  19.5 12.8 %collective-permute-start.6 = (bf16[384,384]{1,0:T(8,128)(2,1)S(1)}, bf16[384,384]{1,0:T(8,128)(2,1)S(1)}, u32[]{:S(2)}, u32[]{:S(2)}) collective-permute-start(bf16[384,384]{1,0:T(8,128)(2,1)S(1)} %get-tuple-element.70), channel_id=1, source_target_pairs={{0,4},{4,8},{8,12},{12,0},{1,5},{5,9},{9,13},{13,1},{2,6},{6,10},{... | collective-permute-start | bytes 884744 | tf_op jit(solution)/shard_map/ppermute | solution.py:343
  23.1 19.8 %collective-permute-start.4 = (bf16[384,384]{1,0:T(8,128)(2,1)S(1)}, bf16[384,384]{1,0:T(8,128)(2,1)S(1)}, u32[]{:S(2)}, u32[]{:S(2)}) collective-permute-start(bf16[384,384]{1,0:T(8,128)(2,1)S(1)} %get-tuple-element.68), channel_id=1, source_target_pairs={{0,8},{4,12},{8,0},{12,4},{1,9},{5,13},{9,1},{13,5},{2,10},{6,14},... | collective-permute-start | bytes 884744 | tf_op jit(solution)/shard_map/ppermute | solution.py:343
  24.7 18.2 %collective-permute-start.5 = (bf16[384,384]{1,0:T(8,128)(2,1)S(1)}, bf16[384,384]{1,0:T(8,128)(2,1)S(1)}, u32[]{:S(2)}, u32[]{:S(2)}) collective-permute-start(bf16[384,384]{1,0:T(8,128)(2,1)S(1)} %get-tuple-element.69), channel_id=1, source_target_pairs={{0,12},{4,0},{8,4},{12,8},{1,13},{5,1},{9,5},{13,9},{2,14},{6,2},{... | collective-permute-start | bytes 884744 | tf_op jit(solution)/shard_map/ppermute | solution.py:343
  32.3 10.6 %collective-permute-start.7 = (bf16[288,384]{1,0:T(8,128)(2,1)S(1)}, bf16[288,384]{1,0:T(8,128)(2,1)S(1)}, u32[]{:S(2)}, u32[]{:S(2)}) collective-permute-start(bf16[288,384]{1,0:T(8,128)(2,1)S(1)} %slice.24), channel_id=1, source_target_pairs={{0,16},{16,0},{1,17},{17,1},{2,18},{18,2},{3,19},{19,3},{4,20},{20... | collective-permute-start | bytes 663560 | tf_op jit(solution)/shard_map/ppermute | solution.py:343
  42.9 9.5 %collective-permute-start.8 = (bf16[2304,128]{1,0:T(8,128)(2,1)S(1)}, bf16[2304,128]{1,0:T(8,128)(2,1)S(1)}, u32[]{:S(2)}, u32[]{:S(2)}) collective-permute-start(bf16[2304,128]{1,0:T(8,128)(2,1)S(1)} %pad_maximum_fusion.refs_0_), channel_id=1, source_target_pairs={{0,1},{1,0},{2,3},{3,2},{4,5},{5,4},{6,7},{7,6},{8,9},{9,8},{10,11... | collective-permute-start | bytes 1769480 | tf_op jit(solution)/shard_map/ppermute | solution.py:343
  43.0 11.7 %collective-permute-start.9 = (bf16[2304,128]{1,0:T(8,128)(2,1)S(1)}, bf16[2304,128]{1,0:T(8,128)(2,1)S(1)}, u32[]{:S(2)}, u32[]{:S(2)}) collective-permute-start(bf16[2304,128]{1,0:T(8,128)(2,1)S(1)} %collective-permute-done.3.refs_1_), channel_id=1, source_target_pairs={{0,1},{1,0},{2,3},{3,2},{4,5},{5,4},{6,7},{7,6},{8,9},{9,8},{10,11... | collective-permute-start | bytes 1769480 | tf_op jit(solution)/shard_map/ppermute | solution.py:343
  43.5 12.6 %collective-permute-start.11 = (bf16[288,384]{1,0:T(8,128)(2,1)S(1)}, bf16[288,384]{1,0:T(8,128)(2,1)S(1)}, u32[]{:S(2)}, u32[]{:S(2)}) collective-permute-start(bf16[288,384]{1,0:T(8,128)(2,1)S(1)} %slice.19), channel_id=1, source_target_pairs={{0,16},{16,0},{1,17},{17,1},{2,18},{18,2},{3,19},{19,3},{4,20},{20... | collective-permute-start | bytes 663560 | tf_op jit(solution)/shard_map/ppermute | solution.py:343
  45.1 11.0 %collective-permute-start.12 = (bf16[288,384]{1,0:T(8,128)(2,1)S(1)}, bf16[288,384]{1,0:T(8,128)(2,1)S(1)}, u32[]{:S(2)}, u32[]{:S(2)}) collective-permute-start(bf16[288,384]{1,0:T(8,128)(2,1)S(1)} %slice.20), channel_id=1, source_target_pairs={{0,16},{16,0},{1,17},{17,1},{2,18},{18,2},{3,19},{19,3},{4,20},{20... | collective-permute-start | bytes 663560 | tf_op jit(solution)/shard_map/ppermute | solution.py:343
  45.7 19.0 %collective-permute-start.10 = (bf16[384,384]{1,0:T(8,128)(2,1)S(1)}, bf16[384,384]{1,0:T(8,128)(2,1)S(1)}, u32[]{:S(2)}, u32[]{:S(2)}) collective-permute-start(bf16[384,384]{1,0:T(8,128)(2,1)S(1)} %get-tuple-element.80), channel_id=1, source_target_pairs={{0,4},{4,8},{8,12},{12,0},{1,5},{5,9},{9,13},{13,1},{2,6},{6,10},{... | collective-permute-start | bytes 884744 | tf_op jit(solution)/shard_map/ppermute | solution.py:343
  52.4 21.2 %collective-permute-start.13 = (bf16[384,384]{1,0:T(8,128)(2,1)S(1)}, bf16[384,384]{1,0:T(8,128)(2,1)S(1)}, u32[]{:S(2)}, u32[]{:S(2)}) collective-permute-start(bf16[384,384]{1,0:T(8,128)(2,1)S(1)} %get-tuple-element.87), channel_id=1, source_target_pairs={{0,8},{4,12},{8,0},{12,4},{1,9},{5,13},{9,1},{13,5},{2,10},{6,14},... | collective-permute-start | bytes 884744 | tf_op jit(solution)/shard_map/ppermute | solution.py:343
  54.7 18.9 %collective-permute-start.14 = (bf16[384,384]{1,0:T(8,128)(2,1)S(1)}, bf16[384,384]{1,0:T(8,128)(2,1)S(1)}, u32[]{:S(2)}, u32[]{:S(2)}) collective-permute-start(bf16[384,384]{1,0:T(8,128)(2,1)S(1)} %get-tuple-element.90), channel_id=1, source_target_pairs={{0,12},{4,0},{8,4},{12,8},{1,13},{5,1},{9,5},{13,9},{2,14},{6,2},{... | collective-permute-start | bytes 884744 | tf_op jit(solution)/shard_map/ppermute | solution.py:343
  73.7 11.2 %collective-permute-start.17 = (bf16[288,384]{1,0:T(8,128)(2,1)S(1)}, bf16[288,384]{1,0:T(8,128)(2,1)S(1)}, u32[]{:S(2)}, u32[]{:S(2)}) collective-permute-start(bf16[288,384]{1,0:T(8,128)(2,1)S(1)} %slice.23), channel_id=1, source_target_pairs={{0,16},{16,0},{1,17},{17,1},{2,18},{18,2},{3,19},{19,3},{4,20},{20... | collective-permute-start | bytes 663560 | tf_op jit(solution)/shard_map/ppermute | solution.py:343
  75.2 11.5 %collective-permute-start.16 = (bf16[288,384]{1,0:T(8,128)(2,1)S(1)}, bf16[288,384]{1,0:T(8,128)(2,1)S(1)}, u32[]{:S(2)}, u32[]{:S(2)}) collective-permute-start(bf16[288,384]{1,0:T(8,128)(2,1)S(1)} %slice.22), channel_id=1, source_target_pairs={{0,16},{16,0},{1,17},{17,1},{2,18},{18,2},{3,19},{19,3},{4,20},{20... | collective-permute-start | bytes 663560 | tf_op jit(solution)/shard_map/ppermute | solution.py:343
  75.9 14.6 %collective-permute-start.15 = (bf16[288,384]{1,0:T(8,128)(2,1)S(1)}, bf16[288,384]{1,0:T(8,128)(2,1)S(1)}, u32[]{:S(2)}, u32[]{:S(2)}) collective-permute-start(bf16[288,384]{1,0:T(8,128)(2,1)S(1)} %slice.21), channel_id=1, source_target_pairs={{0,16},{16,0},{1,17},{17,1},{2,18},{18,2},{3,19},{19,3},{4,20},{20... | collective-permute-start | bytes 663560 | tf_op jit(solution)/shard_map/ppermute | solution.py:343
  77.4 30.9 %collective-permute-start.18 = (bf16[512,384]{1,0:T(8,128)(2,1)S(1)}, bf16[512,384]{1,0:T(8,128)(2,1)S(1)}, u32[]{:S(2)}, u32[]{:S(2)}) collective-permute-start(bf16[512,384]{1,0:T(8,128)(2,1)S(1)} %get-tuple-element.102.refs_0_), channel_id=1, source_target_pairs={{0,8},{4,12},{8,0},{12,4},{1,9},{5,13},{9,1},{13,5},{2,10},{6,14},... | collective-permute-start | bytes 1179656 | tf_op jit(solution)/shard_map/ppermute | solution.py:432
  83.2 25.1 %collective-permute-start.19 = (bf16[512,384]{1,0:T(8,128)(2,1)S(1)}, bf16[512,384]{1,0:T(8,128)(2,1)S(1)}, u32[]{:S(2)}, u32[]{:S(2)}) collective-permute-start(bf16[512,384]{1,0:T(8,128)(2,1)S(1)} %get-tuple-element.102.refs_0_), channel_id=1, source_target_pairs={{0,4},{4,0},{8,12},{12,8},{1,5},{5,1},{9,13},{13,9},{2,6},{6,2},{1... | collective-permute-start | bytes 1179656 | tf_op jit(solution)/shard_map/ppermute | solution.py:433
  100.2 53.3 %all-to-all-start = ((bf16[4,272,256]{2,1,0:T(8,128)(2,1)}), bf16[4,272,256]{2,1,0:T(8,128)(2,1)S(1)}, u32[]{:S(2)}, u32[]{:S(2)}) async-start(bf16[4,272,256]{2,1,0:T(8,128)(2,1)} %get-tuple-element.94), calls=%async_computation | async-start | bytes 1114112 | tf_op jit(solution)/shard_map/all_to_all | solution.py:443
  108.3 7.1 %collective-permute-start.22 = (bf16[512,384]{1,0:T(8,128)(2,1)S(1)}, bf16[512,384]{1,0:T(8,128)(2,1)S(1)}, u32[]{:S(2)}, u32[]{:S(2)}) collective-permute-start(bf16[512,384]{1,0:T(8,128)(2,1)S(1)} %get-tuple-element.102.refs_0_), channel_id=1, source_target_pairs={{4,8},{8,4},{5,9},{9,5},{6,10},{10,6},{7,11},{11,7},{20,24},{24,20... | collective-permute-start | bytes 1179656 | tf_op jit(solution)/shard_map/ppermute | solution.py:438
  109.0 18.2 %collective-permute-start.23 = (bf16[512,384]{1,0:T(8,128)(2,1)S(1)}, bf16[512,384]{1,0:T(8,128)(2,1)S(1)}, u32[]{:S(2)}, u32[]{:S(2)}) collective-permute-start(bf16[512,384]{1,0:T(8,128)(2,1)S(1)} %collective-permute-done.18.refs_2_), channel_id=1, source_target_pairs={{8,12},{4,0},{9,13},{5,1},{10,14},{6,2},{11,15},{7,3},{24,28},{20,... | collective-permute-start | bytes 1179656 | tf_op jit(solution)/shard_map/ppermute | solution.py:439
  110.3 37.8 %collective-permute-start.20 = (bf16[512,384]{1,0:T(8,128)(2,1)S(1)}, bf16[512,384]{1,0:T(8,128)(2,1)S(1)}, u32[]{:S(2)}, u32[]{:S(2)}) collective-permute-start(bf16[512,384]{1,0:T(8,128)(2,1)S(1)} %get-tuple-element.108.refs_0_), channel_id=1, source_target_pairs={{0,8},{4,12},{8,0},{12,4},{1,9},{5,13},{9,1},{13,5},{2,10},{6,14},... | collective-permute-start | bytes 1179656 | tf_op jit(solution)/shard_map/ppermute | solution.py:432
  115.4 32.7 %collective-permute-start.21 = (bf16[512,384]{1,0:T(8,128)(2,1)S(1)}, bf16[512,384]{1,0:T(8,128)(2,1)S(1)}, u32[]{:S(2)}, u32[]{:S(2)}) collective-permute-start(bf16[512,384]{1,0:T(8,128)(2,1)S(1)} %get-tuple-element.108.refs_0_), channel_id=1, source_target_pairs={{0,4},{4,0},{8,12},{12,8},{1,5},{5,1},{9,13},{13,9},{2,6},{6,2},{1... | collective-permute-start | bytes 1179656 | tf_op jit(solution)/shard_map/ppermute | solution.py:433
  148.1 6.3 %collective-permute-start.24 = (bf16[512,384]{1,0:T(8,128)(2,1)S(1)}, bf16[512,384]{1,0:T(8,128)(2,1)S(1)}, u32[]{:S(2)}, u32[]{:S(2)}) collective-permute-start(bf16[512,384]{1,0:T(8,128)(2,1)S(1)} %get-tuple-element.108.refs_0_), channel_id=1, source_target_pairs={{4,8},{8,4},{5,9},{9,5},{6,10},{10,6},{7,11},{11,7},{20,24},{24,20... | collective-permute-start | bytes 1179656 | tf_op jit(solution)/shard_map/ppermute | solution.py:438
  148.8 12.0 %collective-permute-start.25 = (bf16[512,384]{1,0:T(8,128)(2,1)S(1)}, bf16[512,384]{1,0:T(8,128)(2,1)S(1)}, u32[]{:S(2)}, u32[]{:S(2)}) collective-permute-start(bf16[512,384]{1,0:T(8,128)(2,1)S(1)} %collective-permute-done.20.refs_2_), channel_id=1, source_target_pairs={{8,12},{4,0},{9,13},{5,1},{10,14},{6,2},{11,15},{7,3},{24,28},{20,... | collective-permute-start | bytes 1179656 | tf_op jit(solution)/shard_map/ppermute | solution.py:439
  (2 other events, 1.6 us)

commit v10 on v9

--- a/solution.py
+++ b/solution.py
@@ -241,12 +241,10 @@
             out[size + 80 : size + 96, 2 * DK : 3 * DK] = jnp.zeros((16, DK), out.dtype)
 
 
-def head_kernel(ctx, slot, where_ref, *refs):
+def head_kernel(ctx, where_ref, *refs):
     all_ref, refs = refs[0], refs[1:]
     direct, refs = refs[:ctx], refs[ctx:]
     swapped, refs = refs[: ctx - 1], refs[ctx - 1 :]
-    if slot:
-        earlier_ref, refs = refs[0], refs[1:]
     grad_ref, back_ref, w, raw, decay, cot, logit, out, dlogit, ddecay = refs
     place, group = where_ref[0], where_ref[1]
     share = direct[0].shape[0] - EXTRA
@@ -275,13 +273,10 @@
         )
     raw[...] = projected
     recurrence(raw, decay, logit, cot, out, grad_ref, dlogit, ddecay)
-    lane = slice(slot * DK, (slot + 1) * DK)
-    if slot:
-        back_ref[:, :, 0:DK] = earlier_ref[...]
     for n in range(ctx):
-        back_ref[n, 0:CHUNK, lane] = out[n]
-        back_ref[n, CHUNK : 2 * CHUNK, lane] = ddecay[n]
-        back_ref[n, 2 * CHUNK :, lane] = tail_rows(dlogit[n : n + 1, :])
+        back_ref[n, 0:CHUNK, :] = out[n]
+        back_ref[n, CHUNK : 2 * CHUNK, :] = ddecay[n]
+        back_ref[n, 2 * CHUNK :, :] = tail_rows(dlogit[n : n + 1, :])
 
 
 def weight_gradient_kernel(steps, where_ref, own_ref, *refs):
@@ -302,15 +297,15 @@
                 block(jnp.where(where_ref[10] == 1, refs[at + 1][...], refs[at][...]))
 
 
-def unpack_kernel(back_ref, out_ref, dlogit_ref, ddecay_ref):
-    for source in range(back_ref.shape[0]):
-        column = slice(2 * source * DK, 2 * (source + 1) * DK)
-        out_ref[:, column] = back_ref[source, 0:CHUNK, :]
-        ddecay_ref[:, column] = back_ref[source, CHUNK : 2 * CHUNK, :].astype(jnp.float32)
-        tail = back_ref[source, 2 * CHUNK :, :].astype(jnp.float32)
-        row = tail[0:1] + tail[1:2]
-        for s in range(2):
-            dlogit_ref[2 * source + s : 2 * source + s + 1, :] = row[:, s * DK : (s + 1) * DK]
+def unpack_kernel(first_ref, second_ref, out_ref, dlogit_ref, ddecay_ref):
+    for source in range(first_ref.shape[0]):
+        for s, ref in enumerate((first_ref, second_ref)):
+            head = 2 * source + s
+            column = slice(head * DK, (head + 1) * DK)
+            out_ref[:, column] = ref[source, 0:CHUNK, :]
+            ddecay_ref[:, column] = ref[source, CHUNK : 2 * CHUNK, :].astype(jnp.float32)
+            tail = ref[source, 2 * CHUNK :, :].astype(jnp.float32)
+            dlogit_ref[head : head + 1, :] = tail[0:1] + tail[1:2]
 
 
 def head_split(tokens, w_query, w_key, w_value, beta_logit, log_decay, grad_out):
@@ -397,21 +392,17 @@
             name=f"weight_gradient_{slot}_{steps[0]}",
         )(where, own, *parts, *results)
 
-    grads = []
-    back = None
+    grads, backs = [], []
     for slot, direct in enumerate((first, second)):
         if slot:
-            for d in range(ctx - 1):
-                direct[d], back = after(direct[d], back)
             swapped = [along(x[:half], "groups", 1) for x in direct]
-        earlier = [] if back is None else [back]
         grad, back = pl.pallas_call(
-            functools.partial(head_kernel, ctx, slot),
+            functools.partial(head_kernel, ctx),
             out_shape=[
                 shape((total, HEAD_COLUMNS), bf16),
-                shape((ctx, 2 * CHUNK + TAIL, (slot + 1) * DK), bf16),
+                shape((ctx, 2 * CHUNK + TAIL, DK), bf16),
             ],
-            in_specs=[scalars] + [whole] * (1 + ctx + ctx - 1 + slot),
+            in_specs=[scalars] + [whole] * (1 + ctx + ctx - 1),
             out_specs=[whole] * 2,
             scratch_shapes=[
                 pltpu.VMEM((depth, HEAD_COLUMNS), bf16),
@@ -426,9 +417,12 @@
             cost_estimate=pl.CostEstimate(flops=FLOPS[slot], transcendentals=0, bytes_accessed=FLOPS[slot] // 1000),
             compiler_params=pltpu.CompilerParams(vmem_limit_bytes=VMEM_LIMIT),
             name=f"head_{slot}",
-        )(where, all_tokens, packed[slot * ctx], *direct, *swapped, *earlier)
+        )(where, all_tokens, packed[slot * ctx], *direct, *swapped)
+        if not slot:
+            second[:], (grad, back) = after(second, (grad, back))
+        backs.append(lax.all_to_all(back, "ctx", 0, 0))
         if slot:
-            grad, grads[0][1:3] = after(grad, grads[0][1:3])
+            grad, (grads[0][1:3], backs[0]) = after(grad, (grads[0][1:3], backs[0]))
         two = lax.ppermute(grad, "ctx", [(0, 2), (1, 3), (2, 0), (3, 1)])
         pair = lax.ppermute(grad, "ctx", [(0, 1), (1, 0), (2, 3), (3, 2)])
         results = ()
@@ -440,16 +434,15 @@
         grads.append([grad, pair, two, middle, far])
     results = products(1, (0, 1, 2), grads[1][:3], results)
     results = products(1, (3,), grads[1][3:], results)
-    back = lax.all_to_all(back, "ctx", 0, 0)
 
     attn_out, grad_beta, grad_decay = pl.pallas_call(
         unpack_kernel,
         out_shape=[shape((length, columns), bf16), shape((columns // DK, length), f32), shape((length, columns), f32)],
-        in_specs=[whole],
+        in_specs=[whole] * 2,
         out_specs=[whole] * 3,
         compiler_params=pltpu.CompilerParams(vmem_limit_bytes=VMEM_LIMIT),
         name="unpack",
-    )(back)
+    )(*backs)
     return (attn_out, *results, grad_beta, grad_decay)
 
 

time: 163 us -> 158 us (0.969)
  waiting for transfers between devices: 66.2 us -> 49.1 us
  local copies, waits for them, and re-layouts: 7.78 us -> 14.9 us
  starting transfers between devices: 56.2 us -> 59.8 us
    ppermute x2, waiting for transfers between devices: 18.2 us -> 7.77 us  [head_split(): far = lax.ppermute(two, 'ctx', [(2, 3), (1, 0)])]
    ppermute x18, waiting for transfers between devices: 31 us -> 25.1 us  [along(): return lax.ppermute(x, axis, [(i, (i + hop) % count) for i in range(count)])]
    unnamed x14 -> x28, local copies, waits for them, and re-layouts: 7.55 us -> 12.7 us
    ppermute x2, starting transfers between devices: 10.9 us -> 15 us  [head_split(): two = lax.ppermute(grad, 'ctx', [(0, 2), (1, 3), (2, 0), (3, 1)])]
    ppermute x2, waiting for transfers between devices: 17 us -> 14.9 us  [head_split(): two = lax.ppermute(grad, 'ctx', [(0, 2), (1, 3), (2, 0), (3, 1)])]
    slice x3, local copies, waits for them, and re-layouts: 0.07 us -> 2.12 us  [head_split(): swapped = [along(x[:half], 'groups', 1) for x in direct]]
    all_to_all x1 -> x2, starting transfers between devices: 8.15 us -> 7.08 us  [head_split(): backs.append(lax.all_to_all(back, 'ctx', 0, 0))]
  transfers between devices with their start and end apart: 27 -> 28, of which waited for: 9 -> 10; matrix products, arithmetic and copies ran while one was open for 0% -> 1% of each run, Pallas kernels for 18% -> 19%
where the time goes in v10:
time: 158 us
  starting transfers between devices  59.8 us (38%)
  waiting for transfers between devices  49.1 us (31%)
  Pallas kernels  32.9 us (21%)
  local copies, waits for them, and re-layouts  14.9 us (9%)
    ppermute x18, starting transfers between devices, along(): return lax.ppermute(x, axis, [(i, (i + hop) % count) for i in range(count)])  31.5 us
    ppermute x18, waiting for transfers between devices, along(): return lax.ppermute(x, axis, [(i, (i + hop) % count) for i in range(count)])  25.1 us
    pallas_call x2, Pallas kernels, head_split(): pl.pallas_call(functools.partial(head_kernel, ctx), out_shape=[shape((tot...  18.5 us
    ppermute x2, starting transfers between devices, head_split(): two = lax.ppermute(grad, 'ctx', [(0, 2), (1, 3), (2, 0), (3, 1)])  15 us
    ppermute x2, waiting for transfers between devices, head_split(): two = lax.ppermute(grad, 'ctx', [(0, 2), (1, 3), (2, 0), (3, 1)])  14.9 us
    unnamed x28, local copies, waits for them, and re-layouts  12.7 us
    pallas_call x3, Pallas kernels, products(): pl.pallas_call(functools.partial(weight_gradient_kernel, steps), grid_spe...  10.3 us
    ppermute x2, waiting for transfers between devices, head_split(): far = lax.ppermute(two, 'ctx', [(2, 3), (1, 0)])  7.77 us
  transfers between devices with their start and end apart: 28, of which 10 were waited for; matrix products, arithmetic and copies ran while one was open for 1% of the time, Pallas kernels for 19%

profile of v10, /device:TPU:0, one launch (start us, length us, event | category | flops | bytes accessed | tf_op | source)
XLA Modules:
  0.0 157.7 jit_solution(9904006316327850885)
XLA Ops:
  2.4 3.1 %collective-permute-start = (bf16[576,128]{1,0:T(8,128)(2,1)S(1)}, bf16[576,128]{1,0:T(8,128)(2,1)S(1)}, u32[]{:S(2)}, u32[]{:S(2)}) collective-permute-start(bf16[576,128]{1,0:T(8,128)(2,1)S(1)} %pack_tokens.1), channel_id=1, source_target_pairs={{0,4},{4,8},{8,12},{12,0},{1,5},{5,9},{9,13},{13,1},{2,6},{6,10},{... | collective-permute-start | bytes 442376 | tf_op jit(solution)/shard_map/ppermute | solution.py:338
  5.5 2.6 %collective-permute-start.1 = (bf16[576,128]{1,0:T(8,128)(2,1)S(1)}, bf16[576,128]{1,0:T(8,128)(2,1)S(1)}, u32[]{:S(2)}, u32[]{:S(2)}) collective-permute-start(bf16[576,128]{1,0:T(8,128)(2,1)S(1)} %pack_tokens.1), channel_id=1, source_target_pairs={{0,8},{4,12},{8,0},{12,4},{1,9},{5,13},{9,1},{13,5},{2,10},{6,14},... | collective-permute-start | bytes 442376 | tf_op jit(solution)/shard_map/ppermute | solution.py:338
  8.1 1.3 collective-permute-start.2
  17.9 1.6 collective-permute-start.3
  19.5 3.6 %collective-permute-start.6 = (bf16[384,384]{1,0:T(8,128)(2,1)S(1)}, bf16[384,384]{1,0:T(8,128)(2,1)S(1)}, u32[]{:S(2)}, u32[]{:S(2)}) collective-permute-start(bf16[384,384]{1,0:T(8,128)(2,1)S(1)} %get-tuple-element.70), channel_id=1, source_target_pairs={{0,4},{4,8},{8,12},{12,0},{1,5},{5,9},{9,13},{13,1},{2,6},{6,10},{... | collective-permute-start | bytes 884744 | tf_op jit(solution)/shard_map/ppermute | solution.py:338
  23.1 1.6 %collective-permute-start.4 = (bf16[384,384]{1,0:T(8,128)(2,1)S(1)}, bf16[384,384]{1,0:T(8,128)(2,1)S(1)}, u32[]{:S(2)}, u32[]{:S(2)}) collective-permute-start(bf16[384,384]{1,0:T(8,128)(2,1)S(1)} %get-tuple-element.68), channel_id=1, source_target_pairs={{0,8},{4,12},{8,0},{12,4},{1,9},{5,13},{9,1},{13,5},{2,10},{6,14},... | collective-permute-start | bytes 884744 | tf_op jit(solution)/shard_map/ppermute | solution.py:338
  25.5 6.8 %collective-permute-done.6.refs_2_ = bf16[384,384]{1,0:T(8,128)(2,1)S(1)} collective-permute-done((bf16[384,384]{1,0:T(8,128)(2,1)S(1)}, bf16[384,384]{1,0:T(8,128)(2,1)S(1)}, u32[]{:S(2)}, u32[]{:S(2)}) %collective-permute-start.6) | collective-permute-done | bytes 294944 | tf_op jit(solution)/shard_map/ppermute | solution.py:338
  32.3 1.6 %collective-permute-start.7 = (bf16[288,384]{1,0:T(8,128)(2,1)S(1)}, bf16[288,384]{1,0:T(8,128)(2,1)S(1)}, u32[]{:S(2)}, u32[]{:S(2)}) collective-permute-start(bf16[288,384]{1,0:T(8,128)(2,1)S(1)} %slice.24), channel_id=1, source_target_pairs={{0,16},{16,0},{1,17},{17,1},{2,18},{18,2},{3,19},{19,3},{4,20},{20... | collective-permute-start | bytes 663560 | tf_op jit(solution)/shard_map/ppermute | solution.py:338
  33.9 9.1 %collective-permute-done.4.refs_3_ = bf16[384,384]{1,0:T(8,128)(2,1)S(1)} collective-permute-done((bf16[384,384]{1,0:T(8,128)(2,1)S(1)}, bf16[384,384]{1,0:T(8,128)(2,1)S(1)}, u32[]{:S(2)}, u32[]{:S(2)}) %collective-permute-start.4) | collective-permute-done | bytes 294944 | tf_op jit(solution)/shard_map/ppermute | solution.py:338
  43.5 1.6 %collective-permute-start.13 = (bf16[288,384]{1,0:T(8,128)(2,1)S(1)}, bf16[288,384]{1,0:T(8,128)(2,1)S(1)}, u32[]{:S(2)}, u32[]{:S(2)}) collective-permute-start(bf16[288,384]{1,0:T(8,128)(2,1)S(1)} %slice.19), channel_id=1, source_target_pairs={{0,16},{16,0},{1,17},{17,1},{2,18},{18,2},{3,19},{19,3},{4,20},{20... | collective-permute-start | bytes 663560 | tf_op jit(solution)/shard_map/ppermute | solution.py:338
  45.7 6.7 %collective-permute-start.10 = (bf16[384,384]{1,0:T(8,128)(2,1)S(1)}, bf16[384,384]{1,0:T(8,128)(2,1)S(1)}, u32[]{:S(2)}, u32[]{:S(2)}) collective-permute-start(bf16[384,384]{1,0:T(8,128)(2,1)S(1)} %get-tuple-element.80), channel_id=1, source_target_pairs={{0,4},{4,8},{8,12},{12,0},{1,5},{5,9},{9,13},{13,1},{2,6},{6,10},{... | collective-permute-start | bytes 884744 | tf_op jit(solution)/shard_map/ppermute | solution.py:338
  52.4 2.3 %collective-permute-start.11 = (bf16[384,384]{1,0:T(8,128)(2,1)S(1)}, bf16[384,384]{1,0:T(8,128)(2,1)S(1)}, u32[]{:S(2)}, u32[]{:S(2)}) collective-permute-start(bf16[384,384]{1,0:T(8,128)(2,1)S(1)} %get-tuple-element.81), channel_id=1, source_target_pairs={{0,8},{4,12},{8,0},{12,4},{1,9},{5,13},{9,1},{13,5},{2,10},{6,14},... | collective-permute-start | bytes 884744 | tf_op jit(solution)/shard_map/ppermute | solution.py:338
  56.1 9.3 %head_0.1 = (bf16[512,384]{1,0:T(8,128)(2,1)S(1)}, bf16[4,272,128]{2,1,0:T(8,128)(2,1)}) custom-call(s32[11]{0:T(128)S(1)} %stack.48.where_ref, bf16[4,512,576]{2,1,0:T(8,128)(2,1)S(1)} %get-tuple-element.73.refs_0_, bf16[672,384]{1,0:T(8,128)(2,1)S(1)} %get-tuple-element.83.refs_1_, bf16[384,384]{1,0:T(8,128)(2,1)S(1)} %collective-permute-done.6.refs_2_, ...), custom_call_target="tpu_custom_call" | custom-call | flops 12000000000 | bytes 12000000 | tf_op jit(solution)/shard_map/head_0/pallas_call | solution.py:399
  65.5 8.2 %collective-permute-done.11.refs_3_ = bf16[384,384]{1,0:T(8,128)(2,1)S(1)} collective-permute-done((bf16[384,384]{1,0:T(8,128)(2,1)S(1)}, bf16[384,384]{1,0:T(8,128)(2,1)S(1)}, u32[]{:S(2)}, u32[]{:S(2)}) %collective-permute-start.11) | collective-permute-done | bytes 294944 | tf_op jit(solution)/shard_map/ppermute | solution.py:338
  74.3 1.5 collective-permute-start.15
  77.8 1.5 collective-permute-start.17
  79.3 5.8 %collective-permute-start.18 = (bf16[512,384]{1,0:T(8,128)(2,1)S(1)}, bf16[512,384]{1,0:T(8,128)(2,1)S(1)}, u32[]{:S(2)}, u32[]{:S(2)}) collective-permute-start(bf16[512,384]{1,0:T(8,128)(2,1)S(1)} %get-tuple-element.102.refs_0_), channel_id=1, source_target_pairs={{0,8},{4,12},{8,0},{12,4},{1,9},{5,13},{9,1},{13,5},{2,10},{6,14},... | collective-permute-start | bytes 1179656 | tf_op jit(solution)/shard_map/ppermute | solution.py:426
  85.0 1.6 %collective-permute-start.19 = (bf16[512,384]{1,0:T(8,128)(2,1)S(1)}, bf16[512,384]{1,0:T(8,128)(2,1)S(1)}, u32[]{:S(2)}, u32[]{:S(2)}) collective-permute-start(bf16[512,384]{1,0:T(8,128)(2,1)S(1)} %get-tuple-element.102.refs_0_), channel_id=1, source_target_pairs={{0,4},{4,0},{8,12},{12,8},{1,5},{5,1},{9,13},{13,9},{2,6},{6,2},{1... | collective-permute-start | bytes 1179656 | tf_op jit(solution)/shard_map/ppermute | solution.py:427
  86.7 3.6 %all-to-all-start = ((bf16[4,272,128]{2,1,0:T(8,128)(2,1)}), bf16[4,272,128]{2,1,0:T(8,128)(2,1)S(1)}, u32[]{:S(2)}, u32[]{:S(2)}) async-start(bf16[4,272,128]{2,1,0:T(8,128)(2,1)} %get-tuple-element.96), calls=%async_computation | async-start | bytes 557056 | tf_op jit(solution)/shard_map/all_to_all | solution.py:423
  91.4 1.7 %copy-done.9 = bf16[4,512,576]{2,1,0:T(8,128)(2,1)S(1)} copy-done((bf16[4,512,576]{2,1,0:T(8,128)(2,1)S(1)}, bf16[4,512,576]{2,1,0:T(8,128)(2,1)}, u32[]{:S(2)}) %copy-start.9) | copy-done | bytes 2359320
  95.1 9.1 %head_1.1 = (bf16[512,384]{1,0:T(8,128)(2,1)S(1)}, bf16[4,272,128]{2,1,0:T(8,128)(2,1)S(1)}) custom-call(s32[11]{0:T(128)S(1)} %stack.48.where_ref, bf16[4,512,576]{2,1,0:T(8,128)(2,1)S(1)} %copy-done.9, bf16[672,384]{1,0:T(8,128)(2,1)S(1)} %copy-done.11, bf16[384,384]{1,0:T(8,128)(2,1)S(1)} %collective-permute-done.10.refs_2_, ...), custom_call_target="tpu_custom_call" | custom-call | flops 12000000000 | bytes 12000000 | tf_op jit(solution)/shard_map/head_1/pallas_call | solution.py:399
  105.0 1.4 collective-permute-start.22
  106.4 1.3 collective-permute-start.23
  108.1 9.2 %collective-permute-start.20 = (bf16[512,384]{1,0:T(8,128)(2,1)S(1)}, bf16[512,384]{1,0:T(8,128)(2,1)S(1)}, u32[]{:S(2)}, u32[]{:S(2)}) collective-permute-start(bf16[512,384]{1,0:T(8,128)(2,1)S(1)} %get-tuple-element.108.refs_0_), channel_id=1, source_target_pairs={{0,8},{4,12},{8,0},{12,4},{1,9},{5,13},{9,1},{13,5},{2,10},{6,14},... | collective-permute-start | bytes 1179656 | tf_op jit(solution)/shard_map/ppermute | solution.py:426
  117.3 3.5 %all-to-all-start.1 = ((bf16[4,272,128]{2,1,0:T(8,128)(2,1)}), bf16[4,272,128]{2,1,0:T(8,128)(2,1)S(1)}, u32[]{:S(2)}, u32[]{:S(2)}) async-start(bf16[4,272,128]{2,1,0:T(8,128)(2,1)} %copy-done.5), calls=%async_computation.1 | async-start | bytes 557056 | tf_op jit(solution)/shard_map/all_to_all | solution.py:423
  120.8 4.4 %collective-permute-done.23.refs_4_ = bf16[512,384]{1,0:T(8,128)(2,1)} collective-permute-done((bf16[512,384]{1,0:T(8,128)(2,1)S(1)}, bf16[512,384]{1,0:T(8,128)(2,1)}, u32[]{:S(2)}, u32[]{:S(2)}) %collective-permute-start.23) | collective-permute-done | bytes 393248 | tf_op jit(solution)/shard_map/ppermute | solution.py:433
  125.2 5.0 %weight_gradient_0_0.1 = (f32[576,1024]{1,0:T(8,128)}, f32[576,1024]{1,0:T(8,128)}, f32[576,1024]{1,0:T(8,128)}) custom-call(s32[11]{0:T(128)S(1)} %stack.48.where_ref, bf16[576,512]{1,0:T(8,128)(2,1)S(1)} %get-tuple-element.100.own_ref, bf16[512,384]{1,0:T(8,128)(2,1)S(1)} %get-tuple-element.102.refs_0_, ...), custom_call_target="tpu_custom_call" | custom-call | tf_op jit(solution)/shard_map/weight_gradient_0_0/pallas_call | solution.py:381
  130.2 14.9 %collective-permute-done.20.refs_2_ = bf16[512,384]{1,0:T(8,128)(2,1)S(1)} collective-permute-done((bf16[512,384]{1,0:T(8,128)(2,1)S(1)}, bf16[512,384]{1,0:T(8,128)(2,1)S(1)}, u32[]{:S(2)}, u32[]{:S(2)}) %collective-permute-start.20) | collective-permute-done | bytes 393248 | tf_op jit(solution)/shard_map/ppermute | solution.py:426
  145.8 1.3 collective-permute-start.25
  149.1 3.4 %weight_gradient_1_0.1 = (f32[576,1024]{1,0:T(8,128)}, f32[576,1024]{1,0:T(8,128)}, f32[576,1024]{1,0:T(8,128)}) custom-call(s32[11]{0:T(128)S(1)} %stack.48.where_ref, bf16[576,512]{1,0:T(8,128)(2,1)S(1)} %get-tuple-element.100.own_ref, bf16[512,384]{1,0:T(8,128)(2,1)S(1)} %get-tuple-element.108.refs_0_, ...), custom_call_target="tpu_custom_call", output_to_operand_aliasing={{0}: (5, {}), {1}: (6, {}), {2}: (7, {})} | custom-call | tf_op jit(solution)/shard_map/weight_gradient_1_0/pallas_call | solution.py:381
  152.4 3.4 %collective-permute-done.25.refs_1_ = bf16[512,384]{1,0:T(8,128)(2,1)S(1)} collective-permute-done((bf16[512,384]{1,0:T(8,128)(2,1)S(1)}, bf16[512,384]{1,0:T(8,128)(2,1)S(1)}, u32[]{:S(2)}, u32[]{:S(2)}) %collective-permute-start.25) | collective-permute-done | bytes 393248 | tf_op jit(solution)/shard_map/ppermute | solution.py:433
  155.8 1.9 %weight_gradient_1_3.1 = (f32[576,1024]{1,0:T(8,128)}, f32[576,1024]{1,0:T(8,128)}, f32[576,1024]{1,0:T(8,128)}) custom-call(s32[11]{0:T(128)S(1)} %stack.48.where_ref, bf16[576,512]{1,0:T(8,128)(2,1)S(1)} %get-tuple-element.100.own_ref, ...), custom_call_target="tpu_custom_call", output_to_operand_aliasing={{0}: (4, {}), {1}: (5, {}), {2}: (6, {})} | custom-call | tf_op jit(solution)/shard_map/weight_gradient_1_3/pallas_call | solution.py:381
  (69 shorter events, 23.0 us)
Async XLA Ops:
  2.4 14.8 %collective-permute-start = (bf16[576,128]{1,0:T(8,128)(2,1)S(1)}, bf16[576,128]{1,0:T(8,128)(2,1)S(1)}, u32[]{:S(2)}, u32[]{:S(2)}) collective-permute-start(bf16[576,128]{1,0:T(8,128)(2,1)S(1)} %pack_tokens.1), channel_id=1, source_target_pairs={{0,4},{4,8},{8,12},{12,0},{1,5},{5,9},{9,13},{13,1},{2,6},{6,10},{... | collective-permute-start | bytes 442376 | tf_op jit(solution)/shard_map/ppermute | solution.py:338
  5.5 12.4 %collective-permute-start.1 = (bf16[576,128]{1,0:T(8,128)(2,1)S(1)}, bf16[576,128]{1,0:T(8,128)(2,1)S(1)}, u32[]{:S(2)}, u32[]{:S(2)}) collective-permute-start(bf16[576,128]{1,0:T(8,128)(2,1)S(1)} %pack_tokens.1), channel_id=1, source_target_pairs={{0,8},{4,12},{8,0},{12,4},{1,9},{5,13},{9,1},{13,5},{2,10},{6,14},... | collective-permute-start | bytes 442376 | tf_op jit(solution)/shard_map/ppermute | solution.py:338
  8.1 9.8 %collective-permute-start.2 = (bf16[576,128]{1,0:T(8,128)(2,1)S(1)}, bf16[576,128]{1,0:T(8,128)(2,1)S(1)}, u32[]{:S(2)}, u32[]{:S(2)}) collective-permute-start(bf16[576,128]{1,0:T(8,128)(2,1)S(1)} %pack_tokens.1), channel_id=1, source_target_pairs={{0,12},{4,0},{8,4},{12,8},{1,13},{5,1},{9,5},{13,9},{2,14},{6,2},{... | collective-permute-start | bytes 442376 | tf_op jit(solution)/shard_map/ppermute | solution.py:338
  12.0 1.3 copy-start.2
  17.2 37.5 %copy-start.10 = (bf16[672,384]{1,0:T(8,128)(2,1)}, bf16[672,384]{1,0:T(8,128)(2,1)S(1)}, u32[]{:S(2)}) copy-start(bf16[672,384]{1,0:T(8,128)(2,1)S(1)} %get-tuple-element.74.refs_1_) | copy-start | bytes 1548292
  17.9 25.0 %collective-permute-start.3 = (bf16[2304,128]{1,0:T(8,128)(2,1)S(1)}, bf16[2304,128]{1,0:T(8,128)(2,1)S(1)}, u32[]{:S(2)}, u32[]{:S(2)}) collective-permute-start(bf16[2304,128]{1,0:T(8,128)(2,1)S(1)} %pad_maximum_fusion.refs_0_), channel_id=1, source_target_pairs={{0,2},{2,0},{1,3},{3,1},{4,6},{6,4},{5,7},{7,5},{8,10},{10,8},{9,1... | collective-permute-start | bytes 1769480 | tf_op jit(solution)/shard_map/ppermute | solution.py:338
  19.5 12.8 %collective-permute-start.6 = (bf16[384,384]{1,0:T(8,128)(2,1)S(1)}, bf16[384,384]{1,0:T(8,128)(2,1)S(1)}, u32[]{:S(2)}, u32[]{:S(2)}) collective-permute-start(bf16[384,384]{1,0:T(8,128)(2,1)S(1)} %get-tuple-element.70), channel_id=1, source_target_pairs={{0,4},{4,8},{8,12},{12,0},{1,5},{5,9},{9,13},{13,1},{2,6},{6,10},{... | collective-permute-start | bytes 884744 | tf_op jit(solution)/shard_map/ppermute | solution.py:338
  23.1 19.8 %collective-permute-start.4 = (bf16[384,384]{1,0:T(8,128)(2,1)S(1)}, bf16[384,384]{1,0:T(8,128)(2,1)S(1)}, u32[]{:S(2)}, u32[]{:S(2)}) collective-permute-start(bf16[384,384]{1,0:T(8,128)(2,1)S(1)} %get-tuple-element.68), channel_id=1, source_target_pairs={{0,8},{4,12},{8,0},{12,4},{1,9},{5,13},{9,1},{13,5},{2,10},{6,14},... | collective-permute-start | bytes 884744 | tf_op jit(solution)/shard_map/ppermute | solution.py:338
  24.7 18.2 %collective-permute-start.5 = (bf16[384,384]{1,0:T(8,128)(2,1)S(1)}, bf16[384,384]{1,0:T(8,128)(2,1)S(1)}, u32[]{:S(2)}, u32[]{:S(2)}) collective-permute-start(bf16[384,384]{1,0:T(8,128)(2,1)S(1)} %get-tuple-element.69), channel_id=1, source_target_pairs={{0,12},{4,0},{8,4},{12,8},{1,13},{5,1},{9,5},{13,9},{2,14},{6,2},{... | collective-permute-start | bytes 884744 | tf_op jit(solution)/shard_map/ppermute | solution.py:338
  32.3 10.6 %collective-permute-start.7 = (bf16[288,384]{1,0:T(8,128)(2,1)S(1)}, bf16[288,384]{1,0:T(8,128)(2,1)S(1)}, u32[]{:S(2)}, u32[]{:S(2)}) collective-permute-start(bf16[288,384]{1,0:T(8,128)(2,1)S(1)} %slice.24), channel_id=1, source_target_pairs={{0,16},{16,0},{1,17},{17,1},{2,18},{18,2},{3,19},{19,3},{4,20},{20... | collective-permute-start | bytes 663560 | tf_op jit(solution)/shard_map/ppermute | solution.py:338
  42.9 9.5 %collective-permute-start.8 = (bf16[2304,128]{1,0:T(8,128)(2,1)S(1)}, bf16[2304,128]{1,0:T(8,128)(2,1)S(1)}, u32[]{:S(2)}, u32[]{:S(2)}) collective-permute-start(bf16[2304,128]{1,0:T(8,128)(2,1)S(1)} %pad_maximum_fusion.refs_0_), channel_id=1, source_target_pairs={{0,1},{1,0},{2,3},{3,2},{4,5},{5,4},{6,7},{7,6},{8,9},{9,8},{10,11... | collective-permute-start | bytes 1769480 | tf_op jit(solution)/shard_map/ppermute | solution.py:338
  43.0 11.7 %collective-permute-start.9 = (bf16[2304,128]{1,0:T(8,128)(2,1)S(1)}, bf16[2304,128]{1,0:T(8,128)(2,1)S(1)}, u32[]{:S(2)}, u32[]{:S(2)}) collective-permute-start(bf16[2304,128]{1,0:T(8,128)(2,1)S(1)} %collective-permute-done.3.refs_1_), channel_id=1, source_target_pairs={{0,1},{1,0},{2,3},{3,2},{4,5},{5,4},{6,7},{7,6},{8,9},{9,8},{10,11... | collective-permute-start | bytes 1769480 | tf_op jit(solution)/shard_map/ppermute | solution.py:338
  43.5 12.6 %collective-permute-start.13 = (bf16[288,384]{1,0:T(8,128)(2,1)S(1)}, bf16[288,384]{1,0:T(8,128)(2,1)S(1)}, u32[]{:S(2)}, u32[]{:S(2)}) collective-permute-start(bf16[288,384]{1,0:T(8,128)(2,1)S(1)} %slice.19), channel_id=1, source_target_pairs={{0,16},{16,0},{1,17},{17,1},{2,18},{18,2},{3,19},{19,3},{4,20},{20... | collective-permute-start | bytes 663560 | tf_op jit(solution)/shard_map/ppermute | solution.py:338
  45.1 11.0 %collective-permute-start.14 = (bf16[288,384]{1,0:T(8,128)(2,1)S(1)}, bf16[288,384]{1,0:T(8,128)(2,1)S(1)}, u32[]{:S(2)}, u32[]{:S(2)}) collective-permute-start(bf16[288,384]{1,0:T(8,128)(2,1)S(1)} %slice.20), channel_id=1, source_target_pairs={{0,16},{16,0},{1,17},{17,1},{2,18},{18,2},{3,19},{19,3},{4,20},{20... | collective-permute-start | bytes 663560 | tf_op jit(solution)/shard_map/ppermute | solution.py:338
  45.7 19.8 %collective-permute-start.10 = (bf16[384,384]{1,0:T(8,128)(2,1)S(1)}, bf16[384,384]{1,0:T(8,128)(2,1)S(1)}, u32[]{:S(2)}, u32[]{:S(2)}) collective-permute-start(bf16[384,384]{1,0:T(8,128)(2,1)S(1)} %get-tuple-element.80), channel_id=1, source_target_pairs={{0,4},{4,8},{8,12},{12,0},{1,5},{5,9},{9,13},{13,1},{2,6},{6,10},{... | collective-permute-start | bytes 884744 | tf_op jit(solution)/shard_map/ppermute | solution.py:338
  52.4 21.2 %collective-permute-start.11 = (bf16[384,384]{1,0:T(8,128)(2,1)S(1)}, bf16[384,384]{1,0:T(8,128)(2,1)S(1)}, u32[]{:S(2)}, u32[]{:S(2)}) collective-permute-start(bf16[384,384]{1,0:T(8,128)(2,1)S(1)} %get-tuple-element.81), channel_id=1, source_target_pairs={{0,8},{4,12},{8,0},{12,4},{1,9},{5,13},{9,1},{13,5},{2,10},{6,14},... | collective-permute-start | bytes 884744 | tf_op jit(solution)/shard_map/ppermute | solution.py:338
  54.7 18.9 %collective-permute-start.12 = (bf16[384,384]{1,0:T(8,128)(2,1)S(1)}, bf16[384,384]{1,0:T(8,128)(2,1)S(1)}, u32[]{:S(2)}, u32[]{:S(2)}) collective-permute-start(bf16[384,384]{1,0:T(8,128)(2,1)S(1)} %get-tuple-element.82), channel_id=1, source_target_pairs={{0,12},{4,0},{8,4},{12,8},{1,13},{5,1},{9,5},{13,9},{2,14},{6,2},{... | collective-permute-start | bytes 884744 | tf_op jit(solution)/shard_map/ppermute | solution.py:338
  56.1 9.4 %copy-start.8 = (bf16[4,512,576]{2,1,0:T(8,128)(2,1)}, bf16[4,512,576]{2,1,0:T(8,128)(2,1)S(1)}, u32[]{:S(2)}) copy-start(bf16[4,512,576]{2,1,0:T(8,128)(2,1)S(1)} %get-tuple-element.73.refs_0_) | copy-start | bytes 7077892
  74.3 16.0 %collective-permute-start.15 = (bf16[288,384]{1,0:T(8,128)(2,1)}, bf16[288,384]{1,0:T(8,128)(2,1)S(1)}, u32[]{:S(2)}, u32[]{:S(2)}) collective-permute-start(bf16[288,384]{1,0:T(8,128)(2,1)} %slice.21), channel_id=1, source_target_pairs={{0,16},{16,0},{1,17},{17,1},{2,18},{18,2},{3,19},{19,3},{4,20},{20... | collective-permute-start | bytes 663560 | tf_op jit(solution)/shard_map/ppermute | solution.py:338
  76.5 14.5 %collective-permute-start.16 = (bf16[288,384]{1,0:T(8,128)(2,1)}, bf16[288,384]{1,0:T(8,128)(2,1)}, u32[]{:S(2)}, u32[]{:S(2)}) collective-permute-start(bf16[288,384]{1,0:T(8,128)(2,1)} %slice.22), channel_id=1, source_target_pairs={{0,16},{16,0},{1,17},{17,1},{2,18},{18,2},{3,19},{19,3},{4,20},{20... | collective-permute-start | bytes 663560 | tf_op jit(solution)/shard_map/ppermute | solution.py:338
  77.8 13.6 %collective-permute-start.17 = (bf16[288,384]{1,0:T(8,128)(2,1)}, bf16[288,384]{1,0:T(8,128)(2,1)}, u32[]{:S(2)}, u32[]{:S(2)}) collective-permute-start(bf16[288,384]{1,0:T(8,128)(2,1)} %slice.23), channel_id=1, source_target_pairs={{0,16},{16,0},{1,17},{17,1},{2,18},{18,2},{3,19},{19,3},{4,20},{20... | collective-permute-start | bytes 663560 | tf_op jit(solution)/shard_map/ppermute | solution.py:338
  79.3 25.7 %collective-permute-start.18 = (bf16[512,384]{1,0:T(8,128)(2,1)S(1)}, bf16[512,384]{1,0:T(8,128)(2,1)S(1)}, u32[]{:S(2)}, u32[]{:S(2)}) collective-permute-start(bf16[512,384]{1,0:T(8,128)(2,1)S(1)} %get-tuple-element.102.refs_0_), channel_id=1, source_target_pairs={{0,8},{4,12},{8,0},{12,4},{1,9},{5,13},{9,1},{13,5},{2,10},{6,14},... | collective-permute-start | bytes 1179656 | tf_op jit(solution)/shard_map/ppermute | solution.py:426
  85.0 19.9 %collective-permute-start.19 = (bf16[512,384]{1,0:T(8,128)(2,1)S(1)}, bf16[512,384]{1,0:T(8,128)(2,1)S(1)}, u32[]{:S(2)}, u32[]{:S(2)}) collective-permute-start(bf16[512,384]{1,0:T(8,128)(2,1)S(1)} %get-tuple-element.102.refs_0_), channel_id=1, source_target_pairs={{0,4},{4,0},{8,12},{12,8},{1,5},{5,1},{9,13},{13,9},{2,6},{6,2},{1... | collective-permute-start | bytes 1179656 | tf_op jit(solution)/shard_map/ppermute | solution.py:427
  86.7 21.4 %all-to-all-start = ((bf16[4,272,128]{2,1,0:T(8,128)(2,1)}), bf16[4,272,128]{2,1,0:T(8,128)(2,1)S(1)}, u32[]{:S(2)}, u32[]{:S(2)}) async-start(bf16[4,272,128]{2,1,0:T(8,128)(2,1)} %get-tuple-element.96), calls=%async_computation | async-start | bytes 557056 | tf_op jit(solution)/shard_map/all_to_all | solution.py:423
  91.4 1.7 %copy-start.9 = (bf16[4,512,576]{2,1,0:T(8,128)(2,1)S(1)}, bf16[4,512,576]{2,1,0:T(8,128)(2,1)}, u32[]{:S(2)}) copy-start(bf16[4,512,576]{2,1,0:T(8,128)(2,1)} %copy-done.8) | copy-start | bytes 7077892
  105.0 15.8 %collective-permute-start.22 = (bf16[512,384]{1,0:T(8,128)(2,1)S(1)}, bf16[512,384]{1,0:T(8,128)(2,1)}, u32[]{:S(2)}, u32[]{:S(2)}) collective-permute-start(bf16[512,384]{1,0:T(8,128)(2,1)S(1)} %get-tuple-element.102.refs_0_), channel_id=1, source_target_pairs={{4,8},{8,4},{5,9},{9,5},{6,10},{10,6},{7,11},{11,7},{20,24},{24,20... | collective-permute-start | bytes 1179656 | tf_op jit(solution)/shard_map/ppermute | solution.py:432
  106.4 18.8 %collective-permute-start.23 = (bf16[512,384]{1,0:T(8,128)(2,1)S(1)}, bf16[512,384]{1,0:T(8,128)(2,1)}, u32[]{:S(2)}, u32[]{:S(2)}) collective-permute-start(bf16[512,384]{1,0:T(8,128)(2,1)S(1)} %collective-permute-done.18.refs_2_), channel_id=1, source_target_pairs={{8,12},{4,0},{9,13},{5,1},{10,14},{6,2},{11,15},{7,3},{24,28},{20,... | collective-permute-start | bytes 1179656 | tf_op jit(solution)/shard_map/ppermute | solution.py:433
  108.1 37.1 %collective-permute-start.20 = (bf16[512,384]{1,0:T(8,128)(2,1)S(1)}, bf16[512,384]{1,0:T(8,128)(2,1)S(1)}, u32[]{:S(2)}, u32[]{:S(2)}) collective-permute-start(bf16[512,384]{1,0:T(8,128)(2,1)S(1)} %get-tuple-element.108.refs_0_), channel_id=1, source_target_pairs={{0,8},{4,12},{8,0},{12,4},{1,9},{5,13},{9,1},{13,5},{2,10},{6,14},... | collective-permute-start | bytes 1179656 | tf_op jit(solution)/shard_map/ppermute | solution.py:426
  117.3 27.8 %collective-permute-start.21 = (bf16[512,384]{1,0:T(8,128)(2,1)S(1)}, bf16[512,384]{1,0:T(8,128)(2,1)S(1)}, u32[]{:S(2)}, u32[]{:S(2)}) collective-permute-start(bf16[512,384]{1,0:T(8,128)(2,1)S(1)} %get-tuple-element.108.refs_0_), channel_id=1, source_target_pairs={{0,4},{4,0},{8,12},{12,8},{1,5},{5,1},{9,13},{13,9},{2,6},{6,2},{1... | collective-permute-start | bytes 1179656 | tf_op jit(solution)/shard_map/ppermute | solution.py:427
  117.3 30.8 %all-to-all-start.1 = ((bf16[4,272,128]{2,1,0:T(8,128)(2,1)}), bf16[4,272,128]{2,1,0:T(8,128)(2,1)S(1)}, u32[]{:S(2)}, u32[]{:S(2)}) async-start(bf16[4,272,128]{2,1,0:T(8,128)(2,1)} %copy-done.5), calls=%async_computation.1 | async-start | bytes 557056 | tf_op jit(solution)/shard_map/all_to_all | solution.py:423
  145.1 7.3 %collective-permute-start.24 = (bf16[512,384]{1,0:T(8,128)(2,1)S(1)}, bf16[512,384]{1,0:T(8,128)(2,1)S(1)}, u32[]{:S(2)}, u32[]{:S(2)}) collective-permute-start(bf16[512,384]{1,0:T(8,128)(2,1)S(1)} %get-tuple-element.108.refs_0_), channel_id=1, source_target_pairs={{4,8},{8,4},{5,9},{9,5},{6,10},{10,6},{7,11},{11,7},{20,24},{24,20... | collective-permute-start | bytes 1179656 | tf_op jit(solution)/shard_map/ppermute | solution.py:432
  145.8 10.0 %collective-permute-start.25 = (bf16[512,384]{1,0:T(8,128)(2,1)S(1)}, bf16[512,384]{1,0:T(8,128)(2,1)S(1)}, u32[]{:S(2)}, u32[]{:S(2)}) collective-permute-start(bf16[512,384]{1,0:T(8,128)(2,1)S(1)} %collective-permute-done.20.refs_2_), channel_id=1, source_target_pairs={{8,12},{4,0},{9,13},{5,1},{10,14},{6,2},{11,15},{7,3},{24,28},{20,... | collective-permute-start | bytes 1179656 | tf_op jit(solution)/shard_map/ppermute | solution.py:433
  (10 other events, 9.7 us)

commit v11 on v10

--- a/solution.py
+++ b/solution.py
@@ -241,11 +241,12 @@
             out[size + 80 : size + 96, 2 * DK : 3 * DK] = jnp.zeros((16, DK), out.dtype)
 
 
-def head_kernel(ctx, where_ref, *refs):
+def head_kernel(ctx, slot, where_ref, *refs):
     all_ref, refs = refs[0], refs[1:]
     direct, refs = refs[:ctx], refs[ctx:]
     swapped, refs = refs[: ctx - 1], refs[ctx - 1 :]
-    grad_ref, back_ref, w, raw, decay, cot, logit, out, dlogit, ddecay = refs
+    grad_ref, *back_refs = refs[:-8]
+    w, raw, decay, cot, logit, out, dlogit, ddecay = refs[-8:]
     place, group = where_ref[0], where_ref[1]
     share = direct[0].shape[0] - EXTRA
     half = share // 2
@@ -273,10 +274,12 @@
         )
     raw[...] = projected
     recurrence(raw, decay, logit, cot, out, grad_ref, dlogit, ddecay)
-    for n in range(ctx):
-        back_ref[n, 0:CHUNK, :] = out[n]
-        back_ref[n, CHUNK : 2 * CHUNK, :] = ddecay[n]
-        back_ref[n, 2 * CHUNK :, :] = tail_rows(dlogit[n : n + 1, :])
+    for d in range(ctx):
+        target = d if slot else lax.rem(place + d, ctx)
+        back = back_refs[0].at[d] if slot else back_refs[d]
+        back[0:CHUNK, :] = out[target]
+        back[CHUNK : 2 * CHUNK, :] = ddecay[target]
+        back[2 * CHUNK :, :] = tail_rows(dlogit[pl.ds(target, 1), :])
 
 
 def weight_gradient_kernel(steps, where_ref, own_ref, *refs):
@@ -297,15 +300,16 @@
                 block(jnp.where(where_ref[10] == 1, refs[at + 1][...], refs[at][...]))
 
 
-def unpack_kernel(first_ref, second_ref, out_ref, dlogit_ref, ddecay_ref):
-    for source in range(first_ref.shape[0]):
-        for s, ref in enumerate((first_ref, second_ref)):
-            head = 2 * source + s
-            column = slice(head * DK, (head + 1) * DK)
-            out_ref[:, column] = ref[source, 0:CHUNK, :]
-            ddecay_ref[:, column] = ref[source, CHUNK : 2 * CHUNK, :].astype(jnp.float32)
-            tail = ref[source, 2 * CHUNK :, :].astype(jnp.float32)
-            dlogit_ref[head : head + 1, :] = tail[0:1] + tail[1:2]
+def unpack_kernel(ctx, where_ref, *refs):
+    first_refs, second_ref, (out_ref, dlogit_ref, ddecay_ref) = refs[:ctx], refs[ctx], refs[ctx + 1 :]
+    for d in range(ctx):
+        source = lax.rem(where_ref[0] + ctx - d, ctx)
+        for head, ref in ((2 * source, first_refs[d]), (2 * d + 1, second_ref.at[d])):
+            column = lanes(head * DK)
+            out_ref[:, column] = ref[0:CHUNK, :]
+            ddecay_ref[:, column] = ref[CHUNK : 2 * CHUNK, :].astype(jnp.float32)
+            tail = ref[2 * CHUNK :, :].astype(jnp.float32)
+            dlogit_ref[pl.ds(head, 1), :] = tail[0:1] + tail[1:2]
 
 
 def head_split(tokens, w_query, w_key, w_value, beta_logit, log_decay, grad_out):
@@ -396,14 +400,13 @@
     for slot, direct in enumerate((first, second)):
         if slot:
             swapped = [along(x[:half], "groups", 1) for x in direct]
-        grad, back = pl.pallas_call(
-            functools.partial(head_kernel, ctx),
-            out_shape=[
-                shape((total, HEAD_COLUMNS), bf16),
-                shape((ctx, 2 * CHUNK + TAIL, DK), bf16),
-            ],
+        side = (2 * CHUNK + TAIL, DK)
+        grad, *back = pl.pallas_call(
+            functools.partial(head_kernel, ctx, slot),
+            out_shape=[shape((total, HEAD_COLUMNS), bf16)]
+            + ([shape((ctx,) + side, bf16)] if slot else [shape(side, bf16)] * ctx),
             in_specs=[scalars] + [whole] * (1 + ctx + ctx - 1),
-            out_specs=[whole] * 2,
+            out_specs=[whole] * (2 if slot else 1 + ctx),
             scratch_shapes=[
                 pltpu.VMEM((depth, HEAD_COLUMNS), bf16),
                 pltpu.VMEM((total, HEAD_COLUMNS), f32),
@@ -420,9 +423,12 @@
         )(where, all_tokens, packed[slot * ctx], *direct, *swapped)
         if not slot:
             second[:], (grad, back) = after(second, (grad, back))
-        backs.append(lax.all_to_all(back, "ctx", 0, 0))
         if slot:
-            grad, (grads[0][1:3], backs[0]) = after(grad, (grads[0][1:3], backs[0]))
+            backs.append(lax.all_to_all(back[0], "ctx", 0, 0))
+        else:
+            backs += [back[0]] + [along(back[d], "ctx", d) for d in range(1, ctx)]
+        if slot:
+            grad, (grads[0][1:3], backs[:ctx]) = after(grad, (grads[0][1:3], backs[:ctx]))
         two = lax.ppermute(grad, "ctx", [(0, 2), (1, 3), (2, 0), (3, 1)])
         pair = lax.ppermute(grad, "ctx", [(0, 1), (1, 0), (2, 3), (3, 2)])
         results = ()
@@ -436,13 +442,13 @@
     results = products(1, (3,), grads[1][3:], results)
 
     attn_out, grad_beta, grad_decay = pl.pallas_call(
-        unpack_kernel,
+        functools.partial(unpack_kernel, ctx),
         out_shape=[shape((length, columns), bf16), shape((columns // DK, length), f32), shape((length, columns), f32)],
-        in_specs=[whole] * 2,
+        in_specs=[scalars] + [whole] * (ctx + 1),
         out_specs=[whole] * 3,
         compiler_params=pltpu.CompilerParams(vmem_limit_bytes=VMEM_LIMIT),
         name="unpack",
-    )(*backs)
+    )(where, *backs)
     return (attn_out, *results, grad_beta, grad_decay)
 
 

time: 158 us -> 153 us (0.968)
  local copies, waits for them, and re-layouts: 14.9 us -> 7.78 us
  starting transfers between devices: 59.8 us -> 63.8 us
  waiting for transfers between devices: 49.1 us -> 46.8 us
    ppermute x18 -> x21, starting transfers between devices: 31.5 us -> 43.1 us  [along(): return lax.ppermute(x, axis, [(i, (i + hop) % count) for i in range(count)])]
    ppermute x2, starting transfers between devices: 15 us -> 9.68 us  [head_split(): two = lax.ppermute(grad, 'ctx', [(0, 2), (1, 3), (2, 0), (3, 1)])]
    unnamed x28 -> x14, local copies, waits for them, and re-layouts: 12.7 us -> 7.55 us
    all_to_all x2 -> x1, starting transfers between devices: 7.08 us -> 4.12 us  [head_split(): backs.append(lax.all_to_all(back[0], 'ctx', 0, 0))]
    ppermute x2, waiting for transfers between devices: 14.9 us -> 12.6 us  [head_split(): two = lax.ppermute(grad, 'ctx', [(0, 2), (1, 3), (2, 0), (3, 1)])]
    slice x3, local copies, waits for them, and re-layouts: 2.12 us -> 0.07 us  [head_split(): swapped = [along(x[:half], 'groups', 1) for x in direct]]
    ppermute x18 -> x21, waiting for transfers between devices: 25.1 us -> 25.4 us  [along(): return lax.ppermute(x, axis, [(i, (i + hop) % count) for i in range(count)])]
  transfers between devices with their start and end apart: 28 -> 30, of which waited for: 10 -> 8; matrix products, arithmetic and copies ran while one was open for 1% -> 0% of each run, Pallas kernels for 19% -> 20%
where the time goes in v11:
time: 153 us; the launch traced here: 152 us
  starting transfers between devices  63.8 us (42%)
  waiting for transfers between devices  46.8 us (31%)
  Pallas kernels  33 us (22%)
  local copies, waits for them, and re-layouts  7.78 us (5%)
    ppermute x21, starting transfers between devices, along(): return lax.ppermute(x, axis, [(i, (i + hop) % count) for i in range(count)])  43.1 us
    ppermute x21, waiting for transfers between devices, along(): return lax.ppermute(x, axis, [(i, (i + hop) % count) for i in range(count)])  25.4 us
    pallas_call x2, Pallas kernels, head_split(): pl.pallas_call(functools.partial(head_kernel, ctx, slot), out_shape=[shap...  18 us
    ppermute x2, waiting for transfers between devices, head_split(): two = lax.ppermute(grad, 'ctx', [(0, 2), (1, 3), (2, 0), (3, 1)])  12.6 us
    pallas_call x3, Pallas kernels, products(): pl.pallas_call(functools.partial(weight_gradient_kernel, steps), grid_spe...  10.3 us
    ppermute x2, starting transfers between devices, head_split(): two = lax.ppermute(grad, 'ctx', [(0, 2), (1, 3), (2, 0), (3, 1)])  9.68 us
    ppermute x2, waiting for transfers between devices, head_split(): far = lax.ppermute(two, 'ctx', [(2, 3), (1, 0)])  8.24 us
    unnamed x14, local copies, waits for them, and re-layouts  7.55 us
  transfers between devices with their start and end apart: 30, of which 8 were waited for; matrix products, arithmetic and copies ran while one was open for 0% of the time, Pallas kernels for 20%

profile of v11, /device:TPU:0, one launch (start us, length us, event | category | flops | bytes accessed | tf_op | source)
XLA Modules:
  0.0 152.3 jit_solution(7653198121983724900)
XLA Ops:
  2.4 3.1 %collective-permute-start = (bf16[576,128]{1,0:T(8,128)(2,1)S(1)}, bf16[576,128]{1,0:T(8,128)(2,1)S(1)}, u32[]{:S(2)}, u32[]{:S(2)}) collective-permute-start(bf16[576,128]{1,0:T(8,128)(2,1)S(1)} %pack_tokens.1), channel_id=1, source_target_pairs={{0,4},{4,8},{8,12},{12,0},{1,5},{5,9},{9,13},{13,1},{2,6},{6,10},{... | collective-permute-start | bytes 442376 | tf_op jit(solution)/shard_map/ppermute | solution.py:342
  5.5 2.6 %collective-permute-start.1 = (bf16[576,128]{1,0:T(8,128)(2,1)S(1)}, bf16[576,128]{1,0:T(8,128)(2,1)S(1)}, u32[]{:S(2)}, u32[]{:S(2)}) collective-permute-start(bf16[576,128]{1,0:T(8,128)(2,1)S(1)} %pack_tokens.1), channel_id=1, source_target_pairs={{0,8},{4,12},{8,0},{12,4},{1,9},{5,13},{9,1},{13,5},{2,10},{6,14},... | collective-permute-start | bytes 442376 | tf_op jit(solution)/shard_map/ppermute | solution.py:342
  8.1 1.3 collective-permute-start.2
  17.9 1.6 %collective-permute-start.3 = (bf16[2304,128]{1,0:T(8,128)(2,1)S(1)}, bf16[2304,128]{1,0:T(8,128)(2,1)S(1)}, u32[]{:S(2)}, u32[]{:S(2)}) collective-permute-start(bf16[2304,128]{1,0:T(8,128)(2,1)S(1)} %pad_maximum_fusion.refs_0_), channel_id=1, source_target_pairs={{0,2},{2,0},{1,3},{3,1},{4,6},{6,4},{5,7},{7,5},{8,10},{10,8},{9,1... | collective-permute-start | bytes 1769480 | tf_op jit(solution)/shard_map/ppermute | solution.py:342
  19.5 3.6 %collective-permute-start.6 = (bf16[384,384]{1,0:T(8,128)(2,1)S(1)}, bf16[384,384]{1,0:T(8,128)(2,1)S(1)}, u32[]{:S(2)}, u32[]{:S(2)}) collective-permute-start(bf16[384,384]{1,0:T(8,128)(2,1)S(1)} %get-tuple-element.79), channel_id=1, source_target_pairs={{0,4},{4,8},{8,12},{12,0},{1,5},{5,9},{9,13},{13,1},{2,6},{6,10},{... | collective-permute-start | bytes 884744 | tf_op jit(solution)/shard_map/ppermute | solution.py:342
  23.1 1.6 %collective-permute-start.4 = (bf16[384,384]{1,0:T(8,128)(2,1)S(1)}, bf16[384,384]{1,0:T(8,128)(2,1)S(1)}, u32[]{:S(2)}, u32[]{:S(2)}) collective-permute-start(bf16[384,384]{1,0:T(8,128)(2,1)S(1)} %get-tuple-element.77), channel_id=1, source_target_pairs={{0,8},{4,12},{8,0},{12,4},{1,9},{5,13},{9,1},{13,5},{2,10},{6,14},... | collective-permute-start | bytes 884744 | tf_op jit(solution)/shard_map/ppermute | solution.py:342
  25.5 6.8 %collective-permute-done.6.refs_2_ = bf16[384,384]{1,0:T(8,128)(2,1)S(1)} collective-permute-done((bf16[384,384]{1,0:T(8,128)(2,1)S(1)}, bf16[384,384]{1,0:T(8,128)(2,1)S(1)}, u32[]{:S(2)}, u32[]{:S(2)}) %collective-permute-start.6) | collective-permute-done | bytes 294944 | tf_op jit(solution)/shard_map/ppermute | solution.py:342
  32.3 1.6 %collective-permute-start.7 = (bf16[288,384]{1,0:T(8,128)(2,1)S(1)}, bf16[288,384]{1,0:T(8,128)(2,1)S(1)}, u32[]{:S(2)}, u32[]{:S(2)}) collective-permute-start(bf16[288,384]{1,0:T(8,128)(2,1)S(1)} %slice.24), channel_id=1, source_target_pairs={{0,16},{16,0},{1,17},{17,1},{2,18},{18,2},{3,19},{19,3},{4,20},{20... | collective-permute-start | bytes 663560 | tf_op jit(solution)/shard_map/ppermute | solution.py:342
  33.9 9.1 %collective-permute-done.4.refs_3_ = bf16[384,384]{1,0:T(8,128)(2,1)S(1)} collective-permute-done((bf16[384,384]{1,0:T(8,128)(2,1)S(1)}, bf16[384,384]{1,0:T(8,128)(2,1)S(1)}, u32[]{:S(2)}, u32[]{:S(2)}) %collective-permute-start.4) | collective-permute-done | bytes 294944 | tf_op jit(solution)/shard_map/ppermute | solution.py:342
  43.5 1.6 %collective-permute-start.13 = (bf16[288,384]{1,0:T(8,128)(2,1)S(1)}, bf16[288,384]{1,0:T(8,128)(2,1)S(1)}, u32[]{:S(2)}, u32[]{:S(2)}) collective-permute-start(bf16[288,384]{1,0:T(8,128)(2,1)S(1)} %slice.19), channel_id=1, source_target_pairs={{0,16},{16,0},{1,17},{17,1},{2,18},{18,2},{3,19},{19,3},{4,20},{20... | collective-permute-start | bytes 663560 | tf_op jit(solution)/shard_map/ppermute | solution.py:342
  45.7 6.7 %collective-permute-start.10 = (bf16[384,384]{1,0:T(8,128)(2,1)S(1)}, bf16[384,384]{1,0:T(8,128)(2,1)S(1)}, u32[]{:S(2)}, u32[]{:S(2)}) collective-permute-start(bf16[384,384]{1,0:T(8,128)(2,1)S(1)} %get-tuple-element.89), channel_id=1, source_target_pairs={{0,4},{4,8},{8,12},{12,0},{1,5},{5,9},{9,13},{13,1},{2,6},{6,10},{... | collective-permute-start | bytes 884744 | tf_op jit(solution)/shard_map/ppermute | solution.py:342
  52.4 2.3 %collective-permute-start.11 = (bf16[384,384]{1,0:T(8,128)(2,1)S(1)}, bf16[384,384]{1,0:T(8,128)(2,1)S(1)}, u32[]{:S(2)}, u32[]{:S(2)}) collective-permute-start(bf16[384,384]{1,0:T(8,128)(2,1)S(1)} %get-tuple-element.90), channel_id=1, source_target_pairs={{0,8},{4,12},{8,0},{12,4},{1,9},{5,13},{9,1},{13,5},{2,10},{6,14},... | collective-permute-start | bytes 884744 | tf_op jit(solution)/shard_map/ppermute | solution.py:342
  56.1 8.7 %head_0.1 = (bf16[512,384]{1,0:T(8,128)(2,1)S(1)}, bf16[272,128]{1,0:T(8,128)(2,1)S(1)}, bf16[272,128]{1,0:T(8,128)(2,1)S(1)}, bf16[272,128]{1,0:T(8,128)(2,1)S(1)}, bf16[272,128]{1,0:T(8,128)(2,1)S(1)}) custom-call(s32[11]{0:T(128)S(1)} %stack.48.where_ref, bf16[4,512,576]{2,1,0:T(8,128)(2,1)S(1)} %get-tuple-element.82.refs_0_, ...), custom_call_target="tpu_custom_call" | custom-call | flops 12000000000 | bytes 12000000 | tf_op jit(solution)/shard_map/head_0/pallas_call | solution.py:404
  64.8 8.9 %collective-permute-done.11.refs_3_ = bf16[384,384]{1,0:T(8,128)(2,1)S(1)} collective-permute-done((bf16[384,384]{1,0:T(8,128)(2,1)S(1)}, bf16[384,384]{1,0:T(8,128)(2,1)S(1)}, u32[]{:S(2)}, u32[]{:S(2)}) %collective-permute-start.11) | collective-permute-done | bytes 294944 | tf_op jit(solution)/shard_map/ppermute | solution.py:342
  73.7 1.6 %collective-permute-start.15 = (bf16[288,384]{1,0:T(8,128)(2,1)S(1)}, bf16[288,384]{1,0:T(8,128)(2,1)S(1)}, u32[]{:S(2)}, u32[]{:S(2)}) collective-permute-start(bf16[288,384]{1,0:T(8,128)(2,1)S(1)} %slice.21), channel_id=1, source_target_pairs={{0,16},{16,0},{1,17},{17,1},{2,18},{18,2},{3,19},{19,3},{4,20},{20... | collective-permute-start | bytes 663560 | tf_op jit(solution)/shard_map/ppermute | solution.py:342
  75.9 1.6 %collective-permute-start.17 = (bf16[288,384]{1,0:T(8,128)(2,1)S(1)}, bf16[288,384]{1,0:T(8,128)(2,1)S(1)}, u32[]{:S(2)}, u32[]{:S(2)}) collective-permute-start(bf16[288,384]{1,0:T(8,128)(2,1)S(1)} %slice.23), channel_id=1, source_target_pairs={{0,16},{16,0},{1,17},{17,1},{2,18},{18,2},{3,19},{19,3},{4,20},{20... | collective-permute-start | bytes 663560 | tf_op jit(solution)/shard_map/ppermute | solution.py:342
  77.4 5.8 %collective-permute-start.18 = (bf16[512,384]{1,0:T(8,128)(2,1)S(1)}, bf16[512,384]{1,0:T(8,128)(2,1)S(1)}, u32[]{:S(2)}, u32[]{:S(2)}) collective-permute-start(bf16[512,384]{1,0:T(8,128)(2,1)S(1)} %get-tuple-element.120.refs_0_), channel_id=1, source_target_pairs={{0,8},{4,12},{8,0},{12,4},{1,9},{5,13},{9,1},{13,5},{2,10},{6,14},... | collective-permute-start | bytes 1179656 | tf_op jit(solution)/shard_map/ppermute | solution.py:432
  83.2 1.6 %collective-permute-start.19 = (bf16[512,384]{1,0:T(8,128)(2,1)S(1)}, bf16[512,384]{1,0:T(8,128)(2,1)S(1)}, u32[]{:S(2)}, u32[]{:S(2)}) collective-permute-start(bf16[512,384]{1,0:T(8,128)(2,1)S(1)} %get-tuple-element.120.refs_0_), channel_id=1, source_target_pairs={{0,4},{4,0},{8,12},{12,8},{1,5},{5,1},{9,13},{13,9},{2,6},{6,2},{1... | collective-permute-start | bytes 1179656 | tf_op jit(solution)/shard_map/ppermute | solution.py:433
  84.8 4.0 %collective-permute-start.20 = (bf16[272,128]{1,0:T(8,128)(2,1)S(1)}, bf16[272,128]{1,0:T(8,128)(2,1)S(1)}, u32[]{:S(2)}, u32[]{:S(2)}) collective-permute-start(bf16[272,128]{1,0:T(8,128)(2,1)S(1)} %get-tuple-element.109), channel_id=1, source_target_pairs={{0,4},{4,8},{8,12},{12,0},{1,5},{5,9},{9,13},{13,1},{2,6},{6,10},{... | collective-permute-start | bytes 208904 | tf_op jit(solution)/shard_map/ppermute | solution.py:342
  88.8 3.7 %collective-permute-start.21 = (bf16[272,128]{1,0:T(8,128)(2,1)S(1)}, bf16[272,128]{1,0:T(8,128)(2,1)S(1)}, u32[]{:S(2)}, u32[]{:S(2)}) collective-permute-start(bf16[272,128]{1,0:T(8,128)(2,1)S(1)} %get-tuple-element.110), channel_id=1, source_target_pairs={{0,8},{4,12},{8,0},{12,4},{1,9},{5,13},{9,1},{13,5},{2,10},{6,14},... | collective-permute-start | bytes 208904 | tf_op jit(solution)/shard_map/ppermute | solution.py:342
  92.5 3.7 %collective-permute-start.22 = (bf16[272,128]{1,0:T(8,128)(2,1)S(1)}, bf16[272,128]{1,0:T(8,128)(2,1)S(1)}, u32[]{:S(2)}, u32[]{:S(2)}) collective-permute-start(bf16[272,128]{1,0:T(8,128)(2,1)S(1)} %get-tuple-element.111), channel_id=1, source_target_pairs={{0,12},{4,0},{8,4},{12,8},{1,13},{5,1},{9,5},{13,9},{2,14},{6,2},{... | collective-permute-start | bytes 208904 | tf_op jit(solution)/shard_map/ppermute | solution.py:342
  96.3 9.4 %head_1.1 = (bf16[512,384]{1,0:T(8,128)(2,1)S(1)}, bf16[4,272,128]{2,1,0:T(8,128)(2,1)}) custom-call(s32[11]{0:T(128)S(1)} %stack.48.where_ref, bf16[4,512,576]{2,1,0:T(8,128)(2,1)S(1)} %get-tuple-element.82.refs_0_, bf16[672,384]{1,0:T(8,128)(2,1)S(1)} %get-tuple-element.83.refs_1_, bf16[384,384]{1,0:T(8,128)(2,1)S(1)} %collective-permute-done.10.refs_2_, ...), custom_call_target="tpu_custom_call" | custom-call | flops 12000000000 | bytes 12000000 | tf_op jit(solution)/shard_map/head_1/pallas_call | solution.py:404
  105.6 1.4 collective-permute-start.25
  108.3 3.9 %collective-permute-start.23 = (bf16[512,384]{1,0:T(8,128)(2,1)S(1)}, bf16[512,384]{1,0:T(8,128)(2,1)S(1)}, u32[]{:S(2)}, u32[]{:S(2)}) collective-permute-start(bf16[512,384]{1,0:T(8,128)(2,1)S(1)} %get-tuple-element.126.refs_0_), channel_id=1, source_target_pairs={{0,8},{4,12},{8,0},{12,4},{1,9},{5,13},{9,1},{13,5},{2,10},{6,14},... | collective-permute-start | bytes 1179656 | tf_op jit(solution)/shard_map/ppermute | solution.py:432
  112.9 4.1 %all-to-all-start = ((bf16[4,272,128]{2,1,0:T(8,128)(2,1)}), bf16[4,272,128]{2,1,0:T(8,128)(2,1)S(1)}, u32[]{:S(2)}, u32[]{:S(2)}) async-start(bf16[4,272,128]{2,1,0:T(8,128)(2,1)} %get-tuple-element.116), calls=%async_computation | async-start | bytes 557056 | tf_op jit(solution)/shard_map/all_to_all | solution.py:427
  117.0 5.1 %collective-permute-done.26.refs_4_ = bf16[512,384]{1,0:T(8,128)(2,1)} collective-permute-done((bf16[512,384]{1,0:T(8,128)(2,1)S(1)}, bf16[512,384]{1,0:T(8,128)(2,1)}, u32[]{:S(2)}, u32[]{:S(2)}) %collective-permute-start.26) | collective-permute-done | bytes 393248 | tf_op jit(solution)/shard_map/ppermute | solution.py:439
  122.1 5.0 %weight_gradient_0_0.1 = (f32[576,1024]{1,0:T(8,128)}, f32[576,1024]{1,0:T(8,128)}, f32[576,1024]{1,0:T(8,128)}) custom-call(s32[11]{0:T(128)S(1)} %stack.48.where_ref, bf16[576,512]{1,0:T(8,128)(2,1)S(1)} %get-tuple-element.118.own_ref, bf16[512,384]{1,0:T(8,128)(2,1)S(1)} %get-tuple-element.120.refs_0_, ...), custom_call_target="tpu_custom_call" | custom-call | tf_op jit(solution)/shard_map/weight_gradient_0_0/pallas_call | solution.py:385
  127.1 12.6 %collective-permute-done.23.refs_2_ = bf16[512,384]{1,0:T(8,128)(2,1)S(1)} collective-permute-done((bf16[512,384]{1,0:T(8,128)(2,1)S(1)}, bf16[512,384]{1,0:T(8,128)(2,1)S(1)}, u32[]{:S(2)}, u32[]{:S(2)}) %collective-permute-start.23) | collective-permute-done | bytes 393248 | tf_op jit(solution)/shard_map/ppermute | solution.py:432
  142.3 1.5 unpack.1
  143.8 3.4 %weight_gradient_1_0.1 = (f32[576,1024]{1,0:T(8,128)}, f32[576,1024]{1,0:T(8,128)}, f32[576,1024]{1,0:T(8,128)}) custom-call(s32[11]{0:T(128)S(1)} %stack.48.where_ref, bf16[576,512]{1,0:T(8,128)(2,1)S(1)} %get-tuple-element.118.own_ref, bf16[512,384]{1,0:T(8,128)(2,1)S(1)} %get-tuple-element.126.refs_0_, ...), custom_call_target="tpu_custom_call", output_to_operand_aliasing={{0}: (5, {}), {1}: (6, {}), {2}: (7, {})} | custom-call | tf_op jit(solution)/shard_map/weight_gradient_1_0/pallas_call | solution.py:385
  147.2 3.2 %collective-permute-done.28.refs_1_ = bf16[512,384]{1,0:T(8,128)(2,1)S(1)} collective-permute-done((bf16[512,384]{1,0:T(8,128)(2,1)S(1)}, bf16[512,384]{1,0:T(8,128)(2,1)S(1)}, u32[]{:S(2)}, u32[]{:S(2)}) %collective-permute-start.28) | collective-permute-done | bytes 393248 | tf_op jit(solution)/shard_map/ppermute | solution.py:439
  150.3 1.9 %weight_gradient_1_3.1 = (f32[576,1024]{1,0:T(8,128)}, f32[576,1024]{1,0:T(8,128)}, f32[576,1024]{1,0:T(8,128)}) custom-call(s32[11]{0:T(128)S(1)} %stack.48.where_ref, bf16[576,512]{1,0:T(8,128)(2,1)S(1)} %get-tuple-element.118.own_ref, ...), custom_call_target="tpu_custom_call", output_to_operand_aliasing={{0}: (4, {}), {1}: (5, {}), {2}: (6, {})} | custom-call | tf_op jit(solution)/shard_map/weight_gradient_1_3/pallas_call | solution.py:385
  (59 shorter events, 18.8 us)
Async XLA Ops:
  2.4 14.8 %collective-permute-start = (bf16[576,128]{1,0:T(8,128)(2,1)S(1)}, bf16[576,128]{1,0:T(8,128)(2,1)S(1)}, u32[]{:S(2)}, u32[]{:S(2)}) collective-permute-start(bf16[576,128]{1,0:T(8,128)(2,1)S(1)} %pack_tokens.1), channel_id=1, source_target_pairs={{0,4},{4,8},{8,12},{12,0},{1,5},{5,9},{9,13},{13,1},{2,6},{6,10},{... | collective-permute-start | bytes 442376 | tf_op jit(solution)/shard_map/ppermute | solution.py:342
  5.5 12.4 %collective-permute-start.1 = (bf16[576,128]{1,0:T(8,128)(2,1)S(1)}, bf16[576,128]{1,0:T(8,128)(2,1)S(1)}, u32[]{:S(2)}, u32[]{:S(2)}) collective-permute-start(bf16[576,128]{1,0:T(8,128)(2,1)S(1)} %pack_tokens.1), channel_id=1, source_target_pairs={{0,8},{4,12},{8,0},{12,4},{1,9},{5,13},{9,1},{13,5},{2,10},{6,14},... | collective-permute-start | bytes 442376 | tf_op jit(solution)/shard_map/ppermute | solution.py:342
  8.1 9.8 %collective-permute-start.2 = (bf16[576,128]{1,0:T(8,128)(2,1)S(1)}, bf16[576,128]{1,0:T(8,128)(2,1)S(1)}, u32[]{:S(2)}, u32[]{:S(2)}) collective-permute-start(bf16[576,128]{1,0:T(8,128)(2,1)S(1)} %pack_tokens.1), channel_id=1, source_target_pairs={{0,12},{4,0},{8,4},{12,8},{1,13},{5,1},{9,5},{13,9},{2,14},{6,2},{... | collective-permute-start | bytes 442376 | tf_op jit(solution)/shard_map/ppermute | solution.py:342
  9.4 1.3 copy-start
  10.7 1.3 copy-start.1
  17.9 25.0 %collective-permute-start.3 = (bf16[2304,128]{1,0:T(8,128)(2,1)S(1)}, bf16[2304,128]{1,0:T(8,128)(2,1)S(1)}, u32[]{:S(2)}, u32[]{:S(2)}) collective-permute-start(bf16[2304,128]{1,0:T(8,128)(2,1)S(1)} %pad_maximum_fusion.refs_0_), channel_id=1, source_target_pairs={{0,2},{2,0},{1,3},{3,1},{4,6},{6,4},{5,7},{7,5},{8,10},{10,8},{9,1... | collective-permute-start | bytes 1769480 | tf_op jit(solution)/shard_map/ppermute | solution.py:342
  19.5 12.8 %collective-permute-start.6 = (bf16[384,384]{1,0:T(8,128)(2,1)S(1)}, bf16[384,384]{1,0:T(8,128)(2,1)S(1)}, u32[]{:S(2)}, u32[]{:S(2)}) collective-permute-start(bf16[384,384]{1,0:T(8,128)(2,1)S(1)} %get-tuple-element.79), channel_id=1, source_target_pairs={{0,4},{4,8},{8,12},{12,0},{1,5},{5,9},{9,13},{13,1},{2,6},{6,10},{... | collective-permute-start | bytes 884744 | tf_op jit(solution)/shard_map/ppermute | solution.py:342
  23.1 19.8 %collective-permute-start.4 = (bf16[384,384]{1,0:T(8,128)(2,1)S(1)}, bf16[384,384]{1,0:T(8,128)(2,1)S(1)}, u32[]{:S(2)}, u32[]{:S(2)}) collective-permute-start(bf16[384,384]{1,0:T(8,128)(2,1)S(1)} %get-tuple-element.77), channel_id=1, source_target_pairs={{0,8},{4,12},{8,0},{12,4},{1,9},{5,13},{9,1},{13,5},{2,10},{6,14},... | collective-permute-start | bytes 884744 | tf_op jit(solution)/shard_map/ppermute | solution.py:342
  24.7 18.2 %collective-permute-start.5 = (bf16[384,384]{1,0:T(8,128)(2,1)S(1)}, bf16[384,384]{1,0:T(8,128)(2,1)S(1)}, u32[]{:S(2)}, u32[]{:S(2)}) collective-permute-start(bf16[384,384]{1,0:T(8,128)(2,1)S(1)} %get-tuple-element.78), channel_id=1, source_target_pairs={{0,12},{4,0},{8,4},{12,8},{1,13},{5,1},{9,5},{13,9},{2,14},{6,2},{... | collective-permute-start | bytes 884744 | tf_op jit(solution)/shard_map/ppermute | solution.py:342
  32.3 10.6 %collective-permute-start.7 = (bf16[288,384]{1,0:T(8,128)(2,1)S(1)}, bf16[288,384]{1,0:T(8,128)(2,1)S(1)}, u32[]{:S(2)}, u32[]{:S(2)}) collective-permute-start(bf16[288,384]{1,0:T(8,128)(2,1)S(1)} %slice.24), channel_id=1, source_target_pairs={{0,16},{16,0},{1,17},{17,1},{2,18},{18,2},{3,19},{19,3},{4,20},{20... | collective-permute-start | bytes 663560 | tf_op jit(solution)/shard_map/ppermute | solution.py:342
  42.9 9.5 %collective-permute-start.8 = (bf16[2304,128]{1,0:T(8,128)(2,1)S(1)}, bf16[2304,128]{1,0:T(8,128)(2,1)S(1)}, u32[]{:S(2)}, u32[]{:S(2)}) collective-permute-start(bf16[2304,128]{1,0:T(8,128)(2,1)S(1)} %pad_maximum_fusion.refs_0_), channel_id=1, source_target_pairs={{0,1},{1,0},{2,3},{3,2},{4,5},{5,4},{6,7},{7,6},{8,9},{9,8},{10,11... | collective-permute-start | bytes 1769480 | tf_op jit(solution)/shard_map/ppermute | solution.py:342
  43.0 11.7 %collective-permute-start.9 = (bf16[2304,128]{1,0:T(8,128)(2,1)S(1)}, bf16[2304,128]{1,0:T(8,128)(2,1)S(1)}, u32[]{:S(2)}, u32[]{:S(2)}) collective-permute-start(bf16[2304,128]{1,0:T(8,128)(2,1)S(1)} %collective-permute-done.3.refs_1_), channel_id=1, source_target_pairs={{0,1},{1,0},{2,3},{3,2},{4,5},{5,4},{6,7},{7,6},{8,9},{9,8},{10,11... | collective-permute-start | bytes 1769480 | tf_op jit(solution)/shard_map/ppermute | solution.py:342
  43.5 12.6 %collective-permute-start.13 = (bf16[288,384]{1,0:T(8,128)(2,1)S(1)}, bf16[288,384]{1,0:T(8,128)(2,1)S(1)}, u32[]{:S(2)}, u32[]{:S(2)}) collective-permute-start(bf16[288,384]{1,0:T(8,128)(2,1)S(1)} %slice.19), channel_id=1, source_target_pairs={{0,16},{16,0},{1,17},{17,1},{2,18},{18,2},{3,19},{19,3},{4,20},{20... | collective-permute-start | bytes 663560 | tf_op jit(solution)/shard_map/ppermute | solution.py:342
  45.1 11.0 %collective-permute-start.14 = (bf16[288,384]{1,0:T(8,128)(2,1)S(1)}, bf16[288,384]{1,0:T(8,128)(2,1)S(1)}, u32[]{:S(2)}, u32[]{:S(2)}) collective-permute-start(bf16[288,384]{1,0:T(8,128)(2,1)S(1)} %slice.20), channel_id=1, source_target_pairs={{0,16},{16,0},{1,17},{17,1},{2,18},{18,2},{3,19},{19,3},{4,20},{20... | collective-permute-start | bytes 663560 | tf_op jit(solution)/shard_map/ppermute | solution.py:342
  45.7 19.1 %collective-permute-start.10 = (bf16[384,384]{1,0:T(8,128)(2,1)S(1)}, bf16[384,384]{1,0:T(8,128)(2,1)S(1)}, u32[]{:S(2)}, u32[]{:S(2)}) collective-permute-start(bf16[384,384]{1,0:T(8,128)(2,1)S(1)} %get-tuple-element.89), channel_id=1, source_target_pairs={{0,4},{4,8},{8,12},{12,0},{1,5},{5,9},{9,13},{13,1},{2,6},{6,10},{... | collective-permute-start | bytes 884744 | tf_op jit(solution)/shard_map/ppermute | solution.py:342
  52.4 21.2 %collective-permute-start.11 = (bf16[384,384]{1,0:T(8,128)(2,1)S(1)}, bf16[384,384]{1,0:T(8,128)(2,1)S(1)}, u32[]{:S(2)}, u32[]{:S(2)}) collective-permute-start(bf16[384,384]{1,0:T(8,128)(2,1)S(1)} %get-tuple-element.90), channel_id=1, source_target_pairs={{0,8},{4,12},{8,0},{12,4},{1,9},{5,13},{9,1},{13,5},{2,10},{6,14},... | collective-permute-start | bytes 884744 | tf_op jit(solution)/shard_map/ppermute | solution.py:342
  54.7 18.9 %collective-permute-start.12 = (bf16[384,384]{1,0:T(8,128)(2,1)S(1)}, bf16[384,384]{1,0:T(8,128)(2,1)S(1)}, u32[]{:S(2)}, u32[]{:S(2)}) collective-permute-start(bf16[384,384]{1,0:T(8,128)(2,1)S(1)} %get-tuple-element.91), channel_id=1, source_target_pairs={{0,12},{4,0},{8,4},{12,8},{1,13},{5,1},{9,5},{13,9},{2,14},{6,2},{... | collective-permute-start | bytes 884744 | tf_op jit(solution)/shard_map/ppermute | solution.py:342
  73.7 11.2 %collective-permute-start.15 = (bf16[288,384]{1,0:T(8,128)(2,1)S(1)}, bf16[288,384]{1,0:T(8,128)(2,1)S(1)}, u32[]{:S(2)}, u32[]{:S(2)}) collective-permute-start(bf16[288,384]{1,0:T(8,128)(2,1)S(1)} %slice.21), channel_id=1, source_target_pairs={{0,16},{16,0},{1,17},{17,1},{2,18},{18,2},{3,19},{19,3},{4,20},{20... | collective-permute-start | bytes 663560 | tf_op jit(solution)/shard_map/ppermute | solution.py:342
  75.2 13.6 %collective-permute-start.16 = (bf16[288,384]{1,0:T(8,128)(2,1)S(1)}, bf16[288,384]{1,0:T(8,128)(2,1)S(1)}, u32[]{:S(2)}, u32[]{:S(2)}) collective-permute-start(bf16[288,384]{1,0:T(8,128)(2,1)S(1)} %slice.22), channel_id=1, source_target_pairs={{0,16},{16,0},{1,17},{17,1},{2,18},{18,2},{3,19},{19,3},{4,20},{20... | collective-permute-start | bytes 663560 | tf_op jit(solution)/shard_map/ppermute | solution.py:342
  75.9 16.7 %collective-permute-start.17 = (bf16[288,384]{1,0:T(8,128)(2,1)S(1)}, bf16[288,384]{1,0:T(8,128)(2,1)S(1)}, u32[]{:S(2)}, u32[]{:S(2)}) collective-permute-start(bf16[288,384]{1,0:T(8,128)(2,1)S(1)} %slice.23), channel_id=1, source_target_pairs={{0,16},{16,0},{1,17},{17,1},{2,18},{18,2},{3,19},{19,3},{4,20},{20... | collective-permute-start | bytes 663560 | tf_op jit(solution)/shard_map/ppermute | solution.py:342
  77.4 28.2 %collective-permute-start.18 = (bf16[512,384]{1,0:T(8,128)(2,1)S(1)}, bf16[512,384]{1,0:T(8,128)(2,1)S(1)}, u32[]{:S(2)}, u32[]{:S(2)}) collective-permute-start(bf16[512,384]{1,0:T(8,128)(2,1)S(1)} %get-tuple-element.120.refs_0_), channel_id=1, source_target_pairs={{0,8},{4,12},{8,0},{12,4},{1,9},{5,13},{9,1},{13,5},{2,10},{6,14},... | collective-permute-start | bytes 1179656 | tf_op jit(solution)/shard_map/ppermute | solution.py:432
  83.2 22.4 %collective-permute-start.19 = (bf16[512,384]{1,0:T(8,128)(2,1)S(1)}, bf16[512,384]{1,0:T(8,128)(2,1)S(1)}, u32[]{:S(2)}, u32[]{:S(2)}) collective-permute-start(bf16[512,384]{1,0:T(8,128)(2,1)S(1)} %get-tuple-element.120.refs_0_), channel_id=1, source_target_pairs={{0,4},{4,0},{8,12},{12,8},{1,5},{5,1},{9,13},{13,9},{2,6},{6,2},{1... | collective-permute-start | bytes 1179656 | tf_op jit(solution)/shard_map/ppermute | solution.py:433
  84.8 23.5 %collective-permute-start.20 = (bf16[272,128]{1,0:T(8,128)(2,1)S(1)}, bf16[272,128]{1,0:T(8,128)(2,1)S(1)}, u32[]{:S(2)}, u32[]{:S(2)}) collective-permute-start(bf16[272,128]{1,0:T(8,128)(2,1)S(1)} %get-tuple-element.109), channel_id=1, source_target_pairs={{0,4},{4,8},{8,12},{12,0},{1,5},{5,9},{9,13},{13,1},{2,6},{6,10},{... | collective-permute-start | bytes 208904 | tf_op jit(solution)/shard_map/ppermute | solution.py:342
  88.8 19.5 %collective-permute-start.21 = (bf16[272,128]{1,0:T(8,128)(2,1)S(1)}, bf16[272,128]{1,0:T(8,128)(2,1)S(1)}, u32[]{:S(2)}, u32[]{:S(2)}) collective-permute-start(bf16[272,128]{1,0:T(8,128)(2,1)S(1)} %get-tuple-element.110), channel_id=1, source_target_pairs={{0,8},{4,12},{8,0},{12,4},{1,9},{5,13},{9,1},{13,5},{2,10},{6,14},... | collective-permute-start | bytes 208904 | tf_op jit(solution)/shard_map/ppermute | solution.py:342
  92.5 15.8 %collective-permute-start.22 = (bf16[272,128]{1,0:T(8,128)(2,1)S(1)}, bf16[272,128]{1,0:T(8,128)(2,1)S(1)}, u32[]{:S(2)}, u32[]{:S(2)}) collective-permute-start(bf16[272,128]{1,0:T(8,128)(2,1)S(1)} %get-tuple-element.111), channel_id=1, source_target_pairs={{0,12},{4,0},{8,4},{12,8},{1,13},{5,1},{9,5},{13,9},{2,14},{6,2},{... | collective-permute-start | bytes 208904 | tf_op jit(solution)/shard_map/ppermute | solution.py:342
  105.6 11.4 %collective-permute-start.25 = (bf16[512,384]{1,0:T(8,128)(2,1)S(1)}, bf16[512,384]{1,0:T(8,128)(2,1)}, u32[]{:S(2)}, u32[]{:S(2)}) collective-permute-start(bf16[512,384]{1,0:T(8,128)(2,1)S(1)} %get-tuple-element.120.refs_0_), channel_id=1, source_target_pairs={{4,8},{8,4},{5,9},{9,5},{6,10},{10,6},{7,11},{11,7},{20,24},{24,20... | collective-permute-start | bytes 1179656 | tf_op jit(solution)/shard_map/ppermute | solution.py:438
  107.0 15.0 %collective-permute-start.26 = (bf16[512,384]{1,0:T(8,128)(2,1)S(1)}, bf16[512,384]{1,0:T(8,128)(2,1)}, u32[]{:S(2)}, u32[]{:S(2)}) collective-permute-start(bf16[512,384]{1,0:T(8,128)(2,1)S(1)} %collective-permute-done.18.refs_2_), channel_id=1, source_target_pairs={{8,12},{4,0},{9,13},{5,1},{10,14},{6,2},{11,15},{7,3},{24,28},{20,... | collective-permute-start | bytes 1179656 | tf_op jit(solution)/shard_map/ppermute | solution.py:439
  108.3 31.3 %collective-permute-start.23 = (bf16[512,384]{1,0:T(8,128)(2,1)S(1)}, bf16[512,384]{1,0:T(8,128)(2,1)S(1)}, u32[]{:S(2)}, u32[]{:S(2)}) collective-permute-start(bf16[512,384]{1,0:T(8,128)(2,1)S(1)} %get-tuple-element.126.refs_0_), channel_id=1, source_target_pairs={{0,8},{4,12},{8,0},{12,4},{1,9},{5,13},{9,1},{13,5},{2,10},{6,14},... | collective-permute-start | bytes 1179656 | tf_op jit(solution)/shard_map/ppermute | solution.py:432
  112.2 27.4 %collective-permute-start.24 = (bf16[512,384]{1,0:T(8,128)(2,1)S(1)}, bf16[512,384]{1,0:T(8,128)(2,1)S(1)}, u32[]{:S(2)}, u32[]{:S(2)}) collective-permute-start(bf16[512,384]{1,0:T(8,128)(2,1)S(1)} %get-tuple-element.126.refs_0_), channel_id=1, source_target_pairs={{0,4},{4,0},{8,12},{12,8},{1,5},{5,1},{9,13},{13,9},{2,6},{6,2},{1... | collective-permute-start | bytes 1179656 | tf_op jit(solution)/shard_map/ppermute | solution.py:433
  112.9 29.4 %all-to-all-start = ((bf16[4,272,128]{2,1,0:T(8,128)(2,1)}), bf16[4,272,128]{2,1,0:T(8,128)(2,1)S(1)}, u32[]{:S(2)}, u32[]{:S(2)}) async-start(bf16[4,272,128]{2,1,0:T(8,128)(2,1)} %get-tuple-element.116), calls=%async_computation | async-start | bytes 557056 | tf_op jit(solution)/shard_map/all_to_all | solution.py:427
  139.7 7.5 %collective-permute-start.27 = (bf16[512,384]{1,0:T(8,128)(2,1)S(1)}, bf16[512,384]{1,0:T(8,128)(2,1)S(1)}, u32[]{:S(2)}, u32[]{:S(2)}) collective-permute-start(bf16[512,384]{1,0:T(8,128)(2,1)S(1)} %get-tuple-element.126.refs_0_), channel_id=1, source_target_pairs={{4,8},{8,4},{5,9},{9,5},{6,10},{10,6},{7,11},{11,7},{20,24},{24,20... | collective-permute-start | bytes 1179656 | tf_op jit(solution)/shard_map/ppermute | solution.py:438
  140.4 10.0 %collective-permute-start.28 = (bf16[512,384]{1,0:T(8,128)(2,1)S(1)}, bf16[512,384]{1,0:T(8,128)(2,1)S(1)}, u32[]{:S(2)}, u32[]{:S(2)}) collective-permute-start(bf16[512,384]{1,0:T(8,128)(2,1)S(1)} %collective-permute-done.23.refs_2_), channel_id=1, source_target_pairs={{8,12},{4,0},{9,13},{5,1},{10,14},{6,2},{11,15},{7,3},{24,28},{20,... | collective-permute-start | bytes 1179656 | tf_op jit(solution)/shard_map/ppermute | solution.py:439
  (5 other events, 5.0 us)

commit v12 on v11

--- a/solution.py
+++ b/solution.py
@@ -399,7 +399,7 @@
     grads, backs = [], []
     for slot, direct in enumerate((first, second)):
         if slot:
-            swapped = [along(x[:half], "groups", 1) for x in direct]
+            swapped = [early] + [along(x[:half], "groups", 1) for x in direct[1:]]
         side = (2 * CHUNK + TAIL, DK)
         grad, *back = pl.pallas_call(
             functools.partial(head_kernel, ctx, slot),
@@ -422,7 +422,9 @@
             name=f"head_{slot}",
         )(where, all_tokens, packed[slot * ctx], *direct, *swapped)
         if not slot:
-            second[:], (grad, back) = after(second, (grad, back))
+            second[0], grad = after(second[0], grad)
+            early = along(second[0][:half], "groups", 1)
+            (second[1:], grad, back), early = after((second[1:], grad, back), early)
         if slot:
             backs.append(lax.all_to_all(back[0], "ctx", 0, 0))
         else:

time: 153 us -> 149 us (0.974)
  starting transfers between devices: 63.8 us -> 59.9 us
    ppermute x21, starting transfers between devices: 43.1 us -> 40 us  [along(): return lax.ppermute(x, axis, [(i, (i + hop) % count) for i in range(count)])]
  transfers between devices with their start and end apart: 30 -> 30, of which waited for: 8 -> 9; matrix products, arithmetic and copies ran while one was open for 0% -> 0% of each run, Pallas kernels for 20% -> 21%
where the time goes in v12:
time: 149 us; the launch traced here: 148 us
  starting transfers between devices  59.9 us (40%)
  waiting for transfers between devices  46.7 us (31%)
  Pallas kernels  33 us (22%)
  local copies, waits for them, and re-layouts  7.78 us (5%)
    ppermute x21, starting transfers between devices, along(): return lax.ppermute(x, axis, [(i, (i + hop) % count) for i in range(count)])  40 us
    ppermute x21, waiting for transfers between devices, along(): return lax.ppermute(x, axis, [(i, (i + hop) % count) for i in range(count)])  25.1 us
    pallas_call x2, Pallas kernels, head_split(): pl.pallas_call(functools.partial(head_kernel, ctx, slot), out_shape=[shap...  18 us
    ppermute x2, waiting for transfers between devices, head_split(): two = lax.ppermute(grad, 'ctx', [(0, 2), (1, 3), (2, 0), (3, 1)])  12.6 us
    pallas_call x3, Pallas kernels, products(): pl.pallas_call(functools.partial(weight_gradient_kernel, steps), grid_spe...  10.3 us
    ppermute x2, starting transfers between devices, head_split(): two = lax.ppermute(grad, 'ctx', [(0, 2), (1, 3), (2, 0), (3, 1)])  9.95 us
    ppermute x2, waiting for transfers between devices, head_split(): far = lax.ppermute(two, 'ctx', [(2, 3), (1, 0)])  8.1 us
    unnamed x14, local copies, waits for them, and re-layouts  7.55 us
  transfers between devices with their start and end apart: 30, of which 9 were waited for; matrix products, arithmetic and copies ran while one was open for 0% of the time, Pallas kernels for 21%

profile of v12, /device:TPU:0, one launch (start us, length us, event | category | flops | bytes accessed | tf_op | source)
XLA Modules:
  0.0 148.3 jit_solution(10606610941873290597)
XLA Ops:
  2.4 3.1 %collective-permute-start = (bf16[576,128]{1,0:T(8,128)(2,1)S(1)}, bf16[576,128]{1,0:T(8,128)(2,1)S(1)}, u32[]{:S(2)}, u32[]{:S(2)}) collective-permute-start(bf16[576,128]{1,0:T(8,128)(2,1)S(1)} %pack_tokens.1), channel_id=1, source_target_pairs={{0,4},{4,8},{8,12},{12,0},{1,5},{5,9},{9,13},{13,1},{2,6},{6,10},{... | collective-permute-start | bytes 442376 | tf_op jit(solution)/shard_map/ppermute | solution.py:342
  5.5 2.6 %collective-permute-start.1 = (bf16[576,128]{1,0:T(8,128)(2,1)S(1)}, bf16[576,128]{1,0:T(8,128)(2,1)S(1)}, u32[]{:S(2)}, u32[]{:S(2)}) collective-permute-start(bf16[576,128]{1,0:T(8,128)(2,1)S(1)} %pack_tokens.1), channel_id=1, source_target_pairs={{0,8},{4,12},{8,0},{12,4},{1,9},{5,13},{9,1},{13,5},{2,10},{6,14},... | collective-permute-start | bytes 442376 | tf_op jit(solution)/shard_map/ppermute | solution.py:342
  8.1 1.3 collective-permute-start.2
  17.9 1.6 %collective-permute-start.3 = (bf16[2304,128]{1,0:T(8,128)(2,1)S(1)}, bf16[2304,128]{1,0:T(8,128)(2,1)S(1)}, u32[]{:S(2)}, u32[]{:S(2)}) collective-permute-start(bf16[2304,128]{1,0:T(8,128)(2,1)S(1)} %pad_maximum_fusion.refs_0_), channel_id=1, source_target_pairs={{0,2},{2,0},{1,3},{3,1},{4,6},{6,4},{5,7},{7,5},{8,10},{10,8},{9,1... | collective-permute-start | bytes 1769480 | tf_op jit(solution)/shard_map/ppermute | solution.py:342
  19.5 3.6 %collective-permute-start.6 = (bf16[384,384]{1,0:T(8,128)(2,1)S(1)}, bf16[384,384]{1,0:T(8,128)(2,1)S(1)}, u32[]{:S(2)}, u32[]{:S(2)}) collective-permute-start(bf16[384,384]{1,0:T(8,128)(2,1)S(1)} %get-tuple-element.81), channel_id=1, source_target_pairs={{0,4},{4,8},{8,12},{12,0},{1,5},{5,9},{9,13},{13,1},{2,6},{6,10},{... | collective-permute-start | bytes 884744 | tf_op jit(solution)/shard_map/ppermute | solution.py:342
  23.1 1.6 %collective-permute-start.4 = (bf16[384,384]{1,0:T(8,128)(2,1)S(1)}, bf16[384,384]{1,0:T(8,128)(2,1)S(1)}, u32[]{:S(2)}, u32[]{:S(2)}) collective-permute-start(bf16[384,384]{1,0:T(8,128)(2,1)S(1)} %get-tuple-element.79), channel_id=1, source_target_pairs={{0,8},{4,12},{8,0},{12,4},{1,9},{5,13},{9,1},{13,5},{2,10},{6,14},... | collective-permute-start | bytes 884744 | tf_op jit(solution)/shard_map/ppermute | solution.py:342
  25.5 6.8 %collective-permute-done.6.refs_2_ = bf16[384,384]{1,0:T(8,128)(2,1)S(1)} collective-permute-done((bf16[384,384]{1,0:T(8,128)(2,1)S(1)}, bf16[384,384]{1,0:T(8,128)(2,1)S(1)}, u32[]{:S(2)}, u32[]{:S(2)}) %collective-permute-start.6) | collective-permute-done | bytes 294944 | tf_op jit(solution)/shard_map/ppermute | solution.py:342
  32.3 1.6 %collective-permute-start.7 = (bf16[288,384]{1,0:T(8,128)(2,1)S(1)}, bf16[288,384]{1,0:T(8,128)(2,1)S(1)}, u32[]{:S(2)}, u32[]{:S(2)}) collective-permute-start(bf16[288,384]{1,0:T(8,128)(2,1)S(1)} %slice.24), channel_id=1, source_target_pairs={{0,16},{16,0},{1,17},{17,1},{2,18},{18,2},{3,19},{19,3},{4,20},{20... | collective-permute-start | bytes 663560 | tf_op jit(solution)/shard_map/ppermute | solution.py:342
  33.9 9.1 %collective-permute-done.4.refs_3_ = bf16[384,384]{1,0:T(8,128)(2,1)S(1)} collective-permute-done((bf16[384,384]{1,0:T(8,128)(2,1)S(1)}, bf16[384,384]{1,0:T(8,128)(2,1)S(1)}, u32[]{:S(2)}, u32[]{:S(2)}) %collective-permute-start.4) | collective-permute-done | bytes 294944 | tf_op jit(solution)/shard_map/ppermute | solution.py:342
  43.5 1.6 %collective-permute-start.11 = (bf16[288,384]{1,0:T(8,128)(2,1)S(1)}, bf16[288,384]{1,0:T(8,128)(2,1)S(1)}, u32[]{:S(2)}, u32[]{:S(2)}) collective-permute-start(bf16[288,384]{1,0:T(8,128)(2,1)S(1)} %slice.19), channel_id=1, source_target_pairs={{0,16},{16,0},{1,17},{17,1},{2,18},{18,2},{3,19},{19,3},{4,20},{20... | collective-permute-start | bytes 663560 | tf_op jit(solution)/shard_map/ppermute | solution.py:342
  45.7 6.7 %collective-permute-start.10 = (bf16[384,384]{1,0:T(8,128)(2,1)S(1)}, bf16[384,384]{1,0:T(8,128)(2,1)S(1)}, u32[]{:S(2)}, u32[]{:S(2)}) collective-permute-start(bf16[384,384]{1,0:T(8,128)(2,1)S(1)} %get-tuple-element.91), channel_id=1, source_target_pairs={{0,4},{4,8},{8,12},{12,0},{1,5},{5,9},{9,13},{13,1},{2,6},{6,10},{... | collective-permute-start | bytes 884744 | tf_op jit(solution)/shard_map/ppermute | solution.py:342
  52.4 2.3 %collective-permute-start.13 = (bf16[384,384]{1,0:T(8,128)(2,1)S(1)}, bf16[384,384]{1,0:T(8,128)(2,1)S(1)}, u32[]{:S(2)}, u32[]{:S(2)}) collective-permute-start(bf16[384,384]{1,0:T(8,128)(2,1)S(1)} %get-tuple-element.98), channel_id=1, source_target_pairs={{0,8},{4,12},{8,0},{12,4},{1,9},{5,13},{9,1},{13,5},{2,10},{6,14},... | collective-permute-start | bytes 884744 | tf_op jit(solution)/shard_map/ppermute | solution.py:342
  56.1 8.7 %head_0.1 = (bf16[512,384]{1,0:T(8,128)(2,1)S(1)}, bf16[272,128]{1,0:T(8,128)(2,1)S(1)}, bf16[272,128]{1,0:T(8,128)(2,1)S(1)}, bf16[272,128]{1,0:T(8,128)(2,1)S(1)}, bf16[272,128]{1,0:T(8,128)(2,1)S(1)}) custom-call(s32[11]{0:T(128)S(1)} %stack.48.where_ref, bf16[4,512,576]{2,1,0:T(8,128)(2,1)S(1)} %get-tuple-element.84.refs_0_, ...), custom_call_target="tpu_custom_call" | custom-call | flops 12000000000 | bytes 12000000 | tf_op jit(solution)/shard_map/head_0/pallas_call | solution.py:404
  64.8 1.6 %collective-permute-start.15 = (bf16[288,384]{1,0:T(8,128)(2,1)S(1)}, bf16[288,384]{1,0:T(8,128)(2,1)S(1)}, u32[]{:S(2)}, u32[]{:S(2)}) collective-permute-start(bf16[288,384]{1,0:T(8,128)(2,1)S(1)} %slice.21), channel_id=1, source_target_pairs={{0,16},{16,0},{1,17},{17,1},{2,18},{18,2},{3,19},{19,3},{4,20},{20... | collective-permute-start | bytes 663560 | tf_op jit(solution)/shard_map/ppermute | solution.py:342
  66.4 7.2 %collective-permute-done.13.refs_3_ = bf16[384,384]{1,0:T(8,128)(2,1)S(1)} collective-permute-done((bf16[384,384]{1,0:T(8,128)(2,1)S(1)}, bf16[384,384]{1,0:T(8,128)(2,1)S(1)}, u32[]{:S(2)}, u32[]{:S(2)}) %collective-permute-start.13) | collective-permute-done | bytes 294944 | tf_op jit(solution)/shard_map/ppermute | solution.py:342
  73.7 1.6 %collective-permute-start.16 = (bf16[288,384]{1,0:T(8,128)(2,1)S(1)}, bf16[288,384]{1,0:T(8,128)(2,1)S(1)}, u32[]{:S(2)}, u32[]{:S(2)}) collective-permute-start(bf16[288,384]{1,0:T(8,128)(2,1)S(1)} %slice.22), channel_id=1, source_target_pairs={{0,16},{16,0},{1,17},{17,1},{2,18},{18,2},{3,19},{19,3},{4,20},{20... | collective-permute-start | bytes 663560 | tf_op jit(solution)/shard_map/ppermute | solution.py:342
  75.9 5.8 %collective-permute-start.18 = (bf16[512,384]{1,0:T(8,128)(2,1)S(1)}, bf16[512,384]{1,0:T(8,128)(2,1)S(1)}, u32[]{:S(2)}, u32[]{:S(2)}) collective-permute-start(bf16[512,384]{1,0:T(8,128)(2,1)S(1)} %get-tuple-element.124.refs_0_), channel_id=1, source_target_pairs={{0,8},{4,12},{8,0},{12,4},{1,9},{5,13},{9,1},{13,5},{2,10},{6,14},... | collective-permute-start | bytes 1179656 | tf_op jit(solution)/shard_map/ppermute | solution.py:434
  81.6 1.6 %collective-permute-start.19 = (bf16[512,384]{1,0:T(8,128)(2,1)S(1)}, bf16[512,384]{1,0:T(8,128)(2,1)S(1)}, u32[]{:S(2)}, u32[]{:S(2)}) collective-permute-start(bf16[512,384]{1,0:T(8,128)(2,1)S(1)} %get-tuple-element.124.refs_0_), channel_id=1, source_target_pairs={{0,4},{4,0},{8,12},{12,8},{1,5},{5,1},{9,13},{13,9},{2,6},{6,2},{1... | collective-permute-start | bytes 1179656 | tf_op jit(solution)/shard_map/ppermute | solution.py:435
  83.6 4.1 %collective-permute-start.21 = (bf16[272,128]{1,0:T(8,128)(2,1)S(1)}, bf16[272,128]{1,0:T(8,128)(2,1)S(1)}, u32[]{:S(2)}, u32[]{:S(2)}) collective-permute-start(bf16[272,128]{1,0:T(8,128)(2,1)S(1)} %get-tuple-element.114), channel_id=1, source_target_pairs={{0,8},{4,12},{8,0},{12,4},{1,9},{5,13},{9,1},{13,5},{2,10},{6,14},... | collective-permute-start | bytes 208904 | tf_op jit(solution)/shard_map/ppermute | solution.py:342
  87.8 3.7 %collective-permute-start.22 = (bf16[272,128]{1,0:T(8,128)(2,1)S(1)}, bf16[272,128]{1,0:T(8,128)(2,1)S(1)}, u32[]{:S(2)}, u32[]{:S(2)}) collective-permute-start(bf16[272,128]{1,0:T(8,128)(2,1)S(1)} %get-tuple-element.115), channel_id=1, source_target_pairs={{0,12},{4,0},{8,4},{12,8},{1,13},{5,1},{9,5},{13,9},{2,14},{6,2},{... | collective-permute-start | bytes 208904 | tf_op jit(solution)/shard_map/ppermute | solution.py:342
  91.5 9.4 %head_1.1 = (bf16[512,384]{1,0:T(8,128)(2,1)S(1)}, bf16[4,272,128]{2,1,0:T(8,128)(2,1)}) custom-call(s32[11]{0:T(128)S(1)} %stack.48.where_ref, bf16[4,512,576]{2,1,0:T(8,128)(2,1)S(1)} %get-tuple-element.84.refs_0_, bf16[672,384]{1,0:T(8,128)(2,1)S(1)} %get-tuple-element.85.refs_1_, bf16[384,384]{1,0:T(8,128)(2,1)S(1)} %collective-permute-done.10.refs_2_, ...), custom_call_target="tpu_custom_call" | custom-call | flops 12000000000 | bytes 12000000 | tf_op jit(solution)/shard_map/head_1/pallas_call | solution.py:404
  100.9 1.4 collective-permute-start.25
  103.6 1.3 collective-permute-done.20.refs_1_
  104.9 4.2 %collective-permute-start.23 = (bf16[512,384]{1,0:T(8,128)(2,1)S(1)}, bf16[512,384]{1,0:T(8,128)(2,1)S(1)}, u32[]{:S(2)}, u32[]{:S(2)}) collective-permute-start(bf16[512,384]{1,0:T(8,128)(2,1)S(1)} %get-tuple-element.130.refs_0_), channel_id=1, source_target_pairs={{0,8},{4,12},{8,0},{12,4},{1,9},{5,13},{9,1},{13,5},{2,10},{6,14},... | collective-permute-start | bytes 1179656 | tf_op jit(solution)/shard_map/ppermute | solution.py:434
  109.1 3.7 %all-to-all-start = ((bf16[4,272,128]{2,1,0:T(8,128)(2,1)}), bf16[4,272,128]{2,1,0:T(8,128)(2,1)S(1)}, u32[]{:S(2)}, u32[]{:S(2)}) async-start(bf16[4,272,128]{2,1,0:T(8,128)(2,1)} %get-tuple-element.120), calls=%async_computation | async-start | bytes 557056 | tf_op jit(solution)/shard_map/all_to_all | solution.py:429
  112.8 5.1 %collective-permute-done.26.refs_4_ = bf16[512,384]{1,0:T(8,128)(2,1)} collective-permute-done((bf16[512,384]{1,0:T(8,128)(2,1)S(1)}, bf16[512,384]{1,0:T(8,128)(2,1)}, u32[]{:S(2)}, u32[]{:S(2)}) %collective-permute-start.26) | collective-permute-done | bytes 393248 | tf_op jit(solution)/shard_map/ppermute | solution.py:441
  117.9 5.0 %weight_gradient_0_0.1 = (f32[576,1024]{1,0:T(8,128)}, f32[576,1024]{1,0:T(8,128)}, f32[576,1024]{1,0:T(8,128)}) custom-call(s32[11]{0:T(128)S(1)} %stack.48.where_ref, bf16[576,512]{1,0:T(8,128)(2,1)S(1)} %get-tuple-element.122.own_ref, bf16[512,384]{1,0:T(8,128)(2,1)S(1)} %get-tuple-element.124.refs_0_, ...), custom_call_target="tpu_custom_call" | custom-call | tf_op jit(solution)/shard_map/weight_gradient_0_0/pallas_call | solution.py:385
  122.9 12.6 %collective-permute-done.23.refs_2_ = bf16[512,384]{1,0:T(8,128)(2,1)S(1)} collective-permute-done((bf16[512,384]{1,0:T(8,128)(2,1)S(1)}, bf16[512,384]{1,0:T(8,128)(2,1)S(1)}, u32[]{:S(2)}, u32[]{:S(2)}) %collective-permute-start.23) | collective-permute-done | bytes 393248 | tf_op jit(solution)/shard_map/ppermute | solution.py:434
  138.4 1.5 %unpack.1 = (bf16[128,1024]{1,0:T(8,128)(2,1)}, f32[8,128]{1,0:T(8,128)}, f32[128,1024]{1,0:T(8,128)}) custom-call(s32[11]{0:T(128)S(1)} %stack.48.where_ref, bf16[272,128]{1,0:T(8,128)(2,1)S(1)} %get-tuple-element.116.refs_0_, bf16[272,128]{1,0:T(8,128)(2,1)S(1)} %collective-permute-done.20.refs_1_, bf16[272,128]{1,0:T(8,128)(2,1)S(1)} %collective-permute-done.21.refs_2_, ...), custom_call_target="tpu_custom_call" | custom-call | tf_op jit(solution)/shard_map/unpack/pallas_call | solution.py:446
  139.9 3.4 %weight_gradient_1_0.1 = (f32[576,1024]{1,0:T(8,128)}, f32[576,1024]{1,0:T(8,128)}, f32[576,1024]{1,0:T(8,128)}) custom-call(s32[11]{0:T(128)S(1)} %stack.48.where_ref, bf16[576,512]{1,0:T(8,128)(2,1)S(1)} %get-tuple-element.122.own_ref, bf16[512,384]{1,0:T(8,128)(2,1)S(1)} %get-tuple-element.130.refs_0_, ...), custom_call_target="tpu_custom_call", output_to_operand_aliasing={{0}: (5, {}), {1}: (6, {}), {2}: (7, {})} | custom-call | tf_op jit(solution)/shard_map/weight_gradient_1_0/pallas_call | solution.py:385
  143.3 3.0 %collective-permute-done.28.refs_1_ = bf16[512,384]{1,0:T(8,128)(2,1)S(1)} collective-permute-done((bf16[512,384]{1,0:T(8,128)(2,1)S(1)}, bf16[512,384]{1,0:T(8,128)(2,1)S(1)}, u32[]{:S(2)}, u32[]{:S(2)}) %collective-permute-start.28) | collective-permute-done | bytes 393248 | tf_op jit(solution)/shard_map/ppermute | solution.py:441
  146.3 1.9 %weight_gradient_1_3.1 = (f32[576,1024]{1,0:T(8,128)}, f32[576,1024]{1,0:T(8,128)}, f32[576,1024]{1,0:T(8,128)}) custom-call(s32[11]{0:T(128)S(1)} %stack.48.where_ref, bf16[576,512]{1,0:T(8,128)(2,1)S(1)} %get-tuple-element.122.own_ref, ...), custom_call_target="tpu_custom_call", output_to_operand_aliasing={{0}: (4, {}), {1}: (5, {}), {2}: (6, {})} | custom-call | tf_op jit(solution)/shard_map/weight_gradient_1_3/pallas_call | solution.py:385
  (59 shorter events, 18.9 us)
Async XLA Ops:
  2.4 14.8 %collective-permute-start = (bf16[576,128]{1,0:T(8,128)(2,1)S(1)}, bf16[576,128]{1,0:T(8,128)(2,1)S(1)}, u32[]{:S(2)}, u32[]{:S(2)}) collective-permute-start(bf16[576,128]{1,0:T(8,128)(2,1)S(1)} %pack_tokens.1), channel_id=1, source_target_pairs={{0,4},{4,8},{8,12},{12,0},{1,5},{5,9},{9,13},{13,1},{2,6},{6,10},{... | collective-permute-start | bytes 442376 | tf_op jit(solution)/shard_map/ppermute | solution.py:342
  5.5 12.4 %collective-permute-start.1 = (bf16[576,128]{1,0:T(8,128)(2,1)S(1)}, bf16[576,128]{1,0:T(8,128)(2,1)S(1)}, u32[]{:S(2)}, u32[]{:S(2)}) collective-permute-start(bf16[576,128]{1,0:T(8,128)(2,1)S(1)} %pack_tokens.1), channel_id=1, source_target_pairs={{0,8},{4,12},{8,0},{12,4},{1,9},{5,13},{9,1},{13,5},{2,10},{6,14},... | collective-permute-start | bytes 442376 | tf_op jit(solution)/shard_map/ppermute | solution.py:342
  8.1 9.8 %collective-permute-start.2 = (bf16[576,128]{1,0:T(8,128)(2,1)S(1)}, bf16[576,128]{1,0:T(8,128)(2,1)S(1)}, u32[]{:S(2)}, u32[]{:S(2)}) collective-permute-start(bf16[576,128]{1,0:T(8,128)(2,1)S(1)} %pack_tokens.1), channel_id=1, source_target_pairs={{0,12},{4,0},{8,4},{12,8},{1,13},{5,1},{9,5},{13,9},{2,14},{6,2},{... | collective-permute-start | bytes 442376 | tf_op jit(solution)/shard_map/ppermute | solution.py:342
  9.4 1.3 copy-start
  10.7 1.3 copy-start.1
  17.9 25.0 %collective-permute-start.3 = (bf16[2304,128]{1,0:T(8,128)(2,1)S(1)}, bf16[2304,128]{1,0:T(8,128)(2,1)S(1)}, u32[]{:S(2)}, u32[]{:S(2)}) collective-permute-start(bf16[2304,128]{1,0:T(8,128)(2,1)S(1)} %pad_maximum_fusion.refs_0_), channel_id=1, source_target_pairs={{0,2},{2,0},{1,3},{3,1},{4,6},{6,4},{5,7},{7,5},{8,10},{10,8},{9,1... | collective-permute-start | bytes 1769480 | tf_op jit(solution)/shard_map/ppermute | solution.py:342
  19.5 12.8 %collective-permute-start.6 = (bf16[384,384]{1,0:T(8,128)(2,1)S(1)}, bf16[384,384]{1,0:T(8,128)(2,1)S(1)}, u32[]{:S(2)}, u32[]{:S(2)}) collective-permute-start(bf16[384,384]{1,0:T(8,128)(2,1)S(1)} %get-tuple-element.81), channel_id=1, source_target_pairs={{0,4},{4,8},{8,12},{12,0},{1,5},{5,9},{9,13},{13,1},{2,6},{6,10},{... | collective-permute-start | bytes 884744 | tf_op jit(solution)/shard_map/ppermute | solution.py:342
  23.1 19.8 %collective-permute-start.4 = (bf16[384,384]{1,0:T(8,128)(2,1)S(1)}, bf16[384,384]{1,0:T(8,128)(2,1)S(1)}, u32[]{:S(2)}, u32[]{:S(2)}) collective-permute-start(bf16[384,384]{1,0:T(8,128)(2,1)S(1)} %get-tuple-element.79), channel_id=1, source_target_pairs={{0,8},{4,12},{8,0},{12,4},{1,9},{5,13},{9,1},{13,5},{2,10},{6,14},... | collective-permute-start | bytes 884744 | tf_op jit(solution)/shard_map/ppermute | solution.py:342
  24.7 18.2 %collective-permute-start.5 = (bf16[384,384]{1,0:T(8,128)(2,1)S(1)}, bf16[384,384]{1,0:T(8,128)(2,1)S(1)}, u32[]{:S(2)}, u32[]{:S(2)}) collective-permute-start(bf16[384,384]{1,0:T(8,128)(2,1)S(1)} %get-tuple-element.80), channel_id=1, source_target_pairs={{0,12},{4,0},{8,4},{12,8},{1,13},{5,1},{9,5},{13,9},{2,14},{6,2},{... | collective-permute-start | bytes 884744 | tf_op jit(solution)/shard_map/ppermute | solution.py:342
  32.3 10.6 %collective-permute-start.7 = (bf16[288,384]{1,0:T(8,128)(2,1)S(1)}, bf16[288,384]{1,0:T(8,128)(2,1)S(1)}, u32[]{:S(2)}, u32[]{:S(2)}) collective-permute-start(bf16[288,384]{1,0:T(8,128)(2,1)S(1)} %slice.24), channel_id=1, source_target_pairs={{0,16},{16,0},{1,17},{17,1},{2,18},{18,2},{3,19},{19,3},{4,20},{20... | collective-permute-start | bytes 663560 | tf_op jit(solution)/shard_map/ppermute | solution.py:342
  42.9 9.5 %collective-permute-start.8 = (bf16[2304,128]{1,0:T(8,128)(2,1)S(1)}, bf16[2304,128]{1,0:T(8,128)(2,1)S(1)}, u32[]{:S(2)}, u32[]{:S(2)}) collective-permute-start(bf16[2304,128]{1,0:T(8,128)(2,1)S(1)} %pad_maximum_fusion.refs_0_), channel_id=1, source_target_pairs={{0,1},{1,0},{2,3},{3,2},{4,5},{5,4},{6,7},{7,6},{8,9},{9,8},{10,11... | collective-permute-start | bytes 1769480 | tf_op jit(solution)/shard_map/ppermute | solution.py:342
  43.0 11.7 %collective-permute-start.9 = (bf16[2304,128]{1,0:T(8,128)(2,1)S(1)}, bf16[2304,128]{1,0:T(8,128)(2,1)S(1)}, u32[]{:S(2)}, u32[]{:S(2)}) collective-permute-start(bf16[2304,128]{1,0:T(8,128)(2,1)S(1)} %collective-permute-done.3.refs_1_), channel_id=1, source_target_pairs={{0,1},{1,0},{2,3},{3,2},{4,5},{5,4},{6,7},{7,6},{8,9},{9,8},{10,11... | collective-permute-start | bytes 1769480 | tf_op jit(solution)/shard_map/ppermute | solution.py:342
  43.5 12.6 %collective-permute-start.11 = (bf16[288,384]{1,0:T(8,128)(2,1)S(1)}, bf16[288,384]{1,0:T(8,128)(2,1)S(1)}, u32[]{:S(2)}, u32[]{:S(2)}) collective-permute-start(bf16[288,384]{1,0:T(8,128)(2,1)S(1)} %slice.19), channel_id=1, source_target_pairs={{0,16},{16,0},{1,17},{17,1},{2,18},{18,2},{3,19},{19,3},{4,20},{20... | collective-permute-start | bytes 663560 | tf_op jit(solution)/shard_map/ppermute | solution.py:342
  45.1 11.0 %collective-permute-start.12 = (bf16[288,384]{1,0:T(8,128)(2,1)S(1)}, bf16[288,384]{1,0:T(8,128)(2,1)S(1)}, u32[]{:S(2)}, u32[]{:S(2)}) collective-permute-start(bf16[288,384]{1,0:T(8,128)(2,1)S(1)} %slice.20), channel_id=1, source_target_pairs={{0,16},{16,0},{1,17},{17,1},{2,18},{18,2},{3,19},{19,3},{4,20},{20... | collective-permute-start | bytes 663560 | tf_op jit(solution)/shard_map/ppermute | solution.py:342
  45.7 19.1 %collective-permute-start.10 = (bf16[384,384]{1,0:T(8,128)(2,1)S(1)}, bf16[384,384]{1,0:T(8,128)(2,1)S(1)}, u32[]{:S(2)}, u32[]{:S(2)}) collective-permute-start(bf16[384,384]{1,0:T(8,128)(2,1)S(1)} %get-tuple-element.91), channel_id=1, source_target_pairs={{0,4},{4,8},{8,12},{12,0},{1,5},{5,9},{9,13},{13,1},{2,6},{6,10},{... | collective-permute-start | bytes 884744 | tf_op jit(solution)/shard_map/ppermute | solution.py:342
  52.4 21.2 %collective-permute-start.13 = (bf16[384,384]{1,0:T(8,128)(2,1)S(1)}, bf16[384,384]{1,0:T(8,128)(2,1)S(1)}, u32[]{:S(2)}, u32[]{:S(2)}) collective-permute-start(bf16[384,384]{1,0:T(8,128)(2,1)S(1)} %get-tuple-element.98), channel_id=1, source_target_pairs={{0,8},{4,12},{8,0},{12,4},{1,9},{5,13},{9,1},{13,5},{2,10},{6,14},... | collective-permute-start | bytes 884744 | tf_op jit(solution)/shard_map/ppermute | solution.py:342
  54.7 18.9 %collective-permute-start.14 = (bf16[384,384]{1,0:T(8,128)(2,1)S(1)}, bf16[384,384]{1,0:T(8,128)(2,1)S(1)}, u32[]{:S(2)}, u32[]{:S(2)}) collective-permute-start(bf16[384,384]{1,0:T(8,128)(2,1)S(1)} %get-tuple-element.99), channel_id=1, source_target_pairs={{0,12},{4,0},{8,4},{12,8},{1,13},{5,1},{9,5},{13,9},{2,14},{6,2},{... | collective-permute-start | bytes 884744 | tf_op jit(solution)/shard_map/ppermute | solution.py:342
  64.8 8.8 %collective-permute-start.15 = (bf16[288,384]{1,0:T(8,128)(2,1)S(1)}, bf16[288,384]{1,0:T(8,128)(2,1)S(1)}, u32[]{:S(2)}, u32[]{:S(2)}) collective-permute-start(bf16[288,384]{1,0:T(8,128)(2,1)S(1)} %slice.21), channel_id=1, source_target_pairs={{0,16},{16,0},{1,17},{17,1},{2,18},{18,2},{3,19},{19,3},{4,20},{20... | collective-permute-start | bytes 663560 | tf_op jit(solution)/shard_map/ppermute | solution.py:342
  73.7 10.0 %collective-permute-start.16 = (bf16[288,384]{1,0:T(8,128)(2,1)S(1)}, bf16[288,384]{1,0:T(8,128)(2,1)S(1)}, u32[]{:S(2)}, u32[]{:S(2)}) collective-permute-start(bf16[288,384]{1,0:T(8,128)(2,1)S(1)} %slice.22), channel_id=1, source_target_pairs={{0,16},{16,0},{1,17},{17,1},{2,18},{18,2},{3,19},{19,3},{4,20},{20... | collective-permute-start | bytes 663560 | tf_op jit(solution)/shard_map/ppermute | solution.py:342
  75.2 12.5 %collective-permute-start.17 = (bf16[288,384]{1,0:T(8,128)(2,1)S(1)}, bf16[288,384]{1,0:T(8,128)(2,1)S(1)}, u32[]{:S(2)}, u32[]{:S(2)}) collective-permute-start(bf16[288,384]{1,0:T(8,128)(2,1)S(1)} %slice.23), channel_id=1, source_target_pairs={{0,16},{16,0},{1,17},{17,1},{2,18},{18,2},{3,19},{19,3},{4,20},{20... | collective-permute-start | bytes 663560 | tf_op jit(solution)/shard_map/ppermute | solution.py:342
  75.9 25.0 %collective-permute-start.18 = (bf16[512,384]{1,0:T(8,128)(2,1)S(1)}, bf16[512,384]{1,0:T(8,128)(2,1)S(1)}, u32[]{:S(2)}, u32[]{:S(2)}) collective-permute-start(bf16[512,384]{1,0:T(8,128)(2,1)S(1)} %get-tuple-element.124.refs_0_), channel_id=1, source_target_pairs={{0,8},{4,12},{8,0},{12,4},{1,9},{5,13},{9,1},{13,5},{2,10},{6,14},... | collective-permute-start | bytes 1179656 | tf_op jit(solution)/shard_map/ppermute | solution.py:434
  81.6 19.3 %collective-permute-start.19 = (bf16[512,384]{1,0:T(8,128)(2,1)S(1)}, bf16[512,384]{1,0:T(8,128)(2,1)S(1)}, u32[]{:S(2)}, u32[]{:S(2)}) collective-permute-start(bf16[512,384]{1,0:T(8,128)(2,1)S(1)} %get-tuple-element.124.refs_0_), channel_id=1, source_target_pairs={{0,4},{4,0},{8,12},{12,8},{1,5},{5,1},{9,13},{13,9},{2,6},{6,2},{1... | collective-permute-start | bytes 1179656 | tf_op jit(solution)/shard_map/ppermute | solution.py:435
  83.2 21.7 %collective-permute-start.20 = (bf16[272,128]{1,0:T(8,128)(2,1)S(1)}, bf16[272,128]{1,0:T(8,128)(2,1)S(1)}, u32[]{:S(2)}, u32[]{:S(2)}) collective-permute-start(bf16[272,128]{1,0:T(8,128)(2,1)S(1)} %get-tuple-element.113), channel_id=1, source_target_pairs={{0,4},{4,8},{8,12},{12,0},{1,5},{5,9},{9,13},{13,1},{2,6},{6,10},{... | collective-permute-start | bytes 208904 | tf_op jit(solution)/shard_map/ppermute | solution.py:342
  83.6 21.3 %collective-permute-start.21 = (bf16[272,128]{1,0:T(8,128)(2,1)S(1)}, bf16[272,128]{1,0:T(8,128)(2,1)S(1)}, u32[]{:S(2)}, u32[]{:S(2)}) collective-permute-start(bf16[272,128]{1,0:T(8,128)(2,1)S(1)} %get-tuple-element.114), channel_id=1, source_target_pairs={{0,8},{4,12},{8,0},{12,4},{1,9},{5,13},{9,1},{13,5},{2,10},{6,14},... | collective-permute-start | bytes 208904 | tf_op jit(solution)/shard_map/ppermute | solution.py:342
  87.8 17.1 %collective-permute-start.22 = (bf16[272,128]{1,0:T(8,128)(2,1)S(1)}, bf16[272,128]{1,0:T(8,128)(2,1)S(1)}, u32[]{:S(2)}, u32[]{:S(2)}) collective-permute-start(bf16[272,128]{1,0:T(8,128)(2,1)S(1)} %get-tuple-element.115), channel_id=1, source_target_pairs={{0,12},{4,0},{8,4},{12,8},{1,13},{5,1},{9,5},{13,9},{2,14},{6,2},{... | collective-permute-start | bytes 208904 | tf_op jit(solution)/shard_map/ppermute | solution.py:342
  100.9 11.9 %collective-permute-start.25 = (bf16[512,384]{1,0:T(8,128)(2,1)S(1)}, bf16[512,384]{1,0:T(8,128)(2,1)}, u32[]{:S(2)}, u32[]{:S(2)}) collective-permute-start(bf16[512,384]{1,0:T(8,128)(2,1)S(1)} %get-tuple-element.124.refs_0_), channel_id=1, source_target_pairs={{4,8},{8,4},{5,9},{9,5},{6,10},{10,6},{7,11},{11,7},{20,24},{24,20... | collective-permute-start | bytes 1179656 | tf_op jit(solution)/shard_map/ppermute | solution.py:440
  102.3 15.6 %collective-permute-start.26 = (bf16[512,384]{1,0:T(8,128)(2,1)S(1)}, bf16[512,384]{1,0:T(8,128)(2,1)}, u32[]{:S(2)}, u32[]{:S(2)}) collective-permute-start(bf16[512,384]{1,0:T(8,128)(2,1)S(1)} %collective-permute-done.18.refs_2_), channel_id=1, source_target_pairs={{8,12},{4,0},{9,13},{5,1},{10,14},{6,2},{11,15},{7,3},{24,28},{20,... | collective-permute-start | bytes 1179656 | tf_op jit(solution)/shard_map/ppermute | solution.py:441
  104.9 30.6 %collective-permute-start.23 = (bf16[512,384]{1,0:T(8,128)(2,1)S(1)}, bf16[512,384]{1,0:T(8,128)(2,1)S(1)}, u32[]{:S(2)}, u32[]{:S(2)}) collective-permute-start(bf16[512,384]{1,0:T(8,128)(2,1)S(1)} %get-tuple-element.130.refs_0_), channel_id=1, source_target_pairs={{0,8},{4,12},{8,0},{12,4},{1,9},{5,13},{9,1},{13,5},{2,10},{6,14},... | collective-permute-start | bytes 1179656 | tf_op jit(solution)/shard_map/ppermute | solution.py:434
  109.1 26.4 %collective-permute-start.24 = (bf16[512,384]{1,0:T(8,128)(2,1)S(1)}, bf16[512,384]{1,0:T(8,128)(2,1)S(1)}, u32[]{:S(2)}, u32[]{:S(2)}) collective-permute-start(bf16[512,384]{1,0:T(8,128)(2,1)S(1)} %get-tuple-element.130.refs_0_), channel_id=1, source_target_pairs={{0,4},{4,0},{8,12},{12,8},{1,5},{5,1},{9,13},{13,9},{2,6},{6,2},{1... | collective-permute-start | bytes 1179656 | tf_op jit(solution)/shard_map/ppermute | solution.py:435
  109.1 29.3 %all-to-all-start = ((bf16[4,272,128]{2,1,0:T(8,128)(2,1)}), bf16[4,272,128]{2,1,0:T(8,128)(2,1)S(1)}, u32[]{:S(2)}, u32[]{:S(2)}) async-start(bf16[4,272,128]{2,1,0:T(8,128)(2,1)} %get-tuple-element.120), calls=%async_computation | async-start | bytes 557056 | tf_op jit(solution)/shard_map/all_to_all | solution.py:429
  135.5 7.8 %collective-permute-start.27 = (bf16[512,384]{1,0:T(8,128)(2,1)S(1)}, bf16[512,384]{1,0:T(8,128)(2,1)S(1)}, u32[]{:S(2)}, u32[]{:S(2)}) collective-permute-start(bf16[512,384]{1,0:T(8,128)(2,1)S(1)} %get-tuple-element.130.refs_0_), channel_id=1, source_target_pairs={{4,8},{8,4},{5,9},{9,5},{6,10},{10,6},{7,11},{11,7},{20,24},{24,20... | collective-permute-start | bytes 1179656 | tf_op jit(solution)/shard_map/ppermute | solution.py:440
  136.2 10.1 %collective-permute-start.28 = (bf16[512,384]{1,0:T(8,128)(2,1)S(1)}, bf16[512,384]{1,0:T(8,128)(2,1)S(1)}, u32[]{:S(2)}, u32[]{:S(2)}) collective-permute-start(bf16[512,384]{1,0:T(8,128)(2,1)S(1)} %collective-permute-done.23.refs_2_), channel_id=1, source_target_pairs={{8,12},{4,0},{9,13},{5,1},{10,14},{6,2},{11,15},{7,3},{24,28},{20,... | collective-permute-start | bytes 1179656 | tf_op jit(solution)/shard_map/ppermute | solution.py:441
  (5 other events, 5.0 us)
